TPU v7x, 512 devices: a whole 4x4x16 slice. The times are simulated.
512 devices in a mesh: dp: 8 (over z_hi, y), mp: 64 (over z_lo, x, core).
Axes of the slice: x: 4, y: 4, z: 16 (z_hi: 2, z_lo: 8; z = z_hi * 8 + z_lo), core: 2. Of those that a mesh axis runs over, the one named last changes fastest.
Arguments:
- tokens: bfloat16 [512, 6144], P(('dp', 'mp')), may hold values from -6 to 6
- w_in: bfloat16 [6144, 24576], P('dp', 'mp'), may hold values from -0.078125 to 0.078125
- w_out: bfloat16 [24576, 6144], P('mp', 'dp'), may hold values from -0.0390625 to 0.0390625
- cotangent: bfloat16 [512, 6144], P(('dp', 'mp')), may hold values from -6 to 6
Outputs:
- mixed: bfloat16 [512, 6144], P(('dp', 'mp'))
- grad_tokens: bfloat16 [512, 6144], P(('dp', 'mp'))
- grad_w_in: float32 [6144, 24576], P('dp', 'mp')
- grad_w_out: float32 [24576, 6144], P('mp', 'dp')
All inputs are finite; a program needn't handle non-finite values.
Results may differ from a plain program's by a relative error of at most 0.0054.
Values may be sent and summed in bfloat16 or wider, within the bound.
No kernel may reach another device: no remote copies, remote signals or barrier semaphores. Data moves between devices by JAX's collectives and lax.ppermute only.
A program may use at most 64 MiB of HBM per device.

v0:
```python
import jax
import jax.numpy as jnp
from jax import lax
from jax.sharding import PartitionSpec as P

epsilon = 1e-06


def gelu_tanh(values):
    return jax.nn.gelu(values, approximate=True)


def gelu_grad(pre_values, upstream):
    return jax.vjp(gelu_tanh, pre_values)[1](upstream)[0]


def spread(local_rows):
    row_count, feature_count = local_rows.shape
    groups = lax.axis_size("dp")
    width_block = feature_count // groups
    gathered = lax.all_gather(local_rows, "mp", axis=0, tiled=True)
    shaped = gathered.reshape(1, gathered.shape[0], groups, width_block)
    traded = lax.all_to_all(shaped, "dp", split_axis=2, concat_axis=0, tiled=True)
    return traded.reshape(groups * traded.shape[1], width_block)


def collect(partial_value, row_count):
    groups = lax.axis_size("dp")
    peer_count = lax.axis_size("mp")
    width_block = partial_value.shape[1]
    shaped = partial_value.reshape(groups, peer_count, row_count, width_block)
    summed = jnp.sum(lax.all_to_all(shaped, "mp", split_axis=1, concat_axis=1, tiled=True), axis=1)
    arrived = lax.all_to_all(summed, "dp", split_axis=0, concat_axis=2, tiled=True)
    return arrived.reshape(row_count, groups * width_block)


def group_total(term):
    return lax.psum(term, "dp")


def local(tokens, w_in, w_out, cotangent):
    contract_last = (((1,), (1,)), ((), ()))
    contract_first = (((0,), (0,)), ((), ()))
    tokens_wide = tokens.astype(jnp.float32)
    row_mean = jnp.mean(tokens_wide, axis=1, keepdims=True)
    centered = tokens_wide - row_mean
    inv_scale = lax.rsqrt(jnp.mean(centered * centered, axis=1, keepdims=True) + epsilon)
    unit_rows = centered * inv_scale
    normed = unit_rows.astype(jnp.bfloat16)
    row_count = tokens.shape[0]
    flat_normed = spread(normed)
    flat_grad = spread(cotangent)
    pre_all = group_total(jnp.dot(flat_normed, w_in, preferred_element_type=jnp.float32))
    act_all = gelu_tanh(pre_all).astype(jnp.bfloat16)
    branch_out = collect(jnp.dot(act_all, w_out, preferred_element_type=jnp.float32), row_count)
    mixed = (tokens_wide + branch_out).astype(jnp.bfloat16)
    act_grad = group_total(
        lax.dot_general(flat_grad, w_out, contract_last, preferred_element_type=jnp.float32)
    )
    pre_grad = gelu_grad(pre_all, act_grad).astype(jnp.bfloat16)
    grad_w_out = lax.dot_general(
        act_all, flat_grad, contract_first, preferred_element_type=jnp.float32
    )
    grad_w_in = lax.dot_general(
        flat_normed, pre_grad, contract_first, preferred_element_type=jnp.float32
    )
    normed_grad = collect(
        lax.dot_general(pre_grad, w_in, contract_last, preferred_element_type=jnp.float32),
        row_count,
    )
    row_inner = jnp.mean(normed_grad * unit_rows, axis=1, keepdims=True)
    through = inv_scale * (
        normed_grad - jnp.mean(normed_grad, axis=1, keepdims=True) - unit_rows * row_inner
    )
    grad_tokens = (cotangent.astype(jnp.float32) + through).astype(jnp.bfloat16)
    return (mixed, grad_tokens, grad_w_in, grad_w_out)


def solution(mesh):
    return jax.shard_map(
        local,
        mesh=mesh,
        in_specs=(P(("dp", "mp"), None), P("dp", "mp"), P("mp", "dp"), P(("dp", "mp"), None)),
        out_specs=(P(("dp", "mp"), None), P(("dp", "mp"), None), P("dp", "mp"), P("mp", "dp")),
        check_vma=False,
    )
```

profile of v0, /device:TPU:6, one launch (start us, length us, event | category | flops | bytes accessed | tf_op | source)
XLA Modules:
  0.0 757.5 jit_solution(10573223621665218163)
XLA Ops:
  7.2 0.0 copy-start
  7.2 1.5 convert_reduce_fusion
  9.3 1.4 multiply_reduce_fusion.1
  11.4 0.8 convert_bitcast_fusion
  12.2 118.5 %all-gather = bf16[64,1,6144]{2,1,0:T(2,128)(2,1)S(1)} all-gather(bf16[1,1,6144]{2,1,0:T(2,128)(2,1)S(1)} %convert_bitcast_fusion), channel_id=1, replica_groups=mesh['dp'=8,'mp'=64] {'mp'}, dimensions={0}, use_global_device_ids=true | all-gather | bytes 798720 | tf_op jit(solution)/shard_map/all_gather | solution.py:21
  130.7 4.7 reduce.7
  135.4 0.1 copy.14
  135.5 0.0 copy-start.5
  135.5 1.0 copy.10
  136.6 6.8 all-to-all-start
  143.3 0.0 copy-done.5
  143.3 140.7 %all-gather.1 = bf16[64,1,6144]{2,1,0:T(2,128)(2,1)S(1)} all-gather(bf16[1,1,6144]{2,1,0:T(2,128)(2,1)S(1)} %bitcast.46), channel_id=1, replica_groups=mesh['dp'=8,'mp'=64] {'mp'}, dimensions={0}, use_global_device_ids=true | all-gather | bytes 798720 | tf_op jit(solution)/shard_map/all_gather | solution.py:21
  284.1 5.6 reduce.8
  289.6 1.3 copy.15
  290.9 1.0 copy.12
  291.9 0.0 copy-start.3
  291.9 0.0 all-to-all-done
  291.9 17.4 %all-to-all-start.3 = ((bf16[1,64,8,768]{3,1,0,2:T(8,128)(2,1)}), bf16[1,64,8,768]{3,1,0,2:T(8,128)(2,1)S(1)}, u32[]{:S(2)}, u32[]{:S(2)}) async-start(bf16[1,64,8,768]{3,1,0,2:T(8,128)(2,1)} %copy.12), calls=%async_computation.3 | async-start | bytes 1572864 | tf_op jit(solution)/shard_map/all_to_all | solution.py:23
  309.3 0.0 all-reduce.3.cloned.1.call-start
  309.4 0.0 copy-done
  309.4 1.5 fusion.10
  310.8 21.2 %all-to-all-done.3 = bf16[1,64,8,768]{3,1,0,2:T(8,128)(2,1)S(1)} async-done(((bf16[1,64,8,768]{3,1,0,2:T(8,128)(2,1)}), bf16[1,64,8,768]{3,1,0,2:T(8,128)(2,1)S(1)}, u32[]{:S(2)}, u32[]{:S(2)}) %all-to-all-start.3) | async-done | bytes 786464 | tf_op jit(solution)/shard_map/all_to_all | solution.py:23
  332.0 0.0 copy-start.2
  332.0 0.0 copy-done.3
  332.0 1.5 fusion.11
  333.5 0.0 all-reduce.3.cloned.1.call-update
  333.5 0.0 copy-done.2
  333.5 199.2 %all-reduce.3.cloned.1.call-done = (f32[512,384]{1,0:T(8,128)}, f32[512,384]{1,0:T(8,128)}) async-done(((f32[512,384]{1,0:T(8,128)}, f32[512,384]{1,0:T(8,128)}), (f32[512,384]{1,0:T(8,128)}, f32[512,384]{1,0:T(8,128)})) %all-reduce.3.cloned.1.call-update) | async-done | bytes 1572880 | tf_op jit(solution)/shard_map/psum | solution.py:38
  532.7 1.9 fusion.6
  534.6 0.6 fusion.12
  535.2 2.1 copy.13
  537.3 15.0 %all-to-all-start.4 = ((f32[8,64,1,768]{3,0,2,1:T(8,128)}), f32[8,64,1,768]{3,0,2,1:T(8,128)S(1)}, u32[]{:S(2)}, u32[]{:S(2)}) async-start(f32[8,64,1,768]{3,0,2,1:T(8,128)} %copy.13), calls=%async_computation.4 | async-start | bytes 3145728 | tf_op jit(solution)/shard_map/all_to_all | solution.py:32
  552.2 2.0 fusion.9
  554.2 2.1 copy.11
  556.3 69.7 %all-to-all-done.4 = f32[8,64,1,768]{3,0,2,1:T(8,128)S(1)} async-done(((f32[8,64,1,768]{3,0,2,1:T(8,128)}), f32[8,64,1,768]{3,0,2,1:T(8,128)S(1)}, u32[]{:S(2)}, u32[]{:S(2)}) %all-to-all-start.4) | async-done | bytes 1572896 | tf_op jit(solution)/shard_map/all_to_all | solution.py:32
  626.0 0.0 copy-start.1
  626.0 1.1 copy-done.1
  627.1 8.0 %all-to-all-start.1 = ((f32[8,64,1,768]{3,0,2,1:T(8,128)}), f32[8,64,1,768]{3,0,2,1:T(8,128)S(1)}, u32[]{:S(2)}, u32[]{:S(2)}) async-start(f32[8,64,1,768]{3,0,2,1:T(8,128)} %copy.11), calls=%async_computation.1 | async-start | bytes 3145728 | tf_op jit(solution)/shard_map/all_to_all | solution.py:32
  635.1 3.0 fusion.8
  638.1 1.5 reduce_sum.62
  639.6 0.6 reduce_sum.63
  640.3 68.6 %all-to-all-done.1 = f32[8,64,1,768]{3,0,2,1:T(8,128)S(1)} async-done(((f32[8,64,1,768]{3,0,2,1:T(8,128)}), f32[8,64,1,768]{3,0,2,1:T(8,128)S(1)}, u32[]{:S(2)}, u32[]{:S(2)}) %all-to-all-start.1) | async-done | bytes 1572896 | tf_op jit(solution)/shard_map/all_to_all | solution.py:32
  708.9 7.9 %all-to-all-start.5 = ((f32[8,1,768]{2,1,0:T(1,128)}), f32[8,1,768]{2,1,0:T(1,128)S(1)}, u32[]{:S(2)}, u32[]{:S(2)}) async-start(f32[8,1,768]{2,1,0:T(1,128)} %reduce_sum.63), calls=%async_computation.5 | async-start | bytes 49152 | tf_op jit(solution)/shard_map/all_to_all | solution.py:33
  716.8 0.0 copy-start.4
  716.8 1.6 fusion.13
  718.4 0.1 reduce_sum.60
  718.6 0.6 reduce_sum.61
  719.2 12.6 %all-to-all-done.5 = f32[8,1,768]{2,1,0:T(1,128)S(1)} async-done(((f32[8,1,768]{2,1,0:T(1,128)}), f32[8,1,768]{2,1,0:T(1,128)S(1)}, u32[]{:S(2)}, u32[]{:S(2)}) %all-to-all-start.5) | async-done | bytes 24608 | tf_op jit(solution)/shard_map/all_to_all | solution.py:33
  731.7 3.3 all-to-all-start.2
  735.1 0.7 reduce_sum.64
  736.4 0.0 copy-done.4
  736.4 0.7 multiply_reduce_fusion
  737.7 12.3 %all-to-all-done.2 = f32[8,1,768]{2,1,0:T(1,128)S(1)} async-done(((f32[8,1,768]{2,1,0:T(1,128)}), f32[8,1,768]{2,1,0:T(1,128)S(1)}, u32[]{:S(2)}, u32[]{:S(2)}) %all-to-all-start.2) | async-done | bytes 24608 | tf_op jit(solution)/shard_map/all_to_all | solution.py:33
  750.0 0.7 add_convert_fusion
Async XLA Ops:
  7.2 302.2 %copy-start = (bf16[768,384]{1,0:T(8,128)(2,1)S(1)}, bf16[768,384]{1,0:T(8,128)(2,1)}, u32[]{:S(2)}) copy-start(bf16[768,384]{1,0:T(8,128)(2,1)} %param.5) | copy-start | bytes 1769476
  135.5 7.8 %copy-start.5 = (bf16[1,6144]{1,0:T(2,128)(2,1)S(1)}, bf16[1,6144]{1,0:T(2,128)(2,1)}, u32[]{:S(2)}) copy-start(bf16[1,6144]{1,0:T(2,128)(2,1)} %param.7) | copy-start | bytes 36868
  136.6 155.4 %all-to-all-start = ((bf16[1,64,8,768]{3,1,0,2:T(8,128)(2,1)}), bf16[1,64,8,768]{3,1,0,2:T(8,128)(2,1)S(1)}, u32[]{:S(2)}, u32[]{:S(2)}) async-start(bf16[1,64,8,768]{3,1,0,2:T(8,128)(2,1)} %copy.10), calls=%async_computation | async-start | bytes 1572864 | tf_op jit(solution)/shard_map/all_to_all | solution.py:23
  291.9 40.1 %copy-start.3 = (bf16[384,768]{1,0:T(8,128)(2,1)S(1)}, bf16[384,768]{1,0:T(8,128)(2,1)}, u32[]{:S(2)}) copy-start(bf16[384,768]{1,0:T(8,128)(2,1)} %param.6) | copy-start | bytes 1769476
  291.9 40.1 %all-to-all-start.3 = ((bf16[1,64,8,768]{3,1,0,2:T(8,128)(2,1)}), bf16[1,64,8,768]{3,1,0,2:T(8,128)(2,1)S(1)}, u32[]{:S(2)}, u32[]{:S(2)}) async-start(bf16[1,64,8,768]{3,1,0,2:T(8,128)(2,1)} %copy.12), calls=%async_computation.3 | async-start | bytes 1572864 | tf_op jit(solution)/shard_map/all_to_all | solution.py:23
  309.3 223.4 %all-reduce.3.cloned.1.call-start = ((), (), s32[]{:S(2)}) async-start(), calls=%async_computation.6 | async-start | bytes 3145728 | tf_op jit(solution)/shard_map/psum | solution.py:38
  332.0 1.5 copy-start.2
  537.3 88.7 %all-to-all-start.4 = ((f32[8,64,1,768]{3,0,2,1:T(8,128)}), f32[8,64,1,768]{3,0,2,1:T(8,128)S(1)}, u32[]{:S(2)}, u32[]{:S(2)}) async-start(f32[8,64,1,768]{3,0,2,1:T(8,128)} %copy.13), calls=%async_computation.4 | async-start | bytes 3145728 | tf_op jit(solution)/shard_map/all_to_all | solution.py:32
  626.0 1.1 copy-start.1
  627.1 81.8 %all-to-all-start.1 = ((f32[8,64,1,768]{3,0,2,1:T(8,128)}), f32[8,64,1,768]{3,0,2,1:T(8,128)S(1)}, u32[]{:S(2)}, u32[]{:S(2)}) async-start(f32[8,64,1,768]{3,0,2,1:T(8,128)} %copy.11), calls=%async_computation.1 | async-start | bytes 3145728 | tf_op jit(solution)/shard_map/all_to_all | solution.py:32
  708.9 22.8 %all-to-all-start.5 = ((f32[8,1,768]{2,1,0:T(1,128)}), f32[8,1,768]{2,1,0:T(1,128)S(1)}, u32[]{:S(2)}, u32[]{:S(2)}) async-start(f32[8,1,768]{2,1,0:T(1,128)} %reduce_sum.63), calls=%async_computation.5 | async-start | bytes 49152 | tf_op jit(solution)/shard_map/all_to_all | solution.py:33
  716.8 19.6 %copy-start.4 = (bf16[1,6144]{1,0:T(2,128)(2,1)S(1)}, bf16[1,6144]{1,0:T(2,128)(2,1)}, u32[]{:S(2)}) copy-start(bf16[1,6144]{1,0:T(2,128)(2,1)} %param.4) | copy-start | bytes 36868
  731.7 18.2 %all-to-all-start.2 = ((f32[8,1,768]{2,1,0:T(1,128)}), f32[8,1,768]{2,1,0:T(1,128)S(1)}, u32[]{:S(2)}, u32[]{:S(2)}) async-start(f32[8,1,768]{2,1,0:T(1,128)} %reduce_sum.61), calls=%async_computation.2 | async-start | bytes 49152 | tf_op jit(solution)/shard_map/all_to_all | solution.py:33
Sparse Core Ops, SparseCore 0:
  333.6 199.0 all-reduce.2
where the time goes:
time: 758 us
  waiting for transfers between devices  384 us (51%)
  blocking collectives  259 us (34%)
  starting transfers between devices  58.4 us (8%)
  other arithmetic  19.5 us (3%)
  between operations  16.8 us (2%)
  matrix products  10.1 us (1%)
  local copies, waits for them, and re-layouts  10 us (1%)
    all_gather x2, blocking collectives, spread(): gathered = lax.all_gather(local_rows, 'mp', axis=0, tiled=True)  259 us
    psum x1, waiting for transfers between devices, group_total(): return lax.psum(term, 'dp')  199 us
    all_to_all x2, waiting for transfers between devices, collect(): lax.all_to_all(shaped, 'mp', split_axis=1, concat_axis=1, tiled=True)  138 us
    all_to_all x2, waiting for transfers between devices, collect(): lax.all_to_all(summed, 'dp', split_axis=0, concat_axis=2, tiled=True)  24.8 us
    all_to_all x2, starting transfers between devices, spread(): lax.all_to_all(shaped, 'dp', split_axis=2, concat_axis=0, tiled=True)  24.2 us
    all_to_all x2, starting transfers between devices, collect(): lax.all_to_all(shaped, 'mp', split_axis=1, concat_axis=1, tiled=True)  23 us
    all_to_all x2, waiting for transfers between devices, spread(): lax.all_to_all(shaped, 'dp', split_axis=2, concat_axis=0, tiled=True)  21.2 us
  transfers between devices with their start and end apart: 7, of which 6 were waited for; matrix products, arithmetic and copies ran while one was open for 3% of the time, Pallas kernels for 0%

commit v1 on v0

v1 whole, which is shorter than its diff:
```python
import jax
import jax.numpy as jnp
from jax import lax
from jax.sharding import Mesh, PartitionSpec as P

epsilon = 1e-06
AXES = ("zh", "y", "zl", "x", "core")
SIZES = (2, 4, 8, 4, 2)
ZH, Y, ZL, X, CORE = SIZES
f32 = jnp.float32
bf16 = jnp.bfloat16


def gelu_tanh(values):
    return jax.nn.gelu(values, approximate=True)


def gelu_grad(pre_values, upstream):
    return jax.vjp(gelu_tanh, pre_values)[1](upstream)[0]


def swap(values, axis):
    return lax.ppermute(values, axis, [(0, 1), (1, 0)])


def trade(values, axis):
    return lax.all_to_all(values, axis, split_axis=0, concat_axis=0, tiled=True)


def gather(values, axis, count):
    return trade(jnp.broadcast_to(values[None], (count,) + values.shape), axis)


def total(parts):
    return jnp.sum(parts.astype(f32), axis=0)


def local(tokens, w_in, w_out, cotangent):
    contract_last = (((1,), (1,)), ((), ()))
    contract_first = (((0,), (0,)), ((), ()))
    width = w_in.shape[0]
    hidden = w_in.shape[1]
    groups = ZH * Y

    tokens_wide = tokens.astype(f32)
    row_mean = jnp.mean(tokens_wide, axis=1, keepdims=True)
    centered = tokens_wide - row_mean
    inv_scale = lax.rsqrt(jnp.mean(centered * centered, axis=1, keepdims=True) + epsilon)
    unit_rows = centered * inv_scale
    normed = unit_rows.astype(bf16)

    both = jnp.concatenate([normed.reshape(groups, 1, width), cotangent.reshape(groups, 1, width)], axis=1)
    both = trade(both, ("zh", "y")).transpose(1, 0, 2)
    both = gather(both, "zl", ZL).transpose(1, 0, 2, 3).reshape(2, ZL * groups, width)
    both = gather(both, "x", X).transpose(1, 0, 2, 3).reshape(2, X * ZL * groups, width)
    other = swap(both, "core")
    rows = jnp.concatenate([both, other], axis=1)
    flat_normed, flat_grad = rows[0], rows[1]
    count = flat_normed.shape[0]

    pre_part = jnp.dot(flat_normed, w_in, preferred_element_type=f32)
    grad_part = lax.dot_general(flat_grad, w_out, contract_last, preferred_element_type=f32)

    parts = jnp.stack([pre_part.astype(bf16), grad_part.astype(bf16)]).reshape(2, Y, count // Y, hidden)
    parts = total(trade(parts.transpose(1, 0, 2, 3), "y"))
    parts = parts.reshape(2, ZH, count // groups, hidden)
    mine = lax.axis_index("zh")
    keep = lax.dynamic_index_in_dim(parts, mine, 1, keepdims=False)
    give = lax.dynamic_index_in_dim(parts, 1 - mine, 1, keepdims=False).astype(bf16)
    summed = keep + swap(give, "zh").astype(f32)
    pre, act_grad = summed[0], summed[1]
    act = gelu_tanh(pre).astype(bf16)
    pre_grad = gelu_grad(pre, act_grad).astype(bf16)

    own = jnp.stack([act, pre_grad])
    far = swap(own, "zh")
    first = mine == 0
    pair = jnp.stack([jnp.where(first, own, far), jnp.where(first, far, own)], axis=1)
    pair = pair.reshape(2, count // Y, hidden)
    full = gather(pair, "y", Y).transpose(1, 0, 2, 3).reshape(2, count, hidden)
    act_all, pre_grad_all = full[0], full[1]

    out_part = jnp.dot(act_all, w_out, preferred_element_type=f32)
    back_part = lax.dot_general(pre_grad_all, w_in, contract_last, preferred_element_type=f32)
    half = count // CORE
    give = jnp.stack([out_part[half:].astype(bf16), back_part[half:].astype(bf16)])
    sums = jnp.stack([out_part[:half], back_part[:half]]) + swap(give, "core").astype(f32)
    sums = sums.astype(bf16).reshape(2, X, half // X, width).transpose(1, 0, 2, 3)
    sums = total(trade(sums, "x"))
    sums = sums.astype(bf16).reshape(2, ZL, groups, width).transpose(1, 0, 2, 3)
    sums = total(trade(sums, "zl"))
    whole = trade(sums.transpose(1, 0, 2), ("zh", "y")).transpose(1, 0, 2).reshape(2, 1, groups * width)

    grad_w_out = lax.dot_general(act_all, flat_grad, contract_first, preferred_element_type=f32)
    grad_w_in = lax.dot_general(flat_normed, pre_grad_all, contract_first, preferred_element_type=f32)

    mixed = (tokens_wide + whole[0]).astype(bf16)
    normed_grad = whole[1]
    row_inner = jnp.mean(normed_grad * unit_rows, axis=1, keepdims=True)
    through = inv_scale * (
        normed_grad - jnp.mean(normed_grad, axis=1, keepdims=True) - unit_rows * row_inner
    )
    grad_tokens = (cotangent.astype(f32) + through).astype(bf16)
    return (mixed, grad_tokens, grad_w_in, grad_w_out)


def solution(mesh):
    fine = Mesh(mesh.devices.reshape(SIZES), AXES)
    dp, mp = ("zh", "y"), ("zl", "x", "core")
    return jax.shard_map(
        local,
        mesh=fine,
        in_specs=(P(dp + mp, None), P(dp, mp), P(mp, dp), P(dp + mp, None)),
        out_specs=(P(dp + mp, None), P(dp + mp, None), P(dp, mp), P(mp, dp)),
        check_vma=False,
    )
```

time: 758 us -> 207 us (0.27)
  waiting for transfers between devices: 384 us -> 67.2 us
  blocking collectives: 259 us -> 90.2 us
  starting transfers between devices: 58.4 us -> 26.7 us
  between operations: 16.8 us -> 3.54 us
  other arithmetic: 19.5 us -> 8.06 us
  local copies, waits for them, and re-layouts: 10 us -> 2.26 us
    all_gather x2 -> x0, blocking collectives: 259 us -> none  [spread(): gathered = lax.all_gather(local_rows, 'mp', axis=0, tiled=True)]
    psum x1 -> x0, waiting for transfers between devices: 199 us -> none  [group_total(): return lax.psum(term, 'dp')]
    all_to_all x6 -> x3, waiting for transfers between devices: 184 us -> 36.9 us  [trade(): return lax.all_to_all(values, axis, split_axis=0, concat_axis=0, tiled=True)]
    all_to_all x0 -> x5, blocking collectives: none -> 90.2 us  [trade(): return lax.all_to_all(values, axis, split_axis=0, concat_axis=0, tiled=True)]
    all_to_all x6 -> x3, starting transfers between devices: 58.4 us -> 17.7 us  [trade(): return lax.all_to_all(values, axis, split_axis=0, concat_axis=0, tiled=True)]
    ppermute x0 -> x4, waiting for transfers between devices: none -> 30.3 us  [swap(): return lax.ppermute(values, axis, [(0, 1), (1, 0)])]
    all_gather x2 -> x0, other arithmetic: 10.3 us -> none  [spread(): gathered = lax.all_gather(local_rows, 'mp', axis=0, tiled=True)]
    ppermute x0 -> x4, starting transfers between devices: none -> 8.97 us  [swap(): return lax.ppermute(values, axis, [(0, 1), (1, 0)])]
  transfers between devices with their start and end apart: 7 -> 7, of which waited for: 6 -> 7; matrix products, arithmetic and copies ran while one was open for 3% -> 2% of each run, Pallas kernels for 0% -> 0%
where the time goes in v1:
time: 207 us; the launch traced here: 204 us
  blocking collectives  90.2 us (44%)
  waiting for transfers between devices  67.2 us (32%)
  starting transfers between devices  26.7 us (13%)
  other arithmetic  8.06 us (4%)
  matrix products  6.52 us (3%)
  between operations  3.54 us (2%)
  local copies, waits for them, and re-layouts  2.26 us (1%)
    all_to_all x5, blocking collectives, trade(): return lax.all_to_all(values, axis, split_axis=0, concat_axis=0, tiled=True)  90.2 us
    all_to_all x3, waiting for transfers between devices, trade(): return lax.all_to_all(values, axis, split_axis=0, concat_axis=0, tiled=True)  36.9 us
    ppermute x4, waiting for transfers between devices, swap(): return lax.ppermute(values, axis, [(0, 1), (1, 0)])  30.3 us
    all_to_all x3, starting transfers between devices, trade(): return lax.all_to_all(values, axis, split_axis=0, concat_axis=0, tiled=True)  17.7 us
    ppermute x4, starting transfers between devices, swap(): return lax.ppermute(values, axis, [(0, 1), (1, 0)])  8.97 us
  transfers between devices with their start and end apart: 7, of which 7 were waited for; matrix products, arithmetic and copies ran while one was open for 2% of the time, Pallas kernels for 0%

profile of v1, /device:TPU:6, one launch (start us, length us, event | category | flops | bytes accessed | tf_op | source)
XLA Modules:
  0.0 204.4 jit_solution(16235948601034437447)
XLA Ops:
  0.6 0.0 copy-start
  0.6 1.5 convert_reduce_fusion.2
  2.8 1.4 multiply_reduce_fusion.1
  4.8 0.8 fusion.20
  5.6 0.8 pad_maximum_fusion.4
  6.4 32.5 %all_to_all.40 = bf16[8,2,768]{2,1,0:T(2,128)(2,1)S(1)} all-to-all(bf16[8,2,768]{2,1,0:T(2,128)(2,1)S(1)} %pad_maximum_fusion.4), channel_id=1, replica_groups=mesh['zh'=2,'y'=4,'zl'=8,'x'=4,'core'=2] {'zh','y'}, dimensions={0} | all-to-all | bytes 49152 | tf_op jit(solution)/shard_map/all_to_all | solution.py:27
  38.9 17.3 %all_to_all.41 = bf16[8,2,8,768]{3,2,1,0:T(8,128)(2,1)S(1)} all-to-all(bf16[8,2,8,768]{3,2,1,0:T(8,128)(2,1)S(1)} %broadcast_in_dim.10), channel_id=1, replica_groups=mesh['zh'=2,'y'=4,'zl'=8,'x'=4,'core'=2] {'zl'}, dimensions={0} | all-to-all | bytes 393216 | tf_op jit(solution)/shard_map/all_to_all | solution.py:27
  56.2 0.1 broadcast_in_dim.12
  56.3 0.0 copy-start.4
  56.3 12.1 %all_to_all.42 = bf16[4,2,64,768]{3,2,1,0:T(8,128)(2,1)S(1)} all-to-all(bf16[4,2,64,768]{3,2,1,0:T(8,128)(2,1)S(1)} %broadcast_in_dim.12), channel_id=1, replica_groups=mesh['zh'=2,'y'=4,'zl'=8,'x'=4,'core'=2] {'x'}, dimensions={0} | all-to-all | bytes 1572864 | tf_op jit(solution)/shard_map/all_to_all | solution.py:27
  68.4 0.1 copy.26
  68.5 1.9 collective-permute-start
  70.4 2.3 %collective-permute-done = bf16[2,256,768]{2,1,0:T(8,128)(2,1)S(1)} collective-permute-done((bf16[2,256,768]{2,1,0:T(8,128)(2,1)S(1)}, bf16[2,256,768]{2,1,0:T(8,128)(2,1)S(1)}, u32[]{:S(2)}, u32[]{:S(2)}) %collective-permute-start) | collective-permute-done | bytes 786464 | tf_op jit(solution)/shard_map/ppermute | solution.py:23
  72.7 0.0 copy-done.4
  72.7 0.0 copy-start.1
  72.7 0.6 convolution_convert_fusion.1
  73.2 0.3 copy-done.1
  73.6 0.0 copy-done
  73.6 0.6 convolution_convert_fusion
  74.2 1.0 maximum_bitcast_fusion
  75.1 3.5 %all-to-all-start.3 = ((bf16[4,2,128,384]{3,2,1,0:T(8,128)(2,1)}), bf16[4,2,128,384]{3,2,1,0:T(8,128)(2,1)S(1)}, u32[]{:S(2)}, u32[]{:S(2)}) async-start(bf16[4,2,128,384]{3,2,1,0:T(8,128)(2,1)} %maximum_bitcast_fusion), calls=%async_computation.3 | async-start | bytes 1572864 | tf_op jit(solution)/shard_map/all_to_all | solution.py:27
  78.6 12.8 %all-to-all-done.3 = bf16[4,2,128,384]{3,2,1,0:T(8,128)(2,1)S(1)} async-done(((bf16[4,2,128,384]{3,2,1,0:T(8,128)(2,1)}), bf16[4,2,128,384]{3,2,1,0:T(8,128)(2,1)S(1)}, u32[]{:S(2)}, u32[]{:S(2)}) %all-to-all-start.3) | async-done | bytes 786464 | tf_op jit(solution)/shard_map/all_to_all | solution.py:27
  91.5 0.1 convert_reduce_fusion
  91.6 2.7 %collective-permute-start.1 = (bf16[2,64,384]{2,1,0:T(8,128)(2,1)S(1)}, bf16[2,64,384]{2,1,0:T(8,128)(2,1)S(1)}, u32[]{:S(2)}, u32[]{:S(2)}) collective-permute-start(bf16[2,64,384]{2,1,0:T(8,128)(2,1)S(1)} %fusion.16), channel_id=1, source_target_pairs={{0,256},{256,0},{1,257},{257,1},{2,258},{258,2},{3,259},{259,3},{4... | collective-permute-start | bytes 294920 | tf_op jit(solution)/shard_map/ppermute | solution.py:23
  94.3 13.0 %collective-permute-done.1 = bf16[2,64,384]{2,1,0:T(8,128)(2,1)S(1)} collective-permute-done((bf16[2,64,384]{2,1,0:T(8,128)(2,1)S(1)}, bf16[2,64,384]{2,1,0:T(8,128)(2,1)S(1)}, u32[]{:S(2)}, u32[]{:S(2)}) %collective-permute-start.1) | collective-permute-done | bytes 98336 | tf_op jit(solution)/shard_map/ppermute | solution.py:23
  107.4 0.1 multiply_convert_fusion
  107.5 2.4 %collective-permute-start.2 = (bf16[2,64,384]{2,1,0:T(8,128)(2,1)S(1)}, bf16[2,64,384]{2,1,0:T(8,128)(2,1)S(1)}, u32[]{:S(2)}, u32[]{:S(2)}) collective-permute-start(bf16[2,64,384]{2,1,0:T(8,128)(2,1)S(1)} %pad_maximum_fusion.3), channel_id=1, source_target_pairs={{0,256},{256,0},{1,257},{257,1},{2,258},{258,2},{3,259},{259,3},{4... | collective-permute-start | bytes 294920 | tf_op jit(solution)/shard_map/ppermute | solution.py:23
  109.9 12.9 %collective-permute-done.2 = bf16[2,64,384]{2,1,0:T(8,128)(2,1)S(1)} collective-permute-done((bf16[2,64,384]{2,1,0:T(8,128)(2,1)S(1)}, bf16[2,64,384]{2,1,0:T(8,128)(2,1)S(1)}, u32[]{:S(2)}, u32[]{:S(2)}) %collective-permute-start.2) | collective-permute-done | bytes 98336 | tf_op jit(solution)/shard_map/ppermute | solution.py:23
  122.9 0.1 broadcast_in_dim.28
  123.0 12.2 %all_to_all.43 = bf16[4,2,128,384]{3,2,1,0:T(8,128)(2,1)S(1)} all-to-all(bf16[4,2,128,384]{3,2,1,0:T(8,128)(2,1)S(1)} %broadcast_in_dim.28), channel_id=1, replica_groups=mesh['zh'=2,'y'=4,'zl'=8,'x'=4,'core'=2] {'y'}, dimensions={0} | all-to-all | bytes 1572864 | tf_op jit(solution)/shard_map/all_to_all | solution.py:27
  135.2 0.1 fusion.24
  135.3 0.6 fusion.25
  135.8 0.6 fusion.26
  136.4 0.1 fusion.4
  136.5 0.1 pad_maximum_fusion.1
  136.6 1.9 collective-permute-start.3
  138.5 0.1 slice_bitcast_fusion
  138.6 2.1 %collective-permute-done.3 = bf16[2,256,768]{2,1,0:T(8,128)(2,1)S(1)} collective-permute-done((bf16[2,256,768]{2,1,0:T(8,128)(2,1)S(1)}, bf16[2,256,768]{2,1,0:T(8,128)(2,1)S(1)}, u32[]{:S(2)}, u32[]{:S(2)}) %collective-permute-start.3) | collective-permute-done | bytes 786464 | tf_op jit(solution)/shard_map/ppermute | solution.py:23
  140.8 0.2 fusion
  140.9 0.1 copy.35
  141.0 16.1 %all_to_all.44 = bf16[4,2,64,768]{3,2,1,0:T(8,128)(2,1)S(1)} all-to-all(bf16[4,2,64,768]{3,2,1,0:T(8,128)(2,1)S(1)} %bitcast.70), channel_id=1, replica_groups=mesh['zh'=2,'y'=4,'zl'=8,'x'=4,'core'=2] {'x'}, dimensions={0} | all-to-all | bytes 1572864 | tf_op jit(solution)/shard_map/all_to_all | solution.py:27
  157.1 0.1 reduce_sum.69
  157.2 0.7 copy.31
  157.9 10.9 %all-to-all-start.6 = ((bf16[8,2,8,768]{3,2,1,0:T(8,128)(2,1)}), bf16[8,2,8,768]{3,2,1,0:T(8,128)(2,1)S(1)}, u32[]{:S(2)}, u32[]{:S(2)}) async-start(bf16[8,2,8,768]{3,2,1,0:T(8,128)(2,1)} %copy.31), calls=%async_computation.6 | async-start | bytes 393216 | tf_op jit(solution)/shard_map/all_to_all | solution.py:27
  168.8 0.0 copy-start.2
  168.8 2.7 %fusion.21 = f32[768,384]{1,0:T(8,128)} fusion(bf16[512,384]{1,0:T(8,128)(2,1)S(1)} %bitcast.78, bf16[2,256,768]{2,1,0:T(8,128)(2,1)S(1)} %bitcast.74, bf16[2,256,768]{2,1,0:T(8,128)(2,1)} %copy-done.1), kind=kOutput, calls=%fused_computation.52 | convolution fusion | flops 303562752 | bytes 3145728 | tf_op jit(solution)/shard_map/dot_general | solution.py:95
  171.5 10.7 %all-to-all-done.6 = bf16[8,2,8,768]{3,2,1,0:T(8,128)(2,1)S(1)} async-done(((bf16[8,2,8,768]{3,2,1,0:T(8,128)(2,1)}), bf16[8,2,8,768]{3,2,1,0:T(8,128)(2,1)S(1)}, u32[]{:S(2)}, u32[]{:S(2)}) %all-to-all-start.6) | async-done | bytes 196640 | tf_op jit(solution)/shard_map/all_to_all | solution.py:27
  182.2 0.6 copy.32
  182.8 3.3 %all-to-all-start.7 = ((f32[8,2,768]{2,1,0:T(2,128)}), f32[8,2,768]{2,1,0:T(2,128)S(1)}, u32[]{:S(2)}, u32[]{:S(2)}) async-start(f32[8,2,768]{2,1,0:T(2,128)} %copy.32), calls=%async_computation.7 | async-start | bytes 98304 | tf_op jit(solution)/shard_map/all_to_all | solution.py:27
  186.2 0.0 copy-done.2
  186.2 0.0 copy-start.3
  186.2 0.0 copy-start.5
  186.2 1.5 fusion.6
  187.7 13.4 %all-to-all-done.7 = f32[8,2,768]{2,1,0:T(2,128)S(1)} async-done(((f32[8,2,768]{2,1,0:T(2,128)}), f32[8,2,768]{2,1,0:T(2,128)S(1)}, u32[]{:S(2)}, u32[]{:S(2)}) %all-to-all-start.7) | async-done | bytes 49184 | tf_op jit(solution)/shard_map/all_to_all | solution.py:27
  201.1 0.7 slice_reduce_fusion
  201.8 0.0 copy-done.3
  201.8 0.7 multiply_reduce_fusion
  203.7 0.0 copy-done.5
  203.8 0.7 add_convert_fusion
  (10 shorter events, 0.2 us)
Async XLA Ops:
  0.6 72.9 %copy-start = (bf16[384,768]{1,0:T(8,128)(2,1)S(1)}, bf16[384,768]{1,0:T(8,128)(2,1)}, u32[]{:S(2)}) copy-start(bf16[384,768]{1,0:T(8,128)(2,1)} %param.6) | copy-start | bytes 1769476
  56.3 16.4 %copy-start.4 = (bf16[768,384]{1,0:T(8,128)(2,1)S(1)}, bf16[768,384]{1,0:T(8,128)(2,1)}, u32[]{:S(2)}) copy-start(bf16[768,384]{1,0:T(8,128)(2,1)} %param.5) | copy-start | bytes 1769476
  68.5 4.2 %collective-permute-start = (bf16[2,256,768]{2,1,0:T(8,128)(2,1)S(1)}, bf16[2,256,768]{2,1,0:T(8,128)(2,1)S(1)}, u32[]{:S(2)}, u32[]{:S(2)}) collective-permute-start(bf16[2,256,768]{2,1,0:T(8,128)(2,1)S(1)} %bitcast.71), channel_id=1, source_target_pairs={{0,1},{1,0},{2,3},{3,2},{4,5},{5,4},{6,7},{7,6},{8,9},{9,8},{10,11... | collective-permute-start | bytes 2359304 | tf_op jit(solution)/shard_map/ppermute | solution.py:23
  72.7 0.9 copy-start.1
  75.1 16.3 %all-to-all-start.3 = ((bf16[4,2,128,384]{3,2,1,0:T(8,128)(2,1)}), bf16[4,2,128,384]{3,2,1,0:T(8,128)(2,1)S(1)}, u32[]{:S(2)}, u32[]{:S(2)}) async-start(bf16[4,2,128,384]{3,2,1,0:T(8,128)(2,1)} %maximum_bitcast_fusion), calls=%async_computation.3 | async-start | bytes 1572864 | tf_op jit(solution)/shard_map/all_to_all | solution.py:27
  91.6 15.8 %collective-permute-start.1 = (bf16[2,64,384]{2,1,0:T(8,128)(2,1)S(1)}, bf16[2,64,384]{2,1,0:T(8,128)(2,1)S(1)}, u32[]{:S(2)}, u32[]{:S(2)}) collective-permute-start(bf16[2,64,384]{2,1,0:T(8,128)(2,1)S(1)} %fusion.16), channel_id=1, source_target_pairs={{0,256},{256,0},{1,257},{257,1},{2,258},{258,2},{3,259},{259,3},{4... | collective-permute-start | bytes 294920 | tf_op jit(solution)/shard_map/ppermute | solution.py:23
  107.5 15.3 %collective-permute-start.2 = (bf16[2,64,384]{2,1,0:T(8,128)(2,1)S(1)}, bf16[2,64,384]{2,1,0:T(8,128)(2,1)S(1)}, u32[]{:S(2)}, u32[]{:S(2)}) collective-permute-start(bf16[2,64,384]{2,1,0:T(8,128)(2,1)S(1)} %pad_maximum_fusion.3), channel_id=1, source_target_pairs={{0,256},{256,0},{1,257},{257,1},{2,258},{258,2},{3,259},{259,3},{4... | collective-permute-start | bytes 294920 | tf_op jit(solution)/shard_map/ppermute | solution.py:23
  136.6 4.2 %collective-permute-start.3 = (bf16[2,256,768]{2,1,0:T(8,128)(2,1)S(1)}, bf16[2,256,768]{2,1,0:T(8,128)(2,1)S(1)}, u32[]{:S(2)}, u32[]{:S(2)}) collective-permute-start(bf16[2,256,768]{2,1,0:T(8,128)(2,1)S(1)} %pad_maximum_fusion.1), channel_id=1, source_target_pairs={{0,1},{1,0},{2,3},{3,2},{4,5},{5,4},{6,7},{7,6},{8,9},{9,8},{10,11... | collective-permute-start | bytes 2359304 | tf_op jit(solution)/shard_map/ppermute | solution.py:23
  157.9 24.2 %all-to-all-start.6 = ((bf16[8,2,8,768]{3,2,1,0:T(8,128)(2,1)}), bf16[8,2,8,768]{3,2,1,0:T(8,128)(2,1)S(1)}, u32[]{:S(2)}, u32[]{:S(2)}) async-start(bf16[8,2,8,768]{3,2,1,0:T(8,128)(2,1)} %copy.31), calls=%async_computation.6 | async-start | bytes 393216 | tf_op jit(solution)/shard_map/all_to_all | solution.py:27
  168.8 17.4 %copy-start.2 = (bf16[2,256,768]{2,1,0:T(8,128)(2,1)S(1)}, bf16[2,256,768]{2,1,0:T(8,128)(2,1)}, u32[]{:S(2)}) copy-start(bf16[2,256,768]{2,1,0:T(8,128)(2,1)} %copy-done.1) | copy-start | bytes 2359300
  182.8 18.3 %all-to-all-start.7 = ((f32[8,2,768]{2,1,0:T(2,128)}), f32[8,2,768]{2,1,0:T(2,128)S(1)}, u32[]{:S(2)}, u32[]{:S(2)}) async-start(f32[8,2,768]{2,1,0:T(2,128)} %copy.32), calls=%async_computation.7 | async-start | bytes 98304 | tf_op jit(solution)/shard_map/all_to_all | solution.py:27
  186.2 15.6 %copy-start.3 = (bf16[1,6144]{1,0:T(2,128)(2,1)S(1)}, bf16[1,6144]{1,0:T(2,128)(2,1)}, u32[]{:S(2)}) copy-start(bf16[1,6144]{1,0:T(2,128)(2,1)} %param.4) | copy-start | bytes 36868
  186.2 17.5 %copy-start.5 = (bf16[1,6144]{1,0:T(2,128)(2,1)S(1)}, bf16[1,6144]{1,0:T(2,128)(2,1)}, u32[]{:S(2)}) copy-start(bf16[1,6144]{1,0:T(2,128)(2,1)} %param.7) | copy-start | bytes 36868

commit v2 on v1

--- a/solution.py
+++ b/solution.py
@@ -7,6 +7,7 @@
 AXES = ("zh", "y", "zl", "x", "core")
 SIZES = (2, 4, 8, 4, 2)
 ZH, Y, ZL, X, CORE = SIZES
+FAR = ("zh", "y", "zl")
 f32 = jnp.float32
 bf16 = jnp.bfloat16
 
@@ -27,10 +28,6 @@
     return lax.all_to_all(values, axis, split_axis=0, concat_axis=0, tiled=True)
 
 
-def gather(values, axis, count):
-    return trade(jnp.broadcast_to(values[None], (count,) + values.shape), axis)
-
-
 def total(parts):
     return jnp.sum(parts.astype(f32), axis=0)
 
@@ -49,10 +46,10 @@
     unit_rows = centered * inv_scale
     normed = unit_rows.astype(bf16)
 
-    both = jnp.concatenate([normed.reshape(groups, 1, width), cotangent.reshape(groups, 1, width)], axis=1)
-    both = trade(both, ("zh", "y")).transpose(1, 0, 2)
-    both = gather(both, "zl", ZL).transpose(1, 0, 2, 3).reshape(2, ZL * groups, width)
-    both = gather(both, "x", X).transpose(1, 0, 2, 3).reshape(2, X * ZL * groups, width)
+    both = jnp.concatenate([normed.reshape(1, groups, 1, width), cotangent.reshape(1, groups, 1, width)])
+    both = jnp.broadcast_to(both, (2, groups, ZL, width)).reshape(2, groups * ZL, width)
+    both = lax.all_to_all(both, FAR, split_axis=1, concat_axis=1, tiled=True)
+    both = lax.all_gather(both, "x", axis=1, tiled=True)
     other = swap(both, "core")
     rows = jnp.concatenate([both, other], axis=1)
     flat_normed, flat_grad = rows[0], rows[1]
@@ -63,21 +60,12 @@
 
     parts = jnp.stack([pre_part.astype(bf16), grad_part.astype(bf16)]).reshape(2, Y, count // Y, hidden)
     parts = total(trade(parts.transpose(1, 0, 2, 3), "y"))
-    parts = parts.reshape(2, ZH, count // groups, hidden)
-    mine = lax.axis_index("zh")
-    keep = lax.dynamic_index_in_dim(parts, mine, 1, keepdims=False)
-    give = lax.dynamic_index_in_dim(parts, 1 - mine, 1, keepdims=False).astype(bf16)
-    summed = keep + swap(give, "zh").astype(f32)
+    summed = parts + swap(parts.astype(bf16), "zh").astype(f32)
     pre, act_grad = summed[0], summed[1]
     act = gelu_tanh(pre).astype(bf16)
     pre_grad = gelu_grad(pre, act_grad).astype(bf16)
 
-    own = jnp.stack([act, pre_grad])
-    far = swap(own, "zh")
-    first = mine == 0
-    pair = jnp.stack([jnp.where(first, own, far), jnp.where(first, far, own)], axis=1)
-    pair = pair.reshape(2, count // Y, hidden)
-    full = gather(pair, "y", Y).transpose(1, 0, 2, 3).reshape(2, count, hidden)
+    full = lax.all_gather(jnp.stack([act, pre_grad]), "y", axis=1, tiled=True)
     act_all, pre_grad_all = full[0], full[1]
 
     out_part = jnp.dot(act_all, w_out, preferred_element_type=f32)
@@ -87,9 +75,8 @@
     sums = jnp.stack([out_part[:half], back_part[:half]]) + swap(give, "core").astype(f32)
     sums = sums.astype(bf16).reshape(2, X, half // X, width).transpose(1, 0, 2, 3)
     sums = total(trade(sums, "x"))
-    sums = sums.astype(bf16).reshape(2, ZL, groups, width).transpose(1, 0, 2, 3)
-    sums = total(trade(sums, "zl"))
-    whole = trade(sums.transpose(1, 0, 2), ("zh", "y")).transpose(1, 0, 2).reshape(2, 1, groups * width)
+    sums = lax.all_to_all(sums.astype(bf16), FAR, split_axis=1, concat_axis=1, tiled=True)
+    whole = jnp.sum(sums.astype(f32).reshape(2, groups, ZL, width), axis=2).reshape(2, 1, groups * width)
 
     grad_w_out = lax.dot_general(act_all, flat_grad, contract_first, preferred_element_type=f32)
     grad_w_in = lax.dot_general(flat_normed, pre_grad_all, contract_first, preferred_element_type=f32)

time: 207 us -> 174 us (0.84)
  waiting for transfers between devices: 67.2 us -> 41.5 us
  starting transfers between devices: 26.7 us -> 15.2 us
  blocking collectives: 90.2 us -> 97.1 us
    all_to_all x5 -> x2, blocking collectives: 90.2 us -> 30.1 us  [trade(): return lax.all_to_all(values, axis, split_axis=0, concat_axis=0, tiled=True)]
    all_to_all x0 -> x1, blocking collectives: none -> 38.7 us  [local(): both = lax.all_to_all(both, FAR, split_axis=1, concat_axis=1, tiled=True)]
    all_gather x0 -> x2, blocking collectives: none -> 28.3 us  [the longest x1 14.2 us: local(): both = lax.all_gather(both, 'x', axis=1, tiled=True)]
    all_to_all x3 -> x1, waiting for transfers between devices: 36.9 us -> 15 us  [local(): lax.all_to_all(sums.astype(bf16), FAR, split_axis=1, concat_axis=1, tiled...]
    all_to_all x3 -> x1, starting transfers between devices: 17.7 us -> 8.56 us  [local(): lax.all_to_all(sums.astype(bf16), FAR, split_axis=1, concat_axis=1, tiled...]
    ppermute x4 -> x3, waiting for transfers between devices: 30.3 us -> 26.5 us  [swap(): return lax.ppermute(values, axis, [(0, 1), (1, 0)])]
    ppermute x4 -> x3, starting transfers between devices: 8.97 us -> 6.68 us  [swap(): return lax.ppermute(values, axis, [(0, 1), (1, 0)])]
  transfers between devices with their start and end apart: 7 -> 4, of which waited for: 7 -> 4; matrix products, arithmetic and copies ran while one was open for 2% -> 3% of each run, Pallas kernels for 0% -> 0%
where the time goes in v2:
time: 174 us; the launch traced here: 173 us
  blocking collectives  97.1 us (56%)
  waiting for transfers between devices  41.5 us (24%)
  starting transfers between devices  15.2 us (9%)
  other arithmetic  7.45 us (4%)
  matrix products  6.58 us (4%)
  between operations  3.51 us (2%)
    all_to_all x1, blocking collectives, local(): both = lax.all_to_all(both, FAR, split_axis=1, concat_axis=1, tiled=True)  38.7 us
    all_to_all x2, blocking collectives, trade(): return lax.all_to_all(values, axis, split_axis=0, concat_axis=0, tiled=True)  30.1 us
    ppermute x3, waiting for transfers between devices, swap(): return lax.ppermute(values, axis, [(0, 1), (1, 0)])  26.5 us
    all_to_all x1, waiting for transfers between devices, local(): lax.all_to_all(sums.astype(bf16), FAR, split_axis=1, concat_axis=1, tiled...  15 us
    all_gather x1, blocking collectives, local(): both = lax.all_gather(both, 'x', axis=1, tiled=True)  14.2 us
    all_gather x1, blocking collectives, local(): full = lax.all_gather(jnp.stack([act, pre_grad]), 'y', axis=1, tiled=True)  14.1 us
    all_to_all x1, starting transfers between devices, local(): lax.all_to_all(sums.astype(bf16), FAR, split_axis=1, concat_axis=1, tiled...  8.56 us
    ppermute x3, starting transfers between devices, swap(): return lax.ppermute(values, axis, [(0, 1), (1, 0)])  6.68 us
  transfers between devices with their start and end apart: 4, of which 4 were waited for; matrix products, arithmetic and copies ran while one was open for 3% of the time, Pallas kernels for 0%

profile of v2, /device:TPU:6, one launch (start us, length us, event | category | flops | bytes accessed | tf_op | source)
XLA Modules:
  0.0 172.9 jit_solution(14879112155922998508)
XLA Ops:
  0.6 0.0 copy-start
  0.6 1.5 convert_reduce_fusion.3
  2.8 1.4 multiply_reduce_fusion.1
  4.8 0.8 convert_reduce_fusion.2
  5.7 0.8 reduce.7
  6.6 0.1 broadcast_in_dim.5
  6.7 38.7 %all_to_all.20 = bf16[2,64,768]{2,0,1:T(2,128)(2,1)S(1)} all-to-all(bf16[2,64,768]{2,0,1:T(2,128)(2,1)S(1)} %bitcast.50), channel_id=1, replica_groups=mesh['zh'=2,'y'=4,'zl'=8,'x'=4,'core'=2] {'zh','y','zl'}, dimensions={1} | all-to-all | bytes 393216 | tf_op jit(solution)/shard_map/all_to_all | solution.py:51
  45.5 14.2 %all_gather.6 = bf16[2,256,768]{2,1,0:T(8,128)(2,1)S(1)} all-gather(bf16[2,64,768]{2,1,0:T(8,128)(2,1)S(1)} %copy.18), channel_id=1, replica_groups=mesh['zh'=2,'y'=4,'zl'=8,'x'=4,'core'=2] {'x'}, dimensions={1}, use_global_device_ids=true | all-gather | bytes 983040 | tf_op jit(solution)/shard_map/all_gather | solution.py:52
  59.7 0.0 copy-start.4
  59.7 2.0 %collective-permute-start = (bf16[2,256,768]{2,1,0:T(8,128)(2,1)S(1)}, bf16[2,256,768]{2,1,0:T(8,128)(2,1)S(1)}, u32[]{:S(2)}, u32[]{:S(2)}) collective-permute-start(bf16[2,256,768]{2,1,0:T(8,128)(2,1)S(1)} %all_gather.6), channel_id=1, source_target_pairs={{0,1},{1,0},{2,3},{3,2},{4,5},{5,4},{6,7},{7,6},{8,9},{9,8},{10,11... | collective-permute-start | bytes 2359304 | tf_op jit(solution)/shard_map/ppermute | solution.py:24
  61.7 0.1 constant_dynamic-update-slice_fusion.1
  61.8 2.2 %collective-permute-done = bf16[2,256,768]{2,1,0:T(8,128)(2,1)S(1)} collective-permute-done((bf16[2,256,768]{2,1,0:T(8,128)(2,1)S(1)}, bf16[2,256,768]{2,1,0:T(8,128)(2,1)S(1)}, u32[]{:S(2)}, u32[]{:S(2)}) %collective-permute-start) | collective-permute-done | bytes 786464 | tf_op jit(solution)/shard_map/ppermute | solution.py:24
  64.0 0.1 constant_dynamic-update-slice_fusion
  64.0 0.0 copy-done.4
  64.1 0.0 copy-start.1
  64.1 0.6 convolution_convert_fusion.1
  64.6 0.0 copy-done
  64.7 0.6 convolution_convert_fusion
  65.2 0.0 copy-done.1
  65.3 0.1 maximum_bitcast_fusion
  65.4 15.3 %all_to_all.21 = bf16[4,2,128,384]{3,2,1,0:T(8,128)(2,1)S(1)} all-to-all(bf16[4,2,128,384]{3,2,1,0:T(8,128)(2,1)S(1)} %maximum_bitcast_fusion), channel_id=1, replica_groups=mesh['zh'=2,'y'=4,'zl'=8,'x'=4,'core'=2] {'y'}, dimensions={0} | all-to-all | bytes 1572864 | tf_op jit(solution)/shard_map/all_to_all | solution.py:28
  80.6 0.1 convert_reduce_fusion
  80.8 2.7 %collective-permute-start.1 = (bf16[2,128,384]{2,1,0:T(8,128)(2,1)S(1)}, bf16[2,128,384]{2,1,0:T(8,128)(2,1)S(1)}, u32[]{:S(2)}, u32[]{:S(2)}) collective-permute-start(bf16[2,128,384]{2,1,0:T(8,128)(2,1)S(1)} %convert_element_type.54), channel_id=1, source_target_pairs={{0,256},{256,0},{1,257},{257,1},{2,258},{258,2},{3,259},{259,3},{4... | collective-permute-start | bytes 589832 | tf_op jit(solution)/shard_map/ppermute | solution.py:24
  83.5 22.2 %collective-permute-done.1 = bf16[2,128,384]{2,1,0:T(8,128)(2,1)S(1)} collective-permute-done((bf16[2,128,384]{2,1,0:T(8,128)(2,1)S(1)}, bf16[2,128,384]{2,1,0:T(8,128)(2,1)S(1)}, u32[]{:S(2)}, u32[]{:S(2)}) %collective-permute-start.1) | collective-permute-done | bytes 196640 | tf_op jit(solution)/shard_map/ppermute | solution.py:24
  105.8 0.2 multiply_convert_fusion
  106.0 14.1 %all_gather.7 = bf16[2,512,384]{2,1,0:T(8,128)(2,1)S(1)} all-gather(bf16[2,128,384]{2,1,0:T(8,128)(2,1)S(1)} %pad_maximum_fusion.1), channel_id=1, replica_groups=mesh['zh'=2,'y'=4,'zl'=8,'x'=4,'core'=2] {'y'}, dimensions={1}, use_global_device_ids=true | all-gather | bytes 983040 | tf_op jit(solution)/shard_map/all_gather | solution.py:68
  120.1 0.6 fusion.5
  120.6 0.6 fusion.6
  121.2 0.1 fusion.3
  121.3 0.1 pad_maximum_fusion
  121.4 1.9 %collective-permute-start.2 = (bf16[2,256,768]{2,1,0:T(8,128)(2,1)S(1)}, bf16[2,256,768]{2,1,0:T(8,128)(2,1)S(1)}, u32[]{:S(2)}, u32[]{:S(2)}) collective-permute-start(bf16[2,256,768]{2,1,0:T(8,128)(2,1)S(1)} %pad_maximum_fusion), channel_id=1, source_target_pairs={{0,1},{1,0},{2,3},{3,2},{4,5},{5,4},{6,7},{7,6},{8,9},{9,8},{10,11... | collective-permute-start | bytes 2359304 | tf_op jit(solution)/shard_map/ppermute | solution.py:24
  123.3 0.1 slice_bitcast_fusion
  123.4 2.1 %collective-permute-done.2 = bf16[2,256,768]{2,1,0:T(8,128)(2,1)S(1)} collective-permute-done((bf16[2,256,768]{2,1,0:T(8,128)(2,1)S(1)}, bf16[2,256,768]{2,1,0:T(8,128)(2,1)S(1)}, u32[]{:S(2)}, u32[]{:S(2)}) %collective-permute-start.2) | collective-permute-done | bytes 786464 | tf_op jit(solution)/shard_map/ppermute | solution.py:24
  125.6 0.2 fusion
  125.7 0.1 copy.24
  125.8 14.8 %all_to_all.22 = bf16[4,2,64,768]{3,2,1,0:T(8,128)(2,1)S(1)} all-to-all(bf16[4,2,64,768]{3,2,1,0:T(8,128)(2,1)S(1)} %bitcast.48), channel_id=1, replica_groups=mesh['zh'=2,'y'=4,'zl'=8,'x'=4,'core'=2] {'x'}, dimensions={0} | all-to-all | bytes 1572864 | tf_op jit(solution)/shard_map/all_to_all | solution.py:28
  140.6 0.1 reduce_sum.69
  140.7 0.0 copy-start.2
  140.8 0.9 copy.22
  141.6 8.6 %all-to-all-start.3 = ((bf16[2,64,768]{2,0,1:T(2,128)(2,1)}), bf16[2,64,768]{2,0,1:T(2,128)(2,1)S(1)}, u32[]{:S(2)}, u32[]{:S(2)}) async-start(bf16[2,64,768]{2,0,1:T(2,128)(2,1)} %copy.22), calls=%async_computation.3 | async-start | bytes 393216 | tf_op jit(solution)/shard_map/all_to_all | solution.py:78
  150.2 2.7 %fusion.1 = f32[768,384]{1,0:T(8,128)} fusion(bf16[2,512,768]{2,1,0:T(8,128)(2,1)} %copy-done.1, bf16[2,512,384]{2,1,0:T(8,128)(2,1)S(1)} %all_gather.7), kind=kOutput, calls=%fused_computation.14 | convolution fusion | flops 301989888 | bytes 2359296 | tf_op jit(solution)/shard_map/dot_general | solution.py:82
  152.9 0.0 copy-done.2
  152.9 0.0 copy-start.3
  152.9 0.0 copy-start.5
  152.9 1.5 fusion.2
  154.5 15.0 %all-to-all-done.3 = bf16[2,64,768]{2,0,1:T(2,128)(2,1)S(1)} async-done(((bf16[2,64,768]{2,0,1:T(2,128)(2,1)}), bf16[2,64,768]{2,0,1:T(2,128)(2,1)S(1)}, u32[]{:S(2)}, u32[]{:S(2)}) %all-to-all-start.3) | async-done | bytes 196640 | tf_op jit(solution)/shard_map/all_to_all | solution.py:78
  169.4 0.2 convert_reduce_fusion.1
  169.6 0.7 slice_reduce_fusion
  170.2 0.0 copy-done.3
  170.2 0.7 multiply_reduce_fusion
  172.2 0.0 copy-done.5
  172.2 0.7 add_convert_fusion
  (8 shorter events, 0.2 us)
Async XLA Ops:
  0.6 64.0 %copy-start = (bf16[384,768]{1,0:T(8,128)(2,1)S(1)}, bf16[384,768]{1,0:T(8,128)(2,1)}, u32[]{:S(2)}) copy-start(bf16[384,768]{1,0:T(8,128)(2,1)} %param.6) | copy-start | bytes 1769476
  59.7 4.4 %copy-start.4 = (bf16[768,384]{1,0:T(8,128)(2,1)S(1)}, bf16[768,384]{1,0:T(8,128)(2,1)}, u32[]{:S(2)}) copy-start(bf16[768,384]{1,0:T(8,128)(2,1)} %param.5) | copy-start | bytes 1769476
  59.7 4.3 %collective-permute-start = (bf16[2,256,768]{2,1,0:T(8,128)(2,1)S(1)}, bf16[2,256,768]{2,1,0:T(8,128)(2,1)S(1)}, u32[]{:S(2)}, u32[]{:S(2)}) collective-permute-start(bf16[2,256,768]{2,1,0:T(8,128)(2,1)S(1)} %all_gather.6), channel_id=1, source_target_pairs={{0,1},{1,0},{2,3},{3,2},{4,5},{5,4},{6,7},{7,6},{8,9},{9,8},{10,11... | collective-permute-start | bytes 2359304 | tf_op jit(solution)/shard_map/ppermute | solution.py:24
  64.1 1.2 copy-start.1
  80.8 24.9 %collective-permute-start.1 = (bf16[2,128,384]{2,1,0:T(8,128)(2,1)S(1)}, bf16[2,128,384]{2,1,0:T(8,128)(2,1)S(1)}, u32[]{:S(2)}, u32[]{:S(2)}) collective-permute-start(bf16[2,128,384]{2,1,0:T(8,128)(2,1)S(1)} %convert_element_type.54), channel_id=1, source_target_pairs={{0,256},{256,0},{1,257},{257,1},{2,258},{258,2},{3,259},{259,3},{4... | collective-permute-start | bytes 589832 | tf_op jit(solution)/shard_map/ppermute | solution.py:24
  121.4 4.2 %collective-permute-start.2 = (bf16[2,256,768]{2,1,0:T(8,128)(2,1)S(1)}, bf16[2,256,768]{2,1,0:T(8,128)(2,1)S(1)}, u32[]{:S(2)}, u32[]{:S(2)}) collective-permute-start(bf16[2,256,768]{2,1,0:T(8,128)(2,1)S(1)} %pad_maximum_fusion), channel_id=1, source_target_pairs={{0,1},{1,0},{2,3},{3,2},{4,5},{5,4},{6,7},{7,6},{8,9},{9,8},{10,11... | collective-permute-start | bytes 2359304 | tf_op jit(solution)/shard_map/ppermute | solution.py:24
  140.7 12.2 %copy-start.2 = (bf16[2,512,768]{2,1,0:T(8,128)(2,1)S(1)}, bf16[2,512,768]{2,1,0:T(8,128)(2,1)}, u32[]{:S(2)}) copy-start(bf16[2,512,768]{2,1,0:T(8,128)(2,1)} %copy-done.1) | copy-start | bytes 4718596
  141.6 27.8 %all-to-all-start.3 = ((bf16[2,64,768]{2,0,1:T(2,128)(2,1)}), bf16[2,64,768]{2,0,1:T(2,128)(2,1)S(1)}, u32[]{:S(2)}, u32[]{:S(2)}) async-start(bf16[2,64,768]{2,0,1:T(2,128)(2,1)} %copy.22), calls=%async_computation.3 | async-start | bytes 393216 | tf_op jit(solution)/shard_map/all_to_all | solution.py:78
  152.9 17.3 %copy-start.3 = (bf16[1,6144]{1,0:T(2,128)(2,1)S(1)}, bf16[1,6144]{1,0:T(2,128)(2,1)}, u32[]{:S(2)}) copy-start(bf16[1,6144]{1,0:T(2,128)(2,1)} %param.4) | copy-start | bytes 36868
  152.9 19.3 %copy-start.5 = (bf16[1,6144]{1,0:T(2,128)(2,1)S(1)}, bf16[1,6144]{1,0:T(2,128)(2,1)}, u32[]{:S(2)}) copy-start(bf16[1,6144]{1,0:T(2,128)(2,1)} %param.7) | copy-start | bytes 36868

commit v3 on v2

v3 whole, which is shorter than its diff:
```python
import jax
import jax.numpy as jnp
from jax import lax
from jax.sharding import Mesh, PartitionSpec as P

epsilon = 1e-06
AXES = ("zh", "y", "zl", "x", "core")
SIZES = (2, 4, 8, 4, 2)
ZH, Y, ZL, X, CORE = SIZES
FAR = ("zh", "zl")
f32 = jnp.float32
bf16 = jnp.bfloat16


def gelu_tanh(values):
    return jax.nn.gelu(values, approximate=True)


def gelu_grad(pre_values, upstream):
    return jax.vjp(gelu_tanh, pre_values)[1](upstream)[0]


def swap(values, axis):
    return lax.ppermute(values, axis, [(0, 1), (1, 0)])


def shift(values, axis, step):
    count = lax.axis_size(axis)
    return lax.ppermute(values, axis, [(at, (at + step) % count) for at in range(count)])


def trade(values, axis):
    return lax.all_to_all(values, axis, split_axis=0, concat_axis=0, tiled=True)


def total(parts):
    return jnp.sum(parts.astype(f32), axis=0)


def local(tokens, w_in, w_out, cotangent):
    contract_last = (((1,), (1,)), ((), ()))
    contract_first = (((0,), (0,)), ((), ()))
    width = w_in.shape[0]
    hidden = w_in.shape[1]
    features = Y * width
    here = lax.axis_index("y")

    tokens_wide = tokens.astype(f32)
    row_mean = jnp.mean(tokens_wide, axis=1, keepdims=True)
    centered = tokens_wide - row_mean
    inv_scale = lax.rsqrt(jnp.mean(centered * centered, axis=1, keepdims=True) + epsilon)
    unit_rows = centered * inv_scale
    normed = unit_rows.astype(bf16)

    both = jnp.concatenate([normed.reshape(1, ZH, 1, features), cotangent.reshape(1, ZH, 1, features)])
    both = jnp.broadcast_to(both, (2, ZH, ZL, features)).reshape(2, ZH * ZL, features)

    block = jnp.stack([w_in, jnp.concatenate([w_out[:, :hidden], w_out[:, hidden:]], axis=0)])
    both, block = lax.optimization_barrier((both, block))
    below = shift(block, "y", 1)
    above = shift(block, "y", -1)
    far_in = shift(below[0], "y", 1)
    far_out = shift(above[1], "y", -1)
    w_ins = jnp.zeros((Y, width, hidden), bf16)
    w_outs = jnp.zeros((Y, hidden, width), bf16)
    for step, ins, outs in ((0, w_in, block[1]), (3, below[0], below[1]), (1, above[0], above[1]), (2, far_in, far_out)):
        at = lax.rem(here + step, Y)
        w_ins = lax.dynamic_update_slice(w_ins, ins[None], (at, 0, 0))
        w_outs = lax.dynamic_update_slice(w_outs, outs[None, :hidden], (at, 0, 0))
        w_outs = lax.dynamic_update_slice(w_outs, outs[None, hidden:], (at, 0, hidden))
    w_ins = w_ins.reshape(features, hidden)

    both = lax.all_to_all(both, FAR, split_axis=1, concat_axis=1, tiled=True)
    both = lax.all_gather(both, "x", axis=1, tiled=True)
    rows = jnp.concatenate([both, swap(both, "core")], axis=1)
    count = rows.shape[1]

    pre_part = jnp.dot(rows[0], w_ins, preferred_element_type=f32)
    grad_part = sum(
        lax.dot_general(rows[1, :, at : at + width], w_outs[at // width], contract_last, preferred_element_type=f32)
        for at in range(0, features, width)
    )
    parts = jnp.stack([pre_part, grad_part])
    spread = jnp.stack([rows[:, :, at : at + width] for at in range(0, features, width)])
    far, spread = lax.optimization_barrier((parts.astype(bf16), spread))
    far = swap(far, "zh")
    spread = trade(spread, "y")
    far, spread = lax.optimization_barrier((far, spread))
    summed = parts + far.astype(f32)
    pre, act_grad = summed[0], summed[1]
    act = gelu_tanh(pre).astype(bf16)
    pre_grad = gelu_grad(pre, act_grad).astype(bf16)

    out_part = jnp.concatenate([jnp.dot(act, w_outs[at], preferred_element_type=f32) for at in range(Y)], axis=1)
    back_part = lax.dot_general(pre_grad, w_ins, contract_last, preferred_element_type=f32)
    parts = jnp.stack([out_part, back_part])
    half = count // CORE
    sums = parts[:, :half] + swap(parts[:, half:].astype(bf16), "core").astype(f32)
    sums = sums.astype(bf16).reshape(2, X, half // X, features).transpose(1, 0, 2, 3)
    sums = total(trade(sums, "x"))
    sums, pair = lax.optimization_barrier((sums.astype(bf16), jnp.stack([act, pre_grad])))
    sums = lax.all_to_all(sums, FAR, split_axis=1, concat_axis=1, tiled=True)
    whole = jnp.sum(sums.astype(f32).reshape(2, ZH, ZL, features), axis=2).reshape(2, 1, ZH * features)

    flat_normed = spread[:, 0].reshape(Y * count, width)
    flat_grad = spread[:, 1].reshape(Y * count, width)
    full = lax.all_gather(pair, "y", axis=1, tiled=True)
    grad_w_out = lax.dot_general(full[0], flat_grad, contract_first, preferred_element_type=f32)
    grad_w_in = lax.dot_general(flat_normed, full[1], contract_first, preferred_element_type=f32)

    mixed = (tokens_wide + whole[0]).astype(bf16)
    normed_grad = whole[1]
    row_inner = jnp.mean(normed_grad * unit_rows, axis=1, keepdims=True)
    through = inv_scale * (
        normed_grad - jnp.mean(normed_grad, axis=1, keepdims=True) - unit_rows * row_inner
    )
    grad_tokens = (cotangent.astype(f32) + through).astype(bf16)
    return (mixed, grad_tokens, grad_w_in, grad_w_out)


def solution(mesh):
    fine = Mesh(mesh.devices.reshape(SIZES), AXES)
    dp, mp = ("zh", "y"), ("zl", "x", "core")
    return jax.shard_map(
        local,
        mesh=fine,
        in_specs=(P(dp + mp, None), P(dp, mp), P(mp, dp), P(dp + mp, None)),
        out_specs=(P(dp + mp, None), P(dp + mp, None), P(dp, mp), P(mp, dp)),
        check_vma=False,
    )
```

time: 174 us -> 180 us (1.034); the launches traced: 173 us -> 177 us
  blocking collectives: 97.1 us -> 27.8 us
  starting transfers between devices: 15.2 us -> 59 us
  local copies, waits for them, and re-layouts: 1.46 us -> 21 us
  matrix products: 6.58 us -> 15.4 us
  other arithmetic: 7.45 us -> 10.1 us
    all_to_all x3 -> x0, blocking collectives: 68.8 us -> none  [the longest x1 38.7 us: local(): both = lax.all_to_all(both, FAR, split_axis=1, concat_axis=1, tiled=True)]
    all_to_all x1 -> x4, starting transfers between devices: 8.56 us -> 31.8 us  [the longest x1 15.2 us: local(): both = lax.all_to_all(both, FAR, split_axis=1, concat_axis=1, tiled=True)]
    ppermute x0 -> x4, starting transfers between devices: none -> 14.6 us  [shift(): lax.ppermute(values, axis, [(at, (at + step) % count) for at in range(cou...]
    dynamic_update_slice x0 -> x11, local copies, waits for them, and re-layouts: none -> 11.6 us  [the longest x4 5.07 us: local(): lax.dynamic_update_slice(w_outs, outs[None, hidden:], (at, 0, hidden))]
    dot_general x6 -> x12, matrix products: 6.58 us -> 15.4 us  [the longest x4 5.52 us: local(): lax.dot_general(rows[1, :, at:at + width], w_outs[at // width], contract_...]
    ppermute x3, starting transfers between devices: 6.68 us -> 12.6 us  [swap(): return lax.ppermute(values, axis, [(0, 1), (1, 0)])]
    ppermute x0 -> x4, waiting for transfers between devices: none -> 4.75 us  [shift(): lax.ppermute(values, axis, [(at, (at + step) % count) for at in range(cou...]
    ppermute x3, waiting for transfers between devices: 26.5 us -> 23.1 us  [swap(): return lax.ppermute(values, axis, [(0, 1), (1, 0)])]
  transfers between devices with their start and end apart: 4 -> 11, of which waited for: 4 -> 5; matrix products, arithmetic and copies ran while one was open for 3% -> 15% of each run, Pallas kernels for 0% -> 0%
where the time goes in v3:
time: 180 us; the launch traced here: 177 us
  starting transfers between devices  59 us (33%)
  waiting for transfers between devices  39.8 us (22%)
  blocking collectives  27.8 us (15%)
  local copies, waits for them, and re-layouts  21 us (12%)
  matrix products  15.4 us (9%)
  other arithmetic  10.1 us (6%)
  between operations  3.59 us (2%)
    ppermute x3, waiting for transfers between devices, swap(): return lax.ppermute(values, axis, [(0, 1), (1, 0)])  23.1 us
    all_to_all x1, starting transfers between devices, local(): both = lax.all_to_all(both, FAR, split_axis=1, concat_axis=1, tiled=True)  15.2 us
    ppermute x4, starting transfers between devices, shift(): lax.ppermute(values, axis, [(at, (at + step) % count) for at in range(cou...  14.6 us
    all_gather x1, blocking collectives, local(): full = lax.all_gather(pair, 'y', axis=1, tiled=True)  14.5 us
    all_gather x1, blocking collectives, local(): both = lax.all_gather(both, 'x', axis=1, tiled=True)  13.3 us
    ppermute x3, starting transfers between devices, swap(): return lax.ppermute(values, axis, [(0, 1), (1, 0)])  12.6 us
    all_to_all x2, starting transfers between devices, trade(): return lax.all_to_all(values, axis, split_axis=0, concat_axis=0, tiled=True)  9.41 us
    all_to_all x2, waiting for transfers between devices, trade(): return lax.all_to_all(values, axis, split_axis=0, concat_axis=0, tiled=True)  9.01 us
  transfers between devices with their start and end apart: 11, of which 5 were waited for; matrix products, arithmetic and copies ran while one was open for 15% of the time, Pallas kernels for 0%

profile of v3, /device:TPU:6, one launch (start us, length us, event | category | flops | bytes accessed | tf_op | source)
XLA Modules:
  0.0 176.7 jit_solution(7388707733567097478)
XLA Ops:
  0.6 0.9 reduce.7
  1.5 1.4 convert_reduce_fusion.2
  3.6 1.4 multiply_reduce_fusion.1
  5.7 0.8 convert_reduce_fusion.1
  6.6 1.1 fusion.33
  7.8 1.1 pad_maximum_fusion.2
  8.9 0.8 broadcast_in_dim.15
  9.7 15.2 %all-to-all-start = ((bf16[2,16,3072]{2,0,1:T(2,128)(2,1)}), bf16[2,16,3072]{2,0,1:T(2,128)(2,1)}, u32[]{:S(2)}, u32[]{:S(2)}) async-start(bf16[2,16,3072]{2,0,1:T(2,128)(2,1)} %bitcast.1), calls=%async_computation | async-start | bytes 393216 | tf_op jit(solution)/shard_map/all_to_all | solution.py:73
  24.9 3.5 %collective-permute-start.1 = (bf16[2,768,384]{2,1,0:T(8,128)(2,1)}, bf16[2,768,384]{2,1,0:T(8,128)(2,1)}, u32[]{:S(2)}, u32[]{:S(2)}) collective-permute-start(bf16[2,768,384]{2,1,0:T(8,128)(2,1)} %pad_maximum_fusion.2), channel_id=1, source_target_pairs={{0,64},{64,128},{128,192},{192,0},{1,65},{65,129},{129,193},{193,1... | collective-permute-start | bytes 3538952 | tf_op jit(solution)/shard_map/ppermute | solution.py:29
  28.4 3.6 %collective-permute-start.2 = (bf16[2,768,384]{2,1,0:T(8,128)(2,1)}, bf16[2,768,384]{2,1,0:T(8,128)(2,1)S(1)}, u32[]{:S(2)}, u32[]{:S(2)}) collective-permute-start(bf16[2,768,384]{2,1,0:T(8,128)(2,1)} %pad_maximum_fusion.2), channel_id=1, source_target_pairs={{0,192},{64,0},{128,64},{192,128},{1,193},{65,1},{129,65},{193,129... | collective-permute-start | bytes 3538952 | tf_op jit(solution)/shard_map/ppermute | solution.py:29
  32.0 1.6 broadcast_in_dim.18
  33.6 1.7 slice_dynamic-update-slice_fusion.7
  35.3 1.7 slice_dynamic-update-slice_fusion.6
  37.1 0.2 broadcast_in_dim.16
  37.3 1.2 constant_dynamic-update-slice_fusion.2
  38.5 3.0 %all-to-all-done = bf16[2,16,3072]{2,0,1:T(2,128)(2,1)} async-done(((bf16[2,16,3072]{2,0,1:T(2,128)(2,1)}), bf16[2,16,3072]{2,0,1:T(2,128)(2,1)}, u32[]{:S(2)}, u32[]{:S(2)}) %all-to-all-start) | async-done | bytes 196640 | tf_op jit(solution)/shard_map/all_to_all | solution.py:73
  41.4 1.0 copy.14
  42.4 13.3 %all_gather.6 = bf16[2,64,3072]{2,1,0:T(8,128)(2,1)S(1)} all-gather(bf16[2,16,3072]{2,1,0:T(8,128)(2,1)S(1)} %copy.14), channel_id=1, replica_groups=mesh['zh'=2,'y'=4,'zl'=8,'x'=4,'core'=2] {'x'}, dimensions={1}, use_global_device_ids=true | all-gather | bytes 983040 | tf_op jit(solution)/shard_map/all_gather | solution.py:74
  55.7 1.9 %collective-permute-start = (bf16[2,64,3072]{2,1,0:T(8,128)(2,1)S(1)}, bf16[2,64,3072]{2,1,0:T(8,128)(2,1)S(1)}, u32[]{:S(2)}, u32[]{:S(2)}) collective-permute-start(bf16[2,64,3072]{2,1,0:T(8,128)(2,1)S(1)} %all_gather.6), channel_id=1, source_target_pairs={{0,1},{1,0},{2,3},{3,2},{4,5},{5,4},{6,7},{7,6},{8,9},{9,8},{10,11... | collective-permute-start | bytes 2359304 | tf_op jit(solution)/shard_map/ppermute | solution.py:24
  57.7 1.2 slice_bitcast_fusion.15
  59.0 0.2 slice_dynamic-update-slice_fusion
  59.2 5.6 %collective-permute-start.4 = (bf16[768,384]{1,0:T(8,128)(2,1)S(1)}, bf16[768,384]{1,0:T(8,128)(2,1)S(1)}, u32[]{:S(2)}, u32[]{:S(2)}) collective-permute-start(bf16[768,384]{1,0:T(8,128)(2,1)S(1)} %get-tuple-element.29), channel_id=1, source_target_pairs={{0,192},{64,0},{128,64},{192,128},{1,193},{65,1},{129,65},{193,129... | collective-permute-start | bytes 1769480 | tf_op jit(solution)/shard_map/ppermute | solution.py:29
  64.8 1.9 %collective-permute-start.3 = (bf16[768,384]{1,0:T(8,128)(2,1)S(1)}, bf16[768,384]{1,0:T(8,128)(2,1)S(1)}, u32[]{:S(2)}, u32[]{:S(2)}) collective-permute-start(bf16[768,384]{1,0:T(8,128)(2,1)S(1)} %get-tuple-element.26), channel_id=1, source_target_pairs={{0,64},{64,128},{128,192},{192,0},{1,65},{65,129},{129,193},{193,1... | collective-permute-start | bytes 1769480 | tf_op jit(solution)/shard_map/ppermute | solution.py:29
  66.7 1.7 slice_dynamic-update-slice_fusion.5
  68.5 1.7 slice_dynamic-update-slice_fusion.4
  70.2 0.8 slice_dynamic-update-slice_fusion.3
  71.0 0.8 slice_dynamic-update-slice_fusion.2
  71.8 0.1 slice_bitcast_fusion.23
  71.9 1.3 pad_maximum_fusion.1
  73.3 4.7 %collective-permute-done.4 = bf16[768,384]{1,0:T(8,128)(2,1)S(1)} collective-permute-done((bf16[768,384]{1,0:T(8,128)(2,1)S(1)}, bf16[768,384]{1,0:T(8,128)(2,1)S(1)}, u32[]{:S(2)}, u32[]{:S(2)}) %collective-permute-start.4) | collective-permute-done | bytes 589856 | tf_op jit(solution)/shard_map/ppermute | solution.py:29
  78.0 0.8 fusion.18
  78.8 0.8 fusion.17
  79.6 1.4 fusion.13
  81.0 1.4 fusion.11
  82.4 1.4 fusion.9
  83.9 0.6 convolution_bitcast_fusion.1
  84.5 1.4 fusion.6
  85.9 4.9 %all-to-all-start.1 = ((bf16[4,2,128,768]{3,2,1,0:T(8,128)(2,1)}), bf16[4,2,128,768]{3,2,1,0:T(8,128)(2,1)}, u32[]{:S(2)}, u32[]{:S(2)}) async-start(bf16[4,2,128,768]{3,2,1,0:T(8,128)(2,1)} %pad_maximum_fusion.1), calls=%async_computation.1 | async-start | bytes 3145728 | tf_op jit(solution)/shard_map/all_to_all | solution.py:33
  90.9 8.8 %collective-permute-start.5 = (bf16[2,128,384]{2,1,0:T(8,128)(2,1)S(1)}, bf16[2,128,384]{2,1,0:T(8,128)(2,1)S(1)}, u32[]{:S(2)}, u32[]{:S(2)}) collective-permute-start(bf16[2,128,384]{2,1,0:T(8,128)(2,1)S(1)} %fusion.16), channel_id=1, source_target_pairs={{0,256},{256,0},{1,257},{257,1},{2,258},{258,2},{3,259},{259,3},{4... | collective-permute-start | bytes 589832 | tf_op jit(solution)/shard_map/ppermute | solution.py:24
  99.6 20.8 %collective-permute-done.5 = bf16[2,128,384]{2,1,0:T(8,128)(2,1)S(1)} collective-permute-done((bf16[2,128,384]{2,1,0:T(8,128)(2,1)S(1)}, bf16[2,128,384]{2,1,0:T(8,128)(2,1)S(1)}, u32[]{:S(2)}, u32[]{:S(2)}) %collective-permute-start.5) | collective-permute-done | bytes 196640 | tf_op jit(solution)/shard_map/ppermute | solution.py:24
  120.5 0.2 fusion.25
  120.6 1.3 fusion.12
  122.0 1.3 fusion.10
  123.3 1.3 fusion.8
  124.6 1.3 fusion.7
  125.9 0.9 convolution_bitcast_fusion
  126.8 0.2 maximum_bitcast_fusion
  127.1 1.9 %collective-permute-start.6 = (bf16[2,64,3072]{2,1,0:T(8,128)(2,1)S(1)}, bf16[2,64,3072]{2,1,0:T(8,128)(2,1)S(1)}, u32[]{:S(2)}, u32[]{:S(2)}) collective-permute-start(bf16[2,64,3072]{2,1,0:T(8,128)(2,1)S(1)} %fusion.3), channel_id=1, source_target_pairs={{0,1},{1,0},{2,3},{3,2},{4,5},{5,4},{6,7},{7,6},{8,9},{9,8},{10,11... | collective-permute-start | bytes 2359304 | tf_op jit(solution)/shard_map/ppermute | solution.py:24
  129.0 2.3 %collective-permute-done.6 = bf16[2,64,3072]{2,1,0:T(8,128)(2,1)S(1)} collective-permute-done((bf16[2,64,3072]{2,1,0:T(8,128)(2,1)S(1)}, bf16[2,64,3072]{2,1,0:T(8,128)(2,1)S(1)}, u32[]{:S(2)}, u32[]{:S(2)}) %collective-permute-start.6) | collective-permute-done | bytes 786464 | tf_op jit(solution)/shard_map/ppermute | solution.py:24
  131.2 0.2 fusion.2
  131.4 0.9 copy.18
  132.4 4.5 %all-to-all-start.2 = ((bf16[4,2,16,3072]{3,2,1,0:T(8,128)(2,1)}), bf16[4,2,16,3072]{3,2,1,0:T(8,128)(2,1)S(1)}, u32[]{:S(2)}, u32[]{:S(2)}) async-start(bf16[4,2,16,3072]{3,2,1,0:T(8,128)(2,1)} %bitcast.101), calls=%async_computation.2 | async-start | bytes 1572864 | tf_op jit(solution)/shard_map/all_to_all | solution.py:33
  136.9 1.5 fusion.32
  138.4 9.0 %all-to-all-done.2 = bf16[4,2,16,3072]{3,2,1,0:T(8,128)(2,1)S(1)} async-done(((bf16[4,2,16,3072]{3,2,1,0:T(8,128)(2,1)}), bf16[4,2,16,3072]{3,2,1,0:T(8,128)(2,1)S(1)}, u32[]{:S(2)}, u32[]{:S(2)}) %all-to-all-start.2) | async-done | bytes 786464 | tf_op jit(solution)/shard_map/all_to_all | solution.py:33
  147.4 0.2 reduce_sum.59
  147.6 0.9 copy.16
  148.4 7.2 %all-to-all-start.3 = ((bf16[2,16,3072]{2,0,1:T(2,128)(2,1)}), bf16[2,16,3072]{2,0,1:T(2,128)(2,1)S(1)}, u32[]{:S(2)}, u32[]{:S(2)}) async-start(bf16[2,16,3072]{2,0,1:T(2,128)(2,1)} %copy.16), calls=%async_computation.3 | async-start | bytes 393216 | tf_op jit(solution)/shard_map/all_to_all | solution.py:102
  155.6 14.5 %all_gather.7 = bf16[2,512,384]{2,1,0:T(8,128)(2,1)S(1)} all-gather(bf16[2,128,384]{2,1,0:T(8,128)(2,1)S(1)} %pad_maximum_fusion.4), channel_id=1, replica_groups=mesh['zh'=2,'y'=4,'zl'=8,'x'=4,'core'=2] {'y'}, dimensions={1}, use_global_device_ids=true | all-gather | bytes 983040 | tf_op jit(solution)/shard_map/all_gather | solution.py:107
  170.1 1.6 fusion.15
  171.7 1.5 fusion.14
  173.2 0.2 convert_reduce_fusion
  173.4 0.7 slice_reduce_fusion
  174.1 0.7 multiply_reduce_fusion
  176.0 0.7 add_convert_fusion
  (24 shorter events, 0.6 us)
Async XLA Ops:
  0.6 7.1 %copy-start = (bf16[768,384]{1,0:T(8,128)(2,1)S(1)}, bf16[768,384]{1,0:T(8,128)(2,1)}, u32[]{:S(2)}) copy-start(bf16[768,384]{1,0:T(8,128)(2,1)} %param.5) | copy-start | bytes 1769476
  9.7 31.7 %all-to-all-start = ((bf16[2,16,3072]{2,0,1:T(2,128)(2,1)}), bf16[2,16,3072]{2,0,1:T(2,128)(2,1)}, u32[]{:S(2)}, u32[]{:S(2)}) async-start(bf16[2,16,3072]{2,0,1:T(2,128)(2,1)} %bitcast.1), calls=%async_computation | async-start | bytes 393216 | tf_op jit(solution)/shard_map/all_to_all | solution.py:73
  24.9 32.8 %collective-permute-start.1 = (bf16[2,768,384]{2,1,0:T(8,128)(2,1)}, bf16[2,768,384]{2,1,0:T(8,128)(2,1)}, u32[]{:S(2)}, u32[]{:S(2)}) collective-permute-start(bf16[2,768,384]{2,1,0:T(8,128)(2,1)} %pad_maximum_fusion.2), channel_id=1, source_target_pairs={{0,64},{64,128},{128,192},{192,0},{1,65},{65,129},{129,193},{193,1... | collective-permute-start | bytes 3538952 | tf_op jit(solution)/shard_map/ppermute | solution.py:29
  28.4 30.5 %collective-permute-start.2 = (bf16[2,768,384]{2,1,0:T(8,128)(2,1)}, bf16[2,768,384]{2,1,0:T(8,128)(2,1)S(1)}, u32[]{:S(2)}, u32[]{:S(2)}) collective-permute-start(bf16[2,768,384]{2,1,0:T(8,128)(2,1)} %pad_maximum_fusion.2), channel_id=1, source_target_pairs={{0,192},{64,0},{128,64},{192,128},{1,193},{65,1},{129,65},{193,129... | collective-permute-start | bytes 3538952 | tf_op jit(solution)/shard_map/ppermute | solution.py:29
  55.7 16.0 %collective-permute-start = (bf16[2,64,3072]{2,1,0:T(8,128)(2,1)S(1)}, bf16[2,64,3072]{2,1,0:T(8,128)(2,1)S(1)}, u32[]{:S(2)}, u32[]{:S(2)}) collective-permute-start(bf16[2,64,3072]{2,1,0:T(8,128)(2,1)S(1)} %all_gather.6), channel_id=1, source_target_pairs={{0,1},{1,0},{2,3},{3,2},{4,5},{5,4},{6,7},{7,6},{8,9},{9,8},{10,11... | collective-permute-start | bytes 2359304 | tf_op jit(solution)/shard_map/ppermute | solution.py:24
  59.2 18.9 %collective-permute-start.4 = (bf16[768,384]{1,0:T(8,128)(2,1)S(1)}, bf16[768,384]{1,0:T(8,128)(2,1)S(1)}, u32[]{:S(2)}, u32[]{:S(2)}) collective-permute-start(bf16[768,384]{1,0:T(8,128)(2,1)S(1)} %get-tuple-element.29), channel_id=1, source_target_pairs={{0,192},{64,0},{128,64},{192,128},{1,193},{65,1},{129,65},{193,129... | collective-permute-start | bytes 1769480 | tf_op jit(solution)/shard_map/ppermute | solution.py:29
  64.8 19.0 %collective-permute-start.3 = (bf16[768,384]{1,0:T(8,128)(2,1)S(1)}, bf16[768,384]{1,0:T(8,128)(2,1)S(1)}, u32[]{:S(2)}, u32[]{:S(2)}) collective-permute-start(bf16[768,384]{1,0:T(8,128)(2,1)S(1)} %get-tuple-element.26), channel_id=1, source_target_pairs={{0,64},{64,128},{128,192},{192,0},{1,65},{65,129},{129,193},{193,1... | collective-permute-start | bytes 1769480 | tf_op jit(solution)/shard_map/ppermute | solution.py:29
  85.9 34.5 %all-to-all-start.1 = ((bf16[4,2,128,768]{3,2,1,0:T(8,128)(2,1)}), bf16[4,2,128,768]{3,2,1,0:T(8,128)(2,1)}, u32[]{:S(2)}, u32[]{:S(2)}) async-start(bf16[4,2,128,768]{3,2,1,0:T(8,128)(2,1)} %pad_maximum_fusion.1), calls=%async_computation.1 | async-start | bytes 3145728 | tf_op jit(solution)/shard_map/all_to_all | solution.py:33
  90.9 29.6 %collective-permute-start.5 = (bf16[2,128,384]{2,1,0:T(8,128)(2,1)S(1)}, bf16[2,128,384]{2,1,0:T(8,128)(2,1)S(1)}, u32[]{:S(2)}, u32[]{:S(2)}) collective-permute-start(bf16[2,128,384]{2,1,0:T(8,128)(2,1)S(1)} %fusion.16), channel_id=1, source_target_pairs={{0,256},{256,0},{1,257},{257,1},{2,258},{258,2},{3,259},{259,3},{4... | collective-permute-start | bytes 589832 | tf_op jit(solution)/shard_map/ppermute | solution.py:24
  127.1 4.2 %collective-permute-start.6 = (bf16[2,64,3072]{2,1,0:T(8,128)(2,1)S(1)}, bf16[2,64,3072]{2,1,0:T(8,128)(2,1)S(1)}, u32[]{:S(2)}, u32[]{:S(2)}) collective-permute-start(bf16[2,64,3072]{2,1,0:T(8,128)(2,1)S(1)} %fusion.3), channel_id=1, source_target_pairs={{0,1},{1,0},{2,3},{3,2},{4,5},{5,4},{6,7},{7,6},{8,9},{9,8},{10,11... | collective-permute-start | bytes 2359304 | tf_op jit(solution)/shard_map/ppermute | solution.py:24
  132.4 15.0 %all-to-all-start.2 = ((bf16[4,2,16,3072]{3,2,1,0:T(8,128)(2,1)}), bf16[4,2,16,3072]{3,2,1,0:T(8,128)(2,1)S(1)}, u32[]{:S(2)}, u32[]{:S(2)}) async-start(bf16[4,2,16,3072]{3,2,1,0:T(8,128)(2,1)} %bitcast.101), calls=%async_computation.2 | async-start | bytes 1572864 | tf_op jit(solution)/shard_map/all_to_all | solution.py:33
  148.4 24.8 %all-to-all-start.3 = ((bf16[2,16,3072]{2,0,1:T(2,128)(2,1)}), bf16[2,16,3072]{2,0,1:T(2,128)(2,1)S(1)}, u32[]{:S(2)}, u32[]{:S(2)}) async-start(bf16[2,16,3072]{2,0,1:T(2,128)(2,1)} %copy.16), calls=%async_computation.3 | async-start | bytes 393216 | tf_op jit(solution)/shard_map/all_to_all | solution.py:102
  171.7 2.4 %copy-start.1 = (bf16[1,6144]{1,0:T(2,128)(2,1)S(1)}, bf16[1,6144]{1,0:T(2,128)(2,1)}, u32[]{:S(2)}) copy-start(bf16[1,6144]{1,0:T(2,128)(2,1)} %param.4) | copy-start | bytes 36868
  171.7 4.3 %copy-start.2 = (bf16[1,6144]{1,0:T(2,128)(2,1)S(1)}, bf16[1,6144]{1,0:T(2,128)(2,1)}, u32[]{:S(2)}) copy-start(bf16[1,6144]{1,0:T(2,128)(2,1)} %param.7) | copy-start | bytes 36868

commit v4 on v2

v4 whole, which is shorter than its diff:
```python
import jax
import jax.numpy as jnp
from jax import lax
from jax.experimental import pallas as pl
from jax.experimental.pallas import tpu as pltpu
from jax.sharding import Mesh, PartitionSpec as P

epsilon = 1e-06
AXES = ("zh", "y", "zl", "x", "core")
SIZES = (2, 4, 8, 4, 2)
ZH, Y, ZL, X, CORE = SIZES
FAR = ("zh", "zl")
f32 = jnp.float32
bf16 = jnp.bfloat16
LAST = (((1,), (1,)), ((), ()))
FIRST = (((0,), (0,)), ((), ()))
RATE = 0.7978845608028654
CUBE = 0.044715


def swap(values, axis):
    return lax.ppermute(values, axis, [(0, 1), (1, 0)])


def shift(values, axis, step):
    count = lax.axis_size(axis)
    return lax.ppermute(values, axis, [(at, (at + step) % count) for at in range(count)])


def trade(values, axis):
    return lax.all_to_all(values, axis, split_axis=0, concat_axis=0, tiled=True)


def total(parts):
    return jnp.sum(parts.astype(f32), axis=0)


def dot(left, right, contract=(((1,), (0,)), ((), ()))):
    return lax.dot_general(left, right, contract, preferred_element_type=f32)


def call(body, shapes, *args, flops=0):
    moved = sum(a.size * a.dtype.itemsize for a in args) + sum(s.size * s.dtype.itemsize for s in shapes)
    specs = [
        pl.BlockSpec(memory_space=pltpu.SMEM if a.dtype == jnp.int32 else pltpu.VMEM) for a in args
    ]
    return pl.pallas_call(
        body,
        out_shape=shapes,
        in_specs=specs,
        out_specs=[pl.BlockSpec(memory_space=pltpu.VMEM) for _ in shapes],
        compiler_params=pltpu.CompilerParams(vmem_limit_bytes=min(2 * moved + (6 << 20), 40 << 20)),
        cost_estimate=pl.CostEstimate(flops=flops, bytes_accessed=moved, transcendentals=0),
    )(*args)


def unit(tokens):
    width = tokens.shape[1]
    centered = tokens - jnp.sum(tokens, axis=1, keepdims=True) / width
    inv_scale = lax.rsqrt(jnp.sum(centered * centered, axis=1, keepdims=True) / width + epsilon)
    return centered * inv_scale, inv_scale


def pack_body(tokens, cotangent, w_in, w_out, out, block):
    hidden = w_in.shape[1]
    block[0] = w_in[...]
    block[1, :hidden] = w_out[:, :hidden]
    block[1, hidden:] = w_out[:, hidden:]
    features = out.shape[2]
    normed = unit(tokens[...].astype(f32))[0]
    grads = cotangent[...].astype(f32)
    for part in range(ZH):
        cut = slice(part * features, (part + 1) * features)
        pair = jnp.concatenate([normed[:, cut], grads[:, cut]], axis=0).astype(bf16)
        out[part * ZL : (part + 1) * ZL] = jnp.broadcast_to(pair[None], (ZL,) + pair.shape)


def place(here, step, width):
    return pl.multiple_of(lax.rem(here + step, Y) * width, 128)


def hidden_body(here, rows, other, b0, b1, b3, far_in, far_out, out):
    width, hidden = far_in.shape
    pre = grad = None
    for step, (ins, cols) in enumerate(
        ((b0.at[0], b0.at[1]), (b1.at[0], b1.at[1]), (far_in, far_out), (b3.at[0], b3.at[1]))
    ):
        at = place(here[0], step, width)
        left = jnp.concatenate([rows[0, :, pl.ds(at, width)], other[0, :, pl.ds(at, width)]], axis=0)
        terms = [dot(left, ins[...])]
        for part in range(width // hidden):
            cut = pl.ds(pl.multiple_of(at + part * hidden, 128), hidden)
            right = jnp.concatenate([rows[1, :, cut], other[1, :, cut]], axis=0)
            terms.append(dot(right, cols[part * hidden : (part + 1) * hidden], LAST))
        one, two = terms[0], sum(terms[1:])
        pre = one if pre is None else pre + one
        grad = two if grad is None else grad + two
    pre, grad = pre.astype(bf16), grad.astype(bf16)
    for part in range(ZH):
        out[part, 0] = pre
        out[part, 1] = grad


def split_body(here, rows, other, *outs):
    half = rows.shape[1]
    width = outs[0].shape[2]
    for step, out in enumerate(outs):
        at = pl.ds(place(here[0], step, width), width)
        out[:, :half] = rows[:, :, at]
        out[:, half:] = other[:, :, at]


def output_body(here, parts, b0, b1, b3, far_in, far_out, pair, keep, give):
    width, hidden = far_in.shape
    half = keep.shape[1]
    value = parts[0, 0].astype(f32) + parts[1, 0].astype(f32)
    upstream = parts[0, 1].astype(f32) + parts[1, 1].astype(f32)
    square = value * value
    curve = jnp.tanh(RATE * (value + CUBE * (square * value)))
    chance = 0.5 * (1.0 + curve)
    slope = chance + 0.5 * value * (1.0 - curve * curve) * (RATE * (1.0 + 3.0 * CUBE * square))
    act = (value * chance).astype(bf16)
    pre_grad = (upstream * slope).astype(bf16)
    pair[0] = act
    pair[1] = pre_grad
    for step, (ins, cols) in enumerate(
        ((b0.at[0], b0.at[1]), (b1.at[0], b1.at[1]), (far_in, far_out), (b3.at[0], b3.at[1]))
    ):
        at = place(here[0], step, width)
        term = dot(pre_grad, ins[...], LAST)
        keep[1, :, pl.ds(at, width)] = term[:half]
        give[1, :, pl.ds(at, width)] = term[half:].astype(bf16)
        for part in range(width // hidden):
            cut = pl.ds(pl.multiple_of(at + part * hidden, 128), hidden)
            term = dot(act, cols[part * hidden : (part + 1) * hidden])
            keep[0, :, cut] = term[:half]
            give[0, :, cut] = term[half:].astype(bf16)


def weight_body(here, full, r0, r1, r2, r3, grad_w_in, grad_w_out):
    count = r0.shape[1]
    ins = outs = None
    for step, rows in enumerate((r0, r1, r2, r3)):
        at = pl.ds(pl.multiple_of(lax.rem(here[0] + Y - step, Y) * count, 128), count)
        one, two = dot(rows[0], full[1, at], FIRST), dot(full[0, at], rows[1], FIRST)
        ins = one if ins is None else ins + one
        outs = two if outs is None else outs + two
    grad_w_in[...] = ins
    grad_w_out[...] = outs


def final_body(tokens, cotangent, sums, mixed, grad_tokens):
    features = sums.shape[2]
    tokens_wide = tokens[...].astype(f32)
    unit_rows, inv_scale = unit(tokens_wide)
    halves = [
        jnp.sum(sums[part * ZL : (part + 1) * ZL].astype(f32), axis=0) for part in range(ZH)
    ]
    whole = jnp.concatenate(halves, axis=1)
    count = ZH * features
    mixed[...] = (tokens_wide + whole[0:1]).astype(bf16)
    normed_grad = whole[1:2]
    inner = jnp.sum(normed_grad * unit_rows, axis=1, keepdims=True) / count
    mean = jnp.sum(normed_grad, axis=1, keepdims=True) / count
    through = inv_scale * (normed_grad - mean - unit_rows * inner)
    grad_tokens[...] = (cotangent[...].astype(f32) + through).astype(bf16)


def local(tokens, w_in, w_out, cotangent):
    width, hidden = w_in.shape
    features = Y * width
    count = X * ZL * ZH * CORE
    half = count // CORE
    here = lax.axis_index("y").reshape(1).astype(jnp.int32)
    shape = jax.ShapeDtypeStruct
    work = 4 * count * features * hidden

    both, block = call(
        pack_body,
        [shape((ZH * ZL, 2, features), bf16), shape((2, width, hidden), bf16)],
        tokens, cotangent, w_in, w_out,
    )
    both, block = lax.optimization_barrier((both, block))
    both = trade(both, FAR).transpose(1, 0, 2)
    rows = lax.all_gather(both, "x", axis=1, tiled=True)
    other = swap(rows, "core")

    below, above = shift(block, "y", 1), shift(block, "y", -1)
    blocks = (block, above, below, shift(below[0], "y", 1), shift(above[1], "y", -1))

    (parts,) = call(hidden_body, [shape((ZH, 2, count, hidden), bf16)], here, rows, other, *blocks, flops=work)
    parts, rows, other = lax.optimization_barrier((parts, rows, other))
    parts = trade(parts, "zh")
    split = call(split_body, [shape((2, count, width), bf16)] * Y, here, rows, other)
    near = (shift(split[1], "y", 1), shift(split[3], "y", 3))
    parts, near = lax.optimization_barrier((parts, near))
    pair, keep, give = call(
        output_body,
        [shape((2, count, hidden), bf16), shape((2, half, features), f32), shape((2, half, features), bf16)],
        here, parts, *blocks, flops=work,
    )

    sums = keep + swap(give, "core").astype(f32)
    sums = sums.astype(bf16).reshape(2, X, half // X, features).transpose(1, 0, 2, 3)
    sums, pair = lax.optimization_barrier((sums, pair))
    sums, full = trade(sums, "x"), lax.all_gather(pair, "y", axis=1, tiled=True)
    sums, full = lax.optimization_barrier((sums, full))
    sums = total(sums).astype(bf16).transpose(1, 0, 2)
    sums, opposite = lax.optimization_barrier((sums, split[2]))
    sums = trade(sums, FAR)
    mixed, grad_tokens = call(
        final_body, [shape(tokens.shape, bf16)] * 2, tokens, cotangent, sums
    )

    spread = (split[0], near[0], shift(opposite, "y", 2), near[1])
    grad_w_in, grad_w_out = call(
        weight_body,
        [shape((width, hidden), f32), shape((hidden, width), f32)],
        here, full, *spread, flops=work,
    )
    return (mixed, grad_tokens, grad_w_in, grad_w_out)


def solution(mesh):
    fine = Mesh(mesh.devices.reshape(SIZES), AXES)
    dp, mp = ("zh", "y"), ("zl", "x", "core")
    return jax.shard_map(
        local,
        mesh=fine,
        in_specs=(P(dp + mp, None), P(dp, mp), P(mp, dp), P(dp + mp, None)),
        out_specs=(P(dp + mp, None), P(dp + mp, None), P(dp, mp), P(mp, dp)),
        check_vma=False,
    )
```

time: 174 us -> 168 us (0.966)
  blocking collectives: 97.1 us -> 28.5 us
  starting transfers between devices: 15.2 us -> 68.3 us
  Pallas kernels: 0 us -> 12.7 us
  local copies, waits for them, and re-layouts: 1.46 us -> 11 us
  other arithmetic: 7.45 us -> 0.3 us
  matrix products: 6.58 us -> 0 us
  waiting for transfers between devices: 41.5 us -> 45.3 us
  between operations: 3.51 us -> 0.87 us
    all_to_all x3 -> x0, blocking collectives: 68.8 us -> none  [the longest x1 38.7 us: local(): both = lax.all_to_all(both, FAR, split_axis=1, concat_axis=1, tiled=True)]
    all_to_all x1 -> x4, starting transfers between devices: 8.56 us -> 40 us  [trade(): return lax.all_to_all(values, axis, split_axis=0, concat_axis=0, tiled=True)]
    ppermute x0 -> x7, waiting for transfers between devices: none -> 30.3 us  [shift(): lax.ppermute(values, axis, [(at, (at + step) % count) for at in range(cou...]
    ppermute x0 -> x7, starting transfers between devices: none -> 24.5 us  [shift(): lax.ppermute(values, axis, [(at, (at + step) % count) for at in range(cou...]
    ppermute x3 -> x2, waiting for transfers between devices: 26.5 us -> 2.25 us  [swap(): return lax.ppermute(values, axis, [(0, 1), (1, 0)])]
    pallas_call x0 -> x6, Pallas kernels: none -> 12.7 us  [call(): pl.pallas_call(body, out_shape=shapes, in_specs=specs, out_specs=[pl.Bloc...]
    unnamed x13 -> x34, local copies, waits for them, and re-layouts: 0.08 us -> 7.37 us
    dot_general x6 -> x0, matrix products: 6.58 us -> none  [the longest x1 2.75 us: local(): lax.dot_general(flat_normed, pre_grad_all, contract_first, preferred_elem...]
  transfers between devices with their start and end apart: 4 -> 13, of which waited for: 4 -> 8; matrix products, arithmetic and copies ran while one was open for 3% -> 1% of each run, Pallas kernels for 0% -> 2%
where the time goes in v4:
time: 168 us; the launch traced here: 167 us
  starting transfers between devices  68.3 us (41%)
  waiting for transfers between devices  45.3 us (27%)
  blocking collectives  28.5 us (17%)
  Pallas kernels  12.7 us (8%)
  local copies, waits for them, and re-layouts  11 us (7%)
    all_to_all x4, starting transfers between devices, trade(): return lax.all_to_all(values, axis, split_axis=0, concat_axis=0, tiled=True)  40 us
    ppermute x7, waiting for transfers between devices, shift(): lax.ppermute(values, axis, [(at, (at + step) % count) for at in range(cou...  30.3 us
    ppermute x7, starting transfers between devices, shift(): lax.ppermute(values, axis, [(at, (at + step) % count) for at in range(cou...  24.5 us
    all_gather x1, blocking collectives, local(): lax.all_gather(pair, 'y', axis=1, tiled=True)  14.4 us
    all_gather x1, blocking collectives, local(): rows = lax.all_gather(both, 'x', axis=1, tiled=True)  14 us
    all_to_all x4, waiting for transfers between devices, trade(): return lax.all_to_all(values, axis, split_axis=0, concat_axis=0, tiled=True)  12.8 us
    pallas_call x6, Pallas kernels, call(): pl.pallas_call(body, out_shape=shapes, in_specs=specs, out_specs=[pl.Bloc...  12.7 us
    unnamed x34, local copies, waits for them, and re-layouts  7.37 us
  transfers between devices with their start and end apart: 13, of which 8 were waited for; matrix products, arithmetic and copies ran while one was open for 1% of the time, Pallas kernels for 2%

profile of v4, /device:TPU:6, one launch (start us, length us, event | category | flops | bytes accessed | tf_op | source)
XLA Modules:
  0.0 166.9 jit_solution(9923708911511889840)
XLA Ops:
  0.6 0.0 copy-start.1
  0.6 1.1 copy-done.1
  1.7 1.1 copy-done.2
  2.8 0.7 copy-done.11
  3.5 0.7 copy-done.13
  4.2 1.3 shard_map.75
  5.6 3.5 %collective-permute-start.2 = (bf16[2,768,384]{2,1,0:T(8,128)(2,1)}, bf16[2,768,384]{2,1,0:T(8,128)(2,1)S(1)}, u32[]{:S(2)}, u32[]{:S(2)}) collective-permute-start(bf16[2,768,384]{2,1,0:T(8,128)(2,1)} %get-tuple-element.30.b0), channel_id=1, source_target_pairs={{0,64},{64,128},{128,192},{192,0},{1,65},{65,129},{129,193},{193,1... | collective-permute-start | bytes 3538952 | tf_op jit(solution)/shard_map/ppermute | solution.py:27
  9.0 15.2 %all-to-all-start = ((bf16[16,2,3072]{2,1,0:T(2,128)(2,1)}), bf16[16,2,3072]{2,1,0:T(2,128)(2,1)S(1)}, u32[]{:S(2)}, u32[]{:S(2)}) async-start(bf16[16,2,3072]{2,1,0:T(2,128)(2,1)} %get-tuple-element.29), calls=%async_computation | async-start | bytes 393216 | tf_op jit(solution)/shard_map/all_to_all | solution.py:31
  24.3 3.6 %collective-permute-start.1 = (bf16[2,768,384]{2,1,0:T(8,128)(2,1)}, bf16[2,768,384]{2,1,0:T(8,128)(2,1)S(1)}, u32[]{:S(2)}, u32[]{:S(2)}) collective-permute-start(bf16[2,768,384]{2,1,0:T(8,128)(2,1)} %get-tuple-element.30.b0), channel_id=1, source_target_pairs={{0,192},{64,0},{128,64},{192,128},{1,193},{65,1},{129,65},{193,129... | collective-permute-start | bytes 3538952 | tf_op jit(solution)/shard_map/ppermute | solution.py:27
  27.8 12.6 %all-to-all-done = bf16[16,2,3072]{2,1,0:T(2,128)(2,1)S(1)} async-done(((bf16[16,2,3072]{2,1,0:T(2,128)(2,1)}), bf16[16,2,3072]{2,1,0:T(2,128)(2,1)S(1)}, u32[]{:S(2)}, u32[]{:S(2)}) %all-to-all-start) | async-done | bytes 196640 | tf_op jit(solution)/shard_map/all_to_all | solution.py:31
  40.5 14.0 %all_gather.6.rows = bf16[2,64,3072]{2,1,0:T(8,128)(2,1)S(1)} all-gather(bf16[2,16,3072]{2,1,0:T(8,128)(2,1)S(1)} %bitcast.16), channel_id=1, replica_groups=mesh['zh'=2,'y'=4,'zl'=8,'x'=4,'core'=2] {'x'}, dimensions={1}, use_global_device_ids=true | all-gather | bytes 983040 | tf_op jit(solution)/shard_map/all_gather | solution.py:185
  54.5 1.9 %collective-permute-start = (bf16[2,64,3072]{2,1,0:T(8,128)(2,1)S(1)}, bf16[2,64,3072]{2,1,0:T(8,128)(2,1)}, u32[]{:S(2)}, u32[]{:S(2)}) collective-permute-start(bf16[2,64,3072]{2,1,0:T(8,128)(2,1)S(1)} %all_gather.6.rows), channel_id=1, source_target_pairs={{0,1},{1,0},{2,3},{3,2},{4,5},{5,4},{6,7},{7,6},{8,9},{9,8},{10,11... | collective-permute-start | bytes 2359304 | tf_op jit(solution)/shard_map/ppermute | solution.py:22
  56.5 0.0 collective-permute-done.2.b3
  56.5 0.9 slice_bitcast_fusion.1
  57.4 3.5 %collective-permute-start.3 = (bf16[768,384]{1,0:T(8,128)(2,1)}, bf16[768,384]{1,0:T(8,128)(2,1)}, u32[]{:S(2)}, u32[]{:S(2)}) collective-permute-start(bf16[768,384]{1,0:T(8,128)(2,1)} %slice_bitcast_fusion.1), channel_id=1, source_target_pairs={{0,64},{64,128},{128,192},{192,0},{1,65},{65,129},{129,193},{193,1... | collective-permute-start | bytes 1769480 | tf_op jit(solution)/shard_map/ppermute | solution.py:27
  60.8 0.0 collective-permute-done.1.b1
  60.8 0.9 slice_bitcast_fusion
  61.7 3.6 %collective-permute-start.4 = (bf16[768,384]{1,0:T(8,128)(2,1)}, bf16[768,384]{1,0:T(8,128)(2,1)}, u32[]{:S(2)}, u32[]{:S(2)}) collective-permute-start(bf16[768,384]{1,0:T(8,128)(2,1)} %slice_bitcast_fusion), channel_id=1, source_target_pairs={{0,192},{64,0},{128,64},{192,128},{1,193},{65,1},{129,65},{193,129... | collective-permute-start | bytes 1769480 | tf_op jit(solution)/shard_map/ppermute | solution.py:27
  65.3 0.0 collective-permute-done.other
  65.3 11.2 %collective-permute-done.3.far_in = bf16[768,384]{1,0:T(8,128)(2,1)} collective-permute-done((bf16[768,384]{1,0:T(8,128)(2,1)}, bf16[768,384]{1,0:T(8,128)(2,1)}, u32[]{:S(2)}, u32[]{:S(2)}) %collective-permute-start.3) | collective-permute-done | bytes 589856 | tf_op jit(solution)/shard_map/ppermute | solution.py:27
  76.5 2.9 %collective-permute-done.4.far_out = bf16[768,384]{1,0:T(8,128)(2,1)} collective-permute-done((bf16[768,384]{1,0:T(8,128)(2,1)}, bf16[768,384]{1,0:T(8,128)(2,1)}, u32[]{:S(2)}, u32[]{:S(2)}) %collective-permute-start.4) | collective-permute-done | bytes 589856 | tf_op jit(solution)/shard_map/ppermute | solution.py:27
  79.4 3.2 %shard_map.76 = bf16[2,2,128,384]{3,2,1,0:T(8,128)(2,1)S(1)} custom-call(s32[1]{0:T(128)} %bitcast.here, bf16[2,64,3072]{2,1,0:T(8,128)(2,1)S(1)} %all_gather.6.rows, bf16[2,64,3072]{2,1,0:T(8,128)(2,1)} %collective-permute-done.other, bf16[2,768,384]{2,1,0:T(8,128)(2,1)} %get-tuple-element.30.b0, bf16[2,768,384]{2,1,0:T(8,128)(2,1)S(1)} %collective-permute-done.1.b1, ...), custom_call_target="tpu_custom_call" | custom-call | flops 603979776 | bytes 6684676 | tf_op jit(solution)/shard_map/pallas_call | solution.py:47
  82.6 0.0 copy-start
  82.6 0.7 copy-done
  83.3 4.9 %all-to-all-start.1 = ((bf16[2,2,128,384]{3,2,1,0:T(8,128)(2,1)}), bf16[2,2,128,384]{3,2,1,0:T(8,128)(2,1)S(1)}, u32[]{:S(2)}, u32[]{:S(2)}) async-start(bf16[2,2,128,384]{3,2,1,0:T(8,128)(2,1)} %copy-done), calls=%async_computation.1 | async-start | bytes 786432 | tf_op jit(solution)/shard_map/all_to_all | solution.py:31
  88.2 1.2 shard_map.77
  89.5 0.0 copy-start.3
  89.5 0.7 copy-done.3
  90.2 0.8 copy-done.15
  91.0 3.2 %collective-permute-start.5 = (bf16[2,128,768]{2,1,0:T(8,128)(2,1)S(1)}, bf16[2,128,768]{2,1,0:T(8,128)(2,1)S(1)}, u32[]{:S(2)}, u32[]{:S(2)}) collective-permute-start(bf16[2,128,768]{2,1,0:T(8,128)(2,1)S(1)} %get-tuple-element.34), channel_id=1, source_target_pairs={{0,64},{64,128},{128,192},{192,0},{1,65},{65,129},{129,193},{193,1... | collective-permute-start | bytes 1179656 | tf_op jit(solution)/shard_map/ppermute | solution.py:27
  94.2 3.9 %collective-permute-start.6 = (bf16[2,128,768]{2,1,0:T(8,128)(2,1)S(1)}, bf16[2,128,768]{2,1,0:T(8,128)(2,1)S(1)}, u32[]{:S(2)}, u32[]{:S(2)}) collective-permute-start(bf16[2,128,768]{2,1,0:T(8,128)(2,1)S(1)} %get-tuple-element.35), channel_id=1, source_target_pairs={{0,192},{64,0},{128,64},{192,128},{1,193},{65,1},{129,65},{193,129... | collective-permute-start | bytes 1179656 | tf_op jit(solution)/shard_map/ppermute | solution.py:27
  98.0 6.2 %collective-permute-done.5.r1 = bf16[2,128,768]{2,1,0:T(8,128)(2,1)S(1)} collective-permute-done((bf16[2,128,768]{2,1,0:T(8,128)(2,1)S(1)}, bf16[2,128,768]{2,1,0:T(8,128)(2,1)S(1)}, u32[]{:S(2)}, u32[]{:S(2)}) %collective-permute-start.5) | collective-permute-done | bytes 393248 | tf_op jit(solution)/shard_map/ppermute | solution.py:27
  104.2 0.7 copy-done.5
  105.0 1.0 collective-permute-done.6.r3
  105.9 0.7 copy-done.7
  106.7 0.0 all-to-all-done.1.parts
  106.7 3.0 %shard_map.78 = (bf16[2,128,384]{2,1,0:T(8,128)(2,1)S(1)}, f32[2,64,3072]{2,1,0:T(8,128)S(1)}, bf16[2,64,3072]{2,1,0:T(8,128)(2,1)S(1)}) custom-call(s32[1]{0:T(128)} %bitcast.here, bf16[2,2,128,384]{3,2,1,0:T(8,128)(2,1)S(1)} %all-to-all-done.1.parts, bf16[2,768,384]{2,1,0:T(8,128)(2,1)} %get-tuple-element.30.b0, ...), custom_call_target="tpu_custom_call" | custom-call | flops 603979776 | bytes 7667716 | tf_op jit(solution)/shard_map/pallas_call | solution.py:47
  109.7 0.0 copy-start.9
  109.7 1.9 %collective-permute-start.7 = (bf16[2,64,3072]{2,1,0:T(8,128)(2,1)S(1)}, bf16[2,64,3072]{2,1,0:T(8,128)(2,1)S(1)}, u32[]{:S(2)}, u32[]{:S(2)}) collective-permute-start(bf16[2,64,3072]{2,1,0:T(8,128)(2,1)S(1)} %get-tuple-element.38), channel_id=1, source_target_pairs={{0,1},{1,0},{2,3},{3,2},{4,5},{5,4},{6,7},{7,6},{8,9},{9,8},{10,11... | collective-permute-start | bytes 2359304 | tf_op jit(solution)/shard_map/ppermute | solution.py:22
  111.6 2.3 %collective-permute-done.7 = bf16[2,64,3072]{2,1,0:T(8,128)(2,1)S(1)} collective-permute-done((bf16[2,64,3072]{2,1,0:T(8,128)(2,1)S(1)}, bf16[2,64,3072]{2,1,0:T(8,128)(2,1)S(1)}, u32[]{:S(2)}, u32[]{:S(2)}) %collective-permute-start.7) | collective-permute-done | bytes 786464 | tf_op jit(solution)/shard_map/ppermute | solution.py:22
  113.9 0.1 add_convert_fusion
  114.0 0.0 copy-done.9
  114.0 0.9 copy.17
  115.0 11.6 %all-to-all-start.2 = ((bf16[4,2,16,3072]{3,2,1,0:T(8,128)(2,1)}), bf16[4,2,16,3072]{3,2,1,0:T(8,128)(2,1)S(1)}, u32[]{:S(2)}, u32[]{:S(2)}) async-start(bf16[4,2,16,3072]{3,2,1,0:T(8,128)(2,1)} %bitcast.12), calls=%async_computation.2 | async-start | bytes 1572864 | tf_op jit(solution)/shard_map/all_to_all | solution.py:31
  126.5 0.0 copy-done.10
  126.6 0.0 copy-start.8
  126.6 14.4 %all_gather.7.full = bf16[2,512,384]{2,1,0:T(8,128)(2,1)S(1)} all-gather(bf16[2,128,384]{2,1,0:T(8,128)(2,1)S(1)} %copy-done.10), channel_id=1, replica_groups=mesh['zh'=2,'y'=4,'zl'=8,'x'=4,'core'=2] {'y'}, dimensions={1}, use_global_device_ids=true | all-gather | bytes 983040 | tf_op jit(solution)/shard_map/all_gather | solution.py:206
  141.0 0.0 all-to-all-done.2
  141.0 0.2 reduce_sum.12
  141.1 0.9 copy.18
  142.0 8.4 %all-to-all-start.3 = ((bf16[16,2,3072]{2,1,0:T(2,128)(2,1)}), bf16[16,2,3072]{2,1,0:T(2,128)(2,1)S(1)}, u32[]{:S(2)}, u32[]{:S(2)}) async-start(bf16[16,2,3072]{2,1,0:T(2,128)(2,1)} %bitcast.13), calls=%async_computation.3 | async-start | bytes 393216 | tf_op jit(solution)/shard_map/all_to_all | solution.py:31
  150.4 0.0 copy-done.16
  150.4 3.4 %collective-permute-start.8 = (bf16[2,128,768]{2,1,0:T(8,128)(2,1)S(1)}, bf16[2,128,768]{2,1,0:T(8,128)(2,1)S(1)}, u32[]{:S(2)}, u32[]{:S(2)}) collective-permute-start(bf16[2,128,768]{2,1,0:T(8,128)(2,1)S(1)} %copy-done.16), channel_id=1, source_target_pairs={{0,128},{64,192},{128,0},{192,64},{1,129},{65,193},{129,1},{193,65... | collective-permute-start | bytes 1179656 | tf_op jit(solution)/shard_map/ppermute | solution.py:27
  153.8 9.1 %collective-permute-done.8.r2 = bf16[2,128,768]{2,1,0:T(8,128)(2,1)S(1)} collective-permute-done((bf16[2,128,768]{2,1,0:T(8,128)(2,1)S(1)}, bf16[2,128,768]{2,1,0:T(8,128)(2,1)S(1)}, u32[]{:S(2)}, u32[]{:S(2)}) %collective-permute-start.8) | collective-permute-done | bytes 393248 | tf_op jit(solution)/shard_map/ppermute | solution.py:27
  162.9 0.0 copy-done.4
  162.9 0.0 copy-done.6
  162.9 0.0 copy-done.8
  162.9 0.0 copy-start.12
  162.9 0.0 copy-start.14
  162.9 2.7 %shard_map.80 = (f32[768,384]{1,0:T(8,128)}, f32[384,768]{1,0:T(8,128)}) custom-call(s32[1]{0:T(128)} %bitcast.here, bf16[2,512,384]{2,1,0:T(8,128)(2,1)S(1)} %all_gather.7.full, bf16[2,128,768]{2,1,0:T(8,128)(2,1)S(1)} %copy-done.4, bf16[2,128,768]{2,1,0:T(8,128)(2,1)S(1)} %copy-done.6, bf16[2,128,768]{2,1,0:T(8,128)(2,1)S(1)} %collective-permute-done.8.r2, ...), custom_call_target="tpu_custom_call" | custom-call | flops 603979776 | bytes 4718596 | tf_op jit(solution)/shard_map/pallas_call | solution.py:47
  165.6 0.1 all-to-all-done.3.sums
  165.8 0.0 copy-done.12
  165.8 0.0 copy-done.14
  165.8 1.2 shard_map.79
  (11 shorter events, 0.1 us)
Async XLA Ops:
  0.6 1.1 copy-start.1
  1.7 1.1 copy-start.2
  2.8 0.7 copy-start.11
  3.5 0.7 copy-start.13
  5.6 50.9 %collective-permute-start.2 = (bf16[2,768,384]{2,1,0:T(8,128)(2,1)}, bf16[2,768,384]{2,1,0:T(8,128)(2,1)S(1)}, u32[]{:S(2)}, u32[]{:S(2)}) collective-permute-start(bf16[2,768,384]{2,1,0:T(8,128)(2,1)} %get-tuple-element.30.b0), channel_id=1, source_target_pairs={{0,64},{64,128},{128,192},{192,0},{1,65},{65,129},{129,193},{193,1... | collective-permute-start | bytes 3538952 | tf_op jit(solution)/shard_map/ppermute | solution.py:27
  9.0 31.4 %all-to-all-start = ((bf16[16,2,3072]{2,1,0:T(2,128)(2,1)}), bf16[16,2,3072]{2,1,0:T(2,128)(2,1)S(1)}, u32[]{:S(2)}, u32[]{:S(2)}) async-start(bf16[16,2,3072]{2,1,0:T(2,128)(2,1)} %get-tuple-element.29), calls=%async_computation | async-start | bytes 393216 | tf_op jit(solution)/shard_map/all_to_all | solution.py:31
  24.3 36.6 %collective-permute-start.1 = (bf16[2,768,384]{2,1,0:T(8,128)(2,1)}, bf16[2,768,384]{2,1,0:T(8,128)(2,1)S(1)}, u32[]{:S(2)}, u32[]{:S(2)}) collective-permute-start(bf16[2,768,384]{2,1,0:T(8,128)(2,1)} %get-tuple-element.30.b0), channel_id=1, source_target_pairs={{0,192},{64,0},{128,64},{192,128},{1,193},{65,1},{129,65},{193,129... | collective-permute-start | bytes 3538952 | tf_op jit(solution)/shard_map/ppermute | solution.py:27
  54.5 10.8 %collective-permute-start = (bf16[2,64,3072]{2,1,0:T(8,128)(2,1)S(1)}, bf16[2,64,3072]{2,1,0:T(8,128)(2,1)}, u32[]{:S(2)}, u32[]{:S(2)}) collective-permute-start(bf16[2,64,3072]{2,1,0:T(8,128)(2,1)S(1)} %all_gather.6.rows), channel_id=1, source_target_pairs={{0,1},{1,0},{2,3},{3,2},{4,5},{5,4},{6,7},{7,6},{8,9},{9,8},{10,11... | collective-permute-start | bytes 2359304 | tf_op jit(solution)/shard_map/ppermute | solution.py:22
  57.4 19.1 %collective-permute-start.3 = (bf16[768,384]{1,0:T(8,128)(2,1)}, bf16[768,384]{1,0:T(8,128)(2,1)}, u32[]{:S(2)}, u32[]{:S(2)}) collective-permute-start(bf16[768,384]{1,0:T(8,128)(2,1)} %slice_bitcast_fusion.1), channel_id=1, source_target_pairs={{0,64},{64,128},{128,192},{192,0},{1,65},{65,129},{129,193},{193,1... | collective-permute-start | bytes 1769480 | tf_op jit(solution)/shard_map/ppermute | solution.py:27
  61.7 17.6 %collective-permute-start.4 = (bf16[768,384]{1,0:T(8,128)(2,1)}, bf16[768,384]{1,0:T(8,128)(2,1)}, u32[]{:S(2)}, u32[]{:S(2)}) collective-permute-start(bf16[768,384]{1,0:T(8,128)(2,1)} %slice_bitcast_fusion), channel_id=1, source_target_pairs={{0,192},{64,0},{128,64},{192,128},{1,193},{65,1},{129,65},{193,129... | collective-permute-start | bytes 1769480 | tf_op jit(solution)/shard_map/ppermute | solution.py:27
  82.6 0.7 copy-start
  83.3 23.3 %all-to-all-start.1 = ((bf16[2,2,128,384]{3,2,1,0:T(8,128)(2,1)}), bf16[2,2,128,384]{3,2,1,0:T(8,128)(2,1)S(1)}, u32[]{:S(2)}, u32[]{:S(2)}) async-start(bf16[2,2,128,384]{3,2,1,0:T(8,128)(2,1)} %copy-done), calls=%async_computation.1 | async-start | bytes 786432 | tf_op jit(solution)/shard_map/all_to_all | solution.py:31
  89.5 0.7 copy-start.3
  90.2 0.8 copy-start.15
  91.0 13.2 %collective-permute-start.5 = (bf16[2,128,768]{2,1,0:T(8,128)(2,1)S(1)}, bf16[2,128,768]{2,1,0:T(8,128)(2,1)S(1)}, u32[]{:S(2)}, u32[]{:S(2)}) collective-permute-start(bf16[2,128,768]{2,1,0:T(8,128)(2,1)S(1)} %get-tuple-element.34), channel_id=1, source_target_pairs={{0,64},{64,128},{128,192},{192,0},{1,65},{65,129},{129,193},{193,1... | collective-permute-start | bytes 1179656 | tf_op jit(solution)/shard_map/ppermute | solution.py:27
  94.2 11.7 %collective-permute-start.6 = (bf16[2,128,768]{2,1,0:T(8,128)(2,1)S(1)}, bf16[2,128,768]{2,1,0:T(8,128)(2,1)S(1)}, u32[]{:S(2)}, u32[]{:S(2)}) collective-permute-start(bf16[2,128,768]{2,1,0:T(8,128)(2,1)S(1)} %get-tuple-element.35), channel_id=1, source_target_pairs={{0,192},{64,0},{128,64},{192,128},{1,193},{65,1},{129,65},{193,129... | collective-permute-start | bytes 1179656 | tf_op jit(solution)/shard_map/ppermute | solution.py:27
  104.2 0.8 copy-start.5
  105.9 0.7 copy-start.7
  109.7 4.4 %copy-start.9 = (bf16[2,128,384]{2,1,0:T(8,128)(2,1)}, bf16[2,128,384]{2,1,0:T(8,128)(2,1)S(1)}, u32[]{:S(2)}) copy-start(bf16[2,128,384]{2,1,0:T(8,128)(2,1)S(1)} %get-tuple-element.41) | copy-start | bytes 589828
  109.7 4.2 %collective-permute-start.7 = (bf16[2,64,3072]{2,1,0:T(8,128)(2,1)S(1)}, bf16[2,64,3072]{2,1,0:T(8,128)(2,1)S(1)}, u32[]{:S(2)}, u32[]{:S(2)}) collective-permute-start(bf16[2,64,3072]{2,1,0:T(8,128)(2,1)S(1)} %get-tuple-element.38), channel_id=1, source_target_pairs={{0,1},{1,0},{2,3},{3,2},{4,5},{5,4},{6,7},{7,6},{8,9},{9,8},{10,11... | collective-permute-start | bytes 2359304 | tf_op jit(solution)/shard_map/ppermute | solution.py:22
  115.0 11.6 %copy-start.10 = (bf16[2,128,384]{2,1,0:T(8,128)(2,1)S(1)}, bf16[2,128,384]{2,1,0:T(8,128)(2,1)}, u32[]{:S(2)}) copy-start(bf16[2,128,384]{2,1,0:T(8,128)(2,1)} %copy-done.9) | copy-start | bytes 589828
  115.0 26.0 %all-to-all-start.2 = ((bf16[4,2,16,3072]{3,2,1,0:T(8,128)(2,1)}), bf16[4,2,16,3072]{3,2,1,0:T(8,128)(2,1)S(1)}, u32[]{:S(2)}, u32[]{:S(2)}) async-start(bf16[4,2,16,3072]{3,2,1,0:T(8,128)(2,1)} %bitcast.12), calls=%async_computation.2 | async-start | bytes 1572864 | tf_op jit(solution)/shard_map/all_to_all | solution.py:31
  126.5 23.9 %copy-start.16 = (bf16[2,128,768]{2,1,0:T(8,128)(2,1)S(1)}, bf16[2,128,768]{2,1,0:T(8,128)(2,1)}, u32[]{:S(2)}) copy-start(bf16[2,128,768]{2,1,0:T(8,128)(2,1)} %copy-done.15) | copy-start | bytes 1179652
  126.5 36.4 %copy-start.4 = (bf16[2,128,768]{2,1,0:T(8,128)(2,1)S(1)}, bf16[2,128,768]{2,1,0:T(8,128)(2,1)}, u32[]{:S(2)}) copy-start(bf16[2,128,768]{2,1,0:T(8,128)(2,1)} %copy-done.3) | copy-start | bytes 1179652
  126.5 36.4 %copy-start.6 = (bf16[2,128,768]{2,1,0:T(8,128)(2,1)S(1)}, bf16[2,128,768]{2,1,0:T(8,128)(2,1)}, u32[]{:S(2)}) copy-start(bf16[2,128,768]{2,1,0:T(8,128)(2,1)} %copy-done.5) | copy-start | bytes 1179652
  126.6 36.3 %copy-start.8 = (bf16[2,128,768]{2,1,0:T(8,128)(2,1)S(1)}, bf16[2,128,768]{2,1,0:T(8,128)(2,1)}, u32[]{:S(2)}) copy-start(bf16[2,128,768]{2,1,0:T(8,128)(2,1)} %copy-done.7) | copy-start | bytes 1179652
  142.0 23.7 %all-to-all-start.3 = ((bf16[16,2,3072]{2,1,0:T(2,128)(2,1)}), bf16[16,2,3072]{2,1,0:T(2,128)(2,1)S(1)}, u32[]{:S(2)}, u32[]{:S(2)}) async-start(bf16[16,2,3072]{2,1,0:T(2,128)(2,1)} %bitcast.13), calls=%async_computation.3 | async-start | bytes 393216 | tf_op jit(solution)/shard_map/all_to_all | solution.py:31
  150.4 12.5 %collective-permute-start.8 = (bf16[2,128,768]{2,1,0:T(8,128)(2,1)S(1)}, bf16[2,128,768]{2,1,0:T(8,128)(2,1)S(1)}, u32[]{:S(2)}, u32[]{:S(2)}) collective-permute-start(bf16[2,128,768]{2,1,0:T(8,128)(2,1)S(1)} %copy-done.16), channel_id=1, source_target_pairs={{0,128},{64,192},{128,0},{192,64},{1,129},{65,193},{129,1},{193,65... | collective-permute-start | bytes 1179656 | tf_op jit(solution)/shard_map/ppermute | solution.py:27
  162.9 2.8 %copy-start.12 = (bf16[1,6144]{1,0:T(2,128)(2,1)S(1)}, bf16[1,6144]{1,0:T(2,128)(2,1)}, u32[]{:S(2)}) copy-start(bf16[1,6144]{1,0:T(2,128)(2,1)} %tokens.3) | copy-start | bytes 36868
  162.9 2.8 %copy-start.14 = (bf16[1,6144]{1,0:T(2,128)(2,1)S(1)}, bf16[1,6144]{1,0:T(2,128)(2,1)}, u32[]{:S(2)}) copy-start(bf16[1,6144]{1,0:T(2,128)(2,1)} %cotangent.3) | copy-start | bytes 36868

commit v5 on v4

--- a/solution.py
+++ b/solution.py
@@ -49,7 +49,7 @@
         out_shape=shapes,
         in_specs=specs,
         out_specs=[pl.BlockSpec(memory_space=pltpu.VMEM) for _ in shapes],
-        compiler_params=pltpu.CompilerParams(vmem_limit_bytes=min(2 * moved + (6 << 20), 40 << 20)),
+        compiler_params=pltpu.CompilerParams(vmem_limit_bytes=min(2 * moved + (6 << 20), 40 << 20) if body is not pack_body else None),
         cost_estimate=pl.CostEstimate(flops=flops, bytes_accessed=moved, transcendentals=0),
     )(*args)
 
@@ -79,6 +79,10 @@
     return pl.multiple_of(lax.rem(here + step, Y) * width, 128)
 
 
+def line_up(rows, other, index, cut):
+    return jnp.concatenate([ref[at, index, :, cut] for ref in (rows, other) for at in range(X)], axis=0)
+
+
 def hidden_body(here, rows, other, b0, b1, b3, far_in, far_out, out):
     width, hidden = far_in.shape
     pre = grad = None
@@ -86,11 +90,11 @@
         ((b0.at[0], b0.at[1]), (b1.at[0], b1.at[1]), (far_in, far_out), (b3.at[0], b3.at[1]))
     ):
         at = place(here[0], step, width)
-        left = jnp.concatenate([rows[0, :, pl.ds(at, width)], other[0, :, pl.ds(at, width)]], axis=0)
+        left = line_up(rows, other, 0, pl.ds(at, width))
         terms = [dot(left, ins[...])]
         for part in range(width // hidden):
             cut = pl.ds(pl.multiple_of(at + part * hidden, 128), hidden)
-            right = jnp.concatenate([rows[1, :, cut], other[1, :, cut]], axis=0)
+            right = line_up(rows, other, 1, cut)
             terms.append(dot(right, cols[part * hidden : (part + 1) * hidden], LAST))
         one, two = terms[0], sum(terms[1:])
         pre = one if pre is None else pre + one
@@ -102,12 +106,11 @@
 
 
 def split_body(here, rows, other, *outs):
-    half = rows.shape[1]
     width = outs[0].shape[2]
     for step, out in enumerate(outs):
         at = pl.ds(place(here[0], step, width), width)
-        out[:, :half] = rows[:, :, at]
-        out[:, half:] = other[:, :, at]
+        for index in range(2):
+            out[index] = line_up(rows, other, index, at)
 
 
 def output_body(here, parts, b0, b1, b3, far_in, far_out, pair, keep, give):
@@ -181,12 +184,14 @@
         tokens, cotangent, w_in, w_out,
     )
     both, block = lax.optimization_barrier((both, block))
-    both = trade(both, FAR).transpose(1, 0, 2)
-    rows = lax.all_gather(both, "x", axis=1, tiled=True)
+    below, above = shift(block, "y", 1), shift(block, "y", -1)
+    both, near_in, near_out = lax.optimization_barrier((trade(both, FAR), below[0], above[1]))
+    both = both.transpose(1, 0, 2)
+    rows = trade(jnp.broadcast_to(both, (X,) + both.shape), "x")
+    far_in, far_out = shift(near_in, "y", 1), shift(near_out, "y", -1)
+    rows, far_in, far_out = lax.optimization_barrier((rows, far_in, far_out))
     other = swap(rows, "core")
-
-    below, above = shift(block, "y", 1), shift(block, "y", -1)
-    blocks = (block, above, below, shift(below[0], "y", 1), shift(above[1], "y", -1))
+    blocks = (block, above, below, far_in, far_out)
 
     (parts,) = call(hidden_body, [shape((ZH, 2, count, hidden), bf16)], here, rows, other, *blocks, flops=work)
     parts, rows, other = lax.optimization_barrier((parts, rows, other))

time: 168 us -> 169 us (level)
  blocking collectives: 28.5 us -> 14.5 us
  starting transfers between devices: 68.3 us -> 82 us
    all_gather x1 -> x0, blocking collectives: 14 us -> none  [local(): rows = lax.all_gather(both, 'x', axis=1, tiled=True)]
    all_to_all x4 -> x5, starting transfers between devices: 40 us -> 53.5 us  [trade(): return lax.all_to_all(values, axis, split_axis=0, concat_axis=0, tiled=True)]
    all_to_all x4 -> x5, waiting for transfers between devices: 12.8 us -> 2.39 us  [trade(): return lax.all_to_all(values, axis, split_axis=0, concat_axis=0, tiled=True)]
    ppermute x7, waiting for transfers between devices: 30.3 us -> 39.2 us  [shift(): lax.ppermute(values, axis, [(at, (at + step) % count) for at in range(cou...]
    ppermute x2, waiting for transfers between devices: 2.25 us -> 4.63 us  [swap(): return lax.ppermute(values, axis, [(0, 1), (1, 0)])]
    unnamed x34 -> x22, local copies, waits for them, and re-layouts: 7.37 us -> 5.55 us
  transfers between devices with their start and end apart: 13 -> 14, of which waited for: 8 -> 12; matrix products, arithmetic and copies ran while one was open for 1% -> 1% of each run, Pallas kernels for 2% -> 2%
where the time goes in v5:
time: 169 us; the launch traced here: 168 us
  starting transfers between devices  82 us (49%)
  waiting for transfers between devices  46.2 us (27%)
  blocking collectives  14.5 us (9%)
  Pallas kernels  13.2 us (8%)
  local copies, waits for them, and re-layouts  10.2 us (6%)
    all_to_all x5, starting transfers between devices, trade(): return lax.all_to_all(values, axis, split_axis=0, concat_axis=0, tiled=True)  53.5 us
    ppermute x7, waiting for transfers between devices, shift(): lax.ppermute(values, axis, [(at, (at + step) % count) for at in range(cou...  39.2 us
    ppermute x7, starting transfers between devices, shift(): lax.ppermute(values, axis, [(at, (at + step) % count) for at in range(cou...  24.7 us
    all_gather x1, blocking collectives, local(): lax.all_gather(pair, 'y', axis=1, tiled=True)  14.5 us
    pallas_call x6, Pallas kernels, call(): pl.pallas_call(body, out_shape=shapes, in_specs=specs, out_specs=[pl.Bloc...  13.2 us
    unnamed x22, local copies, waits for them, and re-layouts  5.55 us
    ppermute x2, waiting for transfers between devices, swap(): return lax.ppermute(values, axis, [(0, 1), (1, 0)])  4.63 us
    ppermute x2, starting transfers between devices, swap(): return lax.ppermute(values, axis, [(0, 1), (1, 0)])  3.83 us
  transfers between devices with their start and end apart: 14, of which 12 were waited for; matrix products, arithmetic and copies ran while one was open for 1% of the time, Pallas kernels for 2%

profile of v5, /device:TPU:6, one launch (start us, length us, event | category | flops | bytes accessed | tf_op | source)
XLA Modules:
  0.0 168.4 jit_solution(16535181949992936312)
XLA Ops:
  0.6 2.6 %shard_map.75 = (bf16[16,2,3072]{2,1,0:T(2,128)(2,1)}, bf16[2,768,384]{2,1,0:T(8,128)(2,1)}) custom-call(bf16[1,6144]{1,0:T(2,128)(2,1)} %tokens.3, bf16[1,6144]{1,0:T(2,128)(2,1)} %cotangent.3, bf16[768,384]{1,0:T(8,128)(2,1)} %w_in.1, bf16[384,768]{1,0:T(8,128)(2,1)} %w_out.1), custom_call_target="tpu_custom_call" | custom-call | bytes 2580480 | tf_op jit(solution)/shard_map/pallas_call | solution.py:47
  3.2 4.9 %collective-permute-start.1 = (bf16[2,768,384]{2,1,0:T(8,128)(2,1)}, bf16[2,768,384]{2,1,0:T(8,128)(2,1)S(1)}, u32[]{:S(2)}, u32[]{:S(2)}) collective-permute-start(bf16[2,768,384]{2,1,0:T(8,128)(2,1)} %get-tuple-element.36.b0), channel_id=1, source_target_pairs={{0,192},{64,0},{128,64},{192,128},{1,193},{65,1},{129,65},{193,129... | collective-permute-start | bytes 3538952 | tf_op jit(solution)/shard_map/ppermute | solution.py:27
  8.2 1.9 %collective-permute-start = (bf16[2,768,384]{2,1,0:T(8,128)(2,1)}, bf16[2,768,384]{2,1,0:T(8,128)(2,1)S(1)}, u32[]{:S(2)}, u32[]{:S(2)}) collective-permute-start(bf16[2,768,384]{2,1,0:T(8,128)(2,1)} %get-tuple-element.36.b0), channel_id=1, source_target_pairs={{0,64},{64,128},{128,192},{192,0},{1,65},{65,129},{129,193},{193,1... | collective-permute-start | bytes 3538952 | tf_op jit(solution)/shard_map/ppermute | solution.py:27
  10.1 15.2 %all-to-all-start = ((bf16[16,2,3072]{2,1,0:T(2,128)(2,1)}), bf16[16,2,3072]{2,1,0:T(2,128)(2,1)S(1)}, u32[]{:S(2)}, u32[]{:S(2)}) async-start(bf16[16,2,3072]{2,1,0:T(2,128)(2,1)} %get-tuple-element.35), calls=%async_computation | async-start | bytes 393216 | tf_op jit(solution)/shard_map/all_to_all | solution.py:31
  25.3 8.4 %collective-permute-done.1.b1 = bf16[2,768,384]{2,1,0:T(8,128)(2,1)S(1)} collective-permute-done((bf16[2,768,384]{2,1,0:T(8,128)(2,1)}, bf16[2,768,384]{2,1,0:T(8,128)(2,1)S(1)}, u32[]{:S(2)}, u32[]{:S(2)}) %collective-permute-start.1) | collective-permute-done | bytes 1179680 | tf_op jit(solution)/shard_map/ppermute | solution.py:27
  33.7 0.9 slice_bitcast_fusion
  34.6 4.3 %collective-permute-done.b3 = bf16[2,768,384]{2,1,0:T(8,128)(2,1)S(1)} collective-permute-done((bf16[2,768,384]{2,1,0:T(8,128)(2,1)}, bf16[2,768,384]{2,1,0:T(8,128)(2,1)S(1)}, u32[]{:S(2)}, u32[]{:S(2)}) %collective-permute-start) | collective-permute-done | bytes 1179680 | tf_op jit(solution)/shard_map/ppermute | solution.py:27
  38.9 0.9 slice_bitcast_fusion.1
  39.8 1.7 %all-to-all-done = bf16[16,2,3072]{2,1,0:T(2,128)(2,1)S(1)} async-done(((bf16[16,2,3072]{2,1,0:T(2,128)(2,1)}), bf16[16,2,3072]{2,1,0:T(2,128)(2,1)S(1)}, u32[]{:S(2)}, u32[]{:S(2)}) %all-to-all-start) | async-done | bytes 196640 | tf_op jit(solution)/shard_map/all_to_all | solution.py:31
  41.5 1.0 broadcast_in_dim.3
  42.5 4.8 %all-to-all-start.1 = ((bf16[4,2,16,3072]{3,2,1,0:T(8,128)(2,1)}), bf16[4,2,16,3072]{3,2,1,0:T(8,128)(2,1)S(1)}, u32[]{:S(2)}, u32[]{:S(2)}) async-start(bf16[4,2,16,3072]{3,2,1,0:T(8,128)(2,1)} %broadcast_in_dim.3), calls=%async_computation.1 | async-start | bytes 1572864 | tf_op jit(solution)/shard_map/all_to_all | solution.py:31
  47.3 2.2 %collective-permute-start.2 = (bf16[768,384]{1,0:T(8,128)(2,1)}, bf16[768,384]{1,0:T(8,128)(2,1)}, u32[]{:S(2)}, u32[]{:S(2)}) collective-permute-start(bf16[768,384]{1,0:T(8,128)(2,1)} %slice_bitcast_fusion.1), channel_id=1, source_target_pairs={{0,64},{64,128},{128,192},{192,0},{1,65},{65,129},{129,193},{193,1... | collective-permute-start | bytes 1769480 | tf_op jit(solution)/shard_map/ppermute | solution.py:27
  49.5 4.8 %collective-permute-start.3 = (bf16[768,384]{1,0:T(8,128)(2,1)}, bf16[768,384]{1,0:T(8,128)(2,1)}, u32[]{:S(2)}, u32[]{:S(2)}) collective-permute-start(bf16[768,384]{1,0:T(8,128)(2,1)} %slice_bitcast_fusion), channel_id=1, source_target_pairs={{0,192},{64,0},{128,64},{192,128},{1,193},{65,1},{129,65},{193,129... | collective-permute-start | bytes 1769480 | tf_op jit(solution)/shard_map/ppermute | solution.py:27
  54.3 0.4 all-to-all-done.1.rows
  54.7 7.6 %collective-permute-done.2.far_in = bf16[768,384]{1,0:T(8,128)(2,1)} collective-permute-done((bf16[768,384]{1,0:T(8,128)(2,1)}, bf16[768,384]{1,0:T(8,128)(2,1)}, u32[]{:S(2)}, u32[]{:S(2)}) %collective-permute-start.2) | collective-permute-done | bytes 589856 | tf_op jit(solution)/shard_map/ppermute | solution.py:27
  62.3 1.2 collective-permute-done.3.far_out
  63.5 1.9 %collective-permute-start.4 = (bf16[4,2,16,3072]{3,2,1,0:T(8,128)(2,1)S(1)}, bf16[4,2,16,3072]{3,2,1,0:T(8,128)(2,1)}, u32[]{:S(2)}, u32[]{:S(2)}) collective-permute-start(bf16[4,2,16,3072]{3,2,1,0:T(8,128)(2,1)S(1)} %all-to-all-done.1.rows), channel_id=1, source_target_pairs={{0,1},{1,0},{2,3},{3,2},{4,5},{5,4},{6,7},{7,6},{8,9},{9,8},{10,11... | collective-permute-start | bytes 2359304 | tf_op jit(solution)/shard_map/ppermute | solution.py:22
  65.4 2.4 %collective-permute-done.4.other = bf16[4,2,16,3072]{3,2,1,0:T(8,128)(2,1)} collective-permute-done((bf16[4,2,16,3072]{3,2,1,0:T(8,128)(2,1)S(1)}, bf16[4,2,16,3072]{3,2,1,0:T(8,128)(2,1)}, u32[]{:S(2)}, u32[]{:S(2)}) %collective-permute-start.4) | collective-permute-done | bytes 786464 | tf_op jit(solution)/shard_map/ppermute | solution.py:22
  67.8 0.0 copy-start
  67.8 1.3 copy-done
  69.1 2.8 %shard_map.76 = bf16[2,2,128,384]{3,2,1,0:T(8,128)(2,1)S(1)} custom-call(s32[1]{0:T(128)} %bitcast.here, bf16[4,2,16,3072]{3,2,1,0:T(8,128)(2,1)S(1)} %all-to-all-done.1.rows, bf16[4,2,16,3072]{3,2,1,0:T(8,128)(2,1)} %collective-permute-done.4.other, bf16[2,768,384]{2,1,0:T(8,128)(2,1)S(1)} %copy-done, bf16[2,768,384]{2,1,0:T(8,128)(2,1)S(1)} %collective-permute-done.1.b1, ...), custom_call_target="tpu_custom_call" | custom-call | flops 603979776 | bytes 6684676 | tf_op jit(solution)/shard_map/pallas_call | solution.py:47
  71.9 0.0 copy-start.2
  71.9 0.7 copy-done.2
  72.7 15.1 %all-to-all-start.2 = ((bf16[2,2,128,384]{3,2,1,0:T(8,128)(2,1)}), bf16[2,2,128,384]{3,2,1,0:T(8,128)(2,1)S(1)}, u32[]{:S(2)}, u32[]{:S(2)}) async-start(bf16[2,2,128,384]{3,2,1,0:T(8,128)(2,1)} %copy-done.2), calls=%async_computation.2 | async-start | bytes 786432 | tf_op jit(solution)/shard_map/all_to_all | solution.py:31
  87.7 1.2 shard_map.77
  89.0 0.0 copy-start.3
  89.0 0.7 copy-done.3
  89.7 0.0 copy-start.9
  89.7 0.8 copy-done.9
  90.5 1.9 %collective-permute-start.5 = (bf16[2,128,768]{2,1,0:T(8,128)(2,1)S(1)}, bf16[2,128,768]{2,1,0:T(8,128)(2,1)S(1)}, u32[]{:S(2)}, u32[]{:S(2)}) collective-permute-start(bf16[2,128,768]{2,1,0:T(8,128)(2,1)S(1)} %get-tuple-element.46), channel_id=1, source_target_pairs={{0,64},{64,128},{128,192},{192,0},{1,65},{65,129},{129,193},{193,1... | collective-permute-start | bytes 1179656 | tf_op jit(solution)/shard_map/ppermute | solution.py:27
  92.4 5.6 %collective-permute-start.6 = (bf16[2,128,768]{2,1,0:T(8,128)(2,1)S(1)}, bf16[2,128,768]{2,1,0:T(8,128)(2,1)S(1)}, u32[]{:S(2)}, u32[]{:S(2)}) collective-permute-start(bf16[2,128,768]{2,1,0:T(8,128)(2,1)S(1)} %get-tuple-element.47), channel_id=1, source_target_pairs={{0,192},{64,0},{128,64},{192,128},{1,193},{65,1},{129,65},{193,129... | collective-permute-start | bytes 1179656 | tf_op jit(solution)/shard_map/ppermute | solution.py:27
  98.0 7.2 %collective-permute-done.5.r1 = bf16[2,128,768]{2,1,0:T(8,128)(2,1)S(1)} collective-permute-done((bf16[2,128,768]{2,1,0:T(8,128)(2,1)S(1)}, bf16[2,128,768]{2,1,0:T(8,128)(2,1)S(1)}, u32[]{:S(2)}, u32[]{:S(2)}) %collective-permute-start.5) | collective-permute-done | bytes 393248 | tf_op jit(solution)/shard_map/ppermute | solution.py:27
  105.2 1.2 collective-permute-done.6.r3
  106.4 0.0 copy-start.5
  106.4 0.8 copy-done.5
  107.1 0.0 all-to-all-done.2.parts
  107.1 0.0 copy-start.1
  107.1 1.3 copy-done.1
  108.4 2.7 %shard_map.78 = (bf16[2,128,384]{2,1,0:T(8,128)(2,1)S(1)}, f32[2,64,3072]{2,1,0:T(8,128)S(1)}, bf16[2,64,3072]{2,1,0:T(8,128)(2,1)S(1)}) custom-call(s32[1]{0:T(128)} %bitcast.here, bf16[2,2,128,384]{3,2,1,0:T(8,128)(2,1)S(1)} %all-to-all-done.2.parts, bf16[2,768,384]{2,1,0:T(8,128)(2,1)S(1)} %copy-done.1, ...), custom_call_target="tpu_custom_call" | custom-call | flops 603979776 | bytes 7667716 | tf_op jit(solution)/shard_map/pallas_call | solution.py:47
  111.1 1.9 %collective-permute-start.7 = (bf16[2,64,3072]{2,1,0:T(8,128)(2,1)S(1)}, bf16[2,64,3072]{2,1,0:T(8,128)(2,1)S(1)}, u32[]{:S(2)}, u32[]{:S(2)}) collective-permute-start(bf16[2,64,3072]{2,1,0:T(8,128)(2,1)S(1)} %get-tuple-element.50), channel_id=1, source_target_pairs={{0,1},{1,0},{2,3},{3,2},{4,5},{5,4},{6,7},{7,6},{8,9},{9,8},{10,11... | collective-permute-start | bytes 2359304 | tf_op jit(solution)/shard_map/ppermute | solution.py:22
  113.0 2.3 %collective-permute-done.7 = bf16[2,64,3072]{2,1,0:T(8,128)(2,1)S(1)} collective-permute-done((bf16[2,64,3072]{2,1,0:T(8,128)(2,1)S(1)}, bf16[2,64,3072]{2,1,0:T(8,128)(2,1)S(1)}, u32[]{:S(2)}, u32[]{:S(2)}) %collective-permute-start.7) | collective-permute-done | bytes 786464 | tf_op jit(solution)/shard_map/ppermute | solution.py:22
  115.2 0.2 add_convert_fusion
  115.4 0.9 copy.16
  116.4 4.8 %all-to-all-start.3 = ((bf16[4,2,16,3072]{3,2,1,0:T(8,128)(2,1)}), bf16[4,2,16,3072]{3,2,1,0:T(8,128)(2,1)}, u32[]{:S(2)}, u32[]{:S(2)}) async-start(bf16[4,2,16,3072]{3,2,1,0:T(8,128)(2,1)} %bitcast.11), calls=%async_computation.3 | async-start | bytes 1572864 | tf_op jit(solution)/shard_map/all_to_all | solution.py:31
  121.2 0.0 copy-start.10
  121.2 0.0 copy-start.4
  121.2 0.0 copy-start.6
  121.2 14.5 %all_gather.3.full = bf16[2,512,384]{2,1,0:T(8,128)(2,1)S(1)} all-gather(bf16[2,128,384]{2,1,0:T(8,128)(2,1)S(1)} %get-tuple-element.53), channel_id=1, replica_groups=mesh['zh'=2,'y'=4,'zl'=8,'x'=4,'core'=2] {'y'}, dimensions={1}, use_global_device_ids=true | all-gather | bytes 983040 | tf_op jit(solution)/shard_map/all_gather | solution.py:211
  135.7 0.0 all-to-all-done.3
  135.7 1.3 reduce_sum.12
  137.0 0.9 copy.17
  137.9 13.6 %all-to-all-start.4 = ((bf16[16,2,3072]{2,1,0:T(2,128)(2,1)}), bf16[16,2,3072]{2,1,0:T(2,128)(2,1)S(1)}, u32[]{:S(2)}, u32[]{:S(2)}) async-start(bf16[16,2,3072]{2,1,0:T(2,128)(2,1)} %bitcast.12), calls=%async_computation.4 | async-start | bytes 393216 | tf_op jit(solution)/shard_map/all_to_all | solution.py:31
  151.5 0.0 copy-done.10
  151.5 3.4 %collective-permute-start.8 = (bf16[2,128,768]{2,1,0:T(8,128)(2,1)S(1)}, bf16[2,128,768]{2,1,0:T(8,128)(2,1)S(1)}, u32[]{:S(2)}, u32[]{:S(2)}) collective-permute-start(bf16[2,128,768]{2,1,0:T(8,128)(2,1)S(1)} %copy-done.10), channel_id=1, source_target_pairs={{0,128},{64,192},{128,0},{192,64},{1,129},{65,193},{129,1},{193,65... | collective-permute-start | bytes 1179656 | tf_op jit(solution)/shard_map/ppermute | solution.py:27
  154.9 9.3 %collective-permute-done.8.r2 = bf16[2,128,768]{2,1,0:T(8,128)(2,1)S(1)} collective-permute-done((bf16[2,128,768]{2,1,0:T(8,128)(2,1)S(1)}, bf16[2,128,768]{2,1,0:T(8,128)(2,1)S(1)}, u32[]{:S(2)}, u32[]{:S(2)}) %collective-permute-start.8) | collective-permute-done | bytes 393248 | tf_op jit(solution)/shard_map/ppermute | solution.py:27
  164.2 0.0 copy-done.4
  164.2 0.0 copy-done.6
  164.2 0.0 copy-start.7
  164.2 0.0 copy-start.8
  164.2 2.7 %shard_map.80 = (f32[768,384]{1,0:T(8,128)}, f32[384,768]{1,0:T(8,128)}) custom-call(s32[1]{0:T(128)} %bitcast.here, bf16[2,512,384]{2,1,0:T(8,128)(2,1)S(1)} %all_gather.3.full, bf16[2,128,768]{2,1,0:T(8,128)(2,1)S(1)} %copy-done.4, bf16[2,128,768]{2,1,0:T(8,128)(2,1)S(1)} %collective-permute-done.5.r1, bf16[2,128,768]{2,1,0:T(8,128)(2,1)S(1)} %collective-permute-done.8.r2, ...), custom_call_target="tpu_custom_call" | custom-call | flops 603979776 | bytes 4718596 | tf_op jit(solution)/shard_map/pallas_call | solution.py:47
  166.9 0.3 all-to-all-done.4.sums
  167.2 0.0 copy-done.7
  167.2 0.0 copy-done.8
  167.2 1.2 shard_map.79
  (1 shorter events, 0.0 us)
Async XLA Ops:
  3.2 30.4 %collective-permute-start.1 = (bf16[2,768,384]{2,1,0:T(8,128)(2,1)}, bf16[2,768,384]{2,1,0:T(8,128)(2,1)S(1)}, u32[]{:S(2)}, u32[]{:S(2)}) collective-permute-start(bf16[2,768,384]{2,1,0:T(8,128)(2,1)} %get-tuple-element.36.b0), channel_id=1, source_target_pairs={{0,192},{64,0},{128,64},{192,128},{1,193},{65,1},{129,65},{193,129... | collective-permute-start | bytes 3538952 | tf_op jit(solution)/shard_map/ppermute | solution.py:27
  8.2 30.7 %collective-permute-start = (bf16[2,768,384]{2,1,0:T(8,128)(2,1)}, bf16[2,768,384]{2,1,0:T(8,128)(2,1)S(1)}, u32[]{:S(2)}, u32[]{:S(2)}) collective-permute-start(bf16[2,768,384]{2,1,0:T(8,128)(2,1)} %get-tuple-element.36.b0), channel_id=1, source_target_pairs={{0,64},{64,128},{128,192},{192,0},{1,65},{65,129},{129,193},{193,1... | collective-permute-start | bytes 3538952 | tf_op jit(solution)/shard_map/ppermute | solution.py:27
  10.1 31.4 %all-to-all-start = ((bf16[16,2,3072]{2,1,0:T(2,128)(2,1)}), bf16[16,2,3072]{2,1,0:T(2,128)(2,1)S(1)}, u32[]{:S(2)}, u32[]{:S(2)}) async-start(bf16[16,2,3072]{2,1,0:T(2,128)(2,1)} %get-tuple-element.35), calls=%async_computation | async-start | bytes 393216 | tf_op jit(solution)/shard_map/all_to_all | solution.py:31
  42.5 12.2 %all-to-all-start.1 = ((bf16[4,2,16,3072]{3,2,1,0:T(8,128)(2,1)}), bf16[4,2,16,3072]{3,2,1,0:T(8,128)(2,1)S(1)}, u32[]{:S(2)}, u32[]{:S(2)}) async-start(bf16[4,2,16,3072]{3,2,1,0:T(8,128)(2,1)} %broadcast_in_dim.3), calls=%async_computation.1 | async-start | bytes 1572864 | tf_op jit(solution)/shard_map/all_to_all | solution.py:31
  47.3 15.0 %collective-permute-start.2 = (bf16[768,384]{1,0:T(8,128)(2,1)}, bf16[768,384]{1,0:T(8,128)(2,1)}, u32[]{:S(2)}, u32[]{:S(2)}) collective-permute-start(bf16[768,384]{1,0:T(8,128)(2,1)} %slice_bitcast_fusion.1), channel_id=1, source_target_pairs={{0,64},{64,128},{128,192},{192,0},{1,65},{65,129},{129,193},{193,1... | collective-permute-start | bytes 1769480 | tf_op jit(solution)/shard_map/ppermute | solution.py:27
  49.5 14.0 %collective-permute-start.3 = (bf16[768,384]{1,0:T(8,128)(2,1)}, bf16[768,384]{1,0:T(8,128)(2,1)}, u32[]{:S(2)}, u32[]{:S(2)}) collective-permute-start(bf16[768,384]{1,0:T(8,128)(2,1)} %slice_bitcast_fusion), channel_id=1, source_target_pairs={{0,192},{64,0},{128,64},{192,128},{1,193},{65,1},{129,65},{193,129... | collective-permute-start | bytes 1769480 | tf_op jit(solution)/shard_map/ppermute | solution.py:27
  63.5 4.3 %collective-permute-start.4 = (bf16[4,2,16,3072]{3,2,1,0:T(8,128)(2,1)S(1)}, bf16[4,2,16,3072]{3,2,1,0:T(8,128)(2,1)}, u32[]{:S(2)}, u32[]{:S(2)}) collective-permute-start(bf16[4,2,16,3072]{3,2,1,0:T(8,128)(2,1)S(1)} %all-to-all-done.1.rows), channel_id=1, source_target_pairs={{0,1},{1,0},{2,3},{3,2},{4,5},{5,4},{6,7},{7,6},{8,9},{9,8},{10,11... | collective-permute-start | bytes 2359304 | tf_op jit(solution)/shard_map/ppermute | solution.py:22
  67.8 1.3 copy-start
  71.9 0.7 copy-start.2
  72.7 34.5 %all-to-all-start.2 = ((bf16[2,2,128,384]{3,2,1,0:T(8,128)(2,1)}), bf16[2,2,128,384]{3,2,1,0:T(8,128)(2,1)S(1)}, u32[]{:S(2)}, u32[]{:S(2)}) async-start(bf16[2,2,128,384]{3,2,1,0:T(8,128)(2,1)} %copy-done.2), calls=%async_computation.2 | async-start | bytes 786432 | tf_op jit(solution)/shard_map/all_to_all | solution.py:31
  89.0 0.8 copy-start.3
  89.7 0.8 copy-start.9
  90.5 14.7 %collective-permute-start.5 = (bf16[2,128,768]{2,1,0:T(8,128)(2,1)S(1)}, bf16[2,128,768]{2,1,0:T(8,128)(2,1)S(1)}, u32[]{:S(2)}, u32[]{:S(2)}) collective-permute-start(bf16[2,128,768]{2,1,0:T(8,128)(2,1)S(1)} %get-tuple-element.46), channel_id=1, source_target_pairs={{0,64},{64,128},{128,192},{192,0},{1,65},{65,129},{129,193},{193,1... | collective-permute-start | bytes 1179656 | tf_op jit(solution)/shard_map/ppermute | solution.py:27
  92.4 14.0 %collective-permute-start.6 = (bf16[2,128,768]{2,1,0:T(8,128)(2,1)S(1)}, bf16[2,128,768]{2,1,0:T(8,128)(2,1)S(1)}, u32[]{:S(2)}, u32[]{:S(2)}) collective-permute-start(bf16[2,128,768]{2,1,0:T(8,128)(2,1)S(1)} %get-tuple-element.47), channel_id=1, source_target_pairs={{0,192},{64,0},{128,64},{192,128},{1,193},{65,1},{129,65},{193,129... | collective-permute-start | bytes 1179656 | tf_op jit(solution)/shard_map/ppermute | solution.py:27
  106.4 0.8 copy-start.5
  107.1 1.3 copy-start.1
  111.1 4.2 %collective-permute-start.7 = (bf16[2,64,3072]{2,1,0:T(8,128)(2,1)S(1)}, bf16[2,64,3072]{2,1,0:T(8,128)(2,1)S(1)}, u32[]{:S(2)}, u32[]{:S(2)}) collective-permute-start(bf16[2,64,3072]{2,1,0:T(8,128)(2,1)S(1)} %get-tuple-element.50), channel_id=1, source_target_pairs={{0,1},{1,0},{2,3},{3,2},{4,5},{5,4},{6,7},{7,6},{8,9},{9,8},{10,11... | collective-permute-start | bytes 2359304 | tf_op jit(solution)/shard_map/ppermute | solution.py:22
  116.4 19.3 %all-to-all-start.3 = ((bf16[4,2,16,3072]{3,2,1,0:T(8,128)(2,1)}), bf16[4,2,16,3072]{3,2,1,0:T(8,128)(2,1)}, u32[]{:S(2)}, u32[]{:S(2)}) async-start(bf16[4,2,16,3072]{3,2,1,0:T(8,128)(2,1)} %bitcast.11), calls=%async_computation.3 | async-start | bytes 1572864 | tf_op jit(solution)/shard_map/all_to_all | solution.py:31
  121.2 30.3 %copy-start.10 = (bf16[2,128,768]{2,1,0:T(8,128)(2,1)S(1)}, bf16[2,128,768]{2,1,0:T(8,128)(2,1)}, u32[]{:S(2)}) copy-start(bf16[2,128,768]{2,1,0:T(8,128)(2,1)} %copy-done.9) | copy-start | bytes 1179652
  121.2 43.0 %copy-start.4 = (bf16[2,128,768]{2,1,0:T(8,128)(2,1)S(1)}, bf16[2,128,768]{2,1,0:T(8,128)(2,1)}, u32[]{:S(2)}) copy-start(bf16[2,128,768]{2,1,0:T(8,128)(2,1)} %copy-done.3) | copy-start | bytes 1179652
  121.2 43.0 %copy-start.6 = (bf16[2,128,768]{2,1,0:T(8,128)(2,1)S(1)}, bf16[2,128,768]{2,1,0:T(8,128)(2,1)}, u32[]{:S(2)}) copy-start(bf16[2,128,768]{2,1,0:T(8,128)(2,1)} %copy-done.5) | copy-start | bytes 1179652
  137.9 29.4 %all-to-all-start.4 = ((bf16[16,2,3072]{2,1,0:T(2,128)(2,1)}), bf16[16,2,3072]{2,1,0:T(2,128)(2,1)S(1)}, u32[]{:S(2)}, u32[]{:S(2)}) async-start(bf16[16,2,3072]{2,1,0:T(2,128)(2,1)} %bitcast.12), calls=%async_computation.4 | async-start | bytes 393216 | tf_op jit(solution)/shard_map/all_to_all | solution.py:31
  151.5 12.7 %collective-permute-start.8 = (bf16[2,128,768]{2,1,0:T(8,128)(2,1)S(1)}, bf16[2,128,768]{2,1,0:T(8,128)(2,1)S(1)}, u32[]{:S(2)}, u32[]{:S(2)}) collective-permute-start(bf16[2,128,768]{2,1,0:T(8,128)(2,1)S(1)} %copy-done.10), channel_id=1, source_target_pairs={{0,128},{64,192},{128,0},{192,64},{1,129},{65,193},{129,1},{193,65... | collective-permute-start | bytes 1179656 | tf_op jit(solution)/shard_map/ppermute | solution.py:27
  164.2 3.0 %copy-start.7 = (bf16[1,6144]{1,0:T(2,128)(2,1)S(1)}, bf16[1,6144]{1,0:T(2,128)(2,1)}, u32[]{:S(2)}) copy-start(bf16[1,6144]{1,0:T(2,128)(2,1)} %tokens.3) | copy-start | bytes 36868
  164.2 3.0 %copy-start.8 = (bf16[1,6144]{1,0:T(2,128)(2,1)S(1)}, bf16[1,6144]{1,0:T(2,128)(2,1)}, u32[]{:S(2)}) copy-start(bf16[1,6144]{1,0:T(2,128)(2,1)} %cotangent.3) | copy-start | bytes 36868

commit v6 on v5

--- a/solution.py
+++ b/solution.py
@@ -29,10 +29,6 @@
 
 def trade(values, axis):
     return lax.all_to_all(values, axis, split_axis=0, concat_axis=0, tiled=True)
-
-
-def total(parts):
-    return jnp.sum(parts.astype(f32), axis=0)
 
 
 def dot(left, right, contract=(((1,), (0,)), ((), ()))):
@@ -99,25 +95,22 @@
         one, two = terms[0], sum(terms[1:])
         pre = one if pre is None else pre + one
         grad = two if grad is None else grad + two
-    pre, grad = pre.astype(bf16), grad.astype(bf16)
-    for part in range(ZH):
-        out[part, 0] = pre
-        out[part, 1] = grad
-
-
-def split_body(here, rows, other, *outs):
-    width = outs[0].shape[2]
-    for step, out in enumerate(outs):
-        at = pl.ds(place(here[0], step, width), width)
+    out[0] = pre.astype(bf16)
+    out[1] = grad.astype(bf16)
+
+
+def split_body(rows, other, out):
+    width = out.shape[3]
+    for step in range(Y):
         for index in range(2):
-            out[index] = line_up(rows, other, index, at)
-
-
-def output_body(here, parts, b0, b1, b3, far_in, far_out, pair, keep, give):
+            out[step, index] = line_up(rows, other, index, slice(step * width, (step + 1) * width))
+
+
+def output_body(here, parts, far, b0, b1, b3, far_in, far_out, pair, keep, give):
     width, hidden = far_in.shape
     half = keep.shape[1]
-    value = parts[0, 0].astype(f32) + parts[1, 0].astype(f32)
-    upstream = parts[0, 1].astype(f32) + parts[1, 1].astype(f32)
+    value = parts[0].astype(f32) + far[0].astype(f32)
+    upstream = parts[1].astype(f32) + far[1].astype(f32)
     square = value * value
     curve = jnp.tanh(RATE * (value + CUBE * (square * value)))
     chance = 0.5 * (1.0 + curve)
@@ -140,16 +133,32 @@
             give[0, :, cut] = term[half:].astype(bf16)
 
 
-def weight_body(here, full, r0, r1, r2, r3, grad_w_in, grad_w_out):
-    count = r0.shape[1]
+def weight_body(full, rows, grad_w_in, grad_w_out):
+    count = rows.shape[2]
     ins = outs = None
-    for step, rows in enumerate((r0, r1, r2, r3)):
-        at = pl.ds(pl.multiple_of(lax.rem(here[0] + Y - step, Y) * count, 128), count)
-        one, two = dot(rows[0], full[1, at], FIRST), dot(full[0, at], rows[1], FIRST)
+    for step in range(Y):
+        at = slice(step * count, (step + 1) * count)
+        one, two = dot(rows[step, 0], full[1, at], FIRST), dot(full[0, at], rows[step, 1], FIRST)
         ins = one if ins is None else ins + one
         outs = two if outs is None else outs + two
     grad_w_in[...] = ins
     grad_w_out[...] = outs
+
+
+def add_body(keep, far, out):
+    rows = out.shape[2]
+    for step in range(X):
+        at = slice(step * rows, (step + 1) * rows)
+        out[step] = (keep[:, at] + far[:, at].astype(f32)).astype(bf16)
+
+
+def sum_body(parts, out):
+    first, second = (
+        sum(parts[step, index].astype(f32) for step in range(X)).astype(bf16).astype(f32) for index in range(2)
+    )
+    for row in range(out.shape[0]):
+        cut = slice(row, row + 1)
+        out[row] = jnp.concatenate([first[cut], second[cut]], axis=0).astype(bf16)
 
 
 def final_body(tokens, cotangent, sums, mixed, grad_tokens):
@@ -193,35 +202,30 @@
     other = swap(rows, "core")
     blocks = (block, above, below, far_in, far_out)
 
-    (parts,) = call(hidden_body, [shape((ZH, 2, count, hidden), bf16)], here, rows, other, *blocks, flops=work)
+    (parts,) = call(hidden_body, [shape((2, count, hidden), bf16)], here, rows, other, *blocks, flops=work)
     parts, rows, other = lax.optimization_barrier((parts, rows, other))
-    parts = trade(parts, "zh")
-    split = call(split_body, [shape((2, count, width), bf16)] * Y, here, rows, other)
-    near = (shift(split[1], "y", 1), shift(split[3], "y", 3))
-    parts, near = lax.optimization_barrier((parts, near))
+    far = swap(parts, "zh")
+    (spread,) = call(split_body, [shape((Y, 2, count, width), bf16)], rows, other)
+    far, spread = lax.optimization_barrier((far, trade(spread, "y")))
     pair, keep, give = call(
         output_body,
         [shape((2, count, hidden), bf16), shape((2, half, features), f32), shape((2, half, features), bf16)],
-        here, parts, *blocks, flops=work,
-    )
-
-    sums = keep + swap(give, "core").astype(f32)
-    sums = sums.astype(bf16).reshape(2, X, half // X, features).transpose(1, 0, 2, 3)
+        here, parts, far, *blocks, flops=work,
+    )
+
+    (sums,) = call(add_body, [shape((X, 2, half // X, features), bf16)], keep, swap(give, "core"))
     sums, pair = lax.optimization_barrier((sums, pair))
-    sums, full = trade(sums, "x"), lax.all_gather(pair, "y", axis=1, tiled=True)
-    sums, full = lax.optimization_barrier((sums, full))
-    sums = total(sums).astype(bf16).transpose(1, 0, 2)
-    sums, opposite = lax.optimization_barrier((sums, split[2]))
+    sums, full = lax.optimization_barrier((trade(sums, "x"), lax.all_gather(pair, "y", axis=1, tiled=True)))
+    (sums,) = call(sum_body, [shape((half // X, 2, features), bf16)], sums)
     sums = trade(sums, FAR)
     mixed, grad_tokens = call(
         final_body, [shape(tokens.shape, bf16)] * 2, tokens, cotangent, sums
     )
 
-    spread = (split[0], near[0], shift(opposite, "y", 2), near[1])
     grad_w_in, grad_w_out = call(
         weight_body,
         [shape((width, hidden), f32), shape((hidden, width), f32)],
-        here, full, *spread, flops=work,
+        full, spread, flops=work,
     )
     return (mixed, grad_tokens, grad_w_in, grad_w_out)
 

time: 169 us -> 172 us (1.018)
  Pallas kernels: 13.2 us -> 16.7 us
  starting transfers between devices: 82 us -> 85.4 us
  local copies, waits for them, and re-layouts: 10.2 us -> 8.41 us
    ppermute x7 -> x4, waiting for transfers between devices: 39.2 us -> 21.5 us  [shift(): lax.ppermute(values, axis, [(at, (at + step) % count) for at in range(cou...]
    ppermute x2 -> x3, starting transfers between devices: 3.83 us -> 19.5 us  [swap(): return lax.ppermute(values, axis, [(0, 1), (1, 0)])]
    all_to_all x5, waiting for transfers between devices: 2.39 us -> 13.7 us  [trade(): return lax.all_to_all(values, axis, split_axis=0, concat_axis=0, tiled=True)]
    ppermute x7 -> x4, starting transfers between devices: 24.7 us -> 13.9 us  [shift(): lax.ppermute(values, axis, [(at, (at + step) % count) for at in range(cou...]
    ppermute x2 -> x3, waiting for transfers between devices: 4.63 us -> 10 us  [swap(): return lax.ppermute(values, axis, [(0, 1), (1, 0)])]
    pallas_call x6 -> x8, Pallas kernels: 13.2 us -> 16.7 us  [call(): pl.pallas_call(body, out_shape=shapes, in_specs=specs, out_specs=[pl.Bloc...]
  transfers between devices with their start and end apart: 14 -> 12, of which waited for: 12 -> 10; matrix products, arithmetic and copies ran while one was open for 1% -> 1% of each run, Pallas kernels for 2% -> 2%
where the time goes in v6:
time: 172 us; the launch traced here: 171 us
  starting transfers between devices  85.4 us (50%)
  waiting for transfers between devices  45.2 us (26%)
  Pallas kernels  16.7 us (10%)
  blocking collectives  14.2 us (8%)
  local copies, waits for them, and re-layouts  8.41 us (5%)
    all_to_all x5, starting transfers between devices, trade(): return lax.all_to_all(values, axis, split_axis=0, concat_axis=0, tiled=True)  52 us
    ppermute x4, waiting for transfers between devices, shift(): lax.ppermute(values, axis, [(at, (at + step) % count) for at in range(cou...  21.5 us
    ppermute x3, starting transfers between devices, swap(): return lax.ppermute(values, axis, [(0, 1), (1, 0)])  19.5 us
    pallas_call x8, Pallas kernels, call(): pl.pallas_call(body, out_shape=shapes, in_specs=specs, out_specs=[pl.Bloc...  16.7 us
    all_gather x1, blocking collectives, local(): lax.all_gather(pair, 'y', axis=1, tiled=True)  14.2 us
    ppermute x4, starting transfers between devices, shift(): lax.ppermute(values, axis, [(at, (at + step) % count) for at in range(cou...  13.9 us
    all_to_all x5, waiting for transfers between devices, trade(): return lax.all_to_all(values, axis, split_axis=0, concat_axis=0, tiled=True)  13.7 us
    ppermute x3, waiting for transfers between devices, swap(): return lax.ppermute(values, axis, [(0, 1), (1, 0)])  10 us
  transfers between devices with their start and end apart: 12, of which 10 were waited for; matrix products, arithmetic and copies ran while one was open for 1% of the time, Pallas kernels for 2%

profile of v6, /device:TPU:6, one launch (start us, length us, event | category | flops | bytes accessed | tf_op | source)
XLA Modules:
  0.0 170.6 jit_solution(1560253932015636947)
XLA Ops:
  0.6 2.6 %shard_map.75 = (bf16[16,2,3072]{2,1,0:T(2,128)(2,1)}, bf16[2,768,384]{2,1,0:T(8,128)(2,1)}) custom-call(bf16[1,6144]{1,0:T(2,128)(2,1)} %tokens.3, bf16[1,6144]{1,0:T(2,128)(2,1)} %cotangent.3, bf16[768,384]{1,0:T(8,128)(2,1)} %w_in.1, bf16[384,768]{1,0:T(8,128)(2,1)} %w_out.1), custom_call_target="tpu_custom_call" | custom-call | bytes 2580480 | tf_op jit(solution)/shard_map/pallas_call | solution.py:43
  3.2 4.9 %collective-permute-start.1 = (bf16[2,768,384]{2,1,0:T(8,128)(2,1)}, bf16[2,768,384]{2,1,0:T(8,128)(2,1)S(1)}, u32[]{:S(2)}, u32[]{:S(2)}) collective-permute-start(bf16[2,768,384]{2,1,0:T(8,128)(2,1)} %get-tuple-element.29.b0), channel_id=1, source_target_pairs={{0,192},{64,0},{128,64},{192,128},{1,193},{65,1},{129,65},{193,129... | collective-permute-start | bytes 3538952 | tf_op jit(solution)/shard_map/ppermute | solution.py:27
  8.2 1.9 %collective-permute-start = (bf16[2,768,384]{2,1,0:T(8,128)(2,1)}, bf16[2,768,384]{2,1,0:T(8,128)(2,1)S(1)}, u32[]{:S(2)}, u32[]{:S(2)}) collective-permute-start(bf16[2,768,384]{2,1,0:T(8,128)(2,1)} %get-tuple-element.29.b0), channel_id=1, source_target_pairs={{0,64},{64,128},{128,192},{192,0},{1,65},{65,129},{129,193},{193,1... | collective-permute-start | bytes 3538952 | tf_op jit(solution)/shard_map/ppermute | solution.py:27
  10.1 15.2 %all-to-all-start = ((bf16[16,2,3072]{2,1,0:T(2,128)(2,1)}), bf16[16,2,3072]{2,1,0:T(2,128)(2,1)S(1)}, u32[]{:S(2)}, u32[]{:S(2)}) async-start(bf16[16,2,3072]{2,1,0:T(2,128)(2,1)} %get-tuple-element.28), calls=%async_computation | async-start | bytes 393216 | tf_op jit(solution)/shard_map/all_to_all | solution.py:31
  25.3 8.4 %collective-permute-done.1.b1 = bf16[2,768,384]{2,1,0:T(8,128)(2,1)S(1)} collective-permute-done((bf16[2,768,384]{2,1,0:T(8,128)(2,1)}, bf16[2,768,384]{2,1,0:T(8,128)(2,1)S(1)}, u32[]{:S(2)}, u32[]{:S(2)}) %collective-permute-start.1) | collective-permute-done | bytes 1179680 | tf_op jit(solution)/shard_map/ppermute | solution.py:27
  33.7 0.9 slice_bitcast_fusion
  34.5 4.4 %collective-permute-done.b3 = bf16[2,768,384]{2,1,0:T(8,128)(2,1)S(1)} collective-permute-done((bf16[2,768,384]{2,1,0:T(8,128)(2,1)}, bf16[2,768,384]{2,1,0:T(8,128)(2,1)S(1)}, u32[]{:S(2)}, u32[]{:S(2)}) %collective-permute-start) | collective-permute-done | bytes 1179680 | tf_op jit(solution)/shard_map/ppermute | solution.py:27
  38.9 0.9 slice_bitcast_fusion.1
  39.8 1.7 %all-to-all-done = bf16[16,2,3072]{2,1,0:T(2,128)(2,1)S(1)} async-done(((bf16[16,2,3072]{2,1,0:T(2,128)(2,1)}), bf16[16,2,3072]{2,1,0:T(2,128)(2,1)S(1)}, u32[]{:S(2)}, u32[]{:S(2)}) %all-to-all-start) | async-done | bytes 196640 | tf_op jit(solution)/shard_map/all_to_all | solution.py:31
  41.5 1.0 broadcast_in_dim.3
  42.5 4.8 %all-to-all-start.1 = ((bf16[4,2,16,3072]{3,2,1,0:T(8,128)(2,1)}), bf16[4,2,16,3072]{3,2,1,0:T(8,128)(2,1)S(1)}, u32[]{:S(2)}, u32[]{:S(2)}) async-start(bf16[4,2,16,3072]{3,2,1,0:T(8,128)(2,1)} %broadcast_in_dim.3), calls=%async_computation.1 | async-start | bytes 1572864 | tf_op jit(solution)/shard_map/all_to_all | solution.py:31
  47.3 2.2 %collective-permute-start.2 = (bf16[768,384]{1,0:T(8,128)(2,1)}, bf16[768,384]{1,0:T(8,128)(2,1)}, u32[]{:S(2)}, u32[]{:S(2)}) collective-permute-start(bf16[768,384]{1,0:T(8,128)(2,1)} %slice_bitcast_fusion.1), channel_id=1, source_target_pairs={{0,64},{64,128},{128,192},{192,0},{1,65},{65,129},{129,193},{193,1... | collective-permute-start | bytes 1769480 | tf_op jit(solution)/shard_map/ppermute | solution.py:27
  49.5 4.8 %collective-permute-start.3 = (bf16[768,384]{1,0:T(8,128)(2,1)}, bf16[768,384]{1,0:T(8,128)(2,1)}, u32[]{:S(2)}, u32[]{:S(2)}) collective-permute-start(bf16[768,384]{1,0:T(8,128)(2,1)} %slice_bitcast_fusion), channel_id=1, source_target_pairs={{0,192},{64,0},{128,64},{192,128},{1,193},{65,1},{129,65},{193,129... | collective-permute-start | bytes 1769480 | tf_op jit(solution)/shard_map/ppermute | solution.py:27
  54.3 0.4 all-to-all-done.1.rows
  54.7 7.6 %collective-permute-done.2.far_in = bf16[768,384]{1,0:T(8,128)(2,1)} collective-permute-done((bf16[768,384]{1,0:T(8,128)(2,1)}, bf16[768,384]{1,0:T(8,128)(2,1)}, u32[]{:S(2)}, u32[]{:S(2)}) %collective-permute-start.2) | collective-permute-done | bytes 589856 | tf_op jit(solution)/shard_map/ppermute | solution.py:27
  62.3 1.2 collective-permute-done.3.far_out
  63.5 1.9 %collective-permute-start.4 = (bf16[4,2,16,3072]{3,2,1,0:T(8,128)(2,1)S(1)}, bf16[4,2,16,3072]{3,2,1,0:T(8,128)(2,1)}, u32[]{:S(2)}, u32[]{:S(2)}) collective-permute-start(bf16[4,2,16,3072]{3,2,1,0:T(8,128)(2,1)S(1)} %all-to-all-done.1.rows), channel_id=1, source_target_pairs={{0,1},{1,0},{2,3},{3,2},{4,5},{5,4},{6,7},{7,6},{8,9},{9,8},{10,11... | collective-permute-start | bytes 2359304 | tf_op jit(solution)/shard_map/ppermute | solution.py:22
  65.4 2.4 %collective-permute-done.4.other = bf16[4,2,16,3072]{3,2,1,0:T(8,128)(2,1)} collective-permute-done((bf16[4,2,16,3072]{3,2,1,0:T(8,128)(2,1)S(1)}, bf16[4,2,16,3072]{3,2,1,0:T(8,128)(2,1)}, u32[]{:S(2)}, u32[]{:S(2)}) %collective-permute-start.4) | collective-permute-done | bytes 786464 | tf_op jit(solution)/shard_map/ppermute | solution.py:22
  67.8 0.0 copy-start.1
  67.8 1.3 copy-done.1
  69.0 2.8 %shard_map.76.parts = bf16[2,128,384]{2,1,0:T(8,128)(2,1)S(1)} custom-call(s32[1]{0:T(128)} %bitcast.here, bf16[4,2,16,3072]{3,2,1,0:T(8,128)(2,1)S(1)} %all-to-all-done.1.rows, bf16[4,2,16,3072]{3,2,1,0:T(8,128)(2,1)} %collective-permute-done.4.other, bf16[2,768,384]{2,1,0:T(8,128)(2,1)S(1)} %copy-done.1, ...), custom_call_target="tpu_custom_call" | custom-call | flops 603979776 | bytes 6488068 | tf_op jit(solution)/shard_map/pallas_call | solution.py:43
  71.9 0.0 copy-start.3
  71.9 0.7 copy-done.3
  72.6 1.2 shard_map.77
  73.8 0.0 copy-start
  73.8 1.1 copy-done
  75.0 0.0 copy-start.2
  75.0 5.1 %all-to-all-start.2 = ((bf16[4,2,128,768]{3,2,1,0:T(8,128)(2,1)}), bf16[4,2,128,768]{3,2,1,0:T(8,128)(2,1)}, u32[]{:S(2)}, u32[]{:S(2)}) async-start(bf16[4,2,128,768]{3,2,1,0:T(8,128)(2,1)} %copy-done), calls=%async_computation.2 | async-start | bytes 3145728 | tf_op jit(solution)/shard_map/all_to_all | solution.py:31
  80.0 15.7 %collective-permute-start.5 = (bf16[2,128,384]{2,1,0:T(8,128)(2,1)}, bf16[2,128,384]{2,1,0:T(8,128)(2,1)S(1)}, u32[]{:S(2)}, u32[]{:S(2)}) collective-permute-start(bf16[2,128,384]{2,1,0:T(8,128)(2,1)} %copy-done.3), channel_id=1, source_target_pairs={{0,256},{256,0},{1,257},{257,1},{2,258},{258,2},{3,259},{259,3},{4... | collective-permute-start | bytes 589832 | tf_op jit(solution)/shard_map/ppermute | solution.py:22
  95.8 5.4 %collective-permute-done.5.far = bf16[2,128,384]{2,1,0:T(8,128)(2,1)S(1)} collective-permute-done((bf16[2,128,384]{2,1,0:T(8,128)(2,1)}, bf16[2,128,384]{2,1,0:T(8,128)(2,1)S(1)}, u32[]{:S(2)}, u32[]{:S(2)}) %collective-permute-start.5) | collective-permute-done | bytes 196640 | tf_op jit(solution)/shard_map/ppermute | solution.py:22
  101.2 0.0 copy-start.7
  101.2 0.7 copy-done.7
  101.9 0.0 all-to-all-done.2.rows
  101.9 0.0 copy-done.2
  101.9 0.0 copy-start.4
  101.9 0.9 copy-done.4
  102.8 0.0 copy-start.8
  102.8 0.9 copy-done.8
  103.7 2.7 %shard_map.78 = (bf16[2,128,384]{2,1,0:T(8,128)(2,1)S(1)}, f32[2,64,3072]{2,1,0:T(8,128)S(1)}, bf16[2,64,3072]{2,1,0:T(8,128)(2,1)S(1)}) custom-call(s32[1]{0:T(128)} %bitcast.here, bf16[2,128,384]{2,1,0:T(8,128)(2,1)S(1)} %copy-done.4, bf16[2,128,384]{2,1,0:T(8,128)(2,1)S(1)} %copy-done.8, bf16[2,768,384]{2,1,0:T(8,128)(2,1)S(1)} %copy-done.2, ...), custom_call_target="tpu_custom_call" | custom-call | flops 603979776 | bytes 7667716 | tf_op jit(solution)/shard_map/pallas_call | solution.py:43
  106.4 0.0 copy-start.5
  106.4 1.9 %collective-permute-start.6 = (bf16[2,64,3072]{2,1,0:T(8,128)(2,1)S(1)}, bf16[2,64,3072]{2,1,0:T(8,128)(2,1)S(1)}, u32[]{:S(2)}, u32[]{:S(2)}) collective-permute-start(bf16[2,64,3072]{2,1,0:T(8,128)(2,1)S(1)} %get-tuple-element.41), channel_id=1, source_target_pairs={{0,1},{1,0},{2,3},{3,2},{4,5},{5,4},{6,7},{7,6},{8,9},{9,8},{10,11... | collective-permute-start | bytes 2359304 | tf_op jit(solution)/shard_map/ppermute | solution.py:22
  108.3 2.3 %collective-permute-done.6.far = bf16[2,64,3072]{2,1,0:T(8,128)(2,1)S(1)} collective-permute-done((bf16[2,64,3072]{2,1,0:T(8,128)(2,1)S(1)}, bf16[2,64,3072]{2,1,0:T(8,128)(2,1)S(1)}, u32[]{:S(2)}, u32[]{:S(2)}) %collective-permute-start.6) | collective-permute-done | bytes 786464 | tf_op jit(solution)/shard_map/ppermute | solution.py:22
  110.6 1.0 shard_map.79
  111.6 0.0 copy-done.5
  111.6 0.0 copy-start.6
  111.6 4.9 %all-to-all-start.3 = ((bf16[4,2,16,3072]{3,2,1,0:T(8,128)(2,1)}), bf16[4,2,16,3072]{3,2,1,0:T(8,128)(2,1)S(1)}, u32[]{:S(2)}, u32[]{:S(2)}) async-start(bf16[4,2,16,3072]{3,2,1,0:T(8,128)(2,1)} %shard_map.79), calls=%async_computation.3 | async-start | bytes 1572864 | tf_op jit(solution)/shard_map/all_to_all | solution.py:31
  116.5 0.0 copy-done.6
  116.5 14.2 %all_gather.3.full = bf16[2,512,384]{2,1,0:T(8,128)(2,1)S(1)} all-gather(bf16[2,128,384]{2,1,0:T(8,128)(2,1)S(1)} %copy-done.6), channel_id=1, replica_groups=mesh['zh'=2,'y'=4,'zl'=8,'x'=4,'core'=2] {'y'}, dimensions={1}, use_global_device_ids=true | all-gather | bytes 983040 | tf_op jit(solution)/shard_map/all_gather | solution.py:218
  130.7 0.0 all-to-all-done.3.parts
  130.7 1.0 shard_map.80
  131.7 22.0 %all-to-all-start.4 = ((bf16[16,2,3072]{2,1,0:T(2,128)(2,1)}), bf16[16,2,3072]{2,1,0:T(2,128)(2,1)S(1)}, u32[]{:S(2)}, u32[]{:S(2)}) async-start(bf16[16,2,3072]{2,1,0:T(2,128)(2,1)} %shard_map.80), calls=%async_computation.4 | async-start | bytes 393216 | tf_op jit(solution)/shard_map/all_to_all | solution.py:31
  153.7 0.0 copy-start.9
  153.7 0.0 copy-start.10
  153.7 4.1 %shard_map.82 = (f32[768,384]{1,0:T(8,128)}, f32[384,768]{1,0:T(8,128)}) custom-call(bf16[2,512,384]{2,1,0:T(8,128)(2,1)S(1)} %all_gather.3.full, bf16[4,2,128,768]{3,2,1,0:T(8,128)(2,1)} %all-to-all-done.2.rows), custom_call_target="tpu_custom_call" | custom-call | flops 603979776 | bytes 4718592 | tf_op jit(solution)/shard_map/pallas_call | solution.py:43
  157.9 11.6 %all-to-all-done.4.sums = bf16[16,2,3072]{2,1,0:T(2,128)(2,1)S(1)} async-done(((bf16[16,2,3072]{2,1,0:T(2,128)(2,1)}), bf16[16,2,3072]{2,1,0:T(2,128)(2,1)S(1)}, u32[]{:S(2)}, u32[]{:S(2)}) %all-to-all-start.4) | async-done | bytes 196640 | tf_op jit(solution)/shard_map/all_to_all | solution.py:31
  169.4 0.0 copy-done.9
  169.4 0.0 copy-done.10
  169.4 1.2 shard_map.81
  (1 shorter events, 0.0 us)
Async XLA Ops:
  3.2 30.4 %collective-permute-start.1 = (bf16[2,768,384]{2,1,0:T(8,128)(2,1)}, bf16[2,768,384]{2,1,0:T(8,128)(2,1)S(1)}, u32[]{:S(2)}, u32[]{:S(2)}) collective-permute-start(bf16[2,768,384]{2,1,0:T(8,128)(2,1)} %get-tuple-element.29.b0), channel_id=1, source_target_pairs={{0,192},{64,0},{128,64},{192,128},{1,193},{65,1},{129,65},{193,129... | collective-permute-start | bytes 3538952 | tf_op jit(solution)/shard_map/ppermute | solution.py:27
  8.2 30.7 %collective-permute-start = (bf16[2,768,384]{2,1,0:T(8,128)(2,1)}, bf16[2,768,384]{2,1,0:T(8,128)(2,1)S(1)}, u32[]{:S(2)}, u32[]{:S(2)}) collective-permute-start(bf16[2,768,384]{2,1,0:T(8,128)(2,1)} %get-tuple-element.29.b0), channel_id=1, source_target_pairs={{0,64},{64,128},{128,192},{192,0},{1,65},{65,129},{129,193},{193,1... | collective-permute-start | bytes 3538952 | tf_op jit(solution)/shard_map/ppermute | solution.py:27
  10.1 31.4 %all-to-all-start = ((bf16[16,2,3072]{2,1,0:T(2,128)(2,1)}), bf16[16,2,3072]{2,1,0:T(2,128)(2,1)S(1)}, u32[]{:S(2)}, u32[]{:S(2)}) async-start(bf16[16,2,3072]{2,1,0:T(2,128)(2,1)} %get-tuple-element.28), calls=%async_computation | async-start | bytes 393216 | tf_op jit(solution)/shard_map/all_to_all | solution.py:31
  42.5 12.2 %all-to-all-start.1 = ((bf16[4,2,16,3072]{3,2,1,0:T(8,128)(2,1)}), bf16[4,2,16,3072]{3,2,1,0:T(8,128)(2,1)S(1)}, u32[]{:S(2)}, u32[]{:S(2)}) async-start(bf16[4,2,16,3072]{3,2,1,0:T(8,128)(2,1)} %broadcast_in_dim.3), calls=%async_computation.1 | async-start | bytes 1572864 | tf_op jit(solution)/shard_map/all_to_all | solution.py:31
  47.3 15.0 %collective-permute-start.2 = (bf16[768,384]{1,0:T(8,128)(2,1)}, bf16[768,384]{1,0:T(8,128)(2,1)}, u32[]{:S(2)}, u32[]{:S(2)}) collective-permute-start(bf16[768,384]{1,0:T(8,128)(2,1)} %slice_bitcast_fusion.1), channel_id=1, source_target_pairs={{0,64},{64,128},{128,192},{192,0},{1,65},{65,129},{129,193},{193,1... | collective-permute-start | bytes 1769480 | tf_op jit(solution)/shard_map/ppermute | solution.py:27
  49.5 14.0 %collective-permute-start.3 = (bf16[768,384]{1,0:T(8,128)(2,1)}, bf16[768,384]{1,0:T(8,128)(2,1)}, u32[]{:S(2)}, u32[]{:S(2)}) collective-permute-start(bf16[768,384]{1,0:T(8,128)(2,1)} %slice_bitcast_fusion), channel_id=1, source_target_pairs={{0,192},{64,0},{128,64},{192,128},{1,193},{65,1},{129,65},{193,129... | collective-permute-start | bytes 1769480 | tf_op jit(solution)/shard_map/ppermute | solution.py:27
  63.5 4.3 %collective-permute-start.4 = (bf16[4,2,16,3072]{3,2,1,0:T(8,128)(2,1)S(1)}, bf16[4,2,16,3072]{3,2,1,0:T(8,128)(2,1)}, u32[]{:S(2)}, u32[]{:S(2)}) collective-permute-start(bf16[4,2,16,3072]{3,2,1,0:T(8,128)(2,1)S(1)} %all-to-all-done.1.rows), channel_id=1, source_target_pairs={{0,1},{1,0},{2,3},{3,2},{4,5},{5,4},{6,7},{7,6},{8,9},{9,8},{10,11... | collective-permute-start | bytes 2359304 | tf_op jit(solution)/shard_map/ppermute | solution.py:22
  67.8 1.3 copy-start.1
  71.9 0.7 copy-start.3
  73.8 1.2 copy-start
  75.0 26.9 %copy-start.2 = (bf16[2,768,384]{2,1,0:T(8,128)(2,1)S(1)}, bf16[2,768,384]{2,1,0:T(8,128)(2,1)}, u32[]{:S(2)}) copy-start(bf16[2,768,384]{2,1,0:T(8,128)(2,1)} %get-tuple-element.29.b0) | copy-start | bytes 3538948
  75.0 26.9 %all-to-all-start.2 = ((bf16[4,2,128,768]{3,2,1,0:T(8,128)(2,1)}), bf16[4,2,128,768]{3,2,1,0:T(8,128)(2,1)}, u32[]{:S(2)}, u32[]{:S(2)}) async-start(bf16[4,2,128,768]{3,2,1,0:T(8,128)(2,1)} %copy-done), calls=%async_computation.2 | async-start | bytes 3145728 | tf_op jit(solution)/shard_map/all_to_all | solution.py:31
  80.0 21.1 %collective-permute-start.5 = (bf16[2,128,384]{2,1,0:T(8,128)(2,1)}, bf16[2,128,384]{2,1,0:T(8,128)(2,1)S(1)}, u32[]{:S(2)}, u32[]{:S(2)}) collective-permute-start(bf16[2,128,384]{2,1,0:T(8,128)(2,1)} %copy-done.3), channel_id=1, source_target_pairs={{0,256},{256,0},{1,257},{257,1},{2,258},{258,2},{3,259},{259,3},{4... | collective-permute-start | bytes 589832 | tf_op jit(solution)/shard_map/ppermute | solution.py:22
  101.2 0.7 copy-start.7
  101.9 0.9 copy-start.4
  102.8 0.9 copy-start.8
  106.4 5.2 %copy-start.5 = (bf16[2,128,384]{2,1,0:T(8,128)(2,1)}, bf16[2,128,384]{2,1,0:T(8,128)(2,1)S(1)}, u32[]{:S(2)}) copy-start(bf16[2,128,384]{2,1,0:T(8,128)(2,1)S(1)} %get-tuple-element.44) | copy-start | bytes 589828
  106.4 4.2 %collective-permute-start.6 = (bf16[2,64,3072]{2,1,0:T(8,128)(2,1)S(1)}, bf16[2,64,3072]{2,1,0:T(8,128)(2,1)S(1)}, u32[]{:S(2)}, u32[]{:S(2)}) collective-permute-start(bf16[2,64,3072]{2,1,0:T(8,128)(2,1)S(1)} %get-tuple-element.41), channel_id=1, source_target_pairs={{0,1},{1,0},{2,3},{3,2},{4,5},{5,4},{6,7},{7,6},{8,9},{9,8},{10,11... | collective-permute-start | bytes 2359304 | tf_op jit(solution)/shard_map/ppermute | solution.py:22
  111.6 4.9 %copy-start.6 = (bf16[2,128,384]{2,1,0:T(8,128)(2,1)S(1)}, bf16[2,128,384]{2,1,0:T(8,128)(2,1)}, u32[]{:S(2)}) copy-start(bf16[2,128,384]{2,1,0:T(8,128)(2,1)} %copy-done.5) | copy-start | bytes 589828
  111.6 19.1 %all-to-all-start.3 = ((bf16[4,2,16,3072]{3,2,1,0:T(8,128)(2,1)}), bf16[4,2,16,3072]{3,2,1,0:T(8,128)(2,1)S(1)}, u32[]{:S(2)}, u32[]{:S(2)}) async-start(bf16[4,2,16,3072]{3,2,1,0:T(8,128)(2,1)} %shard_map.79), calls=%async_computation.3 | async-start | bytes 1572864 | tf_op jit(solution)/shard_map/all_to_all | solution.py:31
  131.7 37.7 %all-to-all-start.4 = ((bf16[16,2,3072]{2,1,0:T(2,128)(2,1)}), bf16[16,2,3072]{2,1,0:T(2,128)(2,1)S(1)}, u32[]{:S(2)}, u32[]{:S(2)}) async-start(bf16[16,2,3072]{2,1,0:T(2,128)(2,1)} %shard_map.80), calls=%async_computation.4 | async-start | bytes 393216 | tf_op jit(solution)/shard_map/all_to_all | solution.py:31
  153.7 15.7 %copy-start.9 = (bf16[1,6144]{1,0:T(2,128)(2,1)S(1)}, bf16[1,6144]{1,0:T(2,128)(2,1)}, u32[]{:S(2)}) copy-start(bf16[1,6144]{1,0:T(2,128)(2,1)} %tokens.3) | copy-start | bytes 36868
  153.7 15.7 %copy-start.10 = (bf16[1,6144]{1,0:T(2,128)(2,1)S(1)}, bf16[1,6144]{1,0:T(2,128)(2,1)}, u32[]{:S(2)}) copy-start(bf16[1,6144]{1,0:T(2,128)(2,1)} %cotangent.3) | copy-start | bytes 36868

commit v7 on v6

--- a/solution.py
+++ b/solution.py
@@ -99,18 +99,19 @@
     out[1] = grad.astype(bf16)
 
 
-def split_body(rows, other, out):
+def split_body(rows, out):
     width = out.shape[3]
     for step in range(Y):
         for index in range(2):
-            out[step, index] = line_up(rows, other, index, slice(step * width, (step + 1) * width))
-
-
-def output_body(here, parts, far, b0, b1, b3, far_in, far_out, pair, keep, give):
+            cut = slice(step * width, (step + 1) * width)
+            out[step, index] = jnp.concatenate([rows[at, index, :, cut] for at in range(X)], axis=0)
+
+
+def output_body(here, parts, b0, b1, b3, far_in, far_out, pair, keep, give):
     width, hidden = far_in.shape
     half = keep.shape[1]
-    value = parts[0].astype(f32) + far[0].astype(f32)
-    upstream = parts[1].astype(f32) + far[1].astype(f32)
+    value = parts[0, 0].astype(f32) + parts[1, 0].astype(f32)
+    upstream = parts[0, 1].astype(f32) + parts[1, 1].astype(f32)
     square = value * value
     curve = jnp.tanh(RATE * (value + CUBE * (square * value)))
     chance = 0.5 * (1.0 + curve)
@@ -133,12 +134,13 @@
             give[0, :, cut] = term[half:].astype(bf16)
 
 
-def weight_body(full, rows, grad_w_in, grad_w_out):
-    count = rows.shape[2]
+def weight_body(full, mine, theirs, grad_w_in, grad_w_out):
+    count = mine.shape[2]
     ins = outs = None
-    for step in range(Y):
+    for step in range(Y * CORE):
         at = slice(step * count, (step + 1) * count)
-        one, two = dot(rows[step, 0], full[1, at], FIRST), dot(full[0, at], rows[step, 1], FIRST)
+        rows = (mine, theirs)[step % CORE].at[step // CORE]
+        one, two = dot(rows[0], full[1, at], FIRST), dot(full[0, at], rows[1], FIRST)
         ins = one if ins is None else ins + one
         outs = two if outs is None else outs + two
     grad_w_in[...] = ins
@@ -198,34 +200,36 @@
     both = both.transpose(1, 0, 2)
     rows = trade(jnp.broadcast_to(both, (X,) + both.shape), "x")
     far_in, far_out = shift(near_in, "y", 1), shift(near_out, "y", -1)
-    rows, far_in, far_out = lax.optimization_barrier((rows, far_in, far_out))
+    (mine,) = call(split_body, [shape((Y, 2, half, width), bf16)], rows)
+    rows, far_in, far_out, mine = lax.optimization_barrier((rows, far_in, far_out, mine))
     other = swap(rows, "core")
+    mine = trade(mine, "y")
     blocks = (block, above, below, far_in, far_out)
 
     (parts,) = call(hidden_body, [shape((2, count, hidden), bf16)], here, rows, other, *blocks, flops=work)
-    parts, rows, other = lax.optimization_barrier((parts, rows, other))
-    far = swap(parts, "zh")
-    (spread,) = call(split_body, [shape((Y, 2, count, width), bf16)], rows, other)
-    far, spread = lax.optimization_barrier((far, trade(spread, "y")))
+    parts, mine = lax.optimization_barrier((lax.all_gather(parts, "zh"), mine))
     pair, keep, give = call(
         output_body,
         [shape((2, count, hidden), bf16), shape((2, half, features), f32), shape((2, half, features), bf16)],
-        here, parts, far, *blocks, flops=work,
+        here, parts, *blocks, flops=work,
     )
 
     (sums,) = call(add_body, [shape((X, 2, half // X, features), bf16)], keep, swap(give, "core"))
-    sums, pair = lax.optimization_barrier((sums, pair))
-    sums, full = lax.optimization_barrier((trade(sums, "x"), lax.all_gather(pair, "y", axis=1, tiled=True)))
+    sums, pair, mine = lax.optimization_barrier((sums, pair, mine))
+    full = lax.all_gather(pair, "y", axis=1, tiled=True)
+    sums, full, theirs = lax.optimization_barrier((trade(sums, "x"), full, swap(mine, "core")))
     (sums,) = call(sum_body, [shape((half // X, 2, features), bf16)], sums)
     sums = trade(sums, FAR)
-    mixed, grad_tokens = call(
-        final_body, [shape(tokens.shape, bf16)] * 2, tokens, cotangent, sums
-    )
 
     grad_w_in, grad_w_out = call(
         weight_body,
         [shape((width, hidden), f32), shape((hidden, width), f32)],
-        full, spread, flops=work,
+        full, mine, theirs, flops=work,
+    )
+
+    sums, grad_w_in, grad_w_out = lax.optimization_barrier((sums, grad_w_in, grad_w_out))
+    mixed, grad_tokens = call(
+        final_body, [shape(tokens.shape, bf16)] * 2, tokens, cotangent, sums
     )
     return (mixed, grad_tokens, grad_w_in, grad_w_out)
 

time: 172 us -> 165 us (0.959)
  blocking collectives: 14.2 us -> 33.9 us
  starting transfers between devices: 85.4 us -> 72.1 us
  waiting for transfers between devices: 45.2 us -> 35.1 us
  local copies, waits for them, and re-layouts: 8.41 us -> 6.21 us
    all_gather x1 -> x2, blocking collectives: 14.2 us -> 33.9 us  [the longest x1 20.1 us: local(): parts, mine = lax.optimization_barrier((lax.all_gather(parts, 'zh'), mine))]
    ppermute x3, starting transfers between devices: 19.5 us -> 5.86 us  [swap(): return lax.ppermute(values, axis, [(0, 1), (1, 0)])]
    ppermute x3, waiting for transfers between devices: 10 us -> 2.26 us  [swap(): return lax.ppermute(values, axis, [(0, 1), (1, 0)])]
    unnamed x22 -> x10, local copies, waits for them, and re-layouts: 5.65 us -> 3.43 us
  transfers between devices with their start and end apart: 12 -> 12, of which waited for: 10 -> 8; matrix products, arithmetic and copies ran while one was open for 1% -> 1% of each run, Pallas kernels for 2% -> 5%
where the time goes in v7:
time: 165 us
  starting transfers between devices  72.1 us (44%)
  waiting for transfers between devices  35.1 us (21%)
  blocking collectives  33.9 us (21%)
  Pallas kernels  16.4 us (10%)
  local copies, waits for them, and re-layouts  6.21 us (4%)
    all_to_all x5, starting transfers between devices, trade(): return lax.all_to_all(values, axis, split_axis=0, concat_axis=0, tiled=True)  52.4 us
    ppermute x4, waiting for transfers between devices, shift(): lax.ppermute(values, axis, [(at, (at + step) % count) for at in range(cou...  20.5 us
    all_gather x1, blocking collectives, local(): parts, mine = lax.optimization_barrier((lax.all_gather(parts, 'zh'), mine))  20.1 us
    pallas_call x8, Pallas kernels, call(): pl.pallas_call(body, out_shape=shapes, in_specs=specs, out_specs=[pl.Bloc...  16.4 us
    ppermute x4, starting transfers between devices, shift(): lax.ppermute(values, axis, [(at, (at + step) % count) for at in range(cou...  13.9 us
    all_gather x1, blocking collectives, local(): full = lax.all_gather(pair, 'y', axis=1, tiled=True)  13.9 us
    all_to_all x5, waiting for transfers between devices, trade(): return lax.all_to_all(values, axis, split_axis=0, concat_axis=0, tiled=True)  12.3 us
    ppermute x3, starting transfers between devices, swap(): return lax.ppermute(values, axis, [(0, 1), (1, 0)])  5.86 us
  transfers between devices with their start and end apart: 12, of which 8 were waited for; matrix products, arithmetic and copies ran while one was open for 1% of the time, Pallas kernels for 5%

profile of v7, /device:TPU:6, one launch (start us, length us, event | category | flops | bytes accessed | tf_op | source)
XLA Modules:
  0.0 164.6 jit_solution(7236108225961892634)
XLA Ops:
  0.6 2.6 %shard_map.75 = (bf16[16,2,3072]{2,1,0:T(2,128)(2,1)}, bf16[2,768,384]{2,1,0:T(8,128)(2,1)}) custom-call(bf16[1,6144]{1,0:T(2,128)(2,1)} %tokens.3, bf16[1,6144]{1,0:T(2,128)(2,1)} %cotangent.3, bf16[768,384]{1,0:T(8,128)(2,1)} %w_in.1, bf16[384,768]{1,0:T(8,128)(2,1)} %w_out.1), custom_call_target="tpu_custom_call" | custom-call | bytes 2580480 | tf_op jit(solution)/shard_map/pallas_call | solution.py:43
  3.2 4.9 %collective-permute-start.1 = (bf16[2,768,384]{2,1,0:T(8,128)(2,1)}, bf16[2,768,384]{2,1,0:T(8,128)(2,1)S(1)}, u32[]{:S(2)}, u32[]{:S(2)}) collective-permute-start(bf16[2,768,384]{2,1,0:T(8,128)(2,1)} %get-tuple-element.32.b0), channel_id=1, source_target_pairs={{0,192},{64,0},{128,64},{192,128},{1,193},{65,1},{129,65},{193,129... | collective-permute-start | bytes 3538952 | tf_op jit(solution)/shard_map/ppermute | solution.py:27
  8.2 1.9 %collective-permute-start = (bf16[2,768,384]{2,1,0:T(8,128)(2,1)}, bf16[2,768,384]{2,1,0:T(8,128)(2,1)S(1)}, u32[]{:S(2)}, u32[]{:S(2)}) collective-permute-start(bf16[2,768,384]{2,1,0:T(8,128)(2,1)} %get-tuple-element.32.b0), channel_id=1, source_target_pairs={{0,64},{64,128},{128,192},{192,0},{1,65},{65,129},{129,193},{193,1... | collective-permute-start | bytes 3538952 | tf_op jit(solution)/shard_map/ppermute | solution.py:27
  10.1 15.2 %all-to-all-start = ((bf16[16,2,3072]{2,1,0:T(2,128)(2,1)}), bf16[16,2,3072]{2,1,0:T(2,128)(2,1)S(1)}, u32[]{:S(2)}, u32[]{:S(2)}) async-start(bf16[16,2,3072]{2,1,0:T(2,128)(2,1)} %get-tuple-element.31), calls=%async_computation | async-start | bytes 393216 | tf_op jit(solution)/shard_map/all_to_all | solution.py:31
  25.3 8.4 %collective-permute-done.1.b1 = bf16[2,768,384]{2,1,0:T(8,128)(2,1)S(1)} collective-permute-done((bf16[2,768,384]{2,1,0:T(8,128)(2,1)}, bf16[2,768,384]{2,1,0:T(8,128)(2,1)S(1)}, u32[]{:S(2)}, u32[]{:S(2)}) %collective-permute-start.1) | collective-permute-done | bytes 1179680 | tf_op jit(solution)/shard_map/ppermute | solution.py:27
  33.7 0.9 slice_bitcast_fusion
  34.6 4.3 %collective-permute-done.b3 = bf16[2,768,384]{2,1,0:T(8,128)(2,1)S(1)} collective-permute-done((bf16[2,768,384]{2,1,0:T(8,128)(2,1)}, bf16[2,768,384]{2,1,0:T(8,128)(2,1)S(1)}, u32[]{:S(2)}, u32[]{:S(2)}) %collective-permute-start) | collective-permute-done | bytes 1179680 | tf_op jit(solution)/shard_map/ppermute | solution.py:27
  38.9 0.9 slice_bitcast_fusion.1
  39.8 1.7 %all-to-all-done = bf16[16,2,3072]{2,1,0:T(2,128)(2,1)S(1)} async-done(((bf16[16,2,3072]{2,1,0:T(2,128)(2,1)}), bf16[16,2,3072]{2,1,0:T(2,128)(2,1)S(1)}, u32[]{:S(2)}, u32[]{:S(2)}) %all-to-all-start) | async-done | bytes 196640 | tf_op jit(solution)/shard_map/all_to_all | solution.py:31
  41.5 1.0 broadcast_in_dim.3
  42.5 4.8 %all-to-all-start.1 = ((bf16[4,2,16,3072]{3,2,1,0:T(8,128)(2,1)}), bf16[4,2,16,3072]{3,2,1,0:T(8,128)(2,1)S(1)}, u32[]{:S(2)}, u32[]{:S(2)}) async-start(bf16[4,2,16,3072]{3,2,1,0:T(8,128)(2,1)} %broadcast_in_dim.3), calls=%async_computation.1 | async-start | bytes 1572864 | tf_op jit(solution)/shard_map/all_to_all | solution.py:31
  47.3 2.2 %collective-permute-start.2 = (bf16[768,384]{1,0:T(8,128)(2,1)}, bf16[768,384]{1,0:T(8,128)(2,1)}, u32[]{:S(2)}, u32[]{:S(2)}) collective-permute-start(bf16[768,384]{1,0:T(8,128)(2,1)} %slice_bitcast_fusion.1), channel_id=1, source_target_pairs={{0,64},{64,128},{128,192},{192,0},{1,65},{65,129},{129,193},{193,1... | collective-permute-start | bytes 1769480 | tf_op jit(solution)/shard_map/ppermute | solution.py:27
  49.5 4.8 %collective-permute-start.3 = (bf16[768,384]{1,0:T(8,128)(2,1)}, bf16[768,384]{1,0:T(8,128)(2,1)}, u32[]{:S(2)}, u32[]{:S(2)}) collective-permute-start(bf16[768,384]{1,0:T(8,128)(2,1)} %slice_bitcast_fusion), channel_id=1, source_target_pairs={{0,192},{64,0},{128,64},{192,128},{1,193},{65,1},{129,65},{193,129... | collective-permute-start | bytes 1769480 | tf_op jit(solution)/shard_map/ppermute | solution.py:27
  54.3 0.4 all-to-all-done.1.rows
  54.7 0.1 shard_map.76
  54.8 0.0 copy-start.2
  54.8 0.9 copy-done.2
  55.6 6.6 %collective-permute-done.2.far_in = bf16[768,384]{1,0:T(8,128)(2,1)} collective-permute-done((bf16[768,384]{1,0:T(8,128)(2,1)}, bf16[768,384]{1,0:T(8,128)(2,1)}, u32[]{:S(2)}, u32[]{:S(2)}) %collective-permute-start.2) | collective-permute-done | bytes 589856 | tf_op jit(solution)/shard_map/ppermute | solution.py:27
  62.3 1.2 collective-permute-done.3.far_out
  63.5 1.9 %collective-permute-start.4 = (bf16[4,2,16,3072]{3,2,1,0:T(8,128)(2,1)S(1)}, bf16[4,2,16,3072]{3,2,1,0:T(8,128)(2,1)}, u32[]{:S(2)}, u32[]{:S(2)}) collective-permute-start(bf16[4,2,16,3072]{3,2,1,0:T(8,128)(2,1)S(1)} %all-to-all-done.1.rows), channel_id=1, source_target_pairs={{0,1},{1,0},{2,3},{3,2},{4,5},{5,4},{6,7},{7,6},{8,9},{9,8},{10,11... | collective-permute-start | bytes 2359304 | tf_op jit(solution)/shard_map/ppermute | solution.py:22
  65.4 5.0 %all-to-all-start.2 = ((bf16[4,2,64,768]{3,2,1,0:T(8,128)(2,1)}), bf16[4,2,64,768]{3,2,1,0:T(8,128)(2,1)}, u32[]{:S(2)}, u32[]{:S(2)}) async-start(bf16[4,2,64,768]{3,2,1,0:T(8,128)(2,1)} %copy-done.2), calls=%async_computation.2 | async-start | bytes 1572864 | tf_op jit(solution)/shard_map/all_to_all | solution.py:31
  70.4 0.0 collective-permute-done.4.other
  70.4 0.0 copy-start
  70.4 1.3 copy-done
  71.6 2.8 %shard_map.77 = bf16[2,128,384]{2,1,0:T(8,128)(2,1)S(1)} custom-call(s32[1]{0:T(128)} %bitcast.here, bf16[4,2,16,3072]{3,2,1,0:T(8,128)(2,1)S(1)} %all-to-all-done.1.rows, bf16[4,2,16,3072]{3,2,1,0:T(8,128)(2,1)} %collective-permute-done.4.other, bf16[2,768,384]{2,1,0:T(8,128)(2,1)S(1)} %copy-done, bf16[2,768,384]{2,1,0:T(8,128)(2,1)S(1)} %collective-permute-done.1.b1, ...), custom_call_target="tpu_custom_call" | custom-call | flops 603979776 | bytes 6488068 | tf_op jit(solution)/shard_map/pallas_call | solution.py:43
  74.5 20.1 %all-gather = bf16[4,128,384]{2,1,0:T(8,128)(2,1)S(1)} all-gather(bf16[2,128,384]{2,1,0:T(8,128)(2,1)S(1)} %shard_map.77), channel_id=2, replica_groups=mesh['zh'=2,'y'=4,'zl'=8,'x'=4,'core'=2] {'zh'}, dimensions={0}, use_global_device_ids=true | all-gather | bytes 589824 | tf_op jit(solution)/shard_map/all_gather | solution.py:210
  94.5 0.0 all-to-all-done.2.mine
  94.5 0.0 copy-start.1
  94.5 1.3 copy-done.1
  95.8 2.7 %shard_map.78 = (bf16[2,128,384]{2,1,0:T(8,128)(2,1)S(1)}, f32[2,64,3072]{2,1,0:T(8,128)S(1)}, bf16[2,64,3072]{2,1,0:T(8,128)(2,1)S(1)}) custom-call(s32[1]{0:T(128)} %bitcast.here, bf16[2,2,128,384]{3,2,1,0:T(8,128)(2,1)S(1)} %bitcast.7, bf16[2,768,384]{2,1,0:T(8,128)(2,1)S(1)} %copy-done.1, bf16[2,768,384]{2,1,0:T(8,128)(2,1)S(1)} %collective-permute-done.1.b1, ...), custom_call_target="tpu_custom_call" | custom-call | flops 603979776 | bytes 7667716 | tf_op jit(solution)/shard_map/pallas_call | solution.py:43
  98.5 1.9 %collective-permute-start.5 = (bf16[2,64,3072]{2,1,0:T(8,128)(2,1)S(1)}, bf16[2,64,3072]{2,1,0:T(8,128)(2,1)S(1)}, u32[]{:S(2)}, u32[]{:S(2)}) collective-permute-start(bf16[2,64,3072]{2,1,0:T(8,128)(2,1)S(1)} %get-tuple-element.42), channel_id=1, source_target_pairs={{0,1},{1,0},{2,3},{3,2},{4,5},{5,4},{6,7},{7,6},{8,9},{9,8},{10,11... | collective-permute-start | bytes 2359304 | tf_op jit(solution)/shard_map/ppermute | solution.py:22
  100.4 2.3 %collective-permute-done.5.far = bf16[2,64,3072]{2,1,0:T(8,128)(2,1)S(1)} collective-permute-done((bf16[2,64,3072]{2,1,0:T(8,128)(2,1)S(1)}, bf16[2,64,3072]{2,1,0:T(8,128)(2,1)S(1)}, u32[]{:S(2)}, u32[]{:S(2)}) %collective-permute-start.5) | collective-permute-done | bytes 786464 | tf_op jit(solution)/shard_map/ppermute | solution.py:22
  102.7 1.0 shard_map.79
  103.7 2.0 %collective-permute-start.6 = (bf16[4,2,64,768]{3,2,1,0:T(8,128)(2,1)}, bf16[4,2,64,768]{3,2,1,0:T(8,128)(2,1)S(1)}, u32[]{:S(2)}, u32[]{:S(2)}) collective-permute-start(bf16[4,2,64,768]{3,2,1,0:T(8,128)(2,1)} %all-to-all-done.2.mine), channel_id=1, source_target_pairs={{0,1},{1,0},{2,3},{3,2},{4,5},{5,4},{6,7},{7,6},{8,9},{9,8},{10,11... | collective-permute-start | bytes 2359304 | tf_op jit(solution)/shard_map/ppermute | solution.py:22
  105.7 4.8 %all-to-all-start.3 = ((bf16[4,2,16,3072]{3,2,1,0:T(8,128)(2,1)}), bf16[4,2,16,3072]{3,2,1,0:T(8,128)(2,1)S(1)}, u32[]{:S(2)}, u32[]{:S(2)}) async-start(bf16[4,2,16,3072]{3,2,1,0:T(8,128)(2,1)} %shard_map.79), calls=%async_computation.3 | async-start | bytes 1572864 | tf_op jit(solution)/shard_map/all_to_all | solution.py:31
  110.6 13.9 %all_gather.11.full = bf16[2,512,384]{2,1,0:T(8,128)(2,1)S(1)} all-gather(bf16[2,128,384]{2,1,0:T(8,128)(2,1)S(1)} %get-tuple-element.46), channel_id=1, replica_groups=mesh['zh'=2,'y'=4,'zl'=8,'x'=4,'core'=2] {'y'}, dimensions={1}, use_global_device_ids=true | all-gather | bytes 983040 | tf_op jit(solution)/shard_map/all_gather | solution.py:219
  124.4 0.0 all-to-all-done.3.parts
  124.4 0.0 collective-permute-done.6.theirs
  124.4 1.0 shard_map.80
  125.4 22.6 %all-to-all-start.4 = ((bf16[16,2,3072]{2,1,0:T(2,128)(2,1)}), bf16[16,2,3072]{2,1,0:T(2,128)(2,1)S(1)}, u32[]{:S(2)}, u32[]{:S(2)}) async-start(bf16[16,2,3072]{2,1,0:T(2,128)(2,1)} %shard_map.80), calls=%async_computation.4 | async-start | bytes 393216 | tf_op jit(solution)/shard_map/all_to_all | solution.py:31
  148.0 0.0 copy-start.3
  148.1 0.0 copy-start.4
  148.1 5.1 %shard_map.81 = (f32[768,384]{1,0:T(8,128)}, f32[384,768]{1,0:T(8,128)}) custom-call(bf16[2,512,384]{2,1,0:T(8,128)(2,1)S(1)} %all_gather.11.full, bf16[4,2,64,768]{3,2,1,0:T(8,128)(2,1)} %all-to-all-done.2.mine, bf16[4,2,64,768]{3,2,1,0:T(8,128)(2,1)S(1)} %collective-permute-done.6.theirs), custom_call_target="tpu_custom_call" | custom-call | flops 603979776 | bytes 4718592 | tf_op jit(solution)/shard_map/pallas_call | solution.py:43
  153.2 10.2 %all-to-all-done.4.sums = bf16[16,2,3072]{2,1,0:T(2,128)(2,1)S(1)} async-done(((bf16[16,2,3072]{2,1,0:T(2,128)(2,1)}), bf16[16,2,3072]{2,1,0:T(2,128)(2,1)S(1)}, u32[]{:S(2)}, u32[]{:S(2)}) %all-to-all-start.4) | async-done | bytes 196640 | tf_op jit(solution)/shard_map/all_to_all | solution.py:31
  163.4 0.0 copy-done.3
  163.4 0.0 copy-done.4
  163.4 1.2 shard_map.82
  (1 shorter events, 0.0 us)
Async XLA Ops:
  3.2 30.4 %collective-permute-start.1 = (bf16[2,768,384]{2,1,0:T(8,128)(2,1)}, bf16[2,768,384]{2,1,0:T(8,128)(2,1)S(1)}, u32[]{:S(2)}, u32[]{:S(2)}) collective-permute-start(bf16[2,768,384]{2,1,0:T(8,128)(2,1)} %get-tuple-element.32.b0), channel_id=1, source_target_pairs={{0,192},{64,0},{128,64},{192,128},{1,193},{65,1},{129,65},{193,129... | collective-permute-start | bytes 3538952 | tf_op jit(solution)/shard_map/ppermute | solution.py:27
  8.2 30.7 %collective-permute-start = (bf16[2,768,384]{2,1,0:T(8,128)(2,1)}, bf16[2,768,384]{2,1,0:T(8,128)(2,1)S(1)}, u32[]{:S(2)}, u32[]{:S(2)}) collective-permute-start(bf16[2,768,384]{2,1,0:T(8,128)(2,1)} %get-tuple-element.32.b0), channel_id=1, source_target_pairs={{0,64},{64,128},{128,192},{192,0},{1,65},{65,129},{129,193},{193,1... | collective-permute-start | bytes 3538952 | tf_op jit(solution)/shard_map/ppermute | solution.py:27
  10.1 31.4 %all-to-all-start = ((bf16[16,2,3072]{2,1,0:T(2,128)(2,1)}), bf16[16,2,3072]{2,1,0:T(2,128)(2,1)S(1)}, u32[]{:S(2)}, u32[]{:S(2)}) async-start(bf16[16,2,3072]{2,1,0:T(2,128)(2,1)} %get-tuple-element.31), calls=%async_computation | async-start | bytes 393216 | tf_op jit(solution)/shard_map/all_to_all | solution.py:31
  42.5 12.2 %all-to-all-start.1 = ((bf16[4,2,16,3072]{3,2,1,0:T(8,128)(2,1)}), bf16[4,2,16,3072]{3,2,1,0:T(8,128)(2,1)S(1)}, u32[]{:S(2)}, u32[]{:S(2)}) async-start(bf16[4,2,16,3072]{3,2,1,0:T(8,128)(2,1)} %broadcast_in_dim.3), calls=%async_computation.1 | async-start | bytes 1572864 | tf_op jit(solution)/shard_map/all_to_all | solution.py:31
  47.3 15.0 %collective-permute-start.2 = (bf16[768,384]{1,0:T(8,128)(2,1)}, bf16[768,384]{1,0:T(8,128)(2,1)}, u32[]{:S(2)}, u32[]{:S(2)}) collective-permute-start(bf16[768,384]{1,0:T(8,128)(2,1)} %slice_bitcast_fusion.1), channel_id=1, source_target_pairs={{0,64},{64,128},{128,192},{192,0},{1,65},{65,129},{129,193},{193,1... | collective-permute-start | bytes 1769480 | tf_op jit(solution)/shard_map/ppermute | solution.py:27
  49.5 14.0 %collective-permute-start.3 = (bf16[768,384]{1,0:T(8,128)(2,1)}, bf16[768,384]{1,0:T(8,128)(2,1)}, u32[]{:S(2)}, u32[]{:S(2)}) collective-permute-start(bf16[768,384]{1,0:T(8,128)(2,1)} %slice_bitcast_fusion), channel_id=1, source_target_pairs={{0,192},{64,0},{128,64},{192,128},{1,193},{65,1},{129,65},{193,129... | collective-permute-start | bytes 1769480 | tf_op jit(solution)/shard_map/ppermute | solution.py:27
  54.8 0.9 copy-start.2
  63.5 6.9 %collective-permute-start.4 = (bf16[4,2,16,3072]{3,2,1,0:T(8,128)(2,1)S(1)}, bf16[4,2,16,3072]{3,2,1,0:T(8,128)(2,1)}, u32[]{:S(2)}, u32[]{:S(2)}) collective-permute-start(bf16[4,2,16,3072]{3,2,1,0:T(8,128)(2,1)S(1)} %all-to-all-done.1.rows), channel_id=1, source_target_pairs={{0,1},{1,0},{2,3},{3,2},{4,5},{5,4},{6,7},{7,6},{8,9},{9,8},{10,11... | collective-permute-start | bytes 2359304 | tf_op jit(solution)/shard_map/ppermute | solution.py:22
  65.4 29.2 %all-to-all-start.2 = ((bf16[4,2,64,768]{3,2,1,0:T(8,128)(2,1)}), bf16[4,2,64,768]{3,2,1,0:T(8,128)(2,1)}, u32[]{:S(2)}, u32[]{:S(2)}) async-start(bf16[4,2,64,768]{3,2,1,0:T(8,128)(2,1)} %copy-done.2), calls=%async_computation.2 | async-start | bytes 1572864 | tf_op jit(solution)/shard_map/all_to_all | solution.py:31
  70.4 1.3 copy-start
  94.5 1.3 copy-start.1
  98.5 4.2 %collective-permute-start.5 = (bf16[2,64,3072]{2,1,0:T(8,128)(2,1)S(1)}, bf16[2,64,3072]{2,1,0:T(8,128)(2,1)S(1)}, u32[]{:S(2)}, u32[]{:S(2)}) collective-permute-start(bf16[2,64,3072]{2,1,0:T(8,128)(2,1)S(1)} %get-tuple-element.42), channel_id=1, source_target_pairs={{0,1},{1,0},{2,3},{3,2},{4,5},{5,4},{6,7},{7,6},{8,9},{9,8},{10,11... | collective-permute-start | bytes 2359304 | tf_op jit(solution)/shard_map/ppermute | solution.py:22
  103.7 20.7 %collective-permute-start.6 = (bf16[4,2,64,768]{3,2,1,0:T(8,128)(2,1)}, bf16[4,2,64,768]{3,2,1,0:T(8,128)(2,1)S(1)}, u32[]{:S(2)}, u32[]{:S(2)}) collective-permute-start(bf16[4,2,64,768]{3,2,1,0:T(8,128)(2,1)} %all-to-all-done.2.mine), channel_id=1, source_target_pairs={{0,1},{1,0},{2,3},{3,2},{4,5},{5,4},{6,7},{7,6},{8,9},{9,8},{10,11... | collective-permute-start | bytes 2359304 | tf_op jit(solution)/shard_map/ppermute | solution.py:22
  105.7 18.7 %all-to-all-start.3 = ((bf16[4,2,16,3072]{3,2,1,0:T(8,128)(2,1)}), bf16[4,2,16,3072]{3,2,1,0:T(8,128)(2,1)S(1)}, u32[]{:S(2)}, u32[]{:S(2)}) async-start(bf16[4,2,16,3072]{3,2,1,0:T(8,128)(2,1)} %shard_map.79), calls=%async_computation.3 | async-start | bytes 1572864 | tf_op jit(solution)/shard_map/all_to_all | solution.py:31
  125.4 37.9 %all-to-all-start.4 = ((bf16[16,2,3072]{2,1,0:T(2,128)(2,1)}), bf16[16,2,3072]{2,1,0:T(2,128)(2,1)S(1)}, u32[]{:S(2)}, u32[]{:S(2)}) async-start(bf16[16,2,3072]{2,1,0:T(2,128)(2,1)} %shard_map.80), calls=%async_computation.4 | async-start | bytes 393216 | tf_op jit(solution)/shard_map/all_to_all | solution.py:31
  148.0 15.3 %copy-start.3 = (bf16[1,6144]{1,0:T(2,128)(2,1)S(1)}, bf16[1,6144]{1,0:T(2,128)(2,1)}, u32[]{:S(2)}) copy-start(bf16[1,6144]{1,0:T(2,128)(2,1)} %tokens.3) | copy-start | bytes 36868
  148.1 15.3 %copy-start.4 = (bf16[1,6144]{1,0:T(2,128)(2,1)S(1)}, bf16[1,6144]{1,0:T(2,128)(2,1)}, u32[]{:S(2)}) copy-start(bf16[1,6144]{1,0:T(2,128)(2,1)} %cotangent.3) | copy-start | bytes 36868

commit v8 on v7

--- a/solution.py
+++ b/solution.py
@@ -45,7 +45,7 @@
         out_shape=shapes,
         in_specs=specs,
         out_specs=[pl.BlockSpec(memory_space=pltpu.VMEM) for _ in shapes],
-        compiler_params=pltpu.CompilerParams(vmem_limit_bytes=min(2 * moved + (6 << 20), 40 << 20) if body is not pack_body else None),
+        compiler_params=pltpu.CompilerParams(vmem_limit_bytes=(moved + (4 << 20)) if len(args) < 6 else None),
         cost_estimate=pl.CostEstimate(flops=flops, bytes_accessed=moved, transcendentals=0),
     )(*args)
 
@@ -57,11 +57,7 @@
     return centered * inv_scale, inv_scale
 
 
-def pack_body(tokens, cotangent, w_in, w_out, out, block):
-    hidden = w_in.shape[1]
-    block[0] = w_in[...]
-    block[1, :hidden] = w_out[:, :hidden]
-    block[1, hidden:] = w_out[:, hidden:]
+def pack_body(tokens, cotangent, out):
     features = out.shape[2]
     normed = unit(tokens[...].astype(f32))[0]
     grads = cotangent[...].astype(f32)
@@ -79,20 +75,13 @@
     return jnp.concatenate([ref[at, index, :, cut] for ref in (rows, other) for at in range(X)], axis=0)
 
 
-def hidden_body(here, rows, other, b0, b1, b3, far_in, far_out, out):
-    width, hidden = far_in.shape
+def hidden_body(here, rows, other, i0, i1, i2, i3, o0, o1, o2, o3, out):
+    width = i0.shape[0]
     pre = grad = None
-    for step, (ins, cols) in enumerate(
-        ((b0.at[0], b0.at[1]), (b1.at[0], b1.at[1]), (far_in, far_out), (b3.at[0], b3.at[1]))
-    ):
-        at = place(here[0], step, width)
-        left = line_up(rows, other, 0, pl.ds(at, width))
-        terms = [dot(left, ins[...])]
-        for part in range(width // hidden):
-            cut = pl.ds(pl.multiple_of(at + part * hidden, 128), hidden)
-            right = line_up(rows, other, 1, cut)
-            terms.append(dot(right, cols[part * hidden : (part + 1) * hidden], LAST))
-        one, two = terms[0], sum(terms[1:])
+    for step, (ins, outs) in enumerate(((i0, o0), (i1, o1), (i2, o2), (i3, o3))):
+        at = pl.ds(place(here[0], step, width), width)
+        one = dot(line_up(rows, other, 0, at), ins[...])
+        two = dot(line_up(rows, other, 1, at), outs[...], LAST)
         pre = one if pre is None else pre + one
         grad = two if grad is None else grad + two
     out[0] = pre.astype(bf16)
@@ -107,8 +96,8 @@
             out[step, index] = jnp.concatenate([rows[at, index, :, cut] for at in range(X)], axis=0)
 
 
-def output_body(here, parts, b0, b1, b3, far_in, far_out, pair, keep, give):
-    width, hidden = far_in.shape
+def output_body(here, parts, i0, i1, i2, i3, o0, o1, o2, o3, pair, keep, give):
+    width = i0.shape[0]
     half = keep.shape[1]
     value = parts[0, 0].astype(f32) + parts[1, 0].astype(f32)
     upstream = parts[0, 1].astype(f32) + parts[1, 1].astype(f32)
@@ -120,31 +109,19 @@
     pre_grad = (upstream * slope).astype(bf16)
     pair[0] = act
     pair[1] = pre_grad
-    for step, (ins, cols) in enumerate(
-        ((b0.at[0], b0.at[1]), (b1.at[0], b1.at[1]), (far_in, far_out), (b3.at[0], b3.at[1]))
-    ):
-        at = place(here[0], step, width)
-        term = dot(pre_grad, ins[...], LAST)
-        keep[1, :, pl.ds(at, width)] = term[:half]
-        give[1, :, pl.ds(at, width)] = term[half:].astype(bf16)
-        for part in range(width // hidden):
-            cut = pl.ds(pl.multiple_of(at + part * hidden, 128), hidden)
-            term = dot(act, cols[part * hidden : (part + 1) * hidden])
-            keep[0, :, cut] = term[:half]
-            give[0, :, cut] = term[half:].astype(bf16)
+    for step, (ins, outs) in enumerate(((i0, o0), (i1, o1), (i2, o2), (i3, o3))):
+        at = pl.ds(place(here[0], step, width), width)
+        for index, term in enumerate((dot(act, outs[...]), dot(pre_grad, ins[...], LAST))):
+            keep[index, :, at] = term[:half]
+            give[index, :, at] = term[half:].astype(bf16)
 
 
 def weight_body(full, mine, theirs, grad_w_in, grad_w_out):
-    count = mine.shape[2]
-    ins = outs = None
-    for step in range(Y * CORE):
-        at = slice(step * count, (step + 1) * count)
-        rows = (mine, theirs)[step % CORE].at[step // CORE]
-        one, two = dot(rows[0], full[1, at], FIRST), dot(full[0, at], rows[1], FIRST)
-        ins = one if ins is None else ins + one
-        outs = two if outs is None else outs + two
-    grad_w_in[...] = ins
-    grad_w_out[...] = outs
+    def every(index):
+        return jnp.concatenate([ref[step, index] for step in range(Y) for ref in (mine, theirs)], axis=0)
+
+    grad_w_in[...] = dot(every(0), full[1], FIRST)
+    grad_w_out[...] = dot(full[0], every(1), FIRST)
 
 
 def add_body(keep, far, out):
@@ -189,22 +166,21 @@
     shape = jax.ShapeDtypeStruct
     work = 4 * count * features * hidden
 
-    both, block = call(
-        pack_body,
-        [shape((ZH * ZL, 2, features), bf16), shape((2, width, hidden), bf16)],
-        tokens, cotangent, w_in, w_out,
-    )
-    both, block = lax.optimization_barrier((both, block))
-    below, above = shift(block, "y", 1), shift(block, "y", -1)
-    both, near_in, near_out = lax.optimization_barrier((trade(both, FAR), below[0], above[1]))
+    (both,) = call(pack_body, [shape((ZH * ZL, 2, features), bf16)], tokens, cotangent)
+    both, w_in_sent, w_out_sent = lax.optimization_barrier((both, w_in, w_out))
+    i3, o1 = shift(w_in_sent, "y", 1), shift(w_out_sent, "y", -1)
+    i2, o2 = shift(i3, "y", 1), shift(o1, "y", -1)
+    both, i2, o2, w_in_sent, w_out_sent = lax.optimization_barrier(
+        (trade(both, FAR), i2, o2, w_in_sent, w_out_sent)
+    )
     both = both.transpose(1, 0, 2)
     rows = trade(jnp.broadcast_to(both, (X,) + both.shape), "x")
-    far_in, far_out = shift(near_in, "y", 1), shift(near_out, "y", -1)
+    i1, o3 = shift(w_in_sent, "y", -1), shift(w_out_sent, "y", 1)
     (mine,) = call(split_body, [shape((Y, 2, half, width), bf16)], rows)
-    rows, far_in, far_out, mine = lax.optimization_barrier((rows, far_in, far_out, mine))
+    rows, i1, o3, mine = lax.optimization_barrier((rows, i1, o3, mine))
     other = swap(rows, "core")
     mine = trade(mine, "y")
-    blocks = (block, above, below, far_in, far_out)
+    blocks = (w_in, i1, i2, i3, w_out, o1, o2, o3)
 
     (parts,) = call(hidden_body, [shape((2, count, hidden), bf16)], here, rows, other, *blocks, flops=work)
     parts, mine = lax.optimization_barrier((lax.all_gather(parts, "zh"), mine))

time: 165 us -> 172 us (1.042)
  blocking collectives: 33.9 us -> 39.7 us
  waiting for transfers between devices: 35.1 us -> 39.5 us
  starting transfers between devices: 72.1 us -> 68.2 us
    all_to_all x5, starting transfers between devices: 52.4 us -> 40.6 us  [trade(): return lax.all_to_all(values, axis, split_axis=0, concat_axis=0, tiled=True)]
    all_to_all x5, waiting for transfers between devices: 12.3 us -> 22.7 us  [trade(): return lax.all_to_all(values, axis, split_axis=0, concat_axis=0, tiled=True)]
    ppermute x4 -> x6, starting transfers between devices: 13.9 us -> 21.6 us  [shift(): lax.ppermute(values, axis, [(at, (at + step) % count) for at in range(cou...]
    ppermute x4 -> x6, waiting for transfers between devices: 20.5 us -> 14.3 us  [shift(): lax.ppermute(values, axis, [(at, (at + step) % count) for at in range(cou...]
    all_gather x1, blocking collectives: 20.1 us -> 25.8 us  [local(): parts, mine = lax.optimization_barrier((lax.all_gather(parts, 'zh'), mine))]
    squeeze x2 -> x0, local copies, waits for them, and re-layouts: 1.79 us -> none  [the longest x1 0.9 us: local(): above[1]]
    unnamed x10 -> x32, local copies, waits for them, and re-layouts: 3.43 us -> 4.6 us
  transfers between devices with their start and end apart: 12 -> 14, of which waited for: 8 -> 8; matrix products, arithmetic and copies ran while one was open for 1% -> 0% of each run, Pallas kernels for 5% -> 5%
where the time goes in v8:
time: 172 us; the launch traced here: 171 us
  starting transfers between devices  68.2 us (40%)
  blocking collectives  39.7 us (23%)
  waiting for transfers between devices  39.5 us (23%)
  Pallas kernels  17 us (10%)
  local copies, waits for them, and re-layouts  5.59 us (3%)
    all_to_all x5, starting transfers between devices, trade(): return lax.all_to_all(values, axis, split_axis=0, concat_axis=0, tiled=True)  40.6 us
    all_gather x1, blocking collectives, local(): parts, mine = lax.optimization_barrier((lax.all_gather(parts, 'zh'), mine))  25.8 us
    all_to_all x5, waiting for transfers between devices, trade(): return lax.all_to_all(values, axis, split_axis=0, concat_axis=0, tiled=True)  22.7 us
    ppermute x6, starting transfers between devices, shift(): lax.ppermute(values, axis, [(at, (at + step) % count) for at in range(cou...  21.6 us
    pallas_call x8, Pallas kernels, call(): pl.pallas_call(body, out_shape=shapes, in_specs=specs, out_specs=[pl.Bloc...  17 us
    ppermute x6, waiting for transfers between devices, shift(): lax.ppermute(values, axis, [(at, (at + step) % count) for at in range(cou...  14.3 us
    all_gather x1, blocking collectives, local(): full = lax.all_gather(pair, 'y', axis=1, tiled=True)  13.9 us
    ppermute x3, starting transfers between devices, swap(): return lax.ppermute(values, axis, [(0, 1), (1, 0)])  5.98 us
  transfers between devices with their start and end apart: 14, of which 8 were waited for; matrix products, arithmetic and copies ran while one was open for 0% of the time, Pallas kernels for 5%

profile of v8, /device:TPU:6, one launch (start us, length us, event | category | flops | bytes accessed | tf_op | source)
XLA Modules:
  0.0 170.9 jit_solution(3394936423608820954)
XLA Ops:
  0.6 0.0 copy-start.2
  0.6 0.7 copy-done.2
  1.4 0.0 copy-start.4
  1.4 0.7 copy-done.4
  2.1 1.0 shard_map.75
  3.1 3.5 %collective-permute-start = (bf16[768,384]{1,0:T(8,128)(2,1)}, bf16[768,384]{1,0:T(8,128)(2,1)S(1)}, u32[]{:S(2)}, u32[]{:S(2)}) collective-permute-start(bf16[768,384]{1,0:T(8,128)(2,1)} %i0.3), channel_id=1, source_target_pairs={{0,64},{64,128},{128,192},{192,0},{1,65},{65,129},{129,193},{193,1... | collective-permute-start | bytes 1769480 | tf_op jit(solution)/shard_map/ppermute | solution.py:27
  6.6 3.6 %collective-permute-start.2 = (bf16[384,768]{1,0:T(8,128)(2,1)}, bf16[384,768]{1,0:T(8,128)(2,1)S(1)}, u32[]{:S(2)}, u32[]{:S(2)}) collective-permute-start(bf16[384,768]{1,0:T(8,128)(2,1)} %o0.3), channel_id=1, source_target_pairs={{0,192},{64,0},{128,64},{192,128},{1,193},{65,1},{129,65},{193,129... | collective-permute-start | bytes 1769480 | tf_op jit(solution)/shard_map/ppermute | solution.py:27
  10.2 15.2 %all-to-all-start = ((bf16[16,2,3072]{2,1,0:T(2,128)(2,1)}), bf16[16,2,3072]{2,1,0:T(2,128)(2,1)S(1)}, u32[]{:S(2)}, u32[]{:S(2)}) async-start(bf16[16,2,3072]{2,1,0:T(2,128)(2,1)} %shard_map.75), calls=%async_computation | async-start | bytes 393216 | tf_op jit(solution)/shard_map/all_to_all | solution.py:31
  25.4 0.0 collective-permute-done.i3
  25.4 0.0 copy-start.8
  25.4 2.3 %collective-permute-start.1 = (bf16[768,384]{1,0:T(8,128)(2,1)S(1)}, bf16[768,384]{1,0:T(8,128)(2,1)S(1)}, u32[]{:S(2)}, u32[]{:S(2)}) collective-permute-start(bf16[768,384]{1,0:T(8,128)(2,1)S(1)} %collective-permute-done.i3), channel_id=1, source_target_pairs={{0,64},{64,128},{128,192},{192,0},{1,65},{65,129},{129,193},{193,1... | collective-permute-start | bytes 1769480 | tf_op jit(solution)/shard_map/ppermute | solution.py:27
  27.7 0.0 collective-permute-done.2.o1
  27.7 0.0 copy-start.9
  27.7 4.8 %collective-permute-start.3 = (bf16[384,768]{1,0:T(8,128)(2,1)S(1)}, bf16[384,768]{1,0:T(8,128)(2,1)S(1)}, u32[]{:S(2)}, u32[]{:S(2)}) collective-permute-start(bf16[384,768]{1,0:T(8,128)(2,1)S(1)} %collective-permute-done.2.o1), channel_id=1, source_target_pairs={{0,192},{64,0},{128,64},{192,128},{1,193},{65,1},{129,65},{193,129... | collective-permute-start | bytes 1769480 | tf_op jit(solution)/shard_map/ppermute | solution.py:27
  32.5 8.9 %all-to-all-done = bf16[16,2,3072]{2,1,0:T(2,128)(2,1)S(1)} async-done(((bf16[16,2,3072]{2,1,0:T(2,128)(2,1)}), bf16[16,2,3072]{2,1,0:T(2,128)(2,1)S(1)}, u32[]{:S(2)}, u32[]{:S(2)}) %all-to-all-start) | async-done | bytes 196640 | tf_op jit(solution)/shard_map/all_to_all | solution.py:31
  41.4 1.4 collective-permute-done.1.i2
  42.8 1.2 collective-permute-done.3.o2
  44.0 0.8 copy-done.11
  44.8 0.0 copy-start.6
  44.8 0.0 copy-start.7
  44.9 1.0 broadcast_in_dim.3
  45.8 0.0 copy-done.9
  45.8 0.0 copy-done.10
  45.8 0.0 copy-done.8
  45.8 4.8 %all-to-all-start.1 = ((bf16[4,2,16,3072]{3,2,1,0:T(8,128)(2,1)}), bf16[4,2,16,3072]{3,2,1,0:T(8,128)(2,1)S(1)}, u32[]{:S(2)}, u32[]{:S(2)}) async-start(bf16[4,2,16,3072]{3,2,1,0:T(8,128)(2,1)} %broadcast_in_dim.3), calls=%async_computation.1 | async-start | bytes 1572864 | tf_op jit(solution)/shard_map/all_to_all | solution.py:31
  50.6 0.0 copy-done.6
  50.6 5.6 %collective-permute-start.4 = (bf16[768,384]{1,0:T(8,128)(2,1)S(1)}, bf16[768,384]{1,0:T(8,128)(2,1)S(1)}, u32[]{:S(2)}, u32[]{:S(2)}) collective-permute-start(bf16[768,384]{1,0:T(8,128)(2,1)S(1)} %copy-done.6), channel_id=1, source_target_pairs={{0,192},{64,0},{128,64},{192,128},{1,193},{65,1},{129,65},{193,129... | collective-permute-start | bytes 1769480 | tf_op jit(solution)/shard_map/ppermute | solution.py:27
  56.2 0.0 copy-done.7
  56.2 1.9 %collective-permute-start.5 = (bf16[384,768]{1,0:T(8,128)(2,1)S(1)}, bf16[384,768]{1,0:T(8,128)(2,1)S(1)}, u32[]{:S(2)}, u32[]{:S(2)}) collective-permute-start(bf16[384,768]{1,0:T(8,128)(2,1)S(1)} %copy-done.7), channel_id=1, source_target_pairs={{0,64},{64,128},{128,192},{192,0},{1,65},{65,129},{129,193},{193,1... | collective-permute-start | bytes 1769480 | tf_op jit(solution)/shard_map/ppermute | solution.py:27
  58.1 0.8 all-to-all-done.1.rows
  58.9 1.0 shard_map.76
  59.9 6.3 %collective-permute-done.4.i1 = bf16[768,384]{1,0:T(8,128)(2,1)S(1)} collective-permute-done((bf16[768,384]{1,0:T(8,128)(2,1)S(1)}, bf16[768,384]{1,0:T(8,128)(2,1)S(1)}, u32[]{:S(2)}, u32[]{:S(2)}) %collective-permute-start.4) | collective-permute-done | bytes 589856 | tf_op jit(solution)/shard_map/ppermute | solution.py:27
  66.2 5.3 %collective-permute-done.5.o3 = bf16[384,768]{1,0:T(8,128)(2,1)S(1)} collective-permute-done((bf16[384,768]{1,0:T(8,128)(2,1)S(1)}, bf16[384,768]{1,0:T(8,128)(2,1)S(1)}, u32[]{:S(2)}, u32[]{:S(2)}) %collective-permute-start.5) | collective-permute-done | bytes 589856 | tf_op jit(solution)/shard_map/ppermute | solution.py:27
  71.6 1.9 %collective-permute-start.6 = (bf16[4,2,16,3072]{3,2,1,0:T(8,128)(2,1)S(1)}, bf16[4,2,16,3072]{3,2,1,0:T(8,128)(2,1)S(1)}, u32[]{:S(2)}, u32[]{:S(2)}) collective-permute-start(bf16[4,2,16,3072]{3,2,1,0:T(8,128)(2,1)S(1)} %all-to-all-done.1.rows), channel_id=1, source_target_pairs={{0,1},{1,0},{2,3},{3,2},{4,5},{5,4},{6,7},{7,6},{8,9},{9,8},{10,11... | collective-permute-start | bytes 2359304 | tf_op jit(solution)/shard_map/ppermute | solution.py:22
  73.5 0.0 copy-done.13
  73.5 0.0 copy-done
  73.5 3.5 %all-to-all-start.2 = ((bf16[4,2,64,768]{3,2,1,0:T(8,128)(2,1)}), bf16[4,2,64,768]{3,2,1,0:T(8,128)(2,1)S(1)}, u32[]{:S(2)}, u32[]{:S(2)}) async-start(bf16[4,2,64,768]{3,2,1,0:T(8,128)(2,1)} %shard_map.76), calls=%async_computation.2 | async-start | bytes 1572864 | tf_op jit(solution)/shard_map/all_to_all | solution.py:31
  77.0 0.0 collective-permute-done.6.other
  77.0 0.0 copy-start.14
  77.0 0.0 copy-done.12
  77.1 0.9 copy-done.14
  77.9 4.7 %shard_map.77 = bf16[2,128,384]{2,1,0:T(8,128)(2,1)} custom-call(s32[1]{0:T(128)} %bitcast.here, bf16[4,2,16,3072]{3,2,1,0:T(8,128)(2,1)} %copy-done, bf16[4,2,16,3072]{3,2,1,0:T(8,128)(2,1)} %copy-done.14, bf16[768,384]{1,0:T(8,128)(2,1)} %i0.3, bf16[768,384]{1,0:T(8,128)(2,1)} %copy-done.12, bf16[768,384]{1,0:T(8,128)(2,1)} %copy-done.10, ...), custom_call_target="tpu_custom_call" | custom-call | flops 603979776 | bytes 6488068 | tf_op jit(solution)/shard_map/pallas_call | solution.py:43
  82.6 25.8 %all-gather = bf16[4,128,384]{2,1,0:T(8,128)(2,1)} all-gather(bf16[2,128,384]{2,1,0:T(8,128)(2,1)} %shard_map.77), channel_id=2, replica_groups=mesh['zh'=2,'y'=4,'zl'=8,'x'=4,'core'=2] {'zh'}, dimensions={0}, use_global_device_ids=true | all-gather | bytes 589824 | tf_op jit(solution)/shard_map/all_gather | solution.py:186
  108.4 0.0 all-to-all-done.2.mine
  108.4 5.1 %shard_map.78 = (bf16[2,128,384]{2,1,0:T(8,128)(2,1)}, f32[2,64,3072]{2,1,0:T(8,128)}, bf16[2,64,3072]{2,1,0:T(8,128)(2,1)}) custom-call(s32[1]{0:T(128)} %bitcast.here, bf16[2,2,128,384]{3,2,1,0:T(8,128)(2,1)} %bitcast.3, bf16[768,384]{1,0:T(8,128)(2,1)} %i0.3, bf16[768,384]{1,0:T(8,128)(2,1)} %copy-done.12, bf16[768,384]{1,0:T(8,128)(2,1)} %copy-done.10, ...), custom_call_target="tpu_custom_call" | custom-call | flops 603979776 | bytes 7667716 | tf_op jit(solution)/shard_map/pallas_call | solution.py:43
  113.5 1.9 %collective-permute-start.7 = (bf16[2,64,3072]{2,1,0:T(8,128)(2,1)}, bf16[2,64,3072]{2,1,0:T(8,128)(2,1)S(1)}, u32[]{:S(2)}, u32[]{:S(2)}) collective-permute-start(bf16[2,64,3072]{2,1,0:T(8,128)(2,1)} %get-tuple-element.48), channel_id=1, source_target_pairs={{0,1},{1,0},{2,3},{3,2},{4,5},{5,4},{6,7},{7,6},{8,9},{9,8},{10,11... | collective-permute-start | bytes 2359304 | tf_op jit(solution)/shard_map/ppermute | solution.py:22
  115.4 2.5 %collective-permute-done.7.far = bf16[2,64,3072]{2,1,0:T(8,128)(2,1)S(1)} collective-permute-done((bf16[2,64,3072]{2,1,0:T(8,128)(2,1)}, bf16[2,64,3072]{2,1,0:T(8,128)(2,1)S(1)}, u32[]{:S(2)}, u32[]{:S(2)}) %collective-permute-start.7) | collective-permute-done | bytes 786464 | tf_op jit(solution)/shard_map/ppermute | solution.py:22
  117.9 1.4 copy-done.1
  119.3 1.0 shard_map.79
  120.3 2.2 %collective-permute-start.8 = (bf16[4,2,64,768]{3,2,1,0:T(8,128)(2,1)S(1)}, bf16[4,2,64,768]{3,2,1,0:T(8,128)(2,1)S(1)}, u32[]{:S(2)}, u32[]{:S(2)}) collective-permute-start(bf16[4,2,64,768]{3,2,1,0:T(8,128)(2,1)S(1)} %all-to-all-done.2.mine), channel_id=1, source_target_pairs={{0,1},{1,0},{2,3},{3,2},{4,5},{5,4},{6,7},{7,6},{8,9},{9,8},{10,11... | collective-permute-start | bytes 2359304 | tf_op jit(solution)/shard_map/ppermute | solution.py:22
  122.5 4.8 %all-to-all-start.3 = ((bf16[4,2,16,3072]{3,2,1,0:T(8,128)(2,1)}), bf16[4,2,16,3072]{3,2,1,0:T(8,128)(2,1)S(1)}, u32[]{:S(2)}, u32[]{:S(2)}) async-start(bf16[4,2,16,3072]{3,2,1,0:T(8,128)(2,1)} %shard_map.79), calls=%async_computation.3 | async-start | bytes 1572864 | tf_op jit(solution)/shard_map/all_to_all | solution.py:31
  127.3 0.0 copy-done.15
  127.3 13.9 %all_gather.11.full = bf16[2,512,384]{2,1,0:T(8,128)(2,1)S(1)} all-gather(bf16[2,128,384]{2,1,0:T(8,128)(2,1)S(1)} %copy-done.15), channel_id=1, replica_groups=mesh['zh'=2,'y'=4,'zl'=8,'x'=4,'core'=2] {'y'}, dimensions={1}, use_global_device_ids=true | all-gather | bytes 983040 | tf_op jit(solution)/shard_map/all_gather | solution.py:195
  141.2 0.0 all-to-all-done.3.parts
  141.2 0.0 collective-permute-done.8.theirs
  141.2 1.0 shard_map.80
  142.2 12.3 %all-to-all-start.4 = ((bf16[16,2,3072]{2,1,0:T(2,128)(2,1)}), bf16[16,2,3072]{2,1,0:T(2,128)(2,1)S(1)}, u32[]{:S(2)}, u32[]{:S(2)}) async-start(bf16[16,2,3072]{2,1,0:T(2,128)(2,1)} %shard_map.80), calls=%async_computation.4 | async-start | bytes 393216 | tf_op jit(solution)/shard_map/all_to_all | solution.py:31
  154.5 0.0 copy-start.3
  154.5 0.0 copy-start.5
  154.5 2.1 %shard_map.81 = (f32[768,384]{1,0:T(8,128)}, f32[384,768]{1,0:T(8,128)}) custom-call(bf16[2,512,384]{2,1,0:T(8,128)(2,1)S(1)} %all_gather.11.full, bf16[4,2,64,768]{3,2,1,0:T(8,128)(2,1)S(1)} %all-to-all-done.2.mine, bf16[4,2,64,768]{3,2,1,0:T(8,128)(2,1)S(1)} %collective-permute-done.8.theirs), custom_call_target="tpu_custom_call" | custom-call | flops 603979776 | bytes 4718592 | tf_op jit(solution)/shard_map/pallas_call | solution.py:43
  156.6 13.1 %all-to-all-done.4.sums = bf16[16,2,3072]{2,1,0:T(2,128)(2,1)S(1)} async-done(((bf16[16,2,3072]{2,1,0:T(2,128)(2,1)}), bf16[16,2,3072]{2,1,0:T(2,128)(2,1)S(1)}, u32[]{:S(2)}, u32[]{:S(2)}) %all-to-all-start.4) | async-done | bytes 196640 | tf_op jit(solution)/shard_map/all_to_all | solution.py:31
  169.7 0.0 copy-done.3
  169.7 0.0 copy-done.5
  169.7 1.2 shard_map.82
  (8 shorter events, 0.0 us)
Async XLA Ops:
  0.6 0.7 copy-start.2
  1.4 0.7 copy-start.4
  3.1 22.3 %collective-permute-start = (bf16[768,384]{1,0:T(8,128)(2,1)}, bf16[768,384]{1,0:T(8,128)(2,1)S(1)}, u32[]{:S(2)}, u32[]{:S(2)}) collective-permute-start(bf16[768,384]{1,0:T(8,128)(2,1)} %i0.3), channel_id=1, source_target_pairs={{0,64},{64,128},{128,192},{192,0},{1,65},{65,129},{129,193},{193,1... | collective-permute-start | bytes 1769480 | tf_op jit(solution)/shard_map/ppermute | solution.py:27
  6.6 21.1 %collective-permute-start.2 = (bf16[384,768]{1,0:T(8,128)(2,1)}, bf16[384,768]{1,0:T(8,128)(2,1)S(1)}, u32[]{:S(2)}, u32[]{:S(2)}) collective-permute-start(bf16[384,768]{1,0:T(8,128)(2,1)} %o0.3), channel_id=1, source_target_pairs={{0,192},{64,0},{128,64},{192,128},{1,193},{65,1},{129,65},{193,129... | collective-permute-start | bytes 1769480 | tf_op jit(solution)/shard_map/ppermute | solution.py:27
  10.2 31.2 %all-to-all-start = ((bf16[16,2,3072]{2,1,0:T(2,128)(2,1)}), bf16[16,2,3072]{2,1,0:T(2,128)(2,1)S(1)}, u32[]{:S(2)}, u32[]{:S(2)}) async-start(bf16[16,2,3072]{2,1,0:T(2,128)(2,1)} %shard_map.75), calls=%async_computation | async-start | bytes 393216 | tf_op jit(solution)/shard_map/all_to_all | solution.py:31
  25.4 20.4 %copy-start.8 = (bf16[768,384]{1,0:T(8,128)(2,1)}, bf16[768,384]{1,0:T(8,128)(2,1)S(1)}, u32[]{:S(2)}) copy-start(bf16[768,384]{1,0:T(8,128)(2,1)S(1)} %collective-permute-done.i3) | copy-start | bytes 1769476
  25.4 17.4 %collective-permute-start.1 = (bf16[768,384]{1,0:T(8,128)(2,1)S(1)}, bf16[768,384]{1,0:T(8,128)(2,1)S(1)}, u32[]{:S(2)}, u32[]{:S(2)}) collective-permute-start(bf16[768,384]{1,0:T(8,128)(2,1)S(1)} %collective-permute-done.i3), channel_id=1, source_target_pairs={{0,64},{64,128},{128,192},{192,0},{1,65},{65,129},{129,193},{193,1... | collective-permute-start | bytes 1769480 | tf_op jit(solution)/shard_map/ppermute | solution.py:27
  27.7 18.1 %copy-start.9 = (bf16[384,768]{1,0:T(8,128)(2,1)}, bf16[384,768]{1,0:T(8,128)(2,1)S(1)}, u32[]{:S(2)}) copy-start(bf16[384,768]{1,0:T(8,128)(2,1)S(1)} %collective-permute-done.2.o1) | copy-start | bytes 1769476
  27.7 16.3 %collective-permute-start.3 = (bf16[384,768]{1,0:T(8,128)(2,1)S(1)}, bf16[384,768]{1,0:T(8,128)(2,1)S(1)}, u32[]{:S(2)}, u32[]{:S(2)}) collective-permute-start(bf16[384,768]{1,0:T(8,128)(2,1)S(1)} %collective-permute-done.2.o1), channel_id=1, source_target_pairs={{0,192},{64,0},{128,64},{192,128},{1,193},{65,1},{129,65},{193,129... | collective-permute-start | bytes 1769480 | tf_op jit(solution)/shard_map/ppermute | solution.py:27
  42.8 3.0 %copy-start.10 = (bf16[768,384]{1,0:T(8,128)(2,1)}, bf16[768,384]{1,0:T(8,128)(2,1)S(1)}, u32[]{:S(2)}) copy-start(bf16[768,384]{1,0:T(8,128)(2,1)S(1)} %collective-permute-done.1.i2) | copy-start | bytes 1769476
  44.0 0.8 copy-start.11
  44.8 5.8 %copy-start.6 = (bf16[768,384]{1,0:T(8,128)(2,1)S(1)}, bf16[768,384]{1,0:T(8,128)(2,1)}, u32[]{:S(2)}) copy-start(bf16[768,384]{1,0:T(8,128)(2,1)} %i0.3) | copy-start | bytes 1769476
  44.8 11.4 %copy-start.7 = (bf16[384,768]{1,0:T(8,128)(2,1)S(1)}, bf16[384,768]{1,0:T(8,128)(2,1)}, u32[]{:S(2)}) copy-start(bf16[384,768]{1,0:T(8,128)(2,1)} %o0.3) | copy-start | bytes 1769476
  45.8 13.1 %all-to-all-start.1 = ((bf16[4,2,16,3072]{3,2,1,0:T(8,128)(2,1)}), bf16[4,2,16,3072]{3,2,1,0:T(8,128)(2,1)S(1)}, u32[]{:S(2)}, u32[]{:S(2)}) async-start(bf16[4,2,16,3072]{3,2,1,0:T(8,128)(2,1)} %broadcast_in_dim.3), calls=%async_computation.1 | async-start | bytes 1572864 | tf_op jit(solution)/shard_map/all_to_all | solution.py:31
  50.6 15.6 %collective-permute-start.4 = (bf16[768,384]{1,0:T(8,128)(2,1)S(1)}, bf16[768,384]{1,0:T(8,128)(2,1)S(1)}, u32[]{:S(2)}, u32[]{:S(2)}) collective-permute-start(bf16[768,384]{1,0:T(8,128)(2,1)S(1)} %copy-done.6), channel_id=1, source_target_pairs={{0,192},{64,0},{128,64},{192,128},{1,193},{65,1},{129,65},{193,129... | collective-permute-start | bytes 1769480 | tf_op jit(solution)/shard_map/ppermute | solution.py:27
  56.2 15.4 %collective-permute-start.5 = (bf16[384,768]{1,0:T(8,128)(2,1)S(1)}, bf16[384,768]{1,0:T(8,128)(2,1)S(1)}, u32[]{:S(2)}, u32[]{:S(2)}) collective-permute-start(bf16[384,768]{1,0:T(8,128)(2,1)S(1)} %copy-done.7), channel_id=1, source_target_pairs={{0,64},{64,128},{128,192},{192,0},{1,65},{65,129},{129,193},{193,1... | collective-permute-start | bytes 1769480 | tf_op jit(solution)/shard_map/ppermute | solution.py:27
  58.9 14.6 %copy-start = (bf16[4,2,16,3072]{3,2,1,0:T(8,128)(2,1)}, bf16[4,2,16,3072]{3,2,1,0:T(8,128)(2,1)S(1)}, u32[]{:S(2)}) copy-start(bf16[4,2,16,3072]{3,2,1,0:T(8,128)(2,1)S(1)} %all-to-all-done.1.rows) | copy-start | bytes 2359300
  66.2 10.8 %copy-start.12 = (bf16[768,384]{1,0:T(8,128)(2,1)}, bf16[768,384]{1,0:T(8,128)(2,1)S(1)}, u32[]{:S(2)}) copy-start(bf16[768,384]{1,0:T(8,128)(2,1)S(1)} %collective-permute-done.4.i1) | copy-start | bytes 1769476
  71.6 1.9 %copy-start.13 = (bf16[384,768]{1,0:T(8,128)(2,1)}, bf16[384,768]{1,0:T(8,128)(2,1)S(1)}, u32[]{:S(2)}) copy-start(bf16[384,768]{1,0:T(8,128)(2,1)S(1)} %collective-permute-done.5.o3) | copy-start | bytes 1769476
  71.6 5.5 %collective-permute-start.6 = (bf16[4,2,16,3072]{3,2,1,0:T(8,128)(2,1)S(1)}, bf16[4,2,16,3072]{3,2,1,0:T(8,128)(2,1)S(1)}, u32[]{:S(2)}, u32[]{:S(2)}) collective-permute-start(bf16[4,2,16,3072]{3,2,1,0:T(8,128)(2,1)S(1)} %all-to-all-done.1.rows), channel_id=1, source_target_pairs={{0,1},{1,0},{2,3},{3,2},{4,5},{5,4},{6,7},{7,6},{8,9},{9,8},{10,11... | collective-permute-start | bytes 2359304 | tf_op jit(solution)/shard_map/ppermute | solution.py:22
  73.5 34.9 %all-to-all-start.2 = ((bf16[4,2,64,768]{3,2,1,0:T(8,128)(2,1)}), bf16[4,2,64,768]{3,2,1,0:T(8,128)(2,1)S(1)}, u32[]{:S(2)}, u32[]{:S(2)}) async-start(bf16[4,2,64,768]{3,2,1,0:T(8,128)(2,1)} %shard_map.76), calls=%async_computation.2 | async-start | bytes 1572864 | tf_op jit(solution)/shard_map/all_to_all | solution.py:31
  77.0 0.9 copy-start.14
  113.5 4.4 %collective-permute-start.7 = (bf16[2,64,3072]{2,1,0:T(8,128)(2,1)}, bf16[2,64,3072]{2,1,0:T(8,128)(2,1)S(1)}, u32[]{:S(2)}, u32[]{:S(2)}) collective-permute-start(bf16[2,64,3072]{2,1,0:T(8,128)(2,1)} %get-tuple-element.48), channel_id=1, source_target_pairs={{0,1},{1,0},{2,3},{3,2},{4,5},{5,4},{6,7},{7,6},{8,9},{9,8},{10,11... | collective-permute-start | bytes 2359304 | tf_op jit(solution)/shard_map/ppermute | solution.py:22
  117.9 1.4 copy-start.1
  120.3 7.0 %copy-start.15 = (bf16[2,128,384]{2,1,0:T(8,128)(2,1)S(1)}, bf16[2,128,384]{2,1,0:T(8,128)(2,1)}, u32[]{:S(2)}) copy-start(bf16[2,128,384]{2,1,0:T(8,128)(2,1)} %get-tuple-element.52) | copy-start | bytes 589828
  120.3 20.9 %collective-permute-start.8 = (bf16[4,2,64,768]{3,2,1,0:T(8,128)(2,1)S(1)}, bf16[4,2,64,768]{3,2,1,0:T(8,128)(2,1)S(1)}, u32[]{:S(2)}, u32[]{:S(2)}) collective-permute-start(bf16[4,2,64,768]{3,2,1,0:T(8,128)(2,1)S(1)} %all-to-all-done.2.mine), channel_id=1, source_target_pairs={{0,1},{1,0},{2,3},{3,2},{4,5},{5,4},{6,7},{7,6},{8,9},{9,8},{10,11... | collective-permute-start | bytes 2359304 | tf_op jit(solution)/shard_map/ppermute | solution.py:22
  122.5 18.7 %all-to-all-start.3 = ((bf16[4,2,16,3072]{3,2,1,0:T(8,128)(2,1)}), bf16[4,2,16,3072]{3,2,1,0:T(8,128)(2,1)S(1)}, u32[]{:S(2)}, u32[]{:S(2)}) async-start(bf16[4,2,16,3072]{3,2,1,0:T(8,128)(2,1)} %shard_map.79), calls=%async_computation.3 | async-start | bytes 1572864 | tf_op jit(solution)/shard_map/all_to_all | solution.py:31
  142.2 27.6 %all-to-all-start.4 = ((bf16[16,2,3072]{2,1,0:T(2,128)(2,1)}), bf16[16,2,3072]{2,1,0:T(2,128)(2,1)S(1)}, u32[]{:S(2)}, u32[]{:S(2)}) async-start(bf16[16,2,3072]{2,1,0:T(2,128)(2,1)} %shard_map.80), calls=%async_computation.4 | async-start | bytes 393216 | tf_op jit(solution)/shard_map/all_to_all | solution.py:31
  154.5 15.2 %copy-start.3 = (bf16[1,6144]{1,0:T(2,128)(2,1)S(1)}, bf16[1,6144]{1,0:T(2,128)(2,1)}, u32[]{:S(2)}) copy-start(bf16[1,6144]{1,0:T(2,128)(2,1)} %tokens.3) | copy-start | bytes 36868
  154.5 15.2 %copy-start.5 = (bf16[1,6144]{1,0:T(2,128)(2,1)S(1)}, bf16[1,6144]{1,0:T(2,128)(2,1)}, u32[]{:S(2)}) copy-start(bf16[1,6144]{1,0:T(2,128)(2,1)} %cotangent.3) | copy-start | bytes 36868

commit v9 on v7

--- a/solution.py
+++ b/solution.py
@@ -196,10 +196,9 @@
     )
     both, block = lax.optimization_barrier((both, block))
     below, above = shift(block, "y", 1), shift(block, "y", -1)
-    both, near_in, near_out = lax.optimization_barrier((trade(both, FAR), below[0], above[1]))
-    both = both.transpose(1, 0, 2)
+    both = trade(both, FAR).transpose(1, 0, 2)
     rows = trade(jnp.broadcast_to(both, (X,) + both.shape), "x")
-    far_in, far_out = shift(near_in, "y", 1), shift(near_out, "y", -1)
+    far_in, far_out = shift(below[0], "y", 1), shift(above[1], "y", -1)
     (mine,) = call(split_body, [shape((Y, 2, half, width), bf16)], rows)
     rows, far_in, far_out, mine = lax.optimization_barrier((rows, far_in, far_out, mine))
     other = swap(rows, "core")

time: 165 us -> 163 us (0.988)
  blocking collectives: 33.9 us -> 65 us
  starting transfers between devices: 72.1 us -> 50.5 us
  waiting for transfers between devices: 35.1 us -> 22.8 us
    all_to_all x0 -> x1, blocking collectives: none -> 31.4 us  [trade(): return lax.all_to_all(values, axis, split_axis=0, concat_axis=0, tiled=True)]
    all_to_all x5 -> x4, starting transfers between devices: 52.4 us -> 31 us  [trade(): return lax.all_to_all(values, axis, split_axis=0, concat_axis=0, tiled=True)]
    ppermute x4, waiting for transfers between devices: 20.5 us -> 10.4 us  [shift(): lax.ppermute(values, axis, [(at, (at + step) % count) for at in range(cou...]
    all_to_all x5 -> x4, waiting for transfers between devices: 12.3 us -> 10.1 us  [trade(): return lax.all_to_all(values, axis, split_axis=0, concat_axis=0, tiled=True)]
  transfers between devices with their start and end apart: 12 -> 11, of which waited for: 8 -> 4; matrix products, arithmetic and copies ran while one was open for 1% -> 2% of each run, Pallas kernels for 5% -> 5%
where the time goes in v9:
time: 163 us; the launch traced here: 162 us
  blocking collectives  65 us (40%)
  starting transfers between devices  50.5 us (31%)
  waiting for transfers between devices  22.8 us (14%)
  Pallas kernels  16.5 us (10%)
  local copies, waits for them, and re-layouts  6.21 us (4%)
    all_to_all x1, blocking collectives, trade(): return lax.all_to_all(values, axis, split_axis=0, concat_axis=0, tiled=True)  31.4 us
    all_to_all x4, starting transfers between devices, trade(): return lax.all_to_all(values, axis, split_axis=0, concat_axis=0, tiled=True)  31 us
    all_gather x1, blocking collectives, local(): parts, mine = lax.optimization_barrier((lax.all_gather(parts, 'zh'), mine))  19.7 us
    pallas_call x8, Pallas kernels, call(): pl.pallas_call(body, out_shape=shapes, in_specs=specs, out_specs=[pl.Bloc...  16.5 us
    all_gather x1, blocking collectives, local(): full = lax.all_gather(pair, 'y', axis=1, tiled=True)  13.8 us
    ppermute x4, starting transfers between devices, shift(): lax.ppermute(values, axis, [(at, (at + step) % count) for at in range(cou...  13.6 us
    ppermute x4, waiting for transfers between devices, shift(): lax.ppermute(values, axis, [(at, (at + step) % count) for at in range(cou...  10.4 us
    all_to_all x4, waiting for transfers between devices, trade(): return lax.all_to_all(values, axis, split_axis=0, concat_axis=0, tiled=True)  10.1 us
  transfers between devices with their start and end apart: 11, of which 4 were waited for; matrix products, arithmetic and copies ran while one was open for 2% of the time, Pallas kernels for 5%

profile of v9, /device:TPU:6, one launch (start us, length us, event | category | flops | bytes accessed | tf_op | source)
XLA Modules:
  0.0 161.7 jit_solution(14727860636362959676)
XLA Ops:
  0.6 2.6 %shard_map.75 = (bf16[16,2,3072]{2,1,0:T(2,128)(2,1)}, bf16[2,768,384]{2,1,0:T(8,128)(2,1)}) custom-call(bf16[1,6144]{1,0:T(2,128)(2,1)} %tokens.3, bf16[1,6144]{1,0:T(2,128)(2,1)} %cotangent.3, bf16[768,384]{1,0:T(8,128)(2,1)} %w_in.1, bf16[384,768]{1,0:T(8,128)(2,1)} %w_out.1), custom_call_target="tpu_custom_call" | custom-call | bytes 2580480 | tf_op jit(solution)/shard_map/pallas_call | solution.py:43
  3.2 4.9 %collective-permute-start.2 = (bf16[2,768,384]{2,1,0:T(8,128)(2,1)}, bf16[2,768,384]{2,1,0:T(8,128)(2,1)S(1)}, u32[]{:S(2)}, u32[]{:S(2)}) collective-permute-start(bf16[2,768,384]{2,1,0:T(8,128)(2,1)} %get-tuple-element.29.b0), channel_id=1, source_target_pairs={{0,192},{64,0},{128,64},{192,128},{1,193},{65,1},{129,65},{193,129... | collective-permute-start | bytes 3538952 | tf_op jit(solution)/shard_map/ppermute | solution.py:27
  8.2 1.9 %collective-permute-start = (bf16[2,768,384]{2,1,0:T(8,128)(2,1)}, bf16[2,768,384]{2,1,0:T(8,128)(2,1)S(1)}, u32[]{:S(2)}, u32[]{:S(2)}) collective-permute-start(bf16[2,768,384]{2,1,0:T(8,128)(2,1)} %get-tuple-element.29.b0), channel_id=1, source_target_pairs={{0,64},{64,128},{128,192},{192,0},{1,65},{65,129},{129,193},{193,1... | collective-permute-start | bytes 3538952 | tf_op jit(solution)/shard_map/ppermute | solution.py:27
  10.1 31.4 %all_to_all.25 = bf16[16,2,3072]{2,1,0:T(2,128)(2,1)S(1)} all-to-all(bf16[16,2,3072]{2,1,0:T(2,128)(2,1)} %get-tuple-element.28), channel_id=1, replica_groups=mesh['zh'=2,'y'=4,'zl'=8,'x'=4,'core'=2] {'zh','zl'}, dimensions={0} | all-to-all | bytes 393216 | tf_op jit(solution)/shard_map/all_to_all | solution.py:31
  41.5 1.0 broadcast_in_dim.3
  42.5 4.8 %all-to-all-start.1 = ((bf16[4,2,16,3072]{3,2,1,0:T(8,128)(2,1)}), bf16[4,2,16,3072]{3,2,1,0:T(8,128)(2,1)S(1)}, u32[]{:S(2)}, u32[]{:S(2)}) async-start(bf16[4,2,16,3072]{3,2,1,0:T(8,128)(2,1)} %broadcast_in_dim.3), calls=%async_computation.1 | async-start | bytes 1572864 | tf_op jit(solution)/shard_map/all_to_all | solution.py:31
  47.3 0.0 collective-permute-done.2.b1
  47.3 0.9 slice_bitcast_fusion
  48.2 4.9 %collective-permute-start.3 = (bf16[768,384]{1,0:T(8,128)(2,1)}, bf16[768,384]{1,0:T(8,128)(2,1)}, u32[]{:S(2)}, u32[]{:S(2)}) collective-permute-start(bf16[768,384]{1,0:T(8,128)(2,1)} %slice_bitcast_fusion), channel_id=1, source_target_pairs={{0,192},{64,0},{128,64},{192,128},{1,193},{65,1},{129,65},{193,129... | collective-permute-start | bytes 1769480 | tf_op jit(solution)/shard_map/ppermute | solution.py:27
  53.0 0.0 collective-permute-done.b3
  53.0 0.9 slice_bitcast_fusion.1
  54.0 1.9 %collective-permute-start.1 = (bf16[768,384]{1,0:T(8,128)(2,1)}, bf16[768,384]{1,0:T(8,128)(2,1)}, u32[]{:S(2)}, u32[]{:S(2)}) collective-permute-start(bf16[768,384]{1,0:T(8,128)(2,1)} %slice_bitcast_fusion.1), channel_id=1, source_target_pairs={{0,64},{64,128},{128,192},{192,0},{1,65},{65,129},{129,193},{193,1... | collective-permute-start | bytes 1769480 | tf_op jit(solution)/shard_map/ppermute | solution.py:27
  55.9 0.0 all-to-all-done.1.rows
  55.9 0.1 shard_map.76
  55.9 0.0 copy-start.2
  56.0 0.9 copy-done.2
  56.8 4.1 %collective-permute-done.3.far_out = bf16[768,384]{1,0:T(8,128)(2,1)} collective-permute-done((bf16[768,384]{1,0:T(8,128)(2,1)}, bf16[768,384]{1,0:T(8,128)(2,1)}, u32[]{:S(2)}, u32[]{:S(2)}) %collective-permute-start.3) | collective-permute-done | bytes 589856 | tf_op jit(solution)/shard_map/ppermute | solution.py:27
  60.9 6.3 %collective-permute-done.1.far_in = bf16[768,384]{1,0:T(8,128)(2,1)} collective-permute-done((bf16[768,384]{1,0:T(8,128)(2,1)}, bf16[768,384]{1,0:T(8,128)(2,1)}, u32[]{:S(2)}, u32[]{:S(2)}) %collective-permute-start.1) | collective-permute-done | bytes 589856 | tf_op jit(solution)/shard_map/ppermute | solution.py:27
  67.2 1.9 %collective-permute-start.4 = (bf16[4,2,16,3072]{3,2,1,0:T(8,128)(2,1)S(1)}, bf16[4,2,16,3072]{3,2,1,0:T(8,128)(2,1)}, u32[]{:S(2)}, u32[]{:S(2)}) collective-permute-start(bf16[4,2,16,3072]{3,2,1,0:T(8,128)(2,1)S(1)} %all-to-all-done.1.rows), channel_id=1, source_target_pairs={{0,1},{1,0},{2,3},{3,2},{4,5},{5,4},{6,7},{7,6},{8,9},{9,8},{10,11... | collective-permute-start | bytes 2359304 | tf_op jit(solution)/shard_map/ppermute | solution.py:22
  69.2 4.2 %all-to-all-start.2 = ((bf16[4,2,64,768]{3,2,1,0:T(8,128)(2,1)}), bf16[4,2,64,768]{3,2,1,0:T(8,128)(2,1)}, u32[]{:S(2)}, u32[]{:S(2)}) async-start(bf16[4,2,64,768]{3,2,1,0:T(8,128)(2,1)} %copy-done.2), calls=%async_computation.2 | async-start | bytes 1572864 | tf_op jit(solution)/shard_map/all_to_all | solution.py:31
  73.4 0.0 collective-permute-done.4.other
  73.4 0.0 copy-start
  73.4 1.3 copy-done
  74.7 2.8 %shard_map.77 = bf16[2,128,384]{2,1,0:T(8,128)(2,1)S(1)} custom-call(s32[1]{0:T(128)} %bitcast.here, bf16[4,2,16,3072]{3,2,1,0:T(8,128)(2,1)S(1)} %all-to-all-done.1.rows, bf16[4,2,16,3072]{3,2,1,0:T(8,128)(2,1)} %collective-permute-done.4.other, bf16[2,768,384]{2,1,0:T(8,128)(2,1)S(1)} %copy-done, bf16[2,768,384]{2,1,0:T(8,128)(2,1)S(1)} %collective-permute-done.2.b1, ...), custom_call_target="tpu_custom_call" | custom-call | flops 603979776 | bytes 6488068 | tf_op jit(solution)/shard_map/pallas_call | solution.py:43
  77.5 19.7 %all-gather = bf16[4,128,384]{2,1,0:T(8,128)(2,1)S(1)} all-gather(bf16[2,128,384]{2,1,0:T(8,128)(2,1)S(1)} %shard_map.77), channel_id=2, replica_groups=mesh['zh'=2,'y'=4,'zl'=8,'x'=4,'core'=2] {'zh'}, dimensions={0}, use_global_device_ids=true | all-gather | bytes 589824 | tf_op jit(solution)/shard_map/all_gather | solution.py:209
  97.3 0.0 all-to-all-done.2.mine
  97.3 0.0 copy-start.1
  97.3 1.3 copy-done.1
  98.5 2.7 %shard_map.78 = (bf16[2,128,384]{2,1,0:T(8,128)(2,1)S(1)}, f32[2,64,3072]{2,1,0:T(8,128)S(1)}, bf16[2,64,3072]{2,1,0:T(8,128)(2,1)S(1)}) custom-call(s32[1]{0:T(128)} %bitcast.here, bf16[2,2,128,384]{3,2,1,0:T(8,128)(2,1)S(1)} %bitcast.7, bf16[2,768,384]{2,1,0:T(8,128)(2,1)S(1)} %copy-done.1, bf16[2,768,384]{2,1,0:T(8,128)(2,1)S(1)} %collective-permute-done.2.b1, ...), custom_call_target="tpu_custom_call" | custom-call | flops 603979776 | bytes 7667716 | tf_op jit(solution)/shard_map/pallas_call | solution.py:43
  101.2 1.9 %collective-permute-start.5 = (bf16[2,64,3072]{2,1,0:T(8,128)(2,1)S(1)}, bf16[2,64,3072]{2,1,0:T(8,128)(2,1)S(1)}, u32[]{:S(2)}, u32[]{:S(2)}) collective-permute-start(bf16[2,64,3072]{2,1,0:T(8,128)(2,1)S(1)} %get-tuple-element.36), channel_id=1, source_target_pairs={{0,1},{1,0},{2,3},{3,2},{4,5},{5,4},{6,7},{7,6},{8,9},{9,8},{10,11... | collective-permute-start | bytes 2359304 | tf_op jit(solution)/shard_map/ppermute | solution.py:22
  103.1 2.3 %collective-permute-done.5.far = bf16[2,64,3072]{2,1,0:T(8,128)(2,1)S(1)} collective-permute-done((bf16[2,64,3072]{2,1,0:T(8,128)(2,1)S(1)}, bf16[2,64,3072]{2,1,0:T(8,128)(2,1)S(1)}, u32[]{:S(2)}, u32[]{:S(2)}) %collective-permute-start.5) | collective-permute-done | bytes 786464 | tf_op jit(solution)/shard_map/ppermute | solution.py:22
  105.4 1.0 shard_map.79
  106.4 2.0 %collective-permute-start.6 = (bf16[4,2,64,768]{3,2,1,0:T(8,128)(2,1)}, bf16[4,2,64,768]{3,2,1,0:T(8,128)(2,1)S(1)}, u32[]{:S(2)}, u32[]{:S(2)}) collective-permute-start(bf16[4,2,64,768]{3,2,1,0:T(8,128)(2,1)} %all-to-all-done.2.mine), channel_id=1, source_target_pairs={{0,1},{1,0},{2,3},{3,2},{4,5},{5,4},{6,7},{7,6},{8,9},{9,8},{10,11... | collective-permute-start | bytes 2359304 | tf_op jit(solution)/shard_map/ppermute | solution.py:22
  108.5 4.8 %all-to-all-start.3 = ((bf16[4,2,16,3072]{3,2,1,0:T(8,128)(2,1)}), bf16[4,2,16,3072]{3,2,1,0:T(8,128)(2,1)S(1)}, u32[]{:S(2)}, u32[]{:S(2)}) async-start(bf16[4,2,16,3072]{3,2,1,0:T(8,128)(2,1)} %shard_map.79), calls=%async_computation.3 | async-start | bytes 1572864 | tf_op jit(solution)/shard_map/all_to_all | solution.py:31
  113.3 13.8 %all_gather.11.full = bf16[2,512,384]{2,1,0:T(8,128)(2,1)S(1)} all-gather(bf16[2,128,384]{2,1,0:T(8,128)(2,1)S(1)} %get-tuple-element.40), channel_id=1, replica_groups=mesh['zh'=2,'y'=4,'zl'=8,'x'=4,'core'=2] {'y'}, dimensions={1}, use_global_device_ids=true | all-gather | bytes 983040 | tf_op jit(solution)/shard_map/all_gather | solution.py:218
  127.1 0.0 all-to-all-done.3.parts
  127.1 0.0 collective-permute-done.6.theirs
  127.1 1.0 shard_map.80
  128.1 17.2 %all-to-all-start.4 = ((bf16[16,2,3072]{2,1,0:T(2,128)(2,1)}), bf16[16,2,3072]{2,1,0:T(2,128)(2,1)S(1)}, u32[]{:S(2)}, u32[]{:S(2)}) async-start(bf16[16,2,3072]{2,1,0:T(2,128)(2,1)} %shard_map.80), calls=%async_computation.4 | async-start | bytes 393216 | tf_op jit(solution)/shard_map/all_to_all | solution.py:31
  145.3 0.0 copy-start.3
  145.3 0.0 copy-start.4
  145.4 5.1 %shard_map.81 = (f32[768,384]{1,0:T(8,128)}, f32[384,768]{1,0:T(8,128)}) custom-call(bf16[2,512,384]{2,1,0:T(8,128)(2,1)S(1)} %all_gather.11.full, bf16[4,2,64,768]{3,2,1,0:T(8,128)(2,1)} %all-to-all-done.2.mine, bf16[4,2,64,768]{3,2,1,0:T(8,128)(2,1)S(1)} %collective-permute-done.6.theirs), custom_call_target="tpu_custom_call" | custom-call | flops 603979776 | bytes 4718592 | tf_op jit(solution)/shard_map/pallas_call | solution.py:43
  150.4 10.1 %all-to-all-done.4.sums = bf16[16,2,3072]{2,1,0:T(2,128)(2,1)S(1)} async-done(((bf16[16,2,3072]{2,1,0:T(2,128)(2,1)}), bf16[16,2,3072]{2,1,0:T(2,128)(2,1)S(1)}, u32[]{:S(2)}, u32[]{:S(2)}) %all-to-all-start.4) | async-done | bytes 196640 | tf_op jit(solution)/shard_map/all_to_all | solution.py:31
  160.6 0.0 copy-done.3
  160.6 0.0 copy-done.4
  160.6 1.2 shard_map.82
  (1 shorter events, 0.0 us)
Async XLA Ops:
  3.2 44.0 %collective-permute-start.2 = (bf16[2,768,384]{2,1,0:T(8,128)(2,1)}, bf16[2,768,384]{2,1,0:T(8,128)(2,1)S(1)}, u32[]{:S(2)}, u32[]{:S(2)}) collective-permute-start(bf16[2,768,384]{2,1,0:T(8,128)(2,1)} %get-tuple-element.29.b0), channel_id=1, source_target_pairs={{0,192},{64,0},{128,64},{192,128},{1,193},{65,1},{129,65},{193,129... | collective-permute-start | bytes 3538952 | tf_op jit(solution)/shard_map/ppermute | solution.py:27
  8.2 44.9 %collective-permute-start = (bf16[2,768,384]{2,1,0:T(8,128)(2,1)}, bf16[2,768,384]{2,1,0:T(8,128)(2,1)S(1)}, u32[]{:S(2)}, u32[]{:S(2)}) collective-permute-start(bf16[2,768,384]{2,1,0:T(8,128)(2,1)} %get-tuple-element.29.b0), channel_id=1, source_target_pairs={{0,64},{64,128},{128,192},{192,0},{1,65},{65,129},{129,193},{193,1... | collective-permute-start | bytes 3538952 | tf_op jit(solution)/shard_map/ppermute | solution.py:27
  42.5 13.4 %all-to-all-start.1 = ((bf16[4,2,16,3072]{3,2,1,0:T(8,128)(2,1)}), bf16[4,2,16,3072]{3,2,1,0:T(8,128)(2,1)S(1)}, u32[]{:S(2)}, u32[]{:S(2)}) async-start(bf16[4,2,16,3072]{3,2,1,0:T(8,128)(2,1)} %broadcast_in_dim.3), calls=%async_computation.1 | async-start | bytes 1572864 | tf_op jit(solution)/shard_map/all_to_all | solution.py:31
  48.2 12.7 %collective-permute-start.3 = (bf16[768,384]{1,0:T(8,128)(2,1)}, bf16[768,384]{1,0:T(8,128)(2,1)}, u32[]{:S(2)}, u32[]{:S(2)}) collective-permute-start(bf16[768,384]{1,0:T(8,128)(2,1)} %slice_bitcast_fusion), channel_id=1, source_target_pairs={{0,192},{64,0},{128,64},{192,128},{1,193},{65,1},{129,65},{193,129... | collective-permute-start | bytes 1769480 | tf_op jit(solution)/shard_map/ppermute | solution.py:27
  54.0 13.3 %collective-permute-start.1 = (bf16[768,384]{1,0:T(8,128)(2,1)}, bf16[768,384]{1,0:T(8,128)(2,1)}, u32[]{:S(2)}, u32[]{:S(2)}) collective-permute-start(bf16[768,384]{1,0:T(8,128)(2,1)} %slice_bitcast_fusion.1), channel_id=1, source_target_pairs={{0,64},{64,128},{128,192},{192,0},{1,65},{65,129},{129,193},{193,1... | collective-permute-start | bytes 1769480 | tf_op jit(solution)/shard_map/ppermute | solution.py:27
  55.9 0.9 copy-start.2
  67.2 6.1 %collective-permute-start.4 = (bf16[4,2,16,3072]{3,2,1,0:T(8,128)(2,1)S(1)}, bf16[4,2,16,3072]{3,2,1,0:T(8,128)(2,1)}, u32[]{:S(2)}, u32[]{:S(2)}) collective-permute-start(bf16[4,2,16,3072]{3,2,1,0:T(8,128)(2,1)S(1)} %all-to-all-done.1.rows), channel_id=1, source_target_pairs={{0,1},{1,0},{2,3},{3,2},{4,5},{5,4},{6,7},{7,6},{8,9},{9,8},{10,11... | collective-permute-start | bytes 2359304 | tf_op jit(solution)/shard_map/ppermute | solution.py:22
  69.2 28.1 %all-to-all-start.2 = ((bf16[4,2,64,768]{3,2,1,0:T(8,128)(2,1)}), bf16[4,2,64,768]{3,2,1,0:T(8,128)(2,1)}, u32[]{:S(2)}, u32[]{:S(2)}) async-start(bf16[4,2,64,768]{3,2,1,0:T(8,128)(2,1)} %copy-done.2), calls=%async_computation.2 | async-start | bytes 1572864 | tf_op jit(solution)/shard_map/all_to_all | solution.py:31
  73.4 1.3 copy-start
  97.3 1.3 copy-start.1
  101.2 4.2 %collective-permute-start.5 = (bf16[2,64,3072]{2,1,0:T(8,128)(2,1)S(1)}, bf16[2,64,3072]{2,1,0:T(8,128)(2,1)S(1)}, u32[]{:S(2)}, u32[]{:S(2)}) collective-permute-start(bf16[2,64,3072]{2,1,0:T(8,128)(2,1)S(1)} %get-tuple-element.36), channel_id=1, source_target_pairs={{0,1},{1,0},{2,3},{3,2},{4,5},{5,4},{6,7},{7,6},{8,9},{9,8},{10,11... | collective-permute-start | bytes 2359304 | tf_op jit(solution)/shard_map/ppermute | solution.py:22
  106.4 20.7 %collective-permute-start.6 = (bf16[4,2,64,768]{3,2,1,0:T(8,128)(2,1)}, bf16[4,2,64,768]{3,2,1,0:T(8,128)(2,1)S(1)}, u32[]{:S(2)}, u32[]{:S(2)}) collective-permute-start(bf16[4,2,64,768]{3,2,1,0:T(8,128)(2,1)} %all-to-all-done.2.mine), channel_id=1, source_target_pairs={{0,1},{1,0},{2,3},{3,2},{4,5},{5,4},{6,7},{7,6},{8,9},{9,8},{10,11... | collective-permute-start | bytes 2359304 | tf_op jit(solution)/shard_map/ppermute | solution.py:22
  108.5 18.6 %all-to-all-start.3 = ((bf16[4,2,16,3072]{3,2,1,0:T(8,128)(2,1)}), bf16[4,2,16,3072]{3,2,1,0:T(8,128)(2,1)S(1)}, u32[]{:S(2)}, u32[]{:S(2)}) async-start(bf16[4,2,16,3072]{3,2,1,0:T(8,128)(2,1)} %shard_map.79), calls=%async_computation.3 | async-start | bytes 1572864 | tf_op jit(solution)/shard_map/all_to_all | solution.py:31
  128.1 32.5 %all-to-all-start.4 = ((bf16[16,2,3072]{2,1,0:T(2,128)(2,1)}), bf16[16,2,3072]{2,1,0:T(2,128)(2,1)S(1)}, u32[]{:S(2)}, u32[]{:S(2)}) async-start(bf16[16,2,3072]{2,1,0:T(2,128)(2,1)} %shard_map.80), calls=%async_computation.4 | async-start | bytes 393216 | tf_op jit(solution)/shard_map/all_to_all | solution.py:31
  145.3 15.2 %copy-start.3 = (bf16[1,6144]{1,0:T(2,128)(2,1)S(1)}, bf16[1,6144]{1,0:T(2,128)(2,1)}, u32[]{:S(2)}) copy-start(bf16[1,6144]{1,0:T(2,128)(2,1)} %tokens.3) | copy-start | bytes 36868
  145.3 15.2 %copy-start.4 = (bf16[1,6144]{1,0:T(2,128)(2,1)S(1)}, bf16[1,6144]{1,0:T(2,128)(2,1)}, u32[]{:S(2)}) copy-start(bf16[1,6144]{1,0:T(2,128)(2,1)} %cotangent.3) | copy-start | bytes 36868

commit v10 on v9

--- a/solution.py
+++ b/solution.py
@@ -134,17 +134,15 @@
             give[0, :, cut] = term[half:].astype(bf16)
 
 
-def weight_body(full, mine, theirs, grad_w_in, grad_w_out):
-    count = mine.shape[2]
-    ins = outs = None
-    for step in range(Y * CORE):
-        at = slice(step * count, (step + 1) * count)
-        rows = (mine, theirs)[step % CORE].at[step // CORE]
-        one, two = dot(rows[0], full[1, at], FIRST), dot(full[0, at], rows[1], FIRST)
-        ins = one if ins is None else ins + one
-        outs = two if outs is None else outs + two
-    grad_w_in[...] = ins
-    grad_w_out[...] = outs
+def weight_body(full, mine, first, second, grad_w_in, grad_w_out):
+    def every(index):
+        blocks = [ref.at[step] for ref in (first, second) for step in range(Y // 2)]
+        return jnp.concatenate(
+            [ref[index] for step in range(Y) for ref in (mine.at[step], blocks[step])], axis=0
+        )
+
+    grad_w_in[...] = dot(every(0), full[1], FIRST)
+    grad_w_out[...] = dot(full[0], every(1), FIRST)
 
 
 def add_body(keep, far, out):
@@ -214,16 +212,18 @@
     )
 
     (sums,) = call(add_body, [shape((X, 2, half // X, features), bf16)], keep, swap(give, "core"))
-    sums, pair, mine = lax.optimization_barrier((sums, pair, mine))
+    sums, pair = lax.optimization_barrier((sums, pair))
     full = lax.all_gather(pair, "y", axis=1, tiled=True)
-    sums, full, theirs = lax.optimization_barrier((trade(sums, "x"), full, swap(mine, "core")))
+    sums, full = lax.optimization_barrier((trade(sums, "x"), full))
     (sums,) = call(sum_body, [shape((half // X, 2, features), bf16)], sums)
+    sums, *pieces = lax.optimization_barrier((sums, mine[: Y // 2], mine[Y // 2 :]))
     sums = trade(sums, FAR)
+    theirs = [swap(piece, "core") for piece in pieces]
 
     grad_w_in, grad_w_out = call(
         weight_body,
         [shape((width, hidden), f32), shape((hidden, width), f32)],
-        full, mine, theirs, flops=work,
+        full, mine, *theirs, flops=work,
     )
 
     sums, grad_w_in, grad_w_out = lax.optimization_barrier((sums, grad_w_in, grad_w_out))

time: 163 us -> 162 us (level)
  starting transfers between devices: 50.5 us -> 52.7 us
  waiting for transfers between devices: 22.8 us -> 20.7 us
  Pallas kernels: 16.5 us -> 14.6 us
    all_to_all x4, waiting for transfers between devices: 10.1 us -> 6.74 us  [trade(): return lax.all_to_all(values, axis, split_axis=0, concat_axis=0, tiled=True)]
    ppermute x3 -> x4, starting transfers between devices: 5.86 us -> 8.16 us  [swap(): return lax.ppermute(values, axis, [(0, 1), (1, 0)])]
    pallas_call x8, Pallas kernels: 16.5 us -> 14.6 us  [call(): pl.pallas_call(body, out_shape=shapes, in_specs=specs, out_specs=[pl.Bloc...]
    ppermute x3 -> x4, waiting for transfers between devices: 2.26 us -> 3.57 us  [swap(): return lax.ppermute(values, axis, [(0, 1), (1, 0)])]
  transfers between devices with their start and end apart: 11 -> 12, of which waited for: 4 -> 5; matrix products, arithmetic and copies ran while one was open for 2% -> 2% of each run, Pallas kernels for 5% -> 4%
where the time goes in v10:
time: 162 us; the launch traced here: 161 us
  blocking collectives  65 us (40%)
  starting transfers between devices  52.7 us (33%)
  waiting for transfers between devices  20.7 us (13%)
  Pallas kernels  14.6 us (9%)
  local copies, waits for them, and re-layouts  7.37 us (5%)
    all_to_all x1, blocking collectives, trade(): return lax.all_to_all(values, axis, split_axis=0, concat_axis=0, tiled=True)  31.4 us
    all_to_all x4, starting transfers between devices, trade(): return lax.all_to_all(values, axis, split_axis=0, concat_axis=0, tiled=True)  31 us
    all_gather x1, blocking collectives, local(): parts, mine = lax.optimization_barrier((lax.all_gather(parts, 'zh'), mine))  19.8 us
    pallas_call x8, Pallas kernels, call(): pl.pallas_call(body, out_shape=shapes, in_specs=specs, out_specs=[pl.Bloc...  14.6 us
    all_gather x1, blocking collectives, local(): full = lax.all_gather(pair, 'y', axis=1, tiled=True)  13.8 us
    ppermute x4, starting transfers between devices, shift(): lax.ppermute(values, axis, [(at, (at + step) % count) for at in range(cou...  13.6 us
    ppermute x4, waiting for transfers between devices, shift(): lax.ppermute(values, axis, [(at, (at + step) % count) for at in range(cou...  10.4 us
    ppermute x4, starting transfers between devices, swap(): return lax.ppermute(values, axis, [(0, 1), (1, 0)])  8.16 us
  transfers between devices with their start and end apart: 12, of which 5 were waited for; matrix products, arithmetic and copies ran while one was open for 2% of the time, Pallas kernels for 4%

profile of v10, /device:TPU:6, one launch (start us, length us, event | category | flops | bytes accessed | tf_op | source)
XLA Modules:
  0.0 161.3 jit_solution(11991812207213716415)
XLA Ops:
  0.6 2.6 %shard_map.75 = (bf16[16,2,3072]{2,1,0:T(2,128)(2,1)}, bf16[2,768,384]{2,1,0:T(8,128)(2,1)}) custom-call(bf16[1,6144]{1,0:T(2,128)(2,1)} %tokens.3, bf16[1,6144]{1,0:T(2,128)(2,1)} %cotangent.3, bf16[768,384]{1,0:T(8,128)(2,1)} %w_in.1, bf16[384,768]{1,0:T(8,128)(2,1)} %w_out.1), custom_call_target="tpu_custom_call" | custom-call | bytes 2580480 | tf_op jit(solution)/shard_map/pallas_call | solution.py:43
  3.2 4.9 %collective-permute-start.2 = (bf16[2,768,384]{2,1,0:T(8,128)(2,1)}, bf16[2,768,384]{2,1,0:T(8,128)(2,1)S(1)}, u32[]{:S(2)}, u32[]{:S(2)}) collective-permute-start(bf16[2,768,384]{2,1,0:T(8,128)(2,1)} %get-tuple-element.30.b0), channel_id=1, source_target_pairs={{0,192},{64,0},{128,64},{192,128},{1,193},{65,1},{129,65},{193,129... | collective-permute-start | bytes 3538952 | tf_op jit(solution)/shard_map/ppermute | solution.py:27
  8.2 1.9 %collective-permute-start = (bf16[2,768,384]{2,1,0:T(8,128)(2,1)}, bf16[2,768,384]{2,1,0:T(8,128)(2,1)S(1)}, u32[]{:S(2)}, u32[]{:S(2)}) collective-permute-start(bf16[2,768,384]{2,1,0:T(8,128)(2,1)} %get-tuple-element.30.b0), channel_id=1, source_target_pairs={{0,64},{64,128},{128,192},{192,0},{1,65},{65,129},{129,193},{193,1... | collective-permute-start | bytes 3538952 | tf_op jit(solution)/shard_map/ppermute | solution.py:27
  10.1 31.4 %all_to_all.25 = bf16[16,2,3072]{2,1,0:T(2,128)(2,1)S(1)} all-to-all(bf16[16,2,3072]{2,1,0:T(2,128)(2,1)} %get-tuple-element.29), channel_id=1, replica_groups=mesh['zh'=2,'y'=4,'zl'=8,'x'=4,'core'=2] {'zh','zl'}, dimensions={0} | all-to-all | bytes 393216 | tf_op jit(solution)/shard_map/all_to_all | solution.py:31
  41.5 1.0 broadcast_in_dim.3
  42.5 4.8 %all-to-all-start.1 = ((bf16[4,2,16,3072]{3,2,1,0:T(8,128)(2,1)}), bf16[4,2,16,3072]{3,2,1,0:T(8,128)(2,1)S(1)}, u32[]{:S(2)}, u32[]{:S(2)}) async-start(bf16[4,2,16,3072]{3,2,1,0:T(8,128)(2,1)} %broadcast_in_dim.3), calls=%async_computation.1 | async-start | bytes 1572864 | tf_op jit(solution)/shard_map/all_to_all | solution.py:31
  47.3 0.0 collective-permute-done.2.b1
  47.3 0.9 slice_bitcast_fusion
  48.2 4.9 %collective-permute-start.3 = (bf16[768,384]{1,0:T(8,128)(2,1)}, bf16[768,384]{1,0:T(8,128)(2,1)}, u32[]{:S(2)}, u32[]{:S(2)}) collective-permute-start(bf16[768,384]{1,0:T(8,128)(2,1)} %slice_bitcast_fusion), channel_id=1, source_target_pairs={{0,192},{64,0},{128,64},{192,128},{1,193},{65,1},{129,65},{193,129... | collective-permute-start | bytes 1769480 | tf_op jit(solution)/shard_map/ppermute | solution.py:27
  53.0 0.0 collective-permute-done.b3
  53.1 0.9 slice_bitcast_fusion.1
  53.9 1.9 %collective-permute-start.1 = (bf16[768,384]{1,0:T(8,128)(2,1)}, bf16[768,384]{1,0:T(8,128)(2,1)}, u32[]{:S(2)}, u32[]{:S(2)}) collective-permute-start(bf16[768,384]{1,0:T(8,128)(2,1)} %slice_bitcast_fusion.1), channel_id=1, source_target_pairs={{0,64},{64,128},{128,192},{192,0},{1,65},{65,129},{129,193},{193,1... | collective-permute-start | bytes 1769480 | tf_op jit(solution)/shard_map/ppermute | solution.py:27
  55.9 0.0 all-to-all-done.1.rows
  55.9 0.1 shard_map.76
  55.9 0.0 copy-start.2
  55.9 0.9 copy-done.2
  56.8 4.1 %collective-permute-done.3.far_out = bf16[768,384]{1,0:T(8,128)(2,1)} collective-permute-done((bf16[768,384]{1,0:T(8,128)(2,1)}, bf16[768,384]{1,0:T(8,128)(2,1)}, u32[]{:S(2)}, u32[]{:S(2)}) %collective-permute-start.3) | collective-permute-done | bytes 589856 | tf_op jit(solution)/shard_map/ppermute | solution.py:27
  60.9 6.3 %collective-permute-done.1.far_in = bf16[768,384]{1,0:T(8,128)(2,1)} collective-permute-done((bf16[768,384]{1,0:T(8,128)(2,1)}, bf16[768,384]{1,0:T(8,128)(2,1)}, u32[]{:S(2)}, u32[]{:S(2)}) %collective-permute-start.1) | collective-permute-done | bytes 589856 | tf_op jit(solution)/shard_map/ppermute | solution.py:27
  67.2 1.9 %collective-permute-start.4 = (bf16[4,2,16,3072]{3,2,1,0:T(8,128)(2,1)S(1)}, bf16[4,2,16,3072]{3,2,1,0:T(8,128)(2,1)}, u32[]{:S(2)}, u32[]{:S(2)}) collective-permute-start(bf16[4,2,16,3072]{3,2,1,0:T(8,128)(2,1)S(1)} %all-to-all-done.1.rows), channel_id=1, source_target_pairs={{0,1},{1,0},{2,3},{3,2},{4,5},{5,4},{6,7},{7,6},{8,9},{9,8},{10,11... | collective-permute-start | bytes 2359304 | tf_op jit(solution)/shard_map/ppermute | solution.py:22
  69.2 4.2 %all-to-all-start.2 = ((bf16[4,2,64,768]{3,2,1,0:T(8,128)(2,1)}), bf16[4,2,64,768]{3,2,1,0:T(8,128)(2,1)}, u32[]{:S(2)}, u32[]{:S(2)}) async-start(bf16[4,2,64,768]{3,2,1,0:T(8,128)(2,1)} %copy-done.2), calls=%async_computation.2 | async-start | bytes 1572864 | tf_op jit(solution)/shard_map/all_to_all | solution.py:31
  73.4 0.0 collective-permute-done.4.other
  73.4 0.0 copy-start
  73.4 1.3 copy-done
  74.7 2.8 %shard_map.77 = bf16[2,128,384]{2,1,0:T(8,128)(2,1)S(1)} custom-call(s32[1]{0:T(128)} %bitcast.here, bf16[4,2,16,3072]{3,2,1,0:T(8,128)(2,1)S(1)} %all-to-all-done.1.rows, bf16[4,2,16,3072]{3,2,1,0:T(8,128)(2,1)} %collective-permute-done.4.other, bf16[2,768,384]{2,1,0:T(8,128)(2,1)S(1)} %copy-done, bf16[2,768,384]{2,1,0:T(8,128)(2,1)S(1)} %collective-permute-done.2.b1, ...), custom_call_target="tpu_custom_call" | custom-call | flops 603979776 | bytes 6488068 | tf_op jit(solution)/shard_map/pallas_call | solution.py:43
  77.5 19.8 %all-gather = bf16[4,128,384]{2,1,0:T(8,128)(2,1)S(1)} all-gather(bf16[2,128,384]{2,1,0:T(8,128)(2,1)S(1)} %shard_map.77), channel_id=2, replica_groups=mesh['zh'=2,'y'=4,'zl'=8,'x'=4,'core'=2] {'zh'}, dimensions={0}, use_global_device_ids=true | all-gather | bytes 589824 | tf_op jit(solution)/shard_map/all_gather | solution.py:207
  97.3 0.0 all-to-all-done.2.mine
  97.3 0.0 copy-start.1
  97.3 1.3 copy-done.1
  98.5 2.7 %shard_map.78 = (bf16[2,128,384]{2,1,0:T(8,128)(2,1)S(1)}, f32[2,64,3072]{2,1,0:T(8,128)S(1)}, bf16[2,64,3072]{2,1,0:T(8,128)(2,1)S(1)}) custom-call(s32[1]{0:T(128)} %bitcast.here, bf16[2,2,128,384]{3,2,1,0:T(8,128)(2,1)S(1)} %bitcast.7, bf16[2,768,384]{2,1,0:T(8,128)(2,1)S(1)} %copy-done.1, bf16[2,768,384]{2,1,0:T(8,128)(2,1)S(1)} %collective-permute-done.2.b1, ...), custom_call_target="tpu_custom_call" | custom-call | flops 603979776 | bytes 7667716 | tf_op jit(solution)/shard_map/pallas_call | solution.py:43
  101.2 1.9 %collective-permute-start.5 = (bf16[2,64,3072]{2,1,0:T(8,128)(2,1)S(1)}, bf16[2,64,3072]{2,1,0:T(8,128)(2,1)S(1)}, u32[]{:S(2)}, u32[]{:S(2)}) collective-permute-start(bf16[2,64,3072]{2,1,0:T(8,128)(2,1)S(1)} %get-tuple-element.37), channel_id=1, source_target_pairs={{0,1},{1,0},{2,3},{3,2},{4,5},{5,4},{6,7},{7,6},{8,9},{9,8},{10,11... | collective-permute-start | bytes 2359304 | tf_op jit(solution)/shard_map/ppermute | solution.py:22
  103.1 2.3 %collective-permute-done.5.far = bf16[2,64,3072]{2,1,0:T(8,128)(2,1)S(1)} collective-permute-done((bf16[2,64,3072]{2,1,0:T(8,128)(2,1)S(1)}, bf16[2,64,3072]{2,1,0:T(8,128)(2,1)S(1)}, u32[]{:S(2)}, u32[]{:S(2)}) %collective-permute-start.5) | collective-permute-done | bytes 786464 | tf_op jit(solution)/shard_map/ppermute | solution.py:22
  105.4 1.0 shard_map.79
  106.4 4.8 %all-to-all-start.3 = ((bf16[4,2,16,3072]{3,2,1,0:T(8,128)(2,1)}), bf16[4,2,16,3072]{3,2,1,0:T(8,128)(2,1)S(1)}, u32[]{:S(2)}, u32[]{:S(2)}) async-start(bf16[4,2,16,3072]{3,2,1,0:T(8,128)(2,1)} %shard_map.79), calls=%async_computation.3 | async-start | bytes 1572864 | tf_op jit(solution)/shard_map/all_to_all | solution.py:31
  111.2 1.2 fusion
  112.4 13.8 %all_gather.11.full = bf16[2,512,384]{2,1,0:T(8,128)(2,1)S(1)} all-gather(bf16[2,128,384]{2,1,0:T(8,128)(2,1)S(1)} %get-tuple-element.40), channel_id=1, replica_groups=mesh['zh'=2,'y'=4,'zl'=8,'x'=4,'core'=2] {'y'}, dimensions={1}, use_global_device_ids=true | all-gather | bytes 983040 | tf_op jit(solution)/shard_map/all_gather | solution.py:216
  126.2 0.0 all-to-all-done.3.parts
  126.2 1.0 shard_map.80
  127.2 17.2 %all-to-all-start.4 = ((bf16[16,2,3072]{2,1,0:T(2,128)(2,1)}), bf16[16,2,3072]{2,1,0:T(2,128)(2,1)S(1)}, u32[]{:S(2)}, u32[]{:S(2)}) async-start(bf16[16,2,3072]{2,1,0:T(2,128)(2,1)} %shard_map.80), calls=%async_computation.4 | async-start | bytes 393216 | tf_op jit(solution)/shard_map/all_to_all | solution.py:31
  144.4 0.0 copy-start.3
  144.4 0.0 copy-start.4
  144.5 1.9 %collective-permute-start.6 = (bf16[2,2,64,768]{3,2,1,0:T(8,128)(2,1)S(1)}, bf16[2,2,64,768]{3,2,1,0:T(8,128)(2,1)S(1)}, u32[]{:S(2)}, u32[]{:S(2)}) collective-permute-start(bf16[2,2,64,768]{3,2,1,0:T(8,128)(2,1)S(1)} %get-tuple-element.45), channel_id=1, source_target_pairs={{0,1},{1,0},{2,3},{3,2},{4,5},{5,4},{6,7},{7,6},{8,9},{9,8},{10,11... | collective-permute-start | bytes 1179656 | tf_op jit(solution)/shard_map/ppermute | solution.py:22
  146.4 2.4 %collective-permute-start.7 = (bf16[2,2,64,768]{3,2,1,0:T(8,128)(2,1)S(1)}, bf16[2,2,64,768]{3,2,1,0:T(8,128)(2,1)S(1)}, u32[]{:S(2)}, u32[]{:S(2)}) collective-permute-start(bf16[2,2,64,768]{3,2,1,0:T(8,128)(2,1)S(1)} %get-tuple-element.46), channel_id=1, source_target_pairs={{0,1},{1,0},{2,3},{3,2},{4,5},{5,4},{6,7},{7,6},{8,9},{9,8},{10,11... | collective-permute-start | bytes 1179656 | tf_op jit(solution)/shard_map/ppermute | solution.py:22
  148.8 0.0 collective-permute-done.6.first
  148.8 1.3 collective-permute-done.7.second
  150.1 3.3 %shard_map.81 = (f32[768,384]{1,0:T(8,128)}, f32[384,768]{1,0:T(8,128)}) custom-call(bf16[2,512,384]{2,1,0:T(8,128)(2,1)S(1)} %all_gather.11.full, bf16[4,2,64,768]{3,2,1,0:T(8,128)(2,1)} %all-to-all-done.2.mine, bf16[2,2,64,768]{3,2,1,0:T(8,128)(2,1)S(1)} %collective-permute-done.6.first, bf16[2,2,64,768]{3,2,1,0:T(8,128)(2,1)S(1)} %collective-permute-done.7.second), custom_call_target="tpu_custom_call" | custom-call | flops 603979776 | bytes 4718592 | tf_op jit(solution)/shard_map/pallas_call | solution.py:43
  153.4 6.7 %all-to-all-done.4.sums = bf16[16,2,3072]{2,1,0:T(2,128)(2,1)S(1)} async-done(((bf16[16,2,3072]{2,1,0:T(2,128)(2,1)}), bf16[16,2,3072]{2,1,0:T(2,128)(2,1)S(1)}, u32[]{:S(2)}, u32[]{:S(2)}) %all-to-all-start.4) | async-done | bytes 196640 | tf_op jit(solution)/shard_map/all_to_all | solution.py:31
  160.1 0.0 copy-done.3
  160.1 0.0 copy-done.4
  160.1 1.2 shard_map.82
  (1 shorter events, 0.0 us)
Async XLA Ops:
  3.2 44.0 %collective-permute-start.2 = (bf16[2,768,384]{2,1,0:T(8,128)(2,1)}, bf16[2,768,384]{2,1,0:T(8,128)(2,1)S(1)}, u32[]{:S(2)}, u32[]{:S(2)}) collective-permute-start(bf16[2,768,384]{2,1,0:T(8,128)(2,1)} %get-tuple-element.30.b0), channel_id=1, source_target_pairs={{0,192},{64,0},{128,64},{192,128},{1,193},{65,1},{129,65},{193,129... | collective-permute-start | bytes 3538952 | tf_op jit(solution)/shard_map/ppermute | solution.py:27
  8.2 44.9 %collective-permute-start = (bf16[2,768,384]{2,1,0:T(8,128)(2,1)}, bf16[2,768,384]{2,1,0:T(8,128)(2,1)S(1)}, u32[]{:S(2)}, u32[]{:S(2)}) collective-permute-start(bf16[2,768,384]{2,1,0:T(8,128)(2,1)} %get-tuple-element.30.b0), channel_id=1, source_target_pairs={{0,64},{64,128},{128,192},{192,0},{1,65},{65,129},{129,193},{193,1... | collective-permute-start | bytes 3538952 | tf_op jit(solution)/shard_map/ppermute | solution.py:27
  42.5 13.4 %all-to-all-start.1 = ((bf16[4,2,16,3072]{3,2,1,0:T(8,128)(2,1)}), bf16[4,2,16,3072]{3,2,1,0:T(8,128)(2,1)S(1)}, u32[]{:S(2)}, u32[]{:S(2)}) async-start(bf16[4,2,16,3072]{3,2,1,0:T(8,128)(2,1)} %broadcast_in_dim.3), calls=%async_computation.1 | async-start | bytes 1572864 | tf_op jit(solution)/shard_map/all_to_all | solution.py:31
  48.2 12.7 %collective-permute-start.3 = (bf16[768,384]{1,0:T(8,128)(2,1)}, bf16[768,384]{1,0:T(8,128)(2,1)}, u32[]{:S(2)}, u32[]{:S(2)}) collective-permute-start(bf16[768,384]{1,0:T(8,128)(2,1)} %slice_bitcast_fusion), channel_id=1, source_target_pairs={{0,192},{64,0},{128,64},{192,128},{1,193},{65,1},{129,65},{193,129... | collective-permute-start | bytes 1769480 | tf_op jit(solution)/shard_map/ppermute | solution.py:27
  53.9 13.3 %collective-permute-start.1 = (bf16[768,384]{1,0:T(8,128)(2,1)}, bf16[768,384]{1,0:T(8,128)(2,1)}, u32[]{:S(2)}, u32[]{:S(2)}) collective-permute-start(bf16[768,384]{1,0:T(8,128)(2,1)} %slice_bitcast_fusion.1), channel_id=1, source_target_pairs={{0,64},{64,128},{128,192},{192,0},{1,65},{65,129},{129,193},{193,1... | collective-permute-start | bytes 1769480 | tf_op jit(solution)/shard_map/ppermute | solution.py:27
  55.9 0.9 copy-start.2
  67.2 6.1 %collective-permute-start.4 = (bf16[4,2,16,3072]{3,2,1,0:T(8,128)(2,1)S(1)}, bf16[4,2,16,3072]{3,2,1,0:T(8,128)(2,1)}, u32[]{:S(2)}, u32[]{:S(2)}) collective-permute-start(bf16[4,2,16,3072]{3,2,1,0:T(8,128)(2,1)S(1)} %all-to-all-done.1.rows), channel_id=1, source_target_pairs={{0,1},{1,0},{2,3},{3,2},{4,5},{5,4},{6,7},{7,6},{8,9},{9,8},{10,11... | collective-permute-start | bytes 2359304 | tf_op jit(solution)/shard_map/ppermute | solution.py:22
  69.2 28.1 %all-to-all-start.2 = ((bf16[4,2,64,768]{3,2,1,0:T(8,128)(2,1)}), bf16[4,2,64,768]{3,2,1,0:T(8,128)(2,1)}, u32[]{:S(2)}, u32[]{:S(2)}) async-start(bf16[4,2,64,768]{3,2,1,0:T(8,128)(2,1)} %copy-done.2), calls=%async_computation.2 | async-start | bytes 1572864 | tf_op jit(solution)/shard_map/all_to_all | solution.py:31
  73.4 1.3 copy-start
  97.3 1.3 copy-start.1
  101.2 4.2 %collective-permute-start.5 = (bf16[2,64,3072]{2,1,0:T(8,128)(2,1)S(1)}, bf16[2,64,3072]{2,1,0:T(8,128)(2,1)S(1)}, u32[]{:S(2)}, u32[]{:S(2)}) collective-permute-start(bf16[2,64,3072]{2,1,0:T(8,128)(2,1)S(1)} %get-tuple-element.37), channel_id=1, source_target_pairs={{0,1},{1,0},{2,3},{3,2},{4,5},{5,4},{6,7},{7,6},{8,9},{9,8},{10,11... | collective-permute-start | bytes 2359304 | tf_op jit(solution)/shard_map/ppermute | solution.py:22
  106.4 19.8 %all-to-all-start.3 = ((bf16[4,2,16,3072]{3,2,1,0:T(8,128)(2,1)}), bf16[4,2,16,3072]{3,2,1,0:T(8,128)(2,1)S(1)}, u32[]{:S(2)}, u32[]{:S(2)}) async-start(bf16[4,2,16,3072]{3,2,1,0:T(8,128)(2,1)} %shard_map.79), calls=%async_computation.3 | async-start | bytes 1572864 | tf_op jit(solution)/shard_map/all_to_all | solution.py:31
  127.2 32.9 %all-to-all-start.4 = ((bf16[16,2,3072]{2,1,0:T(2,128)(2,1)}), bf16[16,2,3072]{2,1,0:T(2,128)(2,1)S(1)}, u32[]{:S(2)}, u32[]{:S(2)}) async-start(bf16[16,2,3072]{2,1,0:T(2,128)(2,1)} %shard_map.80), calls=%async_computation.4 | async-start | bytes 393216 | tf_op jit(solution)/shard_map/all_to_all | solution.py:31
  144.4 15.7 %copy-start.3 = (bf16[1,6144]{1,0:T(2,128)(2,1)S(1)}, bf16[1,6144]{1,0:T(2,128)(2,1)}, u32[]{:S(2)}) copy-start(bf16[1,6144]{1,0:T(2,128)(2,1)} %tokens.3) | copy-start | bytes 36868
  144.4 15.7 %copy-start.4 = (bf16[1,6144]{1,0:T(2,128)(2,1)S(1)}, bf16[1,6144]{1,0:T(2,128)(2,1)}, u32[]{:S(2)}) copy-start(bf16[1,6144]{1,0:T(2,128)(2,1)} %cotangent.3) | copy-start | bytes 36868
  144.5 4.3 %collective-permute-start.6 = (bf16[2,2,64,768]{3,2,1,0:T(8,128)(2,1)S(1)}, bf16[2,2,64,768]{3,2,1,0:T(8,128)(2,1)S(1)}, u32[]{:S(2)}, u32[]{:S(2)}) collective-permute-start(bf16[2,2,64,768]{3,2,1,0:T(8,128)(2,1)S(1)} %get-tuple-element.45), channel_id=1, source_target_pairs={{0,1},{1,0},{2,3},{3,2},{4,5},{5,4},{6,7},{7,6},{8,9},{9,8},{10,11... | collective-permute-start | bytes 1179656 | tf_op jit(solution)/shard_map/ppermute | solution.py:22
  146.4 3.7 %collective-permute-start.7 = (bf16[2,2,64,768]{3,2,1,0:T(8,128)(2,1)S(1)}, bf16[2,2,64,768]{3,2,1,0:T(8,128)(2,1)S(1)}, u32[]{:S(2)}, u32[]{:S(2)}) collective-permute-start(bf16[2,2,64,768]{3,2,1,0:T(8,128)(2,1)S(1)} %get-tuple-element.46), channel_id=1, source_target_pairs={{0,1},{1,0},{2,3},{3,2},{4,5},{5,4},{6,7},{7,6},{8,9},{9,8},{10,11... | collective-permute-start | bytes 1179656 | tf_op jit(solution)/shard_map/ppermute | solution.py:22

commit v11 on v10

--- a/solution.py
+++ b/solution.py
@@ -198,9 +198,9 @@
     rows = trade(jnp.broadcast_to(both, (X,) + both.shape), "x")
     far_in, far_out = shift(below[0], "y", 1), shift(above[1], "y", -1)
     (mine,) = call(split_body, [shape((Y, 2, half, width), bf16)], rows)
-    rows, far_in, far_out, mine = lax.optimization_barrier((rows, far_in, far_out, mine))
     other = swap(rows, "core")
     mine = trade(mine, "y")
+    rows, far_in, far_out = lax.optimization_barrier((rows, far_in, far_out))
     blocks = (block, above, below, far_in, far_out)
 
     (parts,) = call(hidden_body, [shape((2, count, hidden), bf16)], here, rows, other, *blocks, flops=work)

time: 162 us -> 160 us (0.988)
  blocking collectives: 65 us -> 36.5 us
  waiting for transfers between devices: 20.7 us -> 38.6 us
  starting transfers between devices: 52.7 us -> 61.6 us
    all_to_all x1 -> x0, blocking collectives: 31.4 us -> none  [trade(): return lax.all_to_all(values, axis, split_axis=0, concat_axis=0, tiled=True)]
    all_to_all x4 -> x5, waiting for transfers between devices: 6.74 us -> 22.9 us  [trade(): return lax.all_to_all(values, axis, split_axis=0, concat_axis=0, tiled=True)]
    all_to_all x4 -> x5, starting transfers between devices: 31 us -> 42 us  [trade(): return lax.all_to_all(values, axis, split_axis=0, concat_axis=0, tiled=True)]
    all_gather x1, blocking collectives: 19.8 us -> 22.3 us  [local(): parts, mine = lax.optimization_barrier((lax.all_gather(parts, 'zh'), mine))]
    ppermute x4, starting transfers between devices: 13.6 us -> 11.4 us  [shift(): lax.ppermute(values, axis, [(at, (at + step) % count) for at in range(cou...]
    ppermute x4, waiting for transfers between devices: 10.4 us -> 12.2 us  [shift(): lax.ppermute(values, axis, [(at, (at + step) % count) for at in range(cou...]
  transfers between devices with their start and end apart: 12 -> 13, of which waited for: 5 -> 6; matrix products, arithmetic and copies ran while one was open for 2% -> 2% of each run, Pallas kernels for 4% -> 4%
where the time goes in v11:
time: 160 us; the launch traced here: 159 us
  starting transfers between devices  61.6 us (38%)
  waiting for transfers between devices  38.6 us (24%)
  blocking collectives  36.5 us (23%)
  Pallas kernels  14.6 us (9%)
  local copies, waits for them, and re-layouts  7.33 us (5%)
    all_to_all x5, starting transfers between devices, trade(): return lax.all_to_all(values, axis, split_axis=0, concat_axis=0, tiled=True)  42 us
    all_to_all x5, waiting for transfers between devices, trade(): return lax.all_to_all(values, axis, split_axis=0, concat_axis=0, tiled=True)  22.9 us
    all_gather x1, blocking collectives, local(): parts, mine = lax.optimization_barrier((lax.all_gather(parts, 'zh'), mine))  22.3 us
    pallas_call x8, Pallas kernels, call(): pl.pallas_call(body, out_shape=shapes, in_specs=specs, out_specs=[pl.Bloc...  14.6 us
    all_gather x1, blocking collectives, local(): full = lax.all_gather(pair, 'y', axis=1, tiled=True)  14.2 us
    ppermute x4, waiting for transfers between devices, shift(): lax.ppermute(values, axis, [(at, (at + step) % count) for at in range(cou...  12.2 us
    ppermute x4, starting transfers between devices, shift(): lax.ppermute(values, axis, [(at, (at + step) % count) for at in range(cou...  11.4 us
    ppermute x4, starting transfers between devices, swap(): return lax.ppermute(values, axis, [(0, 1), (1, 0)])  8.16 us
  transfers between devices with their start and end apart: 13, of which 6 were waited for; matrix products, arithmetic and copies ran while one was open for 2% of the time, Pallas kernels for 4%

profile of v11, /device:TPU:6, one launch (start us, length us, event | category | flops | bytes accessed | tf_op | source)
XLA Modules:
  0.0 159.4 jit_solution(8628517926582773117)
XLA Ops:
  0.6 2.6 %shard_map.75 = (bf16[16,2,3072]{2,1,0:T(2,128)(2,1)}, bf16[2,768,384]{2,1,0:T(8,128)(2,1)}) custom-call(bf16[1,6144]{1,0:T(2,128)(2,1)} %tokens.3, bf16[1,6144]{1,0:T(2,128)(2,1)} %cotangent.3, bf16[768,384]{1,0:T(8,128)(2,1)} %w_in.1, bf16[384,768]{1,0:T(8,128)(2,1)} %w_out.1), custom_call_target="tpu_custom_call" | custom-call | bytes 2580480 | tf_op jit(solution)/shard_map/pallas_call | solution.py:43
  3.2 4.9 %collective-permute-start.2 = (bf16[2,768,384]{2,1,0:T(8,128)(2,1)}, bf16[2,768,384]{2,1,0:T(8,128)(2,1)S(1)}, u32[]{:S(2)}, u32[]{:S(2)}) collective-permute-start(bf16[2,768,384]{2,1,0:T(8,128)(2,1)} %get-tuple-element.29.b0), channel_id=1, source_target_pairs={{0,192},{64,0},{128,64},{192,128},{1,193},{65,1},{129,65},{193,129... | collective-permute-start | bytes 3538952 | tf_op jit(solution)/shard_map/ppermute | solution.py:27
  8.2 15.2 %all-to-all-start = ((bf16[16,2,3072]{2,1,0:T(2,128)(2,1)}), bf16[16,2,3072]{2,1,0:T(2,128)(2,1)S(1)}, u32[]{:S(2)}, u32[]{:S(2)}) async-start(bf16[16,2,3072]{2,1,0:T(2,128)(2,1)} %get-tuple-element.28), calls=%async_computation | async-start | bytes 393216 | tf_op jit(solution)/shard_map/all_to_all | solution.py:31
  23.4 1.9 %collective-permute-start = (bf16[2,768,384]{2,1,0:T(8,128)(2,1)}, bf16[2,768,384]{2,1,0:T(8,128)(2,1)S(1)}, u32[]{:S(2)}, u32[]{:S(2)}) collective-permute-start(bf16[2,768,384]{2,1,0:T(8,128)(2,1)} %get-tuple-element.29.b0), channel_id=1, source_target_pairs={{0,64},{64,128},{128,192},{192,0},{1,65},{65,129},{129,193},{193,1... | collective-permute-start | bytes 3538952 | tf_op jit(solution)/shard_map/ppermute | solution.py:27
  25.3 14.3 %all-to-all-done = bf16[16,2,3072]{2,1,0:T(2,128)(2,1)S(1)} async-done(((bf16[16,2,3072]{2,1,0:T(2,128)(2,1)}), bf16[16,2,3072]{2,1,0:T(2,128)(2,1)S(1)}, u32[]{:S(2)}, u32[]{:S(2)}) %all-to-all-start) | async-done | bytes 196640 | tf_op jit(solution)/shard_map/all_to_all | solution.py:31
  39.6 1.0 broadcast_in_dim.3
  40.6 4.8 %all-to-all-start.1 = ((bf16[4,2,16,3072]{3,2,1,0:T(8,128)(2,1)}), bf16[4,2,16,3072]{3,2,1,0:T(8,128)(2,1)S(1)}, u32[]{:S(2)}, u32[]{:S(2)}) async-start(bf16[4,2,16,3072]{3,2,1,0:T(8,128)(2,1)} %broadcast_in_dim.3), calls=%async_computation.1 | async-start | bytes 1572864 | tf_op jit(solution)/shard_map/all_to_all | solution.py:31
  45.3 0.0 collective-permute-done.2.b1
  45.4 0.9 slice_bitcast_fusion
  46.2 2.6 %collective-permute-start.3 = (bf16[768,384]{1,0:T(8,128)(2,1)}, bf16[768,384]{1,0:T(8,128)(2,1)}, u32[]{:S(2)}, u32[]{:S(2)}) collective-permute-start(bf16[768,384]{1,0:T(8,128)(2,1)} %slice_bitcast_fusion), channel_id=1, source_target_pairs={{0,192},{64,0},{128,64},{192,128},{1,193},{65,1},{129,65},{193,129... | collective-permute-start | bytes 1769480 | tf_op jit(solution)/shard_map/ppermute | solution.py:27
  48.9 3.9 %all-to-all-done.1.rows = bf16[4,2,16,3072]{3,2,1,0:T(8,128)(2,1)S(1)} async-done(((bf16[4,2,16,3072]{3,2,1,0:T(8,128)(2,1)}), bf16[4,2,16,3072]{3,2,1,0:T(8,128)(2,1)S(1)}, u32[]{:S(2)}, u32[]{:S(2)}) %all-to-all-start.1) | async-done | bytes 786464 | tf_op jit(solution)/shard_map/all_to_all | solution.py:31
  52.8 1.9 %collective-permute-start.4 = (bf16[4,2,16,3072]{3,2,1,0:T(8,128)(2,1)S(1)}, bf16[4,2,16,3072]{3,2,1,0:T(8,128)(2,1)}, u32[]{:S(2)}, u32[]{:S(2)}) collective-permute-start(bf16[4,2,16,3072]{3,2,1,0:T(8,128)(2,1)S(1)} %all-to-all-done.1.rows), channel_id=1, source_target_pairs={{0,1},{1,0},{2,3},{3,2},{4,5},{5,4},{6,7},{7,6},{8,9},{9,8},{10,11... | collective-permute-start | bytes 2359304 | tf_op jit(solution)/shard_map/ppermute | solution.py:22
  54.7 0.0 collective-permute-done.b3
  54.7 0.9 slice_bitcast_fusion.1
  55.6 1.9 %collective-permute-start.1 = (bf16[768,384]{1,0:T(8,128)(2,1)}, bf16[768,384]{1,0:T(8,128)(2,1)}, u32[]{:S(2)}, u32[]{:S(2)}) collective-permute-start(bf16[768,384]{1,0:T(8,128)(2,1)} %slice_bitcast_fusion.1), channel_id=1, source_target_pairs={{0,64},{64,128},{128,192},{192,0},{1,65},{65,129},{129,193},{193,1... | collective-permute-start | bytes 1769480 | tf_op jit(solution)/shard_map/ppermute | solution.py:27
  57.5 0.1 shard_map.77
  57.6 0.0 copy-start.2
  57.6 0.9 copy-done.2
  58.4 4.5 %all-to-all-start.2 = ((bf16[4,2,64,768]{3,2,1,0:T(8,128)(2,1)}), bf16[4,2,64,768]{3,2,1,0:T(8,128)(2,1)}, u32[]{:S(2)}, u32[]{:S(2)}) async-start(bf16[4,2,64,768]{3,2,1,0:T(8,128)(2,1)} %copy-done.2), calls=%async_computation.2 | async-start | bytes 1572864 | tf_op jit(solution)/shard_map/all_to_all | solution.py:31
  62.9 0.0 collective-permute-done.3.far_out
  62.9 12.2 %collective-permute-done.1.far_in = bf16[768,384]{1,0:T(8,128)(2,1)} collective-permute-done((bf16[768,384]{1,0:T(8,128)(2,1)}, bf16[768,384]{1,0:T(8,128)(2,1)}, u32[]{:S(2)}, u32[]{:S(2)}) %collective-permute-start.1) | collective-permute-done | bytes 589856 | tf_op jit(solution)/shard_map/ppermute | solution.py:27
  75.1 0.0 collective-permute-done.4.other
  75.1 0.0 copy-start
  75.1 1.3 copy-done
  76.4 2.8 %shard_map.76 = bf16[2,128,384]{2,1,0:T(8,128)(2,1)S(1)} custom-call(s32[1]{0:T(128)} %bitcast.here, bf16[4,2,16,3072]{3,2,1,0:T(8,128)(2,1)S(1)} %all-to-all-done.1.rows, bf16[4,2,16,3072]{3,2,1,0:T(8,128)(2,1)} %collective-permute-done.4.other, bf16[2,768,384]{2,1,0:T(8,128)(2,1)S(1)} %copy-done, bf16[2,768,384]{2,1,0:T(8,128)(2,1)S(1)} %collective-permute-done.2.b1, ...), custom_call_target="tpu_custom_call" | custom-call | flops 603979776 | bytes 6488068 | tf_op jit(solution)/shard_map/pallas_call | solution.py:43
  79.2 22.3 %all-gather = bf16[4,128,384]{2,1,0:T(8,128)(2,1)S(1)} all-gather(bf16[2,128,384]{2,1,0:T(8,128)(2,1)S(1)} %shard_map.76), channel_id=2, replica_groups=mesh['zh'=2,'y'=4,'zl'=8,'x'=4,'core'=2] {'zh'}, dimensions={0}, use_global_device_ids=true | all-gather | bytes 589824 | tf_op jit(solution)/shard_map/all_gather | solution.py:207
  101.5 0.0 all-to-all-done.2.mine
  101.5 0.0 copy-start.1
  101.5 1.3 copy-done.1
  102.8 2.7 %shard_map.78 = (bf16[2,128,384]{2,1,0:T(8,128)(2,1)S(1)}, f32[2,64,3072]{2,1,0:T(8,128)S(1)}, bf16[2,64,3072]{2,1,0:T(8,128)(2,1)S(1)}) custom-call(s32[1]{0:T(128)} %bitcast.here, bf16[2,2,128,384]{3,2,1,0:T(8,128)(2,1)S(1)} %bitcast.7, bf16[2,768,384]{2,1,0:T(8,128)(2,1)S(1)} %copy-done.1, bf16[2,768,384]{2,1,0:T(8,128)(2,1)S(1)} %collective-permute-done.2.b1, ...), custom_call_target="tpu_custom_call" | custom-call | flops 603979776 | bytes 7667716 | tf_op jit(solution)/shard_map/pallas_call | solution.py:43
  105.5 1.9 %collective-permute-start.5 = (bf16[2,64,3072]{2,1,0:T(8,128)(2,1)S(1)}, bf16[2,64,3072]{2,1,0:T(8,128)(2,1)S(1)}, u32[]{:S(2)}, u32[]{:S(2)}) collective-permute-start(bf16[2,64,3072]{2,1,0:T(8,128)(2,1)S(1)} %get-tuple-element.35), channel_id=1, source_target_pairs={{0,1},{1,0},{2,3},{3,2},{4,5},{5,4},{6,7},{7,6},{8,9},{9,8},{10,11... | collective-permute-start | bytes 2359304 | tf_op jit(solution)/shard_map/ppermute | solution.py:22
  107.4 2.3 %collective-permute-done.5.far = bf16[2,64,3072]{2,1,0:T(8,128)(2,1)S(1)} collective-permute-done((bf16[2,64,3072]{2,1,0:T(8,128)(2,1)S(1)}, bf16[2,64,3072]{2,1,0:T(8,128)(2,1)S(1)}, u32[]{:S(2)}, u32[]{:S(2)}) %collective-permute-start.5) | collective-permute-done | bytes 786464 | tf_op jit(solution)/shard_map/ppermute | solution.py:22
  109.6 1.0 shard_map.79
  110.7 9.9 %all-to-all-start.3 = ((bf16[4,2,16,3072]{3,2,1,0:T(8,128)(2,1)}), bf16[4,2,16,3072]{3,2,1,0:T(8,128)(2,1)S(1)}, u32[]{:S(2)}, u32[]{:S(2)}) async-start(bf16[4,2,16,3072]{3,2,1,0:T(8,128)(2,1)} %shard_map.79), calls=%async_computation.3 | async-start | bytes 1572864 | tf_op jit(solution)/shard_map/all_to_all | solution.py:31
  120.5 1.2 fusion
  121.7 14.2 %all_gather.11.full = bf16[2,512,384]{2,1,0:T(8,128)(2,1)S(1)} all-gather(bf16[2,128,384]{2,1,0:T(8,128)(2,1)S(1)} %get-tuple-element.38), channel_id=1, replica_groups=mesh['zh'=2,'y'=4,'zl'=8,'x'=4,'core'=2] {'y'}, dimensions={1}, use_global_device_ids=true | all-gather | bytes 983040 | tf_op jit(solution)/shard_map/all_gather | solution.py:216
  135.9 0.0 all-to-all-done.3.parts
  135.9 1.0 shard_map.80
  136.9 7.7 %all-to-all-start.4 = ((bf16[16,2,3072]{2,1,0:T(2,128)(2,1)}), bf16[16,2,3072]{2,1,0:T(2,128)(2,1)S(1)}, u32[]{:S(2)}, u32[]{:S(2)}) async-start(bf16[16,2,3072]{2,1,0:T(2,128)(2,1)} %shard_map.80), calls=%async_computation.4 | async-start | bytes 393216 | tf_op jit(solution)/shard_map/all_to_all | solution.py:31
  144.6 0.0 copy-start.3
  144.6 0.0 copy-start.4
  144.7 1.9 %collective-permute-start.6 = (bf16[2,2,64,768]{3,2,1,0:T(8,128)(2,1)S(1)}, bf16[2,2,64,768]{3,2,1,0:T(8,128)(2,1)S(1)}, u32[]{:S(2)}, u32[]{:S(2)}) collective-permute-start(bf16[2,2,64,768]{3,2,1,0:T(8,128)(2,1)S(1)} %get-tuple-element.43), channel_id=1, source_target_pairs={{0,1},{1,0},{2,3},{3,2},{4,5},{5,4},{6,7},{7,6},{8,9},{9,8},{10,11... | collective-permute-start | bytes 1179656 | tf_op jit(solution)/shard_map/ppermute | solution.py:22
  146.6 2.4 %collective-permute-start.7 = (bf16[2,2,64,768]{3,2,1,0:T(8,128)(2,1)S(1)}, bf16[2,2,64,768]{3,2,1,0:T(8,128)(2,1)S(1)}, u32[]{:S(2)}, u32[]{:S(2)}) collective-permute-start(bf16[2,2,64,768]{3,2,1,0:T(8,128)(2,1)S(1)} %get-tuple-element.44), channel_id=1, source_target_pairs={{0,1},{1,0},{2,3},{3,2},{4,5},{5,4},{6,7},{7,6},{8,9},{9,8},{10,11... | collective-permute-start | bytes 1179656 | tf_op jit(solution)/shard_map/ppermute | solution.py:22
  149.0 0.0 collective-permute-done.6.first
  149.0 1.3 collective-permute-done.7.second
  150.3 3.3 %shard_map.81 = (f32[768,384]{1,0:T(8,128)}, f32[384,768]{1,0:T(8,128)}) custom-call(bf16[2,512,384]{2,1,0:T(8,128)(2,1)S(1)} %all_gather.11.full, bf16[4,2,64,768]{3,2,1,0:T(8,128)(2,1)} %all-to-all-done.2.mine, bf16[2,2,64,768]{3,2,1,0:T(8,128)(2,1)S(1)} %collective-permute-done.6.first, bf16[2,2,64,768]{3,2,1,0:T(8,128)(2,1)S(1)} %collective-permute-done.7.second), custom_call_target="tpu_custom_call" | custom-call | flops 603979776 | bytes 4718592 | tf_op jit(solution)/shard_map/pallas_call | solution.py:43
  153.6 4.7 %all-to-all-done.4.sums = bf16[16,2,3072]{2,1,0:T(2,128)(2,1)S(1)} async-done(((bf16[16,2,3072]{2,1,0:T(2,128)(2,1)}), bf16[16,2,3072]{2,1,0:T(2,128)(2,1)S(1)}, u32[]{:S(2)}, u32[]{:S(2)}) %all-to-all-start.4) | async-done | bytes 196640 | tf_op jit(solution)/shard_map/all_to_all | solution.py:31
  158.2 0.0 copy-done.3
  158.2 0.0 copy-done.4
  158.3 1.2 shard_map.82
  (1 shorter events, 0.0 us)
Async XLA Ops:
  3.2 42.1 %collective-permute-start.2 = (bf16[2,768,384]{2,1,0:T(8,128)(2,1)}, bf16[2,768,384]{2,1,0:T(8,128)(2,1)S(1)}, u32[]{:S(2)}, u32[]{:S(2)}) collective-permute-start(bf16[2,768,384]{2,1,0:T(8,128)(2,1)} %get-tuple-element.29.b0), channel_id=1, source_target_pairs={{0,192},{64,0},{128,64},{192,128},{1,193},{65,1},{129,65},{193,129... | collective-permute-start | bytes 3538952 | tf_op jit(solution)/shard_map/ppermute | solution.py:27
  8.2 31.4 %all-to-all-start = ((bf16[16,2,3072]{2,1,0:T(2,128)(2,1)}), bf16[16,2,3072]{2,1,0:T(2,128)(2,1)S(1)}, u32[]{:S(2)}, u32[]{:S(2)}) async-start(bf16[16,2,3072]{2,1,0:T(2,128)(2,1)} %get-tuple-element.28), calls=%async_computation | async-start | bytes 393216 | tf_op jit(solution)/shard_map/all_to_all | solution.py:31
  23.4 31.3 %collective-permute-start = (bf16[2,768,384]{2,1,0:T(8,128)(2,1)}, bf16[2,768,384]{2,1,0:T(8,128)(2,1)S(1)}, u32[]{:S(2)}, u32[]{:S(2)}) collective-permute-start(bf16[2,768,384]{2,1,0:T(8,128)(2,1)} %get-tuple-element.29.b0), channel_id=1, source_target_pairs={{0,64},{64,128},{128,192},{192,0},{1,65},{65,129},{129,193},{193,1... | collective-permute-start | bytes 3538952 | tf_op jit(solution)/shard_map/ppermute | solution.py:27
  40.6 12.2 %all-to-all-start.1 = ((bf16[4,2,16,3072]{3,2,1,0:T(8,128)(2,1)}), bf16[4,2,16,3072]{3,2,1,0:T(8,128)(2,1)S(1)}, u32[]{:S(2)}, u32[]{:S(2)}) async-start(bf16[4,2,16,3072]{3,2,1,0:T(8,128)(2,1)} %broadcast_in_dim.3), calls=%async_computation.1 | async-start | bytes 1572864 | tf_op jit(solution)/shard_map/all_to_all | solution.py:31
  46.2 16.7 %collective-permute-start.3 = (bf16[768,384]{1,0:T(8,128)(2,1)}, bf16[768,384]{1,0:T(8,128)(2,1)}, u32[]{:S(2)}, u32[]{:S(2)}) collective-permute-start(bf16[768,384]{1,0:T(8,128)(2,1)} %slice_bitcast_fusion), channel_id=1, source_target_pairs={{0,192},{64,0},{128,64},{192,128},{1,193},{65,1},{129,65},{193,129... | collective-permute-start | bytes 1769480 | tf_op jit(solution)/shard_map/ppermute | solution.py:27
  52.8 22.3 %collective-permute-start.4 = (bf16[4,2,16,3072]{3,2,1,0:T(8,128)(2,1)S(1)}, bf16[4,2,16,3072]{3,2,1,0:T(8,128)(2,1)}, u32[]{:S(2)}, u32[]{:S(2)}) collective-permute-start(bf16[4,2,16,3072]{3,2,1,0:T(8,128)(2,1)S(1)} %all-to-all-done.1.rows), channel_id=1, source_target_pairs={{0,1},{1,0},{2,3},{3,2},{4,5},{5,4},{6,7},{7,6},{8,9},{9,8},{10,11... | collective-permute-start | bytes 2359304 | tf_op jit(solution)/shard_map/ppermute | solution.py:22
  55.6 19.5 %collective-permute-start.1 = (bf16[768,384]{1,0:T(8,128)(2,1)}, bf16[768,384]{1,0:T(8,128)(2,1)}, u32[]{:S(2)}, u32[]{:S(2)}) collective-permute-start(bf16[768,384]{1,0:T(8,128)(2,1)} %slice_bitcast_fusion.1), channel_id=1, source_target_pairs={{0,64},{64,128},{128,192},{192,0},{1,65},{65,129},{129,193},{193,1... | collective-permute-start | bytes 1769480 | tf_op jit(solution)/shard_map/ppermute | solution.py:27
  57.6 0.9 copy-start.2
  58.4 43.1 %all-to-all-start.2 = ((bf16[4,2,64,768]{3,2,1,0:T(8,128)(2,1)}), bf16[4,2,64,768]{3,2,1,0:T(8,128)(2,1)}, u32[]{:S(2)}, u32[]{:S(2)}) async-start(bf16[4,2,64,768]{3,2,1,0:T(8,128)(2,1)} %copy-done.2), calls=%async_computation.2 | async-start | bytes 1572864 | tf_op jit(solution)/shard_map/all_to_all | solution.py:31
  75.1 1.3 copy-start
  101.5 1.3 copy-start.1
  105.5 4.2 %collective-permute-start.5 = (bf16[2,64,3072]{2,1,0:T(8,128)(2,1)S(1)}, bf16[2,64,3072]{2,1,0:T(8,128)(2,1)S(1)}, u32[]{:S(2)}, u32[]{:S(2)}) collective-permute-start(bf16[2,64,3072]{2,1,0:T(8,128)(2,1)S(1)} %get-tuple-element.35), channel_id=1, source_target_pairs={{0,1},{1,0},{2,3},{3,2},{4,5},{5,4},{6,7},{7,6},{8,9},{9,8},{10,11... | collective-permute-start | bytes 2359304 | tf_op jit(solution)/shard_map/ppermute | solution.py:22
  110.7 25.3 %all-to-all-start.3 = ((bf16[4,2,16,3072]{3,2,1,0:T(8,128)(2,1)}), bf16[4,2,16,3072]{3,2,1,0:T(8,128)(2,1)S(1)}, u32[]{:S(2)}, u32[]{:S(2)}) async-start(bf16[4,2,16,3072]{3,2,1,0:T(8,128)(2,1)} %shard_map.79), calls=%async_computation.3 | async-start | bytes 1572864 | tf_op jit(solution)/shard_map/all_to_all | solution.py:31
  136.9 21.3 %all-to-all-start.4 = ((bf16[16,2,3072]{2,1,0:T(2,128)(2,1)}), bf16[16,2,3072]{2,1,0:T(2,128)(2,1)S(1)}, u32[]{:S(2)}, u32[]{:S(2)}) async-start(bf16[16,2,3072]{2,1,0:T(2,128)(2,1)} %shard_map.80), calls=%async_computation.4 | async-start | bytes 393216 | tf_op jit(solution)/shard_map/all_to_all | solution.py:31
  144.6 13.6 %copy-start.3 = (bf16[1,6144]{1,0:T(2,128)(2,1)S(1)}, bf16[1,6144]{1,0:T(2,128)(2,1)}, u32[]{:S(2)}) copy-start(bf16[1,6144]{1,0:T(2,128)(2,1)} %tokens.3) | copy-start | bytes 36868
  144.6 13.6 %copy-start.4 = (bf16[1,6144]{1,0:T(2,128)(2,1)S(1)}, bf16[1,6144]{1,0:T(2,128)(2,1)}, u32[]{:S(2)}) copy-start(bf16[1,6144]{1,0:T(2,128)(2,1)} %cotangent.3) | copy-start | bytes 36868
  144.7 4.3 %collective-permute-start.6 = (bf16[2,2,64,768]{3,2,1,0:T(8,128)(2,1)S(1)}, bf16[2,2,64,768]{3,2,1,0:T(8,128)(2,1)S(1)}, u32[]{:S(2)}, u32[]{:S(2)}) collective-permute-start(bf16[2,2,64,768]{3,2,1,0:T(8,128)(2,1)S(1)} %get-tuple-element.43), channel_id=1, source_target_pairs={{0,1},{1,0},{2,3},{3,2},{4,5},{5,4},{6,7},{7,6},{8,9},{9,8},{10,11... | collective-permute-start | bytes 1179656 | tf_op jit(solution)/shard_map/ppermute | solution.py:22
  146.6 3.7 %collective-permute-start.7 = (bf16[2,2,64,768]{3,2,1,0:T(8,128)(2,1)S(1)}, bf16[2,2,64,768]{3,2,1,0:T(8,128)(2,1)S(1)}, u32[]{:S(2)}, u32[]{:S(2)}) collective-permute-start(bf16[2,2,64,768]{3,2,1,0:T(8,128)(2,1)S(1)} %get-tuple-element.44), channel_id=1, source_target_pairs={{0,1},{1,0},{2,3},{3,2},{4,5},{5,4},{6,7},{7,6},{8,9},{9,8},{10,11... | collective-permute-start | bytes 1179656 | tf_op jit(solution)/shard_map/ppermute | solution.py:22

commit v12 on v11

--- a/solution.py
+++ b/solution.py
@@ -199,8 +199,8 @@
     far_in, far_out = shift(below[0], "y", 1), shift(above[1], "y", -1)
     (mine,) = call(split_body, [shape((Y, 2, half, width), bf16)], rows)
     other = swap(rows, "core")
+    far_in, far_out, mine = lax.optimization_barrier((far_in, far_out, mine))
     mine = trade(mine, "y")
-    rows, far_in, far_out = lax.optimization_barrier((rows, far_in, far_out))
     blocks = (block, above, below, far_in, far_out)
 
     (parts,) = call(hidden_body, [shape((2, count, hidden), bf16)], here, rows, other, *blocks, flops=work)
@@ -216,9 +216,9 @@
     full = lax.all_gather(pair, "y", axis=1, tiled=True)
     sums, full = lax.optimization_barrier((trade(sums, "x"), full))
     (sums,) = call(sum_body, [shape((half // X, 2, features), bf16)], sums)
-    sums, *pieces = lax.optimization_barrier((sums, mine[: Y // 2], mine[Y // 2 :]))
+    sums, mine = lax.optimization_barrier((sums, mine))
     sums = trade(sums, FAR)
-    theirs = [swap(piece, "core") for piece in pieces]
+    theirs = [swap(piece, "core") for piece in (mine[: Y // 2], mine[Y // 2 :])]
 
     grad_w_in, grad_w_out = call(
         weight_body,

time: 160 us -> 154 us (0.963)
  blocking collectives: 36.5 us -> 64.3 us
  waiting for transfers between devices: 38.6 us -> 14 us
  starting transfers between devices: 61.6 us -> 51.7 us
    all_to_all x0 -> x1, blocking collectives: none -> 31.2 us  [trade(): return lax.all_to_all(values, axis, split_axis=0, concat_axis=0, tiled=True)]
    all_to_all x5 -> x4, waiting for transfers between devices: 22.9 us -> 5.63 us  [trade(): return lax.all_to_all(values, axis, split_axis=0, concat_axis=0, tiled=True)]
    all_to_all x5 -> x4, starting transfers between devices: 42 us -> 29.4 us  [trade(): return lax.all_to_all(values, axis, split_axis=0, concat_axis=0, tiled=True)]
    ppermute x4, waiting for transfers between devices: 12.2 us -> 4.82 us  [shift(): lax.ppermute(values, axis, [(at, (at + step) % count) for at in range(cou...]
    all_gather x1, blocking collectives: 22.3 us -> 19.3 us  [local(): parts, mine = lax.optimization_barrier((lax.all_gather(parts, 'zh'), mine))]
    ppermute x4, starting transfers between devices: 11.4 us -> 14.1 us  [shift(): lax.ppermute(values, axis, [(at, (at + step) % count) for at in range(cou...]
  transfers between devices with their start and end apart: 13 -> 12, of which waited for: 6 -> 5; matrix products, arithmetic and copies ran while one was open for 2% -> 3% of each run, Pallas kernels for 4% -> 4%
where the time goes in v12:
time: 154 us; the launch traced here: 153 us
  blocking collectives  64.3 us (42%)
  starting transfers between devices  51.7 us (34%)
  Pallas kernels  14.6 us (9%)
  waiting for transfers between devices  14 us (9%)
  local copies, waits for them, and re-layouts  7.36 us (5%)
    all_to_all x1, blocking collectives, trade(): return lax.all_to_all(values, axis, split_axis=0, concat_axis=0, tiled=True)  31.2 us
    all_to_all x4, starting transfers between devices, trade(): return lax.all_to_all(values, axis, split_axis=0, concat_axis=0, tiled=True)  29.4 us
    all_gather x1, blocking collectives, local(): parts, mine = lax.optimization_barrier((lax.all_gather(parts, 'zh'), mine))  19.3 us
    pallas_call x8, Pallas kernels, call(): pl.pallas_call(body, out_shape=shapes, in_specs=specs, out_specs=[pl.Bloc...  14.6 us
    ppermute x4, starting transfers between devices, shift(): lax.ppermute(values, axis, [(at, (at + step) % count) for at in range(cou...  14.1 us
    all_gather x1, blocking collectives, local(): full = lax.all_gather(pair, 'y', axis=1, tiled=True)  13.9 us
    ppermute x4, starting transfers between devices, swap(): return lax.ppermute(values, axis, [(0, 1), (1, 0)])  8.17 us
    all_to_all x4, waiting for transfers between devices, trade(): return lax.all_to_all(values, axis, split_axis=0, concat_axis=0, tiled=True)  5.63 us
  transfers between devices with their start and end apart: 12, of which 5 were waited for; matrix products, arithmetic and copies ran while one was open for 3% of the time, Pallas kernels for 4%

profile of v12, /device:TPU:6, one launch (start us, length us, event | category | flops | bytes accessed | tf_op | source)
XLA Modules:
  0.0 152.8 jit_solution(15214993667178664246)
XLA Ops:
  0.6 2.6 %shard_map.75 = (bf16[16,2,3072]{2,1,0:T(2,128)(2,1)}, bf16[2,768,384]{2,1,0:T(8,128)(2,1)}) custom-call(bf16[1,6144]{1,0:T(2,128)(2,1)} %tokens.3, bf16[1,6144]{1,0:T(2,128)(2,1)} %cotangent.3, bf16[768,384]{1,0:T(8,128)(2,1)} %w_in.1, bf16[384,768]{1,0:T(8,128)(2,1)} %w_out.1), custom_call_target="tpu_custom_call" | custom-call | bytes 2580480 | tf_op jit(solution)/shard_map/pallas_call | solution.py:43
  3.2 3.5 %collective-permute-start.2 = (bf16[2,768,384]{2,1,0:T(8,128)(2,1)}, bf16[2,768,384]{2,1,0:T(8,128)(2,1)S(1)}, u32[]{:S(2)}, u32[]{:S(2)}) collective-permute-start(bf16[2,768,384]{2,1,0:T(8,128)(2,1)} %get-tuple-element.28.b0), channel_id=1, source_target_pairs={{0,64},{64,128},{128,192},{192,0},{1,65},{65,129},{129,193},{193,1... | collective-permute-start | bytes 3538952 | tf_op jit(solution)/shard_map/ppermute | solution.py:27
  6.7 3.6 %collective-permute-start.1 = (bf16[2,768,384]{2,1,0:T(8,128)(2,1)}, bf16[2,768,384]{2,1,0:T(8,128)(2,1)S(1)}, u32[]{:S(2)}, u32[]{:S(2)}) collective-permute-start(bf16[2,768,384]{2,1,0:T(8,128)(2,1)} %get-tuple-element.28.b0), channel_id=1, source_target_pairs={{0,192},{64,0},{128,64},{192,128},{1,193},{65,1},{129,65},{193,129... | collective-permute-start | bytes 3538952 | tf_op jit(solution)/shard_map/ppermute | solution.py:27
  10.3 31.2 %all_to_all.25 = bf16[16,2,3072]{2,1,0:T(2,128)(2,1)S(1)} all-to-all(bf16[16,2,3072]{2,1,0:T(2,128)(2,1)} %get-tuple-element.27), channel_id=1, replica_groups=mesh['zh'=2,'y'=4,'zl'=8,'x'=4,'core'=2] {'zh','zl'}, dimensions={0} | all-to-all | bytes 393216 | tf_op jit(solution)/shard_map/all_to_all | solution.py:31
  41.5 1.0 broadcast_in_dim.3
  42.5 4.8 %all-to-all-start.1 = ((bf16[4,2,16,3072]{3,2,1,0:T(8,128)(2,1)}), bf16[4,2,16,3072]{3,2,1,0:T(8,128)(2,1)S(1)}, u32[]{:S(2)}, u32[]{:S(2)}) async-start(bf16[4,2,16,3072]{3,2,1,0:T(8,128)(2,1)} %broadcast_in_dim.3), calls=%async_computation.1 | async-start | bytes 1572864 | tf_op jit(solution)/shard_map/all_to_all | solution.py:31
  47.3 0.0 collective-permute-done.2.b3
  47.3 0.9 slice_bitcast_fusion.1
  48.2 2.2 %collective-permute-start.3 = (bf16[768,384]{1,0:T(8,128)(2,1)}, bf16[768,384]{1,0:T(8,128)(2,1)}, u32[]{:S(2)}, u32[]{:S(2)}) collective-permute-start(bf16[768,384]{1,0:T(8,128)(2,1)} %slice_bitcast_fusion.1), channel_id=1, source_target_pairs={{0,64},{64,128},{128,192},{192,0},{1,65},{65,129},{129,193},{193,1... | collective-permute-start | bytes 1769480 | tf_op jit(solution)/shard_map/ppermute | solution.py:27
  50.4 0.0 collective-permute-done.1.b1
  50.4 0.9 slice_bitcast_fusion
  51.3 4.8 %collective-permute-start.4 = (bf16[768,384]{1,0:T(8,128)(2,1)}, bf16[768,384]{1,0:T(8,128)(2,1)}, u32[]{:S(2)}, u32[]{:S(2)}) collective-permute-start(bf16[768,384]{1,0:T(8,128)(2,1)} %slice_bitcast_fusion), channel_id=1, source_target_pairs={{0,192},{64,0},{128,64},{192,128},{1,193},{65,1},{129,65},{193,129... | collective-permute-start | bytes 1769480 | tf_op jit(solution)/shard_map/ppermute | solution.py:27
  56.1 0.0 all-to-all-done.1.rows
  56.1 1.9 %collective-permute-start = (bf16[4,2,16,3072]{3,2,1,0:T(8,128)(2,1)S(1)}, bf16[4,2,16,3072]{3,2,1,0:T(8,128)(2,1)}, u32[]{:S(2)}, u32[]{:S(2)}) collective-permute-start(bf16[4,2,16,3072]{3,2,1,0:T(8,128)(2,1)S(1)} %all-to-all-done.1.rows), channel_id=1, source_target_pairs={{0,1},{1,0},{2,3},{3,2},{4,5},{5,4},{6,7},{7,6},{8,9},{9,8},{10,11... | collective-permute-start | bytes 2359304 | tf_op jit(solution)/shard_map/ppermute | solution.py:22
  58.0 0.1 shard_map.76
  58.1 0.0 copy-start.2
  58.1 0.9 copy-done.2
  59.0 2.7 %collective-permute-done.3.far_in = bf16[768,384]{1,0:T(8,128)(2,1)} collective-permute-done((bf16[768,384]{1,0:T(8,128)(2,1)}, bf16[768,384]{1,0:T(8,128)(2,1)}, u32[]{:S(2)}, u32[]{:S(2)}) %collective-permute-start.3) | collective-permute-done | bytes 589856 | tf_op jit(solution)/shard_map/ppermute | solution.py:27
  61.7 2.1 %collective-permute-done.4.far_out = bf16[768,384]{1,0:T(8,128)(2,1)} collective-permute-done((bf16[768,384]{1,0:T(8,128)(2,1)}, bf16[768,384]{1,0:T(8,128)(2,1)}, u32[]{:S(2)}, u32[]{:S(2)}) %collective-permute-start.4) | collective-permute-done | bytes 589856 | tf_op jit(solution)/shard_map/ppermute | solution.py:27
  63.8 5.0 %all-to-all-start.2 = ((bf16[4,2,64,768]{3,2,1,0:T(8,128)(2,1)}), bf16[4,2,64,768]{3,2,1,0:T(8,128)(2,1)}, u32[]{:S(2)}, u32[]{:S(2)}) async-start(bf16[4,2,64,768]{3,2,1,0:T(8,128)(2,1)} %copy-done.2), calls=%async_computation.2 | async-start | bytes 1572864 | tf_op jit(solution)/shard_map/all_to_all | solution.py:31
  68.8 0.0 collective-permute-done.other
  68.8 0.0 copy-start
  68.8 1.3 copy-done
  70.0 2.8 %shard_map.77 = bf16[2,128,384]{2,1,0:T(8,128)(2,1)S(1)} custom-call(s32[1]{0:T(128)} %bitcast.here, bf16[4,2,16,3072]{3,2,1,0:T(8,128)(2,1)S(1)} %all-to-all-done.1.rows, bf16[4,2,16,3072]{3,2,1,0:T(8,128)(2,1)} %collective-permute-done.other, bf16[2,768,384]{2,1,0:T(8,128)(2,1)S(1)} %copy-done, bf16[2,768,384]{2,1,0:T(8,128)(2,1)S(1)} %collective-permute-done.1.b1, ...), custom_call_target="tpu_custom_call" | custom-call | flops 603979776 | bytes 6488068 | tf_op jit(solution)/shard_map/pallas_call | solution.py:43
  72.9 19.3 %all-gather = bf16[4,128,384]{2,1,0:T(8,128)(2,1)S(1)} all-gather(bf16[2,128,384]{2,1,0:T(8,128)(2,1)S(1)} %shard_map.77), channel_id=2, replica_groups=mesh['zh'=2,'y'=4,'zl'=8,'x'=4,'core'=2] {'zh'}, dimensions={0}, use_global_device_ids=true | all-gather | bytes 589824 | tf_op jit(solution)/shard_map/all_gather | solution.py:207
  92.2 0.0 all-to-all-done.2.mine
  92.2 0.0 copy-start.1
  92.2 1.3 copy-done.1
  93.4 2.7 %shard_map.78 = (bf16[2,128,384]{2,1,0:T(8,128)(2,1)S(1)}, f32[2,64,3072]{2,1,0:T(8,128)S(1)}, bf16[2,64,3072]{2,1,0:T(8,128)(2,1)S(1)}) custom-call(s32[1]{0:T(128)} %bitcast.here, bf16[2,2,128,384]{3,2,1,0:T(8,128)(2,1)S(1)} %bitcast.7, bf16[2,768,384]{2,1,0:T(8,128)(2,1)S(1)} %copy-done.1, bf16[2,768,384]{2,1,0:T(8,128)(2,1)S(1)} %collective-permute-done.1.b1, ...), custom_call_target="tpu_custom_call" | custom-call | flops 603979776 | bytes 7667716 | tf_op jit(solution)/shard_map/pallas_call | solution.py:43
  96.1 1.9 %collective-permute-start.5 = (bf16[2,64,3072]{2,1,0:T(8,128)(2,1)S(1)}, bf16[2,64,3072]{2,1,0:T(8,128)(2,1)S(1)}, u32[]{:S(2)}, u32[]{:S(2)}) collective-permute-start(bf16[2,64,3072]{2,1,0:T(8,128)(2,1)S(1)} %get-tuple-element.34), channel_id=1, source_target_pairs={{0,1},{1,0},{2,3},{3,2},{4,5},{5,4},{6,7},{7,6},{8,9},{9,8},{10,11... | collective-permute-start | bytes 2359304 | tf_op jit(solution)/shard_map/ppermute | solution.py:22
  98.0 2.3 %collective-permute-done.5.far = bf16[2,64,3072]{2,1,0:T(8,128)(2,1)S(1)} collective-permute-done((bf16[2,64,3072]{2,1,0:T(8,128)(2,1)S(1)}, bf16[2,64,3072]{2,1,0:T(8,128)(2,1)S(1)}, u32[]{:S(2)}, u32[]{:S(2)}) %collective-permute-start.5) | collective-permute-done | bytes 786464 | tf_op jit(solution)/shard_map/ppermute | solution.py:22
  100.3 1.0 shard_map.79
  101.3 4.8 %all-to-all-start.3 = ((bf16[4,2,16,3072]{3,2,1,0:T(8,128)(2,1)}), bf16[4,2,16,3072]{3,2,1,0:T(8,128)(2,1)S(1)}, u32[]{:S(2)}, u32[]{:S(2)}) async-start(bf16[4,2,16,3072]{3,2,1,0:T(8,128)(2,1)} %shard_map.79), calls=%async_computation.3 | async-start | bytes 1572864 | tf_op jit(solution)/shard_map/all_to_all | solution.py:31
  106.1 13.9 %all_gather.11.full = bf16[2,512,384]{2,1,0:T(8,128)(2,1)S(1)} all-gather(bf16[2,128,384]{2,1,0:T(8,128)(2,1)S(1)} %get-tuple-element.37), channel_id=1, replica_groups=mesh['zh'=2,'y'=4,'zl'=8,'x'=4,'core'=2] {'y'}, dimensions={1}, use_global_device_ids=true | all-gather | bytes 983040 | tf_op jit(solution)/shard_map/all_gather | solution.py:216
  120.0 0.0 all-to-all-done.3.parts
  120.0 1.0 shard_map.80
  121.0 14.9 %all-to-all-start.4 = ((bf16[16,2,3072]{2,1,0:T(2,128)(2,1)}), bf16[16,2,3072]{2,1,0:T(2,128)(2,1)S(1)}, u32[]{:S(2)}, u32[]{:S(2)}) async-start(bf16[16,2,3072]{2,1,0:T(2,128)(2,1)} %shard_map.80), calls=%async_computation.4 | async-start | bytes 393216 | tf_op jit(solution)/shard_map/all_to_all | solution.py:31
  135.9 1.2 fusion
  137.1 1.9 %collective-permute-start.7 = (bf16[2,2,64,768]{3,2,1,0:T(8,128)(2,1)S(1)}, bf16[2,2,64,768]{3,2,1,0:T(8,128)(2,1)S(1)}, u32[]{:S(2)}, u32[]{:S(2)}) collective-permute-start(bf16[2,2,64,768]{3,2,1,0:T(8,128)(2,1)S(1)} %get-tuple-element.50), channel_id=1, source_target_pairs={{0,1},{1,0},{2,3},{3,2},{4,5},{5,4},{6,7},{7,6},{8,9},{9,8},{10,11... | collective-permute-start | bytes 1179656 | tf_op jit(solution)/shard_map/ppermute | solution.py:22
  139.0 0.0 copy-start.3
  139.0 0.0 copy-start.4
  139.0 2.4 %collective-permute-start.6 = (bf16[2,2,64,768]{3,2,1,0:T(8,128)(2,1)S(1)}, bf16[2,2,64,768]{3,2,1,0:T(8,128)(2,1)S(1)}, u32[]{:S(2)}, u32[]{:S(2)}) collective-permute-start(bf16[2,2,64,768]{3,2,1,0:T(8,128)(2,1)S(1)} %get-tuple-element.51), channel_id=1, source_target_pairs={{0,1},{1,0},{2,3},{3,2},{4,5},{5,4},{6,7},{7,6},{8,9},{9,8},{10,11... | collective-permute-start | bytes 1179656 | tf_op jit(solution)/shard_map/ppermute | solution.py:22
  141.4 0.0 collective-permute-done.7.second
  141.4 1.3 collective-permute-done.6.first
  142.8 3.3 %shard_map.81 = (f32[768,384]{1,0:T(8,128)}, f32[384,768]{1,0:T(8,128)}) custom-call(bf16[2,512,384]{2,1,0:T(8,128)(2,1)S(1)} %all_gather.11.full, bf16[4,2,64,768]{3,2,1,0:T(8,128)(2,1)} %all-to-all-done.2.mine, bf16[2,2,64,768]{3,2,1,0:T(8,128)(2,1)S(1)} %collective-permute-done.6.first, bf16[2,2,64,768]{3,2,1,0:T(8,128)(2,1)S(1)} %collective-permute-done.7.second), custom_call_target="tpu_custom_call" | custom-call | flops 603979776 | bytes 4718592 | tf_op jit(solution)/shard_map/pallas_call | solution.py:43
  146.0 5.6 %all-to-all-done.4.sums = bf16[16,2,3072]{2,1,0:T(2,128)(2,1)S(1)} async-done(((bf16[16,2,3072]{2,1,0:T(2,128)(2,1)}), bf16[16,2,3072]{2,1,0:T(2,128)(2,1)S(1)}, u32[]{:S(2)}, u32[]{:S(2)}) %all-to-all-start.4) | async-done | bytes 196640 | tf_op jit(solution)/shard_map/all_to_all | solution.py:31
  151.7 0.0 copy-done.3
  151.7 0.0 copy-done.4
  151.7 1.2 shard_map.82
  (1 shorter events, 0.0 us)
Async XLA Ops:
  3.2 44.0 %collective-permute-start.2 = (bf16[2,768,384]{2,1,0:T(8,128)(2,1)}, bf16[2,768,384]{2,1,0:T(8,128)(2,1)S(1)}, u32[]{:S(2)}, u32[]{:S(2)}) collective-permute-start(bf16[2,768,384]{2,1,0:T(8,128)(2,1)} %get-tuple-element.28.b0), channel_id=1, source_target_pairs={{0,64},{64,128},{128,192},{192,0},{1,65},{65,129},{129,193},{193,1... | collective-permute-start | bytes 3538952 | tf_op jit(solution)/shard_map/ppermute | solution.py:27
  6.7 43.7 %collective-permute-start.1 = (bf16[2,768,384]{2,1,0:T(8,128)(2,1)}, bf16[2,768,384]{2,1,0:T(8,128)(2,1)S(1)}, u32[]{:S(2)}, u32[]{:S(2)}) collective-permute-start(bf16[2,768,384]{2,1,0:T(8,128)(2,1)} %get-tuple-element.28.b0), channel_id=1, source_target_pairs={{0,192},{64,0},{128,64},{192,128},{1,193},{65,1},{129,65},{193,129... | collective-permute-start | bytes 3538952 | tf_op jit(solution)/shard_map/ppermute | solution.py:27
  42.5 13.6 %all-to-all-start.1 = ((bf16[4,2,16,3072]{3,2,1,0:T(8,128)(2,1)}), bf16[4,2,16,3072]{3,2,1,0:T(8,128)(2,1)S(1)}, u32[]{:S(2)}, u32[]{:S(2)}) async-start(bf16[4,2,16,3072]{3,2,1,0:T(8,128)(2,1)} %broadcast_in_dim.3), calls=%async_computation.1 | async-start | bytes 1572864 | tf_op jit(solution)/shard_map/all_to_all | solution.py:31
  48.2 13.5 %collective-permute-start.3 = (bf16[768,384]{1,0:T(8,128)(2,1)}, bf16[768,384]{1,0:T(8,128)(2,1)}, u32[]{:S(2)}, u32[]{:S(2)}) collective-permute-start(bf16[768,384]{1,0:T(8,128)(2,1)} %slice_bitcast_fusion.1), channel_id=1, source_target_pairs={{0,64},{64,128},{128,192},{192,0},{1,65},{65,129},{129,193},{193,1... | collective-permute-start | bytes 1769480 | tf_op jit(solution)/shard_map/ppermute | solution.py:27
  51.3 12.5 %collective-permute-start.4 = (bf16[768,384]{1,0:T(8,128)(2,1)}, bf16[768,384]{1,0:T(8,128)(2,1)}, u32[]{:S(2)}, u32[]{:S(2)}) collective-permute-start(bf16[768,384]{1,0:T(8,128)(2,1)} %slice_bitcast_fusion), channel_id=1, source_target_pairs={{0,192},{64,0},{128,64},{192,128},{1,193},{65,1},{129,65},{193,129... | collective-permute-start | bytes 1769480 | tf_op jit(solution)/shard_map/ppermute | solution.py:27
  56.1 12.6 %collective-permute-start = (bf16[4,2,16,3072]{3,2,1,0:T(8,128)(2,1)S(1)}, bf16[4,2,16,3072]{3,2,1,0:T(8,128)(2,1)}, u32[]{:S(2)}, u32[]{:S(2)}) collective-permute-start(bf16[4,2,16,3072]{3,2,1,0:T(8,128)(2,1)S(1)} %all-to-all-done.1.rows), channel_id=1, source_target_pairs={{0,1},{1,0},{2,3},{3,2},{4,5},{5,4},{6,7},{7,6},{8,9},{9,8},{10,11... | collective-permute-start | bytes 2359304 | tf_op jit(solution)/shard_map/ppermute | solution.py:22
  58.1 0.9 copy-start.2
  63.8 28.4 %all-to-all-start.2 = ((bf16[4,2,64,768]{3,2,1,0:T(8,128)(2,1)}), bf16[4,2,64,768]{3,2,1,0:T(8,128)(2,1)}, u32[]{:S(2)}, u32[]{:S(2)}) async-start(bf16[4,2,64,768]{3,2,1,0:T(8,128)(2,1)} %copy-done.2), calls=%async_computation.2 | async-start | bytes 1572864 | tf_op jit(solution)/shard_map/all_to_all | solution.py:31
  68.8 1.3 copy-start
  92.2 1.3 copy-start.1
  96.1 4.2 %collective-permute-start.5 = (bf16[2,64,3072]{2,1,0:T(8,128)(2,1)S(1)}, bf16[2,64,3072]{2,1,0:T(8,128)(2,1)S(1)}, u32[]{:S(2)}, u32[]{:S(2)}) collective-permute-start(bf16[2,64,3072]{2,1,0:T(8,128)(2,1)S(1)} %get-tuple-element.34), channel_id=1, source_target_pairs={{0,1},{1,0},{2,3},{3,2},{4,5},{5,4},{6,7},{7,6},{8,9},{9,8},{10,11... | collective-permute-start | bytes 2359304 | tf_op jit(solution)/shard_map/ppermute | solution.py:22
  101.3 18.6 %all-to-all-start.3 = ((bf16[4,2,16,3072]{3,2,1,0:T(8,128)(2,1)}), bf16[4,2,16,3072]{3,2,1,0:T(8,128)(2,1)S(1)}, u32[]{:S(2)}, u32[]{:S(2)}) async-start(bf16[4,2,16,3072]{3,2,1,0:T(8,128)(2,1)} %shard_map.79), calls=%async_computation.3 | async-start | bytes 1572864 | tf_op jit(solution)/shard_map/all_to_all | solution.py:31
  121.0 30.7 %all-to-all-start.4 = ((bf16[16,2,3072]{2,1,0:T(2,128)(2,1)}), bf16[16,2,3072]{2,1,0:T(2,128)(2,1)S(1)}, u32[]{:S(2)}, u32[]{:S(2)}) async-start(bf16[16,2,3072]{2,1,0:T(2,128)(2,1)} %shard_map.80), calls=%async_computation.4 | async-start | bytes 393216 | tf_op jit(solution)/shard_map/all_to_all | solution.py:31
  137.1 4.4 %collective-permute-start.7 = (bf16[2,2,64,768]{3,2,1,0:T(8,128)(2,1)S(1)}, bf16[2,2,64,768]{3,2,1,0:T(8,128)(2,1)S(1)}, u32[]{:S(2)}, u32[]{:S(2)}) collective-permute-start(bf16[2,2,64,768]{3,2,1,0:T(8,128)(2,1)S(1)} %get-tuple-element.50), channel_id=1, source_target_pairs={{0,1},{1,0},{2,3},{3,2},{4,5},{5,4},{6,7},{7,6},{8,9},{9,8},{10,11... | collective-permute-start | bytes 1179656 | tf_op jit(solution)/shard_map/ppermute | solution.py:22
  139.0 12.7 %copy-start.3 = (bf16[1,6144]{1,0:T(2,128)(2,1)S(1)}, bf16[1,6144]{1,0:T(2,128)(2,1)}, u32[]{:S(2)}) copy-start(bf16[1,6144]{1,0:T(2,128)(2,1)} %tokens.3) | copy-start | bytes 36868
  139.0 12.6 %copy-start.4 = (bf16[1,6144]{1,0:T(2,128)(2,1)S(1)}, bf16[1,6144]{1,0:T(2,128)(2,1)}, u32[]{:S(2)}) copy-start(bf16[1,6144]{1,0:T(2,128)(2,1)} %cotangent.3) | copy-start | bytes 36868
  139.0 3.7 %collective-permute-start.6 = (bf16[2,2,64,768]{3,2,1,0:T(8,128)(2,1)S(1)}, bf16[2,2,64,768]{3,2,1,0:T(8,128)(2,1)S(1)}, u32[]{:S(2)}, u32[]{:S(2)}) collective-permute-start(bf16[2,2,64,768]{3,2,1,0:T(8,128)(2,1)S(1)} %get-tuple-element.51), channel_id=1, source_target_pairs={{0,1},{1,0},{2,3},{3,2},{4,5},{5,4},{6,7},{7,6},{8,9},{9,8},{10,11... | collective-permute-start | bytes 1179656 | tf_op jit(solution)/shard_map/ppermute | solution.py:22

commit v13 on v12

--- a/solution.py
+++ b/solution.py
@@ -212,13 +212,12 @@
     )
 
     (sums,) = call(add_body, [shape((X, 2, half // X, features), bf16)], keep, swap(give, "core"))
+    sums, mine = lax.optimization_barrier((sums, mine))
+    theirs = [swap(piece, "core") for piece in (mine[: Y // 2], mine[Y // 2 :])]
+    sums, theirs = lax.optimization_barrier((trade(sums, "x"), theirs))
+    (sums,) = call(sum_body, [shape((half // X, 2, features), bf16)], sums)
     sums, pair = lax.optimization_barrier((sums, pair))
-    full = lax.all_gather(pair, "y", axis=1, tiled=True)
-    sums, full = lax.optimization_barrier((trade(sums, "x"), full))
-    (sums,) = call(sum_body, [shape((half // X, 2, features), bf16)], sums)
-    sums, mine = lax.optimization_barrier((sums, mine))
-    sums = trade(sums, FAR)
-    theirs = [swap(piece, "core") for piece in (mine[: Y // 2], mine[Y // 2 :])]
+    sums, full = trade(sums, FAR), lax.all_gather(pair, "y", axis=1, tiled=True)
 
     grad_w_in, grad_w_out = call(
         weight_body,

time: 154 us -> 154 us (level); the launches traced: 153 us -> 151 us
  waiting for transfers between devices: 14 us -> 12.1 us
    all_to_all x4, waiting for transfers between devices: 5.63 us -> 3.69 us  [trade(): return lax.all_to_all(values, axis, split_axis=0, concat_axis=0, tiled=True)]
where the time goes in v13:
time: 154 us; the launch traced here: 151 us
  blocking collectives  64.7 us (42%)
  starting transfers between devices  51.5 us (33%)
  Pallas kernels  14.6 us (9%)
  waiting for transfers between devices  12.1 us (8%)
  local copies, waits for them, and re-layouts  7.36 us (5%)
    all_to_all x1, blocking collectives, trade(): return lax.all_to_all(values, axis, split_axis=0, concat_axis=0, tiled=True)  31.2 us
    all_to_all x4, starting transfers between devices, trade(): return lax.all_to_all(values, axis, split_axis=0, concat_axis=0, tiled=True)  29.3 us
    all_gather x1, blocking collectives, local(): parts, mine = lax.optimization_barrier((lax.all_gather(parts, 'zh'), mine))  19.3 us
    pallas_call x8, Pallas kernels, call(): pl.pallas_call(body, out_shape=shapes, in_specs=specs, out_specs=[pl.Bloc...  14.6 us
    all_gather x1, blocking collectives, local(): lax.all_gather(pair, 'y', axis=1, tiled=True)  14.2 us
    ppermute x4, starting transfers between devices, shift(): lax.ppermute(values, axis, [(at, (at + step) % count) for at in range(cou...  14.1 us
    ppermute x4, starting transfers between devices, swap(): return lax.ppermute(values, axis, [(0, 1), (1, 0)])  8.17 us
    ppermute x4, waiting for transfers between devices, shift(): lax.ppermute(values, axis, [(at, (at + step) % count) for at in range(cou...  4.82 us
  transfers between devices with their start and end apart: 12, of which 5 were waited for; matrix products, arithmetic and copies ran while one was open for 3% of the time, Pallas kernels for 4%

profile of v13, /device:TPU:6, one launch (start us, length us, event | category | flops | bytes accessed | tf_op | source)
XLA Modules:
  0.0 151.1 jit_solution(16421911073098615907)
XLA Ops:
  0.6 2.6 %shard_map.75 = (bf16[16,2,3072]{2,1,0:T(2,128)(2,1)}, bf16[2,768,384]{2,1,0:T(8,128)(2,1)}) custom-call(bf16[1,6144]{1,0:T(2,128)(2,1)} %tokens.3, bf16[1,6144]{1,0:T(2,128)(2,1)} %cotangent.3, bf16[768,384]{1,0:T(8,128)(2,1)} %w_in.1, bf16[384,768]{1,0:T(8,128)(2,1)} %w_out.1), custom_call_target="tpu_custom_call" | custom-call | bytes 2580480 | tf_op jit(solution)/shard_map/pallas_call | solution.py:43
  3.2 3.5 %collective-permute-start.2 = (bf16[2,768,384]{2,1,0:T(8,128)(2,1)}, bf16[2,768,384]{2,1,0:T(8,128)(2,1)S(1)}, u32[]{:S(2)}, u32[]{:S(2)}) collective-permute-start(bf16[2,768,384]{2,1,0:T(8,128)(2,1)} %get-tuple-element.29.b0), channel_id=1, source_target_pairs={{0,64},{64,128},{128,192},{192,0},{1,65},{65,129},{129,193},{193,1... | collective-permute-start | bytes 3538952 | tf_op jit(solution)/shard_map/ppermute | solution.py:27
  6.7 3.6 %collective-permute-start.1 = (bf16[2,768,384]{2,1,0:T(8,128)(2,1)}, bf16[2,768,384]{2,1,0:T(8,128)(2,1)S(1)}, u32[]{:S(2)}, u32[]{:S(2)}) collective-permute-start(bf16[2,768,384]{2,1,0:T(8,128)(2,1)} %get-tuple-element.29.b0), channel_id=1, source_target_pairs={{0,192},{64,0},{128,64},{192,128},{1,193},{65,1},{129,65},{193,129... | collective-permute-start | bytes 3538952 | tf_op jit(solution)/shard_map/ppermute | solution.py:27
  10.3 31.2 %all_to_all.25 = bf16[16,2,3072]{2,1,0:T(2,128)(2,1)S(1)} all-to-all(bf16[16,2,3072]{2,1,0:T(2,128)(2,1)} %get-tuple-element.28), channel_id=1, replica_groups=mesh['zh'=2,'y'=4,'zl'=8,'x'=4,'core'=2] {'zh','zl'}, dimensions={0} | all-to-all | bytes 393216 | tf_op jit(solution)/shard_map/all_to_all | solution.py:31
  41.5 1.0 broadcast_in_dim.3
  42.5 4.8 %all-to-all-start.1 = ((bf16[4,2,16,3072]{3,2,1,0:T(8,128)(2,1)}), bf16[4,2,16,3072]{3,2,1,0:T(8,128)(2,1)S(1)}, u32[]{:S(2)}, u32[]{:S(2)}) async-start(bf16[4,2,16,3072]{3,2,1,0:T(8,128)(2,1)} %broadcast_in_dim.3), calls=%async_computation.1 | async-start | bytes 1572864 | tf_op jit(solution)/shard_map/all_to_all | solution.py:31
  47.3 0.0 collective-permute-done.2.b3
  47.3 0.9 slice_bitcast_fusion.1
  48.2 2.2 %collective-permute-start.3 = (bf16[768,384]{1,0:T(8,128)(2,1)}, bf16[768,384]{1,0:T(8,128)(2,1)}, u32[]{:S(2)}, u32[]{:S(2)}) collective-permute-start(bf16[768,384]{1,0:T(8,128)(2,1)} %slice_bitcast_fusion.1), channel_id=1, source_target_pairs={{0,64},{64,128},{128,192},{192,0},{1,65},{65,129},{129,193},{193,1... | collective-permute-start | bytes 1769480 | tf_op jit(solution)/shard_map/ppermute | solution.py:27
  50.4 0.0 collective-permute-done.1.b1
  50.4 0.9 slice_bitcast_fusion
  51.3 4.8 %collective-permute-start.4 = (bf16[768,384]{1,0:T(8,128)(2,1)}, bf16[768,384]{1,0:T(8,128)(2,1)}, u32[]{:S(2)}, u32[]{:S(2)}) collective-permute-start(bf16[768,384]{1,0:T(8,128)(2,1)} %slice_bitcast_fusion), channel_id=1, source_target_pairs={{0,192},{64,0},{128,64},{192,128},{1,193},{65,1},{129,65},{193,129... | collective-permute-start | bytes 1769480 | tf_op jit(solution)/shard_map/ppermute | solution.py:27
  56.1 0.0 all-to-all-done.1.rows
  56.1 1.9 %collective-permute-start = (bf16[4,2,16,3072]{3,2,1,0:T(8,128)(2,1)S(1)}, bf16[4,2,16,3072]{3,2,1,0:T(8,128)(2,1)}, u32[]{:S(2)}, u32[]{:S(2)}) collective-permute-start(bf16[4,2,16,3072]{3,2,1,0:T(8,128)(2,1)S(1)} %all-to-all-done.1.rows), channel_id=1, source_target_pairs={{0,1},{1,0},{2,3},{3,2},{4,5},{5,4},{6,7},{7,6},{8,9},{9,8},{10,11... | collective-permute-start | bytes 2359304 | tf_op jit(solution)/shard_map/ppermute | solution.py:22
  58.0 0.1 shard_map.76
  58.1 0.0 copy-start.2
  58.1 0.9 copy-done.2
  59.0 2.7 %collective-permute-done.3.far_in = bf16[768,384]{1,0:T(8,128)(2,1)} collective-permute-done((bf16[768,384]{1,0:T(8,128)(2,1)}, bf16[768,384]{1,0:T(8,128)(2,1)}, u32[]{:S(2)}, u32[]{:S(2)}) %collective-permute-start.3) | collective-permute-done | bytes 589856 | tf_op jit(solution)/shard_map/ppermute | solution.py:27
  61.7 2.1 %collective-permute-done.4.far_out = bf16[768,384]{1,0:T(8,128)(2,1)} collective-permute-done((bf16[768,384]{1,0:T(8,128)(2,1)}, bf16[768,384]{1,0:T(8,128)(2,1)}, u32[]{:S(2)}, u32[]{:S(2)}) %collective-permute-start.4) | collective-permute-done | bytes 589856 | tf_op jit(solution)/shard_map/ppermute | solution.py:27
  63.8 5.0 %all-to-all-start.2 = ((bf16[4,2,64,768]{3,2,1,0:T(8,128)(2,1)}), bf16[4,2,64,768]{3,2,1,0:T(8,128)(2,1)}, u32[]{:S(2)}, u32[]{:S(2)}) async-start(bf16[4,2,64,768]{3,2,1,0:T(8,128)(2,1)} %copy-done.2), calls=%async_computation.2 | async-start | bytes 1572864 | tf_op jit(solution)/shard_map/all_to_all | solution.py:31
  68.8 0.0 collective-permute-done.other
  68.8 0.0 copy-start
  68.8 1.3 copy-done
  70.0 2.8 %shard_map.77 = bf16[2,128,384]{2,1,0:T(8,128)(2,1)S(1)} custom-call(s32[1]{0:T(128)} %bitcast.here, bf16[4,2,16,3072]{3,2,1,0:T(8,128)(2,1)S(1)} %all-to-all-done.1.rows, bf16[4,2,16,3072]{3,2,1,0:T(8,128)(2,1)} %collective-permute-done.other, bf16[2,768,384]{2,1,0:T(8,128)(2,1)S(1)} %copy-done, bf16[2,768,384]{2,1,0:T(8,128)(2,1)S(1)} %collective-permute-done.1.b1, ...), custom_call_target="tpu_custom_call" | custom-call | flops 603979776 | bytes 6488068 | tf_op jit(solution)/shard_map/pallas_call | solution.py:43
  72.9 19.3 %all-gather = bf16[4,128,384]{2,1,0:T(8,128)(2,1)S(1)} all-gather(bf16[2,128,384]{2,1,0:T(8,128)(2,1)S(1)} %shard_map.77), channel_id=2, replica_groups=mesh['zh'=2,'y'=4,'zl'=8,'x'=4,'core'=2] {'zh'}, dimensions={0}, use_global_device_ids=true | all-gather | bytes 589824 | tf_op jit(solution)/shard_map/all_gather | solution.py:207
  92.2 0.0 all-to-all-done.2.mine
  92.2 0.0 copy-start.1
  92.2 1.3 copy-done.1
  93.4 2.7 %shard_map.78 = (bf16[2,128,384]{2,1,0:T(8,128)(2,1)S(1)}, f32[2,64,3072]{2,1,0:T(8,128)S(1)}, bf16[2,64,3072]{2,1,0:T(8,128)(2,1)S(1)}) custom-call(s32[1]{0:T(128)} %bitcast.here, bf16[2,2,128,384]{3,2,1,0:T(8,128)(2,1)S(1)} %bitcast.7, bf16[2,768,384]{2,1,0:T(8,128)(2,1)S(1)} %copy-done.1, bf16[2,768,384]{2,1,0:T(8,128)(2,1)S(1)} %collective-permute-done.1.b1, ...), custom_call_target="tpu_custom_call" | custom-call | flops 603979776 | bytes 7667716 | tf_op jit(solution)/shard_map/pallas_call | solution.py:43
  96.1 1.9 %collective-permute-start.5 = (bf16[2,64,3072]{2,1,0:T(8,128)(2,1)S(1)}, bf16[2,64,3072]{2,1,0:T(8,128)(2,1)S(1)}, u32[]{:S(2)}, u32[]{:S(2)}) collective-permute-start(bf16[2,64,3072]{2,1,0:T(8,128)(2,1)S(1)} %get-tuple-element.35), channel_id=1, source_target_pairs={{0,1},{1,0},{2,3},{3,2},{4,5},{5,4},{6,7},{7,6},{8,9},{9,8},{10,11... | collective-permute-start | bytes 2359304 | tf_op jit(solution)/shard_map/ppermute | solution.py:22
  98.0 2.3 %collective-permute-done.5.far = bf16[2,64,3072]{2,1,0:T(8,128)(2,1)S(1)} collective-permute-done((bf16[2,64,3072]{2,1,0:T(8,128)(2,1)S(1)}, bf16[2,64,3072]{2,1,0:T(8,128)(2,1)S(1)}, u32[]{:S(2)}, u32[]{:S(2)}) %collective-permute-start.5) | collective-permute-done | bytes 786464 | tf_op jit(solution)/shard_map/ppermute | solution.py:22
  100.3 1.0 shard_map.79
  101.3 4.8 %all-to-all-start.3 = ((bf16[4,2,16,3072]{3,2,1,0:T(8,128)(2,1)}), bf16[4,2,16,3072]{3,2,1,0:T(8,128)(2,1)S(1)}, u32[]{:S(2)}, u32[]{:S(2)}) async-start(bf16[4,2,16,3072]{3,2,1,0:T(8,128)(2,1)} %shard_map.79), calls=%async_computation.3 | async-start | bytes 1572864 | tf_op jit(solution)/shard_map/all_to_all | solution.py:31
  106.1 1.2 fusion
  107.3 1.9 %collective-permute-start.7 = (bf16[2,2,64,768]{3,2,1,0:T(8,128)(2,1)S(1)}, bf16[2,2,64,768]{3,2,1,0:T(8,128)(2,1)S(1)}, u32[]{:S(2)}, u32[]{:S(2)}) collective-permute-start(bf16[2,2,64,768]{3,2,1,0:T(8,128)(2,1)S(1)} %get-tuple-element.52), channel_id=1, source_target_pairs={{0,1},{1,0},{2,3},{3,2},{4,5},{5,4},{6,7},{7,6},{8,9},{9,8},{10,11... | collective-permute-start | bytes 1179656 | tf_op jit(solution)/shard_map/ppermute | solution.py:22
  109.2 2.4 %collective-permute-start.6 = (bf16[2,2,64,768]{3,2,1,0:T(8,128)(2,1)S(1)}, bf16[2,2,64,768]{3,2,1,0:T(8,128)(2,1)S(1)}, u32[]{:S(2)}, u32[]{:S(2)}) collective-permute-start(bf16[2,2,64,768]{3,2,1,0:T(8,128)(2,1)S(1)} %get-tuple-element.53), channel_id=1, source_target_pairs={{0,1},{1,0},{2,3},{3,2},{4,5},{5,4},{6,7},{7,6},{8,9},{9,8},{10,11... | collective-permute-start | bytes 1179656 | tf_op jit(solution)/shard_map/ppermute | solution.py:22
  111.6 0.0 collective-permute-done.7.second
  111.6 1.3 collective-permute-done.6.first
  112.9 3.7 %all-to-all-done.3.parts = bf16[4,2,16,3072]{3,2,1,0:T(8,128)(2,1)S(1)} async-done(((bf16[4,2,16,3072]{3,2,1,0:T(8,128)(2,1)}), bf16[4,2,16,3072]{3,2,1,0:T(8,128)(2,1)S(1)}, u32[]{:S(2)}, u32[]{:S(2)}) %all-to-all-start.3) | async-done | bytes 786464 | tf_op jit(solution)/shard_map/all_to_all | solution.py:31
  116.6 1.0 shard_map.80
  117.6 14.8 %all-to-all-start.4 = ((bf16[16,2,3072]{2,1,0:T(2,128)(2,1)}), bf16[16,2,3072]{2,1,0:T(2,128)(2,1)S(1)}, u32[]{:S(2)}, u32[]{:S(2)}) async-start(bf16[16,2,3072]{2,1,0:T(2,128)(2,1)} %shard_map.80), calls=%async_computation.4 | async-start | bytes 393216 | tf_op jit(solution)/shard_map/all_to_all | solution.py:31
  132.4 14.2 %all_gather.11.full = bf16[2,512,384]{2,1,0:T(8,128)(2,1)S(1)} all-gather(bf16[2,128,384]{2,1,0:T(8,128)(2,1)S(1)} %get-tuple-element.42), channel_id=1, replica_groups=mesh['zh'=2,'y'=4,'zl'=8,'x'=4,'core'=2] {'y'}, dimensions={1}, use_global_device_ids=true | all-gather | bytes 983040 | tf_op jit(solution)/shard_map/all_gather | solution.py:220
  146.7 0.0 copy-start.3
  146.7 0.0 copy-start.4
  146.7 3.3 %shard_map.81 = (f32[768,384]{1,0:T(8,128)}, f32[384,768]{1,0:T(8,128)}) custom-call(bf16[2,512,384]{2,1,0:T(8,128)(2,1)S(1)} %all_gather.11.full, bf16[4,2,64,768]{3,2,1,0:T(8,128)(2,1)} %all-to-all-done.2.mine, bf16[2,2,64,768]{3,2,1,0:T(8,128)(2,1)S(1)} %collective-permute-done.6.first, bf16[2,2,64,768]{3,2,1,0:T(8,128)(2,1)S(1)} %collective-permute-done.7.second), custom_call_target="tpu_custom_call" | custom-call | flops 603979776 | bytes 4718592 | tf_op jit(solution)/shard_map/pallas_call | solution.py:43
  149.9 0.0 all-to-all-done.4.sums
  149.9 0.0 copy-done.3
  149.9 0.0 copy-done.4
  149.9 1.2 shard_map.82
  (1 shorter events, 0.0 us)
Async XLA Ops:
  3.2 44.0 %collective-permute-start.2 = (bf16[2,768,384]{2,1,0:T(8,128)(2,1)}, bf16[2,768,384]{2,1,0:T(8,128)(2,1)S(1)}, u32[]{:S(2)}, u32[]{:S(2)}) collective-permute-start(bf16[2,768,384]{2,1,0:T(8,128)(2,1)} %get-tuple-element.29.b0), channel_id=1, source_target_pairs={{0,64},{64,128},{128,192},{192,0},{1,65},{65,129},{129,193},{193,1... | collective-permute-start | bytes 3538952 | tf_op jit(solution)/shard_map/ppermute | solution.py:27
  6.7 43.7 %collective-permute-start.1 = (bf16[2,768,384]{2,1,0:T(8,128)(2,1)}, bf16[2,768,384]{2,1,0:T(8,128)(2,1)S(1)}, u32[]{:S(2)}, u32[]{:S(2)}) collective-permute-start(bf16[2,768,384]{2,1,0:T(8,128)(2,1)} %get-tuple-element.29.b0), channel_id=1, source_target_pairs={{0,192},{64,0},{128,64},{192,128},{1,193},{65,1},{129,65},{193,129... | collective-permute-start | bytes 3538952 | tf_op jit(solution)/shard_map/ppermute | solution.py:27
  42.5 13.6 %all-to-all-start.1 = ((bf16[4,2,16,3072]{3,2,1,0:T(8,128)(2,1)}), bf16[4,2,16,3072]{3,2,1,0:T(8,128)(2,1)S(1)}, u32[]{:S(2)}, u32[]{:S(2)}) async-start(bf16[4,2,16,3072]{3,2,1,0:T(8,128)(2,1)} %broadcast_in_dim.3), calls=%async_computation.1 | async-start | bytes 1572864 | tf_op jit(solution)/shard_map/all_to_all | solution.py:31
  48.2 13.5 %collective-permute-start.3 = (bf16[768,384]{1,0:T(8,128)(2,1)}, bf16[768,384]{1,0:T(8,128)(2,1)}, u32[]{:S(2)}, u32[]{:S(2)}) collective-permute-start(bf16[768,384]{1,0:T(8,128)(2,1)} %slice_bitcast_fusion.1), channel_id=1, source_target_pairs={{0,64},{64,128},{128,192},{192,0},{1,65},{65,129},{129,193},{193,1... | collective-permute-start | bytes 1769480 | tf_op jit(solution)/shard_map/ppermute | solution.py:27
  51.3 12.5 %collective-permute-start.4 = (bf16[768,384]{1,0:T(8,128)(2,1)}, bf16[768,384]{1,0:T(8,128)(2,1)}, u32[]{:S(2)}, u32[]{:S(2)}) collective-permute-start(bf16[768,384]{1,0:T(8,128)(2,1)} %slice_bitcast_fusion), channel_id=1, source_target_pairs={{0,192},{64,0},{128,64},{192,128},{1,193},{65,1},{129,65},{193,129... | collective-permute-start | bytes 1769480 | tf_op jit(solution)/shard_map/ppermute | solution.py:27
  56.1 12.6 %collective-permute-start = (bf16[4,2,16,3072]{3,2,1,0:T(8,128)(2,1)S(1)}, bf16[4,2,16,3072]{3,2,1,0:T(8,128)(2,1)}, u32[]{:S(2)}, u32[]{:S(2)}) collective-permute-start(bf16[4,2,16,3072]{3,2,1,0:T(8,128)(2,1)S(1)} %all-to-all-done.1.rows), channel_id=1, source_target_pairs={{0,1},{1,0},{2,3},{3,2},{4,5},{5,4},{6,7},{7,6},{8,9},{9,8},{10,11... | collective-permute-start | bytes 2359304 | tf_op jit(solution)/shard_map/ppermute | solution.py:22
  58.1 0.9 copy-start.2
  63.8 28.4 %all-to-all-start.2 = ((bf16[4,2,64,768]{3,2,1,0:T(8,128)(2,1)}), bf16[4,2,64,768]{3,2,1,0:T(8,128)(2,1)}, u32[]{:S(2)}, u32[]{:S(2)}) async-start(bf16[4,2,64,768]{3,2,1,0:T(8,128)(2,1)} %copy-done.2), calls=%async_computation.2 | async-start | bytes 1572864 | tf_op jit(solution)/shard_map/all_to_all | solution.py:31
  68.8 1.3 copy-start
  92.2 1.3 copy-start.1
  96.1 4.2 %collective-permute-start.5 = (bf16[2,64,3072]{2,1,0:T(8,128)(2,1)S(1)}, bf16[2,64,3072]{2,1,0:T(8,128)(2,1)S(1)}, u32[]{:S(2)}, u32[]{:S(2)}) collective-permute-start(bf16[2,64,3072]{2,1,0:T(8,128)(2,1)S(1)} %get-tuple-element.35), channel_id=1, source_target_pairs={{0,1},{1,0},{2,3},{3,2},{4,5},{5,4},{6,7},{7,6},{8,9},{9,8},{10,11... | collective-permute-start | bytes 2359304 | tf_op jit(solution)/shard_map/ppermute | solution.py:22
  101.3 15.3 %all-to-all-start.3 = ((bf16[4,2,16,3072]{3,2,1,0:T(8,128)(2,1)}), bf16[4,2,16,3072]{3,2,1,0:T(8,128)(2,1)S(1)}, u32[]{:S(2)}, u32[]{:S(2)}) async-start(bf16[4,2,16,3072]{3,2,1,0:T(8,128)(2,1)} %shard_map.79), calls=%async_computation.3 | async-start | bytes 1572864 | tf_op jit(solution)/shard_map/all_to_all | solution.py:31
  107.3 4.3 %collective-permute-start.7 = (bf16[2,2,64,768]{3,2,1,0:T(8,128)(2,1)S(1)}, bf16[2,2,64,768]{3,2,1,0:T(8,128)(2,1)S(1)}, u32[]{:S(2)}, u32[]{:S(2)}) collective-permute-start(bf16[2,2,64,768]{3,2,1,0:T(8,128)(2,1)S(1)} %get-tuple-element.52), channel_id=1, source_target_pairs={{0,1},{1,0},{2,3},{3,2},{4,5},{5,4},{6,7},{7,6},{8,9},{9,8},{10,11... | collective-permute-start | bytes 1179656 | tf_op jit(solution)/shard_map/ppermute | solution.py:22
  109.2 3.7 %collective-permute-start.6 = (bf16[2,2,64,768]{3,2,1,0:T(8,128)(2,1)S(1)}, bf16[2,2,64,768]{3,2,1,0:T(8,128)(2,1)S(1)}, u32[]{:S(2)}, u32[]{:S(2)}) collective-permute-start(bf16[2,2,64,768]{3,2,1,0:T(8,128)(2,1)S(1)} %get-tuple-element.53), channel_id=1, source_target_pairs={{0,1},{1,0},{2,3},{3,2},{4,5},{5,4},{6,7},{7,6},{8,9},{9,8},{10,11... | collective-permute-start | bytes 1179656 | tf_op jit(solution)/shard_map/ppermute | solution.py:22
  117.6 32.3 %all-to-all-start.4 = ((bf16[16,2,3072]{2,1,0:T(2,128)(2,1)}), bf16[16,2,3072]{2,1,0:T(2,128)(2,1)S(1)}, u32[]{:S(2)}, u32[]{:S(2)}) async-start(bf16[16,2,3072]{2,1,0:T(2,128)(2,1)} %shard_map.80), calls=%async_computation.4 | async-start | bytes 393216 | tf_op jit(solution)/shard_map/all_to_all | solution.py:31
  146.7 3.3 %copy-start.3 = (bf16[1,6144]{1,0:T(2,128)(2,1)S(1)}, bf16[1,6144]{1,0:T(2,128)(2,1)}, u32[]{:S(2)}) copy-start(bf16[1,6144]{1,0:T(2,128)(2,1)} %tokens.3) | copy-start | bytes 36868
  146.7 3.3 %copy-start.4 = (bf16[1,6144]{1,0:T(2,128)(2,1)S(1)}, bf16[1,6144]{1,0:T(2,128)(2,1)}, u32[]{:S(2)}) copy-start(bf16[1,6144]{1,0:T(2,128)(2,1)} %cotangent.3) | copy-start | bytes 36868

commit v14 on v12

--- a/solution.py
+++ b/solution.py
@@ -134,13 +134,17 @@
             give[0, :, cut] = term[half:].astype(bf16)
 
 
-def weight_body(full, mine, first, second, grad_w_in, grad_w_out):
+def weight_body(here, p0, p1, p2, p3, mine, first, second, grad_w_in, grad_w_out):
     def every(index):
-        blocks = [ref.at[step] for ref in (first, second) for step in range(Y // 2)]
-        return jnp.concatenate(
-            [ref[index] for step in range(Y) for ref in (mine.at[step], blocks[step])], axis=0
-        )
-
+        found = []
+        for step in range(Y):
+            at = lax.rem(here[0] + Y - step, Y)
+            low = first[lax.rem(at, Y // 2), index]
+            high = second[lax.rem(at, Y // 2), index]
+            found += [mine[at, index], jnp.where(at < Y // 2, low, high)]
+        return jnp.concatenate(found, axis=0)
+
+    full = [jnp.concatenate([ref[index] for ref in (p0, p1, p2, p3)], axis=0) for index in range(2)]
     grad_w_in[...] = dot(every(0), full[1], FIRST)
     grad_w_out[...] = dot(full[0], every(1), FIRST)
 
@@ -213,17 +217,18 @@
 
     (sums,) = call(add_body, [shape((X, 2, half // X, features), bf16)], keep, swap(give, "core"))
     sums, pair = lax.optimization_barrier((sums, pair))
-    full = lax.all_gather(pair, "y", axis=1, tiled=True)
-    sums, full = lax.optimization_barrier((trade(sums, "x"), full))
+    side = (shift(pair, "y", 1), shift(pair, "y", 3))
+    sums, side = lax.optimization_barrier((trade(sums, "x"), side))
     (sums,) = call(sum_body, [shape((half // X, 2, features), bf16)], sums)
-    sums, mine = lax.optimization_barrier((sums, mine))
+    sums, mine, last = lax.optimization_barrier((sums, mine, pair))
     sums = trade(sums, FAR)
+    held = (pair, side[0], shift(last, "y", 2), side[1])
     theirs = [swap(piece, "core") for piece in (mine[: Y // 2], mine[Y // 2 :])]
 
     grad_w_in, grad_w_out = call(
         weight_body,
         [shape((width, hidden), f32), shape((hidden, width), f32)],
-        full, mine, *theirs, flops=work,
+        here, *held, mine, *theirs, flops=work,
     )
 
     sums, grad_w_in, grad_w_out = lax.optimization_barrier((sums, grad_w_in, grad_w_out))

time: 154 us -> 156 us (1.013)
  blocking collectives: 64.3 us -> 50.8 us
  starting transfers between devices: 51.7 us -> 60.2 us
  waiting for transfers between devices: 14 us -> 21.6 us
    ppermute x4 -> x7, waiting for transfers between devices: 4.82 us -> 19.3 us  [shift(): lax.ppermute(values, axis, [(at, (at + step) % count) for at in range(cou...]
    all_gather x1 -> x0, blocking collectives: 13.9 us -> none  [local(): full = lax.all_gather(pair, 'y', axis=1, tiled=True)]
    ppermute x4 -> x7, starting transfers between devices: 14.1 us -> 22.7 us  [shift(): lax.ppermute(values, axis, [(at, (at + step) % count) for at in range(cou...]
    all_to_all x4, waiting for transfers between devices: 5.63 us -> 0.01 us  [trade(): return lax.all_to_all(values, axis, split_axis=0, concat_axis=0, tiled=True)]
    unnamed x10 -> x14, local copies, waits for them, and re-layouts: 3.43 us -> 3.44 us
  transfers between devices with their start and end apart: 12 -> 15, of which waited for: 5 -> 6; matrix products, arithmetic and copies ran while one was open for 3% -> 2% of each run, Pallas kernels for 4% -> 4%
where the time goes in v14:
time: 156 us; the launch traced here: 155 us
  starting transfers between devices  60.2 us (39%)
  blocking collectives  50.8 us (33%)
  waiting for transfers between devices  21.6 us (14%)
  Pallas kernels  14.9 us (10%)
  local copies, waits for them, and re-layouts  6.25 us (4%)
    all_to_all x1, blocking collectives, trade(): return lax.all_to_all(values, axis, split_axis=0, concat_axis=0, tiled=True)  31.2 us
    all_to_all x4, starting transfers between devices, trade(): return lax.all_to_all(values, axis, split_axis=0, concat_axis=0, tiled=True)  29.3 us
    ppermute x7, starting transfers between devices, shift(): lax.ppermute(values, axis, [(at, (at + step) % count) for at in range(cou...  22.7 us
    all_gather x1, blocking collectives, local(): parts, mine = lax.optimization_barrier((lax.all_gather(parts, 'zh'), mine))  19.6 us
    ppermute x7, waiting for transfers between devices, shift(): lax.ppermute(values, axis, [(at, (at + step) % count) for at in range(cou...  19.3 us
    pallas_call x8, Pallas kernels, call(): pl.pallas_call(body, out_shape=shapes, in_specs=specs, out_specs=[pl.Bloc...  14.9 us
    ppermute x4, starting transfers between devices, swap(): return lax.ppermute(values, axis, [(0, 1), (1, 0)])  8.17 us
    unnamed x14, local copies, waits for them, and re-layouts  3.44 us
  transfers between devices with their start and end apart: 15, of which 6 were waited for; matrix products, arithmetic and copies ran while one was open for 2% of the time, Pallas kernels for 4%

profile of v14, /device:TPU:6, one launch (start us, length us, event | category | flops | bytes accessed | tf_op | source)
XLA Modules:
  0.0 154.6 jit_solution(15553791076816014239)
XLA Ops:
  0.6 2.6 %shard_map.75 = (bf16[16,2,3072]{2,1,0:T(2,128)(2,1)}, bf16[2,768,384]{2,1,0:T(8,128)(2,1)}) custom-call(bf16[1,6144]{1,0:T(2,128)(2,1)} %tokens.3, bf16[1,6144]{1,0:T(2,128)(2,1)} %cotangent.3, bf16[768,384]{1,0:T(8,128)(2,1)} %w_in.1, bf16[384,768]{1,0:T(8,128)(2,1)} %w_out.1), custom_call_target="tpu_custom_call" | custom-call | bytes 2580480 | tf_op jit(solution)/shard_map/pallas_call | solution.py:43
  3.2 3.5 %collective-permute-start.2 = (bf16[2,768,384]{2,1,0:T(8,128)(2,1)}, bf16[2,768,384]{2,1,0:T(8,128)(2,1)S(1)}, u32[]{:S(2)}, u32[]{:S(2)}) collective-permute-start(bf16[2,768,384]{2,1,0:T(8,128)(2,1)} %get-tuple-element.30.b0), channel_id=1, source_target_pairs={{0,64},{64,128},{128,192},{192,0},{1,65},{65,129},{129,193},{193,1... | collective-permute-start | bytes 3538952 | tf_op jit(solution)/shard_map/ppermute | solution.py:27
  6.7 3.6 %collective-permute-start.1 = (bf16[2,768,384]{2,1,0:T(8,128)(2,1)}, bf16[2,768,384]{2,1,0:T(8,128)(2,1)S(1)}, u32[]{:S(2)}, u32[]{:S(2)}) collective-permute-start(bf16[2,768,384]{2,1,0:T(8,128)(2,1)} %get-tuple-element.30.b0), channel_id=1, source_target_pairs={{0,192},{64,0},{128,64},{192,128},{1,193},{65,1},{129,65},{193,129... | collective-permute-start | bytes 3538952 | tf_op jit(solution)/shard_map/ppermute | solution.py:27
  10.3 31.2 %all_to_all.25 = bf16[16,2,3072]{2,1,0:T(2,128)(2,1)S(1)} all-to-all(bf16[16,2,3072]{2,1,0:T(2,128)(2,1)} %get-tuple-element.29), channel_id=1, replica_groups=mesh['zh'=2,'y'=4,'zl'=8,'x'=4,'core'=2] {'zh','zl'}, dimensions={0} | all-to-all | bytes 393216 | tf_op jit(solution)/shard_map/all_to_all | solution.py:31
  41.5 1.0 broadcast_in_dim.3
  42.5 4.8 %all-to-all-start.1 = ((bf16[4,2,16,3072]{3,2,1,0:T(8,128)(2,1)}), bf16[4,2,16,3072]{3,2,1,0:T(8,128)(2,1)}, u32[]{:S(2)}, u32[]{:S(2)}) async-start(bf16[4,2,16,3072]{3,2,1,0:T(8,128)(2,1)} %broadcast_in_dim.3), calls=%async_computation.1 | async-start | bytes 1572864 | tf_op jit(solution)/shard_map/all_to_all | solution.py:31
  47.3 0.0 collective-permute-done.2.b3
  47.3 0.9 slice_bitcast_fusion.1
  48.2 2.2 %collective-permute-start.3 = (bf16[768,384]{1,0:T(8,128)(2,1)}, bf16[768,384]{1,0:T(8,128)(2,1)}, u32[]{:S(2)}, u32[]{:S(2)}) collective-permute-start(bf16[768,384]{1,0:T(8,128)(2,1)} %slice_bitcast_fusion.1), channel_id=1, source_target_pairs={{0,64},{64,128},{128,192},{192,0},{1,65},{65,129},{129,193},{193,1... | collective-permute-start | bytes 1769480 | tf_op jit(solution)/shard_map/ppermute | solution.py:27
  50.4 0.0 collective-permute-done.1.b1
  50.4 0.9 slice_bitcast_fusion
  51.3 4.8 %collective-permute-start.4 = (bf16[768,384]{1,0:T(8,128)(2,1)}, bf16[768,384]{1,0:T(8,128)(2,1)}, u32[]{:S(2)}, u32[]{:S(2)}) collective-permute-start(bf16[768,384]{1,0:T(8,128)(2,1)} %slice_bitcast_fusion), channel_id=1, source_target_pairs={{0,192},{64,0},{128,64},{192,128},{1,193},{65,1},{129,65},{193,129... | collective-permute-start | bytes 1769480 | tf_op jit(solution)/shard_map/ppermute | solution.py:27
  56.1 0.0 all-to-all-done.1.rows
  56.1 1.9 %collective-permute-start = (bf16[4,2,16,3072]{3,2,1,0:T(8,128)(2,1)}, bf16[4,2,16,3072]{3,2,1,0:T(8,128)(2,1)}, u32[]{:S(2)}, u32[]{:S(2)}) collective-permute-start(bf16[4,2,16,3072]{3,2,1,0:T(8,128)(2,1)} %all-to-all-done.1.rows), channel_id=1, source_target_pairs={{0,1},{1,0},{2,3},{3,2},{4,5},{5,4},{6,7},{7,6},{8,9},{9,8},{10,11... | collective-permute-start | bytes 2359304 | tf_op jit(solution)/shard_map/ppermute | solution.py:22
  58.0 1.2 shard_map.76
  59.2 0.0 copy-start.2
  59.2 0.9 copy-done.2
  60.1 1.7 %collective-permute-done.3.far_in = bf16[768,384]{1,0:T(8,128)(2,1)} collective-permute-done((bf16[768,384]{1,0:T(8,128)(2,1)}, bf16[768,384]{1,0:T(8,128)(2,1)}, u32[]{:S(2)}, u32[]{:S(2)}) %collective-permute-start.3) | collective-permute-done | bytes 589856 | tf_op jit(solution)/shard_map/ppermute | solution.py:27
  61.8 2.1 %collective-permute-done.4.far_out = bf16[768,384]{1,0:T(8,128)(2,1)} collective-permute-done((bf16[768,384]{1,0:T(8,128)(2,1)}, bf16[768,384]{1,0:T(8,128)(2,1)}, u32[]{:S(2)}, u32[]{:S(2)}) %collective-permute-start.4) | collective-permute-done | bytes 589856 | tf_op jit(solution)/shard_map/ppermute | solution.py:27
  63.9 5.0 %all-to-all-start.2 = ((bf16[4,2,64,768]{3,2,1,0:T(8,128)(2,1)}), bf16[4,2,64,768]{3,2,1,0:T(8,128)(2,1)S(1)}, u32[]{:S(2)}, u32[]{:S(2)}) async-start(bf16[4,2,64,768]{3,2,1,0:T(8,128)(2,1)} %copy-done.2), calls=%async_computation.2 | async-start | bytes 1572864 | tf_op jit(solution)/shard_map/all_to_all | solution.py:31
  68.8 0.0 collective-permute-done.other
  68.8 0.0 copy-start
  68.8 1.3 copy-done
  70.1 3.1 %shard_map.77 = bf16[2,128,384]{2,1,0:T(8,128)(2,1)S(1)} custom-call(s32[1]{0:T(128)} %bitcast.here, bf16[4,2,16,3072]{3,2,1,0:T(8,128)(2,1)} %all-to-all-done.1.rows, bf16[4,2,16,3072]{3,2,1,0:T(8,128)(2,1)} %collective-permute-done.other, bf16[2,768,384]{2,1,0:T(8,128)(2,1)S(1)} %copy-done, bf16[2,768,384]{2,1,0:T(8,128)(2,1)S(1)} %collective-permute-done.1.b1, ...), custom_call_target="tpu_custom_call" | custom-call | flops 603979776 | bytes 6488068 | tf_op jit(solution)/shard_map/pallas_call | solution.py:43
  73.2 19.6 %all-gather = bf16[4,128,384]{2,1,0:T(8,128)(2,1)S(1)} all-gather(bf16[2,128,384]{2,1,0:T(8,128)(2,1)S(1)} %shard_map.77), channel_id=2, replica_groups=mesh['zh'=2,'y'=4,'zl'=8,'x'=4,'core'=2] {'zh'}, dimensions={0}, use_global_device_ids=true | all-gather | bytes 589824 | tf_op jit(solution)/shard_map/all_gather | solution.py:211
  92.8 0.0 all-to-all-done.2.mine
  92.8 0.0 copy-start.1
  92.8 1.3 copy-done.1
  94.1 2.7 %shard_map.78 = (bf16[2,128,384]{2,1,0:T(8,128)(2,1)S(1)}, f32[2,64,3072]{2,1,0:T(8,128)S(1)}, bf16[2,64,3072]{2,1,0:T(8,128)(2,1)S(1)}) custom-call(s32[1]{0:T(128)} %bitcast.here, bf16[2,2,128,384]{3,2,1,0:T(8,128)(2,1)S(1)} %bitcast.7, bf16[2,768,384]{2,1,0:T(8,128)(2,1)S(1)} %copy-done.1, bf16[2,768,384]{2,1,0:T(8,128)(2,1)S(1)} %collective-permute-done.1.b1, ...), custom_call_target="tpu_custom_call" | custom-call | flops 603979776 | bytes 7667716 | tf_op jit(solution)/shard_map/pallas_call | solution.py:43
  96.7 0.0 copy-start.3
  96.7 1.9 %collective-permute-start.5 = (bf16[2,64,3072]{2,1,0:T(8,128)(2,1)S(1)}, bf16[2,64,3072]{2,1,0:T(8,128)(2,1)S(1)}, u32[]{:S(2)}, u32[]{:S(2)}) collective-permute-start(bf16[2,64,3072]{2,1,0:T(8,128)(2,1)S(1)} %get-tuple-element.36), channel_id=1, source_target_pairs={{0,1},{1,0},{2,3},{3,2},{4,5},{5,4},{6,7},{7,6},{8,9},{9,8},{10,11... | collective-permute-start | bytes 2359304 | tf_op jit(solution)/shard_map/ppermute | solution.py:22
  98.7 2.3 %collective-permute-done.5.far = bf16[2,64,3072]{2,1,0:T(8,128)(2,1)S(1)} collective-permute-done((bf16[2,64,3072]{2,1,0:T(8,128)(2,1)S(1)}, bf16[2,64,3072]{2,1,0:T(8,128)(2,1)S(1)}, u32[]{:S(2)}, u32[]{:S(2)}) %collective-permute-start.5) | collective-permute-done | bytes 786464 | tf_op jit(solution)/shard_map/ppermute | solution.py:22
  100.9 1.0 shard_map.79
  102.0 0.0 copy-done.3
  102.0 0.0 copy-start.4
  102.0 4.9 %all-to-all-start.3 = ((bf16[4,2,16,3072]{3,2,1,0:T(8,128)(2,1)}), bf16[4,2,16,3072]{3,2,1,0:T(8,128)(2,1)S(1)}, u32[]{:S(2)}, u32[]{:S(2)}) async-start(bf16[4,2,16,3072]{3,2,1,0:T(8,128)(2,1)} %shard_map.79), calls=%async_computation.3 | async-start | bytes 1572864 | tf_op jit(solution)/shard_map/all_to_all | solution.py:31
  106.9 0.0 copy-done.4
  106.9 4.8 %collective-permute-start.7 = (bf16[2,128,384]{2,1,0:T(8,128)(2,1)S(1)}, bf16[2,128,384]{2,1,0:T(8,128)(2,1)S(1)}, u32[]{:S(2)}, u32[]{:S(2)}) collective-permute-start(bf16[2,128,384]{2,1,0:T(8,128)(2,1)S(1)} %copy-done.4), channel_id=1, source_target_pairs={{0,192},{64,0},{128,64},{192,128},{1,193},{65,1},{129,65},{193,129... | collective-permute-start | bytes 589832 | tf_op jit(solution)/shard_map/ppermute | solution.py:27
  111.7 1.9 %collective-permute-start.6 = (bf16[2,128,384]{2,1,0:T(8,128)(2,1)S(1)}, bf16[2,128,384]{2,1,0:T(8,128)(2,1)S(1)}, u32[]{:S(2)}, u32[]{:S(2)}) collective-permute-start(bf16[2,128,384]{2,1,0:T(8,128)(2,1)S(1)} %copy-done.4), channel_id=1, source_target_pairs={{0,64},{64,128},{128,192},{192,0},{1,65},{65,129},{129,193},{193,1... | collective-permute-start | bytes 589832 | tf_op jit(solution)/shard_map/ppermute | solution.py:27
  113.7 2.0 %collective-permute-done.7.p3 = bf16[2,128,384]{2,1,0:T(8,128)(2,1)S(1)} collective-permute-done((bf16[2,128,384]{2,1,0:T(8,128)(2,1)S(1)}, bf16[2,128,384]{2,1,0:T(8,128)(2,1)S(1)}, u32[]{:S(2)}, u32[]{:S(2)}) %collective-permute-start.7) | collective-permute-done | bytes 196640 | tf_op jit(solution)/shard_map/ppermute | solution.py:27
  115.6 5.3 %collective-permute-done.6.p1 = bf16[2,128,384]{2,1,0:T(8,128)(2,1)S(1)} collective-permute-done((bf16[2,128,384]{2,1,0:T(8,128)(2,1)S(1)}, bf16[2,128,384]{2,1,0:T(8,128)(2,1)S(1)}, u32[]{:S(2)}, u32[]{:S(2)}) %collective-permute-start.6) | collective-permute-done | bytes 196640 | tf_op jit(solution)/shard_map/ppermute | solution.py:27
  120.9 0.0 all-to-all-done.3.parts
  120.9 1.0 shard_map.80
  121.9 14.7 %all-to-all-start.4 = ((bf16[16,2,3072]{2,1,0:T(2,128)(2,1)}), bf16[16,2,3072]{2,1,0:T(2,128)(2,1)S(1)}, u32[]{:S(2)}, u32[]{:S(2)}) async-start(bf16[16,2,3072]{2,1,0:T(2,128)(2,1)} %shard_map.80), calls=%async_computation.4 | async-start | bytes 393216 | tf_op jit(solution)/shard_map/all_to_all | solution.py:31
  136.6 0.1 fusion
  136.7 1.9 %collective-permute-start.10 = (bf16[2,2,64,768]{3,2,1,0:T(8,128)(2,1)S(1)}, bf16[2,2,64,768]{3,2,1,0:T(8,128)(2,1)S(1)}, u32[]{:S(2)}, u32[]{:S(2)}) collective-permute-start(bf16[2,2,64,768]{3,2,1,0:T(8,128)(2,1)S(1)} %get-tuple-element.54), channel_id=1, source_target_pairs={{0,1},{1,0},{2,3},{3,2},{4,5},{5,4},{6,7},{7,6},{8,9},{9,8},{10,11... | collective-permute-start | bytes 1179656 | tf_op jit(solution)/shard_map/ppermute | solution.py:22
  138.6 0.0 copy-start.5
  138.6 0.0 copy-start.6
  138.6 2.4 %collective-permute-start.9 = (bf16[2,2,64,768]{3,2,1,0:T(8,128)(2,1)S(1)}, bf16[2,2,64,768]{3,2,1,0:T(8,128)(2,1)S(1)}, u32[]{:S(2)}, u32[]{:S(2)}) collective-permute-start(bf16[2,2,64,768]{3,2,1,0:T(8,128)(2,1)S(1)} %get-tuple-element.55), channel_id=1, source_target_pairs={{0,1},{1,0},{2,3},{3,2},{4,5},{5,4},{6,7},{7,6},{8,9},{9,8},{10,11... | collective-permute-start | bytes 1179656 | tf_op jit(solution)/shard_map/ppermute | solution.py:22
  141.1 1.9 %collective-permute-start.8 = (bf16[2,128,384]{2,1,0:T(8,128)(2,1)S(1)}, bf16[2,128,384]{2,1,0:T(8,128)(2,1)S(1)}, u32[]{:S(2)}, u32[]{:S(2)}) collective-permute-start(bf16[2,128,384]{2,1,0:T(8,128)(2,1)S(1)} %copy-done.4), channel_id=1, source_target_pairs={{0,128},{64,192},{128,0},{192,64},{1,129},{65,193},{129,1},{193,65... | collective-permute-start | bytes 589832 | tf_op jit(solution)/shard_map/ppermute | solution.py:27
  143.0 8.3 %collective-permute-done.8.p2 = bf16[2,128,384]{2,1,0:T(8,128)(2,1)S(1)} collective-permute-done((bf16[2,128,384]{2,1,0:T(8,128)(2,1)S(1)}, bf16[2,128,384]{2,1,0:T(8,128)(2,1)S(1)}, u32[]{:S(2)}, u32[]{:S(2)}) %collective-permute-start.8) | collective-permute-done | bytes 196640 | tf_op jit(solution)/shard_map/ppermute | solution.py:27
  151.3 0.0 collective-permute-done.10.second
  151.3 0.0 collective-permute-done.9.first
  151.3 2.2 %shard_map.81 = (f32[768,384]{1,0:T(8,128)}, f32[384,768]{1,0:T(8,128)}) custom-call(s32[1]{0:T(128)} %bitcast.here, bf16[2,128,384]{2,1,0:T(8,128)(2,1)S(1)} %copy-done.4, bf16[2,128,384]{2,1,0:T(8,128)(2,1)S(1)} %collective-permute-done.6.p1, bf16[2,128,384]{2,1,0:T(8,128)(2,1)S(1)} %collective-permute-done.8.p2, ...), custom_call_target="tpu_custom_call" | custom-call | flops 603979776 | bytes 4718596 | tf_op jit(solution)/shard_map/pallas_call | solution.py:43
  153.4 0.0 all-to-all-done.4.sums
  153.4 0.0 copy-done.5
  153.4 0.0 copy-done.6
  153.5 1.2 shard_map.82
  (1 shorter events, 0.0 us)
Async XLA Ops:
  3.2 44.0 %collective-permute-start.2 = (bf16[2,768,384]{2,1,0:T(8,128)(2,1)}, bf16[2,768,384]{2,1,0:T(8,128)(2,1)S(1)}, u32[]{:S(2)}, u32[]{:S(2)}) collective-permute-start(bf16[2,768,384]{2,1,0:T(8,128)(2,1)} %get-tuple-element.30.b0), channel_id=1, source_target_pairs={{0,64},{64,128},{128,192},{192,0},{1,65},{65,129},{129,193},{193,1... | collective-permute-start | bytes 3538952 | tf_op jit(solution)/shard_map/ppermute | solution.py:27
  6.7 43.7 %collective-permute-start.1 = (bf16[2,768,384]{2,1,0:T(8,128)(2,1)}, bf16[2,768,384]{2,1,0:T(8,128)(2,1)S(1)}, u32[]{:S(2)}, u32[]{:S(2)}) collective-permute-start(bf16[2,768,384]{2,1,0:T(8,128)(2,1)} %get-tuple-element.30.b0), channel_id=1, source_target_pairs={{0,192},{64,0},{128,64},{192,128},{1,193},{65,1},{129,65},{193,129... | collective-permute-start | bytes 3538952 | tf_op jit(solution)/shard_map/ppermute | solution.py:27
  42.5 13.6 %all-to-all-start.1 = ((bf16[4,2,16,3072]{3,2,1,0:T(8,128)(2,1)}), bf16[4,2,16,3072]{3,2,1,0:T(8,128)(2,1)}, u32[]{:S(2)}, u32[]{:S(2)}) async-start(bf16[4,2,16,3072]{3,2,1,0:T(8,128)(2,1)} %broadcast_in_dim.3), calls=%async_computation.1 | async-start | bytes 1572864 | tf_op jit(solution)/shard_map/all_to_all | solution.py:31
  48.2 13.6 %collective-permute-start.3 = (bf16[768,384]{1,0:T(8,128)(2,1)}, bf16[768,384]{1,0:T(8,128)(2,1)}, u32[]{:S(2)}, u32[]{:S(2)}) collective-permute-start(bf16[768,384]{1,0:T(8,128)(2,1)} %slice_bitcast_fusion.1), channel_id=1, source_target_pairs={{0,64},{64,128},{128,192},{192,0},{1,65},{65,129},{129,193},{193,1... | collective-permute-start | bytes 1769480 | tf_op jit(solution)/shard_map/ppermute | solution.py:27
  51.3 12.6 %collective-permute-start.4 = (bf16[768,384]{1,0:T(8,128)(2,1)}, bf16[768,384]{1,0:T(8,128)(2,1)}, u32[]{:S(2)}, u32[]{:S(2)}) collective-permute-start(bf16[768,384]{1,0:T(8,128)(2,1)} %slice_bitcast_fusion), channel_id=1, source_target_pairs={{0,192},{64,0},{128,64},{192,128},{1,193},{65,1},{129,65},{193,129... | collective-permute-start | bytes 1769480 | tf_op jit(solution)/shard_map/ppermute | solution.py:27
  56.1 12.7 %collective-permute-start = (bf16[4,2,16,3072]{3,2,1,0:T(8,128)(2,1)}, bf16[4,2,16,3072]{3,2,1,0:T(8,128)(2,1)}, u32[]{:S(2)}, u32[]{:S(2)}) collective-permute-start(bf16[4,2,16,3072]{3,2,1,0:T(8,128)(2,1)} %all-to-all-done.1.rows), channel_id=1, source_target_pairs={{0,1},{1,0},{2,3},{3,2},{4,5},{5,4},{6,7},{7,6},{8,9},{9,8},{10,11... | collective-permute-start | bytes 2359304 | tf_op jit(solution)/shard_map/ppermute | solution.py:22
  59.2 0.9 copy-start.2
  63.9 28.9 %all-to-all-start.2 = ((bf16[4,2,64,768]{3,2,1,0:T(8,128)(2,1)}), bf16[4,2,64,768]{3,2,1,0:T(8,128)(2,1)S(1)}, u32[]{:S(2)}, u32[]{:S(2)}) async-start(bf16[4,2,64,768]{3,2,1,0:T(8,128)(2,1)} %copy-done.2), calls=%async_computation.2 | async-start | bytes 1572864 | tf_op jit(solution)/shard_map/all_to_all | solution.py:31
  68.8 1.3 copy-start
  92.8 1.3 copy-start.1
  96.7 5.2 %copy-start.3 = (bf16[2,128,384]{2,1,0:T(8,128)(2,1)}, bf16[2,128,384]{2,1,0:T(8,128)(2,1)S(1)}, u32[]{:S(2)}) copy-start(bf16[2,128,384]{2,1,0:T(8,128)(2,1)S(1)} %get-tuple-element.44.p0) | copy-start | bytes 589828
  96.7 4.2 %collective-permute-start.5 = (bf16[2,64,3072]{2,1,0:T(8,128)(2,1)S(1)}, bf16[2,64,3072]{2,1,0:T(8,128)(2,1)S(1)}, u32[]{:S(2)}, u32[]{:S(2)}) collective-permute-start(bf16[2,64,3072]{2,1,0:T(8,128)(2,1)S(1)} %get-tuple-element.36), channel_id=1, source_target_pairs={{0,1},{1,0},{2,3},{3,2},{4,5},{5,4},{6,7},{7,6},{8,9},{9,8},{10,11... | collective-permute-start | bytes 2359304 | tf_op jit(solution)/shard_map/ppermute | solution.py:22
  102.0 4.9 %copy-start.4 = (bf16[2,128,384]{2,1,0:T(8,128)(2,1)S(1)}, bf16[2,128,384]{2,1,0:T(8,128)(2,1)}, u32[]{:S(2)}) copy-start(bf16[2,128,384]{2,1,0:T(8,128)(2,1)} %copy-done.3) | copy-start | bytes 589828
  102.0 19.0 %all-to-all-start.3 = ((bf16[4,2,16,3072]{3,2,1,0:T(8,128)(2,1)}), bf16[4,2,16,3072]{3,2,1,0:T(8,128)(2,1)S(1)}, u32[]{:S(2)}, u32[]{:S(2)}) async-start(bf16[4,2,16,3072]{3,2,1,0:T(8,128)(2,1)} %shard_map.79), calls=%async_computation.3 | async-start | bytes 1572864 | tf_op jit(solution)/shard_map/all_to_all | solution.py:31
  106.9 8.7 %collective-permute-start.7 = (bf16[2,128,384]{2,1,0:T(8,128)(2,1)S(1)}, bf16[2,128,384]{2,1,0:T(8,128)(2,1)S(1)}, u32[]{:S(2)}, u32[]{:S(2)}) collective-permute-start(bf16[2,128,384]{2,1,0:T(8,128)(2,1)S(1)} %copy-done.4), channel_id=1, source_target_pairs={{0,192},{64,0},{128,64},{192,128},{1,193},{65,1},{129,65},{193,129... | collective-permute-start | bytes 589832 | tf_op jit(solution)/shard_map/ppermute | solution.py:27
  111.7 9.2 %collective-permute-start.6 = (bf16[2,128,384]{2,1,0:T(8,128)(2,1)S(1)}, bf16[2,128,384]{2,1,0:T(8,128)(2,1)S(1)}, u32[]{:S(2)}, u32[]{:S(2)}) collective-permute-start(bf16[2,128,384]{2,1,0:T(8,128)(2,1)S(1)} %copy-done.4), channel_id=1, source_target_pairs={{0,64},{64,128},{128,192},{192,0},{1,65},{65,129},{129,193},{193,1... | collective-permute-start | bytes 589832 | tf_op jit(solution)/shard_map/ppermute | solution.py:27
  121.9 31.5 %all-to-all-start.4 = ((bf16[16,2,3072]{2,1,0:T(2,128)(2,1)}), bf16[16,2,3072]{2,1,0:T(2,128)(2,1)S(1)}, u32[]{:S(2)}, u32[]{:S(2)}) async-start(bf16[16,2,3072]{2,1,0:T(2,128)(2,1)} %shard_map.80), calls=%async_computation.4 | async-start | bytes 393216 | tf_op jit(solution)/shard_map/all_to_all | solution.py:31
  136.7 14.6 %collective-permute-start.10 = (bf16[2,2,64,768]{3,2,1,0:T(8,128)(2,1)S(1)}, bf16[2,2,64,768]{3,2,1,0:T(8,128)(2,1)S(1)}, u32[]{:S(2)}, u32[]{:S(2)}) collective-permute-start(bf16[2,2,64,768]{3,2,1,0:T(8,128)(2,1)S(1)} %get-tuple-element.54), channel_id=1, source_target_pairs={{0,1},{1,0},{2,3},{3,2},{4,5},{5,4},{6,7},{7,6},{8,9},{9,8},{10,11... | collective-permute-start | bytes 1179656 | tf_op jit(solution)/shard_map/ppermute | solution.py:22
  138.6 14.8 %copy-start.5 = (bf16[1,6144]{1,0:T(2,128)(2,1)S(1)}, bf16[1,6144]{1,0:T(2,128)(2,1)}, u32[]{:S(2)}) copy-start(bf16[1,6144]{1,0:T(2,128)(2,1)} %tokens.3) | copy-start | bytes 36868
  138.6 14.8 %copy-start.6 = (bf16[1,6144]{1,0:T(2,128)(2,1)S(1)}, bf16[1,6144]{1,0:T(2,128)(2,1)}, u32[]{:S(2)}) copy-start(bf16[1,6144]{1,0:T(2,128)(2,1)} %cotangent.3) | copy-start | bytes 36868
  138.6 12.6 %collective-permute-start.9 = (bf16[2,2,64,768]{3,2,1,0:T(8,128)(2,1)S(1)}, bf16[2,2,64,768]{3,2,1,0:T(8,128)(2,1)S(1)}, u32[]{:S(2)}, u32[]{:S(2)}) collective-permute-start(bf16[2,2,64,768]{3,2,1,0:T(8,128)(2,1)S(1)} %get-tuple-element.55), channel_id=1, source_target_pairs={{0,1},{1,0},{2,3},{3,2},{4,5},{5,4},{6,7},{7,6},{8,9},{9,8},{10,11... | collective-permute-start | bytes 1179656 | tf_op jit(solution)/shard_map/ppermute | solution.py:22
  141.1 10.2 %collective-permute-start.8 = (bf16[2,128,384]{2,1,0:T(8,128)(2,1)S(1)}, bf16[2,128,384]{2,1,0:T(8,128)(2,1)S(1)}, u32[]{:S(2)}, u32[]{:S(2)}) collective-permute-start(bf16[2,128,384]{2,1,0:T(8,128)(2,1)S(1)} %copy-done.4), channel_id=1, source_target_pairs={{0,128},{64,192},{128,0},{192,64},{1,129},{65,193},{129,1},{193,65... | collective-permute-start | bytes 589832 | tf_op jit(solution)/shard_map/ppermute | solution.py:27
